TPU v7x, 256 devices: a whole 4x4x8 slice. The times are simulated.
256 devices in a mesh: rows: 32 (over x, y, core), grp: 8 (over z).
Axes of the slice: x: 4, y: 4, z: 8, core: 2. Of those that a mesh axis runs over, the one named last changes fastest.
Arguments:
- pivot_columns: bfloat16 [128, 10240, 256], P('rows', 'grp'), may hold values from -6 to 6
- previous: bfloat16 [128, 10240, 512], P('rows', 'grp'), may hold values from -0.59765625 to 0.59765625
- pivots: int32 [256], replicated, may hold values from 0 to 1310719, as said below
- pivot_inverse: bfloat16 [256, 256], replicated, may hold values from -0.4 to 1.5
- orbitals: bfloat16 [10240, 1024], P('grp'), may hold values from -0.0625 to 0.0625
- slab_orbitals: bfloat16 [128, 1024], replicated, may hold values from -0.5 to 0.5
Outputs:
- new_vectors: bfloat16 [128, 10240, 256], P('rows', 'grp')
- mo_block: bfloat16 [256, 1024, 1024], P('rows', None, 'grp')
Inputs may be any that keep to these rules, and one draw needn't show every extreme that they name: `pivots`: distinct entries.
All inputs are finite; a program needn't handle non-finite values.
Results may differ from a plain program's by a relative error of at most 0.0038.
The roundings to bfloat16 on the way count: a program that leaves them out, or rounds other values in their place, can miss the bound.
Values may be sent and summed in bfloat16 or wider, within the bound.
No kernel may reach another device: no remote copies, remote signals or barrier semaphores. Data moves between devices by JAX's collectives and lax.ppermute only.
A program may use at most 64 MiB of HBM per device.

v0:
```python
import jax
import jax.numpy as jnp
from jax import lax
from jax.sharding import PartitionSpec as P

NBAS = 10240


def per_device(pivot_columns, previous, pivots, pivot_inverse, orbitals, slab_orbitals):
    mu_dev, nu_dev, prev_count = previous.shape
    pivot_count = pivot_columns.shape[2]
    row_index = lax.axis_index("rows")
    grp_index = lax.axis_index("grp")
    first_local = pivots // NBAS - row_index * mu_dev
    second_local = pivots % NBAS - grp_index * nu_dev
    owned = (
        (first_local >= 0) & (first_local < mu_dev) & (second_local >= 0) & (second_local < nu_dev)
    )
    local_row = jnp.where(owned, first_local * nu_dev + second_local, 0)
    flat_prev = previous.reshape(mu_dev * nu_dev, prev_count)
    picked = jnp.where(
        owned[:, None], jnp.take(flat_prev, local_row, axis=0).astype(jnp.float32), 0.0
    )
    pivot_rows = lax.psum(picked, ("rows", "grp")).astype(jnp.bfloat16)
    correction = jnp.dot(flat_prev, pivot_rows.T, preferred_element_type=jnp.float32)
    flat_columns = pivot_columns.reshape(mu_dev * nu_dev, pivot_count)
    residual_columns = (flat_columns.astype(jnp.float32) - correction).astype(jnp.bfloat16)
    upper = jnp.triu(pivot_inverse)
    new_flat = jnp.dot(residual_columns, upper, preferred_element_type=jnp.float32).astype(
        jnp.bfloat16
    )
    new_vectors = new_flat.reshape(mu_dev, nu_dev, pivot_count)
    half = lax.psum_scatter(
        jnp.einsum("nj,mnp->jmp", orbitals, new_vectors, preferred_element_type=jnp.float32),
        "grp",
        scatter_dimension=0,
        tiled=True,
    ).astype(jnp.bfloat16)
    summed = jnp.einsum(
        "mi,jmp->pij",
        slab_orbitals,
        lax.all_to_all(half, "rows", split_axis=2, concat_axis=1, tiled=True),
        preferred_element_type=jnp.float32,
    )
    mo_block = summed.astype(jnp.bfloat16)
    return (new_vectors, mo_block)


def solution(mesh):
    in_specs = (P("rows", "grp", None), P("rows", "grp", None), P(), P(), P("grp", None), P())
    out_specs = (P("rows", "grp", None), P("rows", None, "grp"))
    return jax.shard_map(
        per_device, mesh=mesh, in_specs=in_specs, out_specs=out_specs, check_vma=False
    )
```

profile of v0, /device:TPU:1, one launch (start us, length us, event | category | flops | bytes accessed | tf_op | source)
XLA Modules:
  0.0 203.1 jit_solution(7495050297349627063)
XLA Ops:
  7.2 0.0 copy-start
  7.2 0.0 reduce-scatter.2.cloned.1.call-start
  7.2 4.6 %bitcast_convert_fusion = f32[5120,256]{1,0:T(8,128)} fusion(bf16[4,1280,256]{2,1,0:T(8,128)(2,1)} %param.6), kind=kLoop, calls=%fused_computation.5 | loop fusion | flops 1310720 | bytes 7864320 | tf_op jit(solution)/shard_map/convert_element_type | solution.py:27
  11.8 0.0 copy-start.3
  11.8 0.0 copy-start.2
  11.8 5.9 %copy.28 = f32[5120,256]{0,1:T(8,128)} copy(f32[5120,256]{1,0:T(8,128)} %bitcast_convert_fusion) | data formatting | bytes 10485760 | tf_op jit(solution)/shard_map/convert_element_type | solution.py:27
  17.8 0.0 copy-done.3
  17.8 4.4 %gather_fusion = bf16[256,512]{1,0:T(8,128)(2,1)S(1)} fusion(bf16[5120,512]{1,0:T(8,128)(2,1)} %bitcast.34, s32[1024]{0:T(1024)S(1)} %pad_clamp_fusion), kind=kCustom, calls=%fused_computation | custom fusion | bytes 525312 | tf_op jit(solution)/shard_map/jit(_take)/gather | solution.py:22
  22.2 0.1 convert_select_fusion
  22.4 83.7 %all-reduce.1 = bf16[256,512]{1,0:T(8,128)(2,1)S(1)} all-reduce(f32[256,512]{1,0:T(8,128)S(1)} %convert_select_fusion), channel_id=1, replica_groups=mesh['rows'=32,'grp'=8] {'rows','grp'}, use_global_device_ids=true, to_apply=%region_0.1 | all-reduce | flops 131072 | bytes 786432 | tf_op jit(solution)/shard_map/psum | solution.py:24
  106.1 0.0 copy-done.2
  106.1 7.8 %convolution_convert_fusion = bf16[5120,256]{1,0:T(8,128)(2,1)} fusion(f32[5120,256]{0,1:T(8,128)} %copy.28, bf16[5120,512]{1,0:T(8,128)(2,1)} %bitcast.35, bf16[256,512]{1,0:T(8,128)(2,1)S(1)} %all-reduce.1, bf16[256,256]{1,0:T(8,128)(2,1)S(1)} %copy-done.2, s32[256]{0:T(256)S(1)} %iota_add_fusion), kind=kOutput, calls=%fused_computation.4 | convolution fusion | flops 2017329152 | bytes 13501440 | tf_op jit(solution)/shard_map/dot_general | solution.py:29
  113.9 0.0 copy-done
  113.9 6.2 %fusion.4 = f32[1024,4,256]{0,2,1:T(8,128)} fusion(bf16[4,1280,256]{2,1,0:T(8,128)(2,1)} %bitcast.36, bf16[1280,1024]{1,0:T(8,128)(2,1)S(1)} %copy-done), kind=kOutput, calls=%fused_computation.8 | convolution fusion | flops 2684354560 | bytes 9437184 | tf_op jit(solution)/shard_map/nj,mnp->jmp/dot_general | solution.py:34
  120.1 0.0 copy-start.1
  120.1 0.0 reduce-scatter.2.cloned.1.call-update
  120.1 52.4 %reduce-scatter.2.cloned.1.call-done = f32[128,4,256]{0,2,1:T(8,128)} async-done(((f32[1024,4,256]{0,2,1:T(8,128)}), f32[128,4,256]{0,2,1:T(8,128)}) %reduce-scatter.2.cloned.1.call-update) | async-done | bytes 524304 | tf_op jit(solution)/shard_map/reduce_scatter | solution.py:33
  172.5 1.1 convert_element_type.33
  173.6 0.2 copy.22
  173.8 16.3 %all_to_all.18 = bf16[128,4,256]{0,1,2:T(4,128)(2,1)S(1)} all-to-all(bf16[128,4,256]{0,1,2:T(4,128)(2,1)S(1)} %copy.22), channel_id=1, replica_groups=mesh['rows'=32,'grp'=8] {'rows'}, dimensions={2} | all-to-all | bytes 524288 | tf_op jit(solution)/shard_map/all_to_all | solution.py:42
  190.2 0.0 copy-done.1
  190.2 2.1 %convert_bitcast_fusion = bf16[8,1024,128]{1,2,0:T(8,128)(2,1)} fusion(bf16[128,1024]{1,0:T(8,128)(2,1)S(1)} %copy-done.1, bf16[128,128,8]{0,2,1:T(8,128)(2,1)S(1)} %bitcast.38), kind=kOutput, calls=%fused_computation.9 | convolution fusion | flops 269484032 | bytes 2621440 | tf_op jit(solution)/shard_map/mi,jmp->pij/dot_general | solution.py:39
  192.3 3.9 %copy.26 = bf16[8,1024,128]{2,1,0:T(8,128)(2,1)} copy(bf16[8,1024,128]{1,2,0:T(8,128)(2,1)} %convert_bitcast_fusion) | data formatting | bytes 4194304
  (5 shorter events, 0.1 us)
Async XLA Ops:
  7.2 106.7 %copy-start = (bf16[1280,1024]{1,0:T(8,128)(2,1)S(1)}, bf16[1280,1024]{1,0:T(8,128)(2,1)}, u32[]{:S(2)}) copy-start(bf16[1280,1024]{1,0:T(8,128)(2,1)} %param.10) | copy-start | bytes 7864324
  7.2 165.4 %reduce-scatter.2.cloned.1.call-start = ((), (), s32[]{:S(2)}) async-start(), calls=%async_computation.2 | async-start | bytes 4718592 | tf_op jit(solution)/shard_map/reduce_scatter | solution.py:33
  11.8 6.0 %copy-start.3 = (s32[256]{0:T(256)S(1)}, s32[256]{0:T(256)}, u32[]{:S(2)}) copy-start(s32[256]{0:T(256)} %param.8) | copy-start | bytes 3076
  11.8 94.3 %copy-start.2 = (bf16[256,256]{1,0:T(8,128)(2,1)S(1)}, bf16[256,256]{1,0:T(8,128)(2,1)}, u32[]{:S(2)}) copy-start(bf16[256,256]{1,0:T(8,128)(2,1)} %param.9) | copy-start | bytes 393220
  120.1 70.1 %copy-start.1 = (bf16[128,1024]{1,0:T(8,128)(2,1)S(1)}, bf16[128,1024]{1,0:T(8,128)(2,1)}, u32[]{:S(2)}) copy-start(bf16[128,1024]{1,0:T(8,128)(2,1)} %param.11) | copy-start | bytes 786436
Sparse Core Ops, SparseCore 0:
  120.2 52.2 reduce-scatter.1
where the time goes:
time: 204 us; the launch traced here: 203 us
  blocking collectives  100 us (49%)
  waiting for transfers between devices  52.5 us (26%)
  matrix products  16.1 us (8%)
  local copies, waits for them, and re-layouts  14.5 us (7%)
  between operations  14.1 us (7%)
  other arithmetic  5.85 us (3%)
    psum x1, blocking collectives, per_device(): pivot_rows = lax.psum(picked, ('rows', 'grp')).astype(jnp.bfloat16)  83.7 us
    reduce_scatter x1, waiting for transfers between devices, per_device(): lax.psum_scatter(jnp.einsum('nj,mnp->jmp', orbitals, new_vectors, preferr...  52.4 us
    all_to_all x1, blocking collectives, per_device(): lax.all_to_all(half, 'rows', split_axis=2, concat_axis=1, tiled=True)  16.3 us
    dot_general x1, matrix products, per_device(): jnp.dot(residual_columns, upper, preferred_element_type=jnp.float32)  7.8 us
    dot_general x1, matrix products, per_device(): jnp.einsum('nj,mnp->jmp', orbitals, new_vectors, preferred_element_type=j...  6.18 us
    convert_element_type x1, local copies, waits for them, and re-layouts, per_device(): flat_columns.astype(jnp.float32) - correction  5.94 us
    convert_element_type x1, other arithmetic, per_device(): flat_columns.astype(jnp.float32) - correction  4.6 us
    gather x1, local copies, waits for them, and re-layouts, per_device(): jnp.take(flat_prev, local_row, axis=0).astype(jnp.float32)  4.37 us
  transfers between devices with their start and end apart: 1, of which 1 were waited for; matrix products, arithmetic and copies ran while one was open for 0% of the time, Pallas kernels for 0%

commit v1 on v0

v1 whole, which is shorter than its diff:
```python
import functools

import jax
import jax.numpy as jnp
from jax import lax
from jax.experimental import pallas as pl
from jax.experimental.pallas import tpu as pltpu
from jax.sharding import PartitionSpec as P

NBAS = 10240
F32 = jnp.float32
BF16 = jnp.bfloat16


def pick_kernel(base_ref, piv_ref, prev_ref, out_ref, acc_ref):
    m = pl.program_id(0)
    nu = prev_ref.shape[1]
    local = piv_ref[...] - (base_ref[0] + m * NBAS)
    hot = (local == lax.broadcasted_iota(jnp.int32, (local.shape[0], nu), 1)).astype(F32).astype(BF16)
    picked = jnp.dot(hot, prev_ref[0], preferred_element_type=F32)

    @pl.when(m == 0)
    def _():
        acc_ref[...] = picked

    @pl.when(m > 0)
    def _():
        acc_ref[...] += picked

    @pl.when(m == pl.num_programs(0) - 1)
    def _():
        out_ref[...] = acc_ref[...].astype(BF16)


def pick_rows(base, pivots, previous):
    mu, nu, k = previous.shape
    n = pivots.shape[0]
    return pl.pallas_call(
        pick_kernel,
        out_shape=jax.ShapeDtypeStruct((n, k), BF16),
        grid_spec=pltpu.PrefetchScalarGridSpec(
            num_scalar_prefetch=1,
            grid=(mu,),
            in_specs=[
                pl.BlockSpec((n, 1), lambda m, b: (0, 0)),
                pl.BlockSpec((1, nu, k), lambda m, b: (m, 0, 0)),
            ],
            out_specs=pl.BlockSpec((n, k), lambda m, b: (0, 0)),
            scratch_shapes=[pltpu.VMEM((n, k), F32)],
        ),
        cost_estimate=pl.CostEstimate(
            flops=2 * n * mu * nu * k, bytes_accessed=2 * mu * nu * k, transcendentals=0
        ),
        name="pick_rows",
    )(base, pivots.reshape(n, 1), previous)


def block_kernel(cols_ref, prev_ref, rows_ref, inv_ref, orb_ref, new_ref, part_ref):
    contract = (((1,), (1,)), ((), ()))
    correction = lax.dot_general(prev_ref[0], rows_ref[...], contract, preferred_element_type=F32)
    residual = (cols_ref[0].astype(F32) - correction).astype(BF16)
    inv = inv_ref[...]
    below = lax.broadcasted_iota(jnp.int32, inv.shape, 0) > lax.broadcasted_iota(jnp.int32, inv.shape, 1)
    upper = jnp.where(below, 0.0, inv.astype(F32)).astype(BF16)
    new = jnp.dot(residual, upper, preferred_element_type=F32).astype(BF16)
    new_ref[0] = new
    part = lax.dot_general(new, orb_ref[...], (((0,), (0,)), ((), ())), preferred_element_type=F32)
    owners, dests, _, keep, width = part_ref.shape
    for g in range(owners):
        part_ref[g, :, 0] = part[:, g * width : (g + 1) * width].reshape(dests, keep, width)


def block(pivot_columns, previous, rows, pivot_inverse, orbitals, owners, dests):
    mu, nu, k = previous.shape
    n = pivot_columns.shape[2]
    occ = orbitals.shape[1]
    part_shape = (owners, dests, mu, n // dests, occ // owners)
    return pl.pallas_call(
        block_kernel,
        grid=(mu,),
        out_shape=(
            jax.ShapeDtypeStruct((mu, nu, n), BF16),
            jax.ShapeDtypeStruct(part_shape, F32),
        ),
        in_specs=[
            pl.BlockSpec((1, nu, n), lambda m: (m, 0, 0)),
            pl.BlockSpec((1, nu, k), lambda m: (m, 0, 0)),
            pl.BlockSpec((n, k), lambda m: (0, 0)),
            pl.BlockSpec((n, n), lambda m: (0, 0)),
            pl.BlockSpec((nu, occ), lambda m: (0, 0)),
        ],
        out_specs=(
            pl.BlockSpec((1, nu, n), lambda m: (m, 0, 0)),
            pl.BlockSpec(part_shape[:2] + (1,) + part_shape[3:], lambda m: (0, 0, m, 0, 0)),
        ),
        compiler_params=pltpu.CompilerParams(vmem_limit_bytes=40 << 20),
        cost_estimate=pl.CostEstimate(
            flops=2 * mu * nu * n * (k + n + occ),
            bytes_accessed=2 * mu * nu * (k + 2 * n) + 4 * mu * n * occ,
            transcendentals=0,
        ),
        name="block",
    )(pivot_columns, previous, rows, pivot_inverse, orbitals)


def final_kernel(half_ref, slab_ref, out_ref, wide_ref):
    mu, keep, width = half_ref.shape
    wide_ref[...] = half_ref[...].astype(F32).reshape(mu * keep, width)
    slab_t = slab_ref[...].T
    for p in range(0, keep, 2):
        pair = [wide_ref[pl.ds(q, mu, stride=keep), :].astype(BF16) for q in (p, p + 1)]
        both = jnp.dot(slab_t, jnp.concatenate(pair, axis=1), preferred_element_type=F32)
        out_ref[p] = both[:, :width].astype(BF16)
        out_ref[p + 1] = both[:, width:].astype(BF16)


def final(half, slab):
    mu, keep, width = half.shape
    occ = slab.shape[1]
    return pl.pallas_call(
        final_kernel,
        out_shape=jax.ShapeDtypeStruct((keep, occ, width), BF16),
        scratch_shapes=[pltpu.VMEM((mu * keep, width), F32)],
        compiler_params=pltpu.CompilerParams(vmem_limit_bytes=32 << 20),
        cost_estimate=pl.CostEstimate(
            flops=2 * mu * keep * width * occ,
            bytes_accessed=2 * keep * width * (mu + occ),
            transcendentals=0,
        ),
        name="final",
    )(half, slab)


def exchange(x, axis):
    return lax.all_to_all(x, axis, split_axis=0, concat_axis=0, tiled=True)


def sum_rows(x):
    return jnp.sum(x.astype(F32), axis=0).astype(BF16)


def per_device(n_rows, n_grp, pivot_columns, previous, pivots, pivot_inverse, orbitals, slab_orbitals):
    mu, nu, k = previous.shape
    n = pivot_columns.shape[2]
    base = lax.axis_index("rows") * (mu * NBAS) + lax.axis_index("grp") * nu
    picked = pick_rows(base.reshape(1).astype(jnp.int32), pivots, previous)
    mine = sum_rows(exchange(picked.reshape(n_rows, n // n_rows, k), "rows"))
    mine = sum_rows(exchange(jnp.broadcast_to(mine, (n_grp,) + mine.shape), "grp"))
    rows = exchange(jnp.broadcast_to(mine, (n_rows,) + mine.shape), "rows").reshape(n, k)
    new_vectors, part = block(
        pivot_columns, previous, rows, pivot_inverse, orbitals, n_grp, n_rows
    )
    width = part.shape[-1]
    half = lax.psum_scatter(part.reshape(-1, width), "grp", scatter_dimension=0, tiled=True)
    half = half.astype(BF16).reshape(part.shape[1:])
    half = exchange(half, "rows").reshape(n_rows * mu, n // n_rows, width)
    return new_vectors, final(half, slab_orbitals)


def solution(mesh):
    in_specs = (P("rows", "grp", None), P("rows", "grp", None), P(), P(), P("grp", None), P())
    out_specs = (P("rows", "grp", None), P("rows", None, "grp"))
    body = functools.partial(per_device, mesh.shape["rows"], mesh.shape["grp"])
    return jax.shard_map(body, mesh=mesh, in_specs=in_specs, out_specs=out_specs, check_vma=False)
```

time: 204 us -> 149 us (0.73)
  blocking collectives: 100 us -> 63 us
  Pallas kernels: 0 us -> 17.9 us
  matrix products: 16.1 us -> 0 us
  local copies, waits for them, and re-layouts: 14.5 us -> 5.19 us
  other arithmetic: 5.85 us -> 1.13 us
  waiting for transfers between devices: 52.5 us -> 47.8 us
    psum x1 -> x0, blocking collectives: 83.7 us -> none  [per_device(): pivot_rows = lax.psum(picked, ('rows', 'grp')).astype(jnp.bfloat16)]
    all_to_all x1 -> x4, blocking collectives: 16.3 us -> 63 us  [exchange(): return lax.all_to_all(x, axis, split_axis=0, concat_axis=0, tiled=True)]
    pallas_call x0 -> x3, Pallas kernels: none -> 17.9 us  [the longest x1 10.2 us: block(): pl.pallas_call(block_kernel, grid=(mu,), out_shape=(jax.ShapeDtypeStruct(...]
    dot_general x3 -> x0, matrix products: 16.1 us -> none  [the longest x1 7.8 us: per_device(): jnp.dot(residual_columns, upper, preferred_element_type=jnp.float32)]
    convert_element_type x2 -> x0, local copies, waits for them, and re-layouts: 6.15 us -> none  [the longest x1 5.94 us: per_device(): flat_columns.astype(jnp.float32) - correction]
    reduce_scatter x1, waiting for transfers between devices: 52.4 us -> 47.8 us  [per_device(): lax.psum_scatter(part.reshape(-1, width), 'grp', scatter_dimension=0, til...]
    convert_element_type x2 -> x1, other arithmetic: 5.68 us -> 1.07 us  [per_device(): half = half.astype(BF16).reshape(part.shape[1:])]
    gather x1 -> x0, local copies, waits for them, and re-layouts: 4.37 us -> none  [per_device(): jnp.take(flat_prev, local_row, axis=0).astype(jnp.float32)]
where the time goes in v1:
time: 149 us
  blocking collectives  63 us (42%)
  waiting for transfers between devices  47.8 us (32%)
  Pallas kernels  17.9 us (12%)
  between operations  14.1 us (9%)
  local copies, waits for them, and re-layouts  5.19 us (3%)
    all_to_all x4, blocking collectives, exchange(): return lax.all_to_all(x, axis, split_axis=0, concat_axis=0, tiled=True)  63 us
    reduce_scatter x1, waiting for transfers between devices, per_device(): lax.psum_scatter(part.reshape(-1, width), 'grp', scatter_dimension=0, til...  47.8 us
    pallas_call x1, Pallas kernels, block(): pl.pallas_call(block_kernel, grid=(mu,), out_shape=(jax.ShapeDtypeStruct(...  10.2 us
    pallas_call x1, Pallas kernels, pick_rows(): pl.pallas_call(pick_kernel, out_shape=jax.ShapeDtypeStruct((n, k), BF16),...  5.55 us
    unnamed x10, local copies, waits for them, and re-layouts  3.68 us
  transfers between devices with their start and end apart: 1, of which 1 were waited for; matrix products, arithmetic and copies ran while one was open for 0% of the time, Pallas kernels for 0%

profile of v1, /device:TPU:1, one launch (start us, length us, event | category | flops | bytes accessed | tf_op | source)
XLA Modules:
  0.0 149.0 jit_solution(8677459615758535364)
XLA Ops:
  7.2 0.0 reduce-scatter.2.cloned.1.call-start
  7.2 1.5 copy.9.piv_ref
  8.7 0.0 copy-start.2
  8.7 0.0 copy-start.4
  8.7 5.5 %pick_rows.1 = bf16[256,512]{1,0:T(8,128)(2,1)} custom-call(s32[1]{0:T(128)} %bitcast.base_ref, s32[256,1]{1,0:T(8,128)} %copy.9.piv_ref, bf16[4,1280,512]{2,1,0:T(8,128)(2,1)} %prev_ref.3), custom_call_target="tpu_custom_call" | custom-call | flops 1342177280 | bytes 5242880 | tf_op jit(solution)/shard_map/pick_rows/pallas_call | solution.py:38
  14.2 17.6 %all_to_all.20 = bf16[32,8,512]{2,1,0:T(8,128)(2,1)S(1)} all-to-all(bf16[32,8,512]{2,1,0:T(8,128)(2,1)} %bitcast.10), channel_id=1, replica_groups=mesh['rows'=32,'grp'=8] {'rows'}, dimensions={0} | all-to-all | bytes 524288 | tf_op jit(solution)/shard_map/all_to_all | solution.py:135
  31.8 0.1 reduce_sum.24
  31.9 15.2 %all_to_all.21 = bf16[8,8,512]{2,1,0:T(8,128)(2,1)S(1)} all-to-all(bf16[8,8,512]{2,1,0:T(8,128)(2,1)S(1)} %broadcast_in_dim.6), channel_id=1, replica_groups=mesh['rows'=32,'grp'=8] {'grp'}, dimensions={0} | all-to-all | bytes 131072 | tf_op jit(solution)/shard_map/all_to_all | solution.py:135
  47.1 13.9 %all_to_all.22 = bf16[32,8,512]{2,1,0:T(8,128)(2,1)S(1)} all-to-all(bf16[32,8,512]{2,1,0:T(8,128)(2,1)S(1)} %broadcast_in_dim.7), channel_id=1, replica_groups=mesh['rows'=32,'grp'=8] {'rows'}, dimensions={0} | all-to-all | bytes 524288 | tf_op jit(solution)/shard_map/all_to_all | solution.py:135
  61.0 0.0 copy-done.2
  61.0 0.0 copy-done.4
  61.0 0.0 copy-start.3
  61.0 1.7 %copy-done.3 = bf16[1280,1024]{1,0:T(8,128)(2,1)S(1)} copy-done((bf16[1280,1024]{1,0:T(8,128)(2,1)S(1)}, bf16[1280,1024]{1,0:T(8,128)(2,1)}, u32[]{:S(2)}) %copy-start.3) | copy-done | bytes 2621464
  62.8 10.2 %block.1 = (bf16[4,1280,256]{2,1,0:T(8,128)(2,1)}, f32[8,32,4,8,128]{4,3,2,1,0:T(8,128)S(1)}) custom-call(bf16[4,1280,256]{2,1,0:T(8,128)(2,1)S(1)} %copy-done.2, bf16[4,1280,512]{2,1,0:T(8,128)(2,1)} %prev_ref.3, bf16[256,512]{1,0:T(8,128)(2,1)S(1)} %bitcast.9, bf16[256,256]{1,0:T(8,128)(2,1)S(1)} %copy-done.4, bf16[1280,1024]{1,0:T(8,128)(2,1)S(1)} %copy-done.3), custom_call_target="tpu_custom_call" | custom-call | flops 4697620480 | bytes 14680064 | tf_op jit(solution)/shard_map/block/pallas_call | solution.py:78
  73.0 0.0 copy-start
  73.0 1.9 %copy-done = f32[8,32,4,8,128]{4,3,2,1,0:T(8,128)} copy-done((f32[8,32,4,8,128]{4,3,2,1,0:T(8,128)}, f32[8,32,4,8,128]{4,3,2,1,0:T(8,128)S(1)}, u32[]{:S(2)}) %copy-start) | copy-done | bytes 4194328
  74.9 0.0 copy-start.1
  74.9 0.0 reduce-scatter.2.cloned.1.call-update
  75.0 47.8 %reduce-scatter.2.cloned.1.call-done = f32[1024,128]{1,0:T(8,128)} async-done(((f32[8192,128]{1,0:T(8,128)}), f32[1024,128]{1,0:T(8,128)}) %reduce-scatter.2.cloned.1.call-update) | async-done | bytes 524304 | tf_op jit(solution)/shard_map/reduce_scatter | solution.py:154
  122.7 1.1 convert_element_type.2
  123.8 16.3 %all_to_all.23 = bf16[32,4,8,128]{3,2,1,0:T(8,128)(2,1)S(1)} all-to-all(bf16[32,4,8,128]{3,2,1,0:T(8,128)(2,1)S(1)} %bitcast.11), channel_id=1, replica_groups=mesh['rows'=32,'grp'=8] {'rows'}, dimensions={0} | all-to-all | bytes 524288 | tf_op jit(solution)/shard_map/all_to_all | solution.py:135
  140.1 0.0 copy-done.1
  140.1 2.1 %final.1 = bf16[8,1024,128]{2,1,0:T(8,128)(2,1)} custom-call(bf16[128,8,128]{2,1,0:T(8,128)(2,1)S(1)} %bitcast.8, bf16[128,1024]{1,0:T(8,128)(2,1)S(1)} %copy-done.1), custom_call_target="tpu_custom_call" | custom-call | flops 268435456 | bytes 2359296 | tf_op jit(solution)/shard_map/final/pallas_call | solution.py:120
  (3 shorter events, 0.0 us)
Async XLA Ops:
  7.2 115.6 %reduce-scatter.2.cloned.1.call-start = ((), (), s32[]{:S(2)}) async-start(), calls=%async_computation.5 | async-start | bytes 4718592 | tf_op jit(solution)/shard_map/reduce_scatter | solution.py:154
  8.7 52.3 %copy-start.2 = (bf16[4,1280,256]{2,1,0:T(8,128)(2,1)S(1)}, bf16[4,1280,256]{2,1,0:T(8,128)(2,1)}, u32[]{:S(2)}) copy-start(bf16[4,1280,256]{2,1,0:T(8,128)(2,1)} %cols_ref.1) | copy-start | bytes 7864324
  8.7 52.3 %copy-start.4 = (bf16[256,256]{1,0:T(8,128)(2,1)S(1)}, bf16[256,256]{1,0:T(8,128)(2,1)}, u32[]{:S(2)}) copy-start(bf16[256,256]{1,0:T(8,128)(2,1)} %inv_ref.1) | copy-start | bytes 393220
  61.0 1.7 %copy-start.3 = (bf16[1280,1024]{1,0:T(8,128)(2,1)S(1)}, bf16[1280,1024]{1,0:T(8,128)(2,1)}, u32[]{:S(2)}) copy-start(bf16[1280,1024]{1,0:T(8,128)(2,1)} %orb_ref.1) | copy-start | bytes 7864324
  73.0 1.9 %copy-start = (f32[8,32,4,8,128]{4,3,2,1,0:T(8,128)}, f32[8,32,4,8,128]{4,3,2,1,0:T(8,128)S(1)}, u32[]{:S(2)}) copy-start(f32[8,32,4,8,128]{4,3,2,1,0:T(8,128)S(1)} %get-tuple-element.5) | copy-start | bytes 12582916
  74.9 65.1 %copy-start.1 = (bf16[128,1024]{1,0:T(8,128)(2,1)S(1)}, bf16[128,1024]{1,0:T(8,128)(2,1)}, u32[]{:S(2)}) copy-start(bf16[128,1024]{1,0:T(8,128)(2,1)} %slab_ref.1) | copy-start | bytes 786436
Sparse Core Ops, SparseCore 0:
  75.1 47.5 reduce-scatter.1

commit v2 on v1

v2 whole, which is shorter than its diff:
```python
import functools

import jax
import jax.numpy as jnp
from jax import lax
from jax.experimental import pallas as pl
from jax.experimental.pallas import tpu as pltpu
from jax.sharding import PartitionSpec as P

NBAS = 10240
F32 = jnp.float32
BF16 = jnp.bfloat16
STREAMS = 2


def pick_kernel(base_ref, piv_ref, prev_ref, out_ref, acc_ref, slots, sems, where_ref):
    mu, nu, _ = prev_ref.shape
    depth, group, _ = slots.shape
    n = acc_ref.shape[0]
    acc_ref[...] = jnp.zeros_like(acc_ref)
    offset = piv_ref[...] - base_ref[0]
    local = jnp.full_like(offset, -1)
    for m in range(mu):
        inside = offset - m * NBAS
        local = jnp.where((inside >= 0) & (inside < nu), inside + m * nu, local)
    order = lax.broadcasted_iota(jnp.int32, local.shape, 0) * local.shape[1] + lax.broadcasted_iota(
        jnp.int32, local.shape, 1
    )
    total = jnp.sum((local >= 0).astype(jnp.int32))

    def find(count, last):
        p = jnp.min(jnp.where((local >= 0) & (order > last), order, n))
        where_ref[0, count] = p
        where_ref[1, count] = jnp.max(jnp.where(order == p, local, -1))
        return p

    lax.fori_loop(0, total, find, jnp.int32(-1))

    def fetch(row, slot):
        m = jnp.int32(0)
        for step in range(1, mu):
            m += (row >= step * nu).astype(jnp.int32)
        start = pl.multiple_of((row - m * nu) // group * group, group)
        return pltpu.make_async_copy(
            prev_ref.at[m, pl.ds(start, group)], slots.at[slot], sems.at[slot]
        )

    def batch(b, _):
        first = b * depth
        size = jnp.minimum(total - first, depth)

        def begin(i, _):
            fetch(where_ref[1, first + i], i).start()
            return 0

        def end(i, _):
            row = where_ref[1, first + i]
            fetch(row, i).wait()
            rows = slots[i].astype(F32)
            keep = lax.broadcasted_iota(jnp.int32, rows.shape, 0) == row % group
            picked = jnp.sum(jnp.where(keep, rows, 0.0), axis=0, keepdims=True)
            acc_ref[pl.ds(where_ref[0, first + i], 1), :] = picked
            return 0

        lax.fori_loop(0, size, begin, 0)
        lax.fori_loop(0, size, end, 0)
        return 0

    lax.fori_loop(0, (total + depth - 1) // depth, batch, 0)
    out_ref[...] = acc_ref[...].astype(BF16)


def pick_rows(base, pivots, previous):
    mu, nu, k = previous.shape
    n = pivots.shape[0]
    lanes = 128
    return pl.pallas_call(
        pick_kernel,
        out_shape=jax.ShapeDtypeStruct((n, k), BF16),
        in_specs=[
            pl.BlockSpec(memory_space=pltpu.SMEM),
            pl.BlockSpec(memory_space=pltpu.VMEM),
            pl.BlockSpec(memory_space=pltpu.HBM),
        ],
        out_specs=pl.BlockSpec(memory_space=pltpu.VMEM),
        scratch_shapes=[
            pltpu.VMEM((n, k), F32),
            pltpu.VMEM((16, 16, k), BF16),
            pltpu.SemaphoreType.DMA((16,)),
            pltpu.SMEM((2, n), jnp.int32),
        ],
        compiler_params=pltpu.CompilerParams(vmem_limit_bytes=4 << 20),
        cost_estimate=pl.CostEstimate(flops=n * k, bytes_accessed=2 * n * k, transcendentals=0),
        name="pick_rows",
    )(base, pivots.reshape(n // lanes, lanes), previous)


def block_kernel(me_ref, cols_ref, prev_ref, rows_ref, inv_ref, orb_ref, *rest):
    new_ref, part_ref, right_ref, left_ref, turned_ref = rest[-5:]
    owners, dests, mus, keep, width = part_ref.shape
    n = dests * keep
    i = pl.program_id(0)

    @pl.when(i < mus)
    def _():
        contract = (((1,), (1,)), ((), ()))
        correction = lax.dot_general(
            prev_ref[0], rows_ref[...], contract, preferred_element_type=F32
        )
        residual = (cols_ref[0].astype(F32) - correction).astype(BF16)
        inv = inv_ref[...]
        row, column = (lax.broadcasted_iota(jnp.int32, inv.shape, d) for d in (0, 1))
        upper = jnp.where(row > column, 0.0, inv.astype(F32)).astype(BF16)
        new = jnp.dot(residual, upper, preferred_element_type=F32).astype(BF16)
        new_ref[0] = new
        turned_ref[pl.ds(pl.multiple_of(i * n, n), n), :] = new.T

    @pl.when(i >= mus)
    def _():
        part = jnp.dot(turned_ref[...], orb_ref[...], preferred_element_type=F32)
        for q in range(part.shape[1] // width):
            owner = (i - mus) * (part.shape[1] // width) + q
            ahead = lax.rem(owner - me_ref[0] + owners, owners)
            for m in range(mus):
                piece = part[m * n : (m + 1) * n, q * width : (q + 1) * width]
                piece = piece.reshape(dests, keep, width)
                part_ref[ahead, :, m] = piece

                @pl.when(ahead == owners // 2)
                def _():
                    right_ref[:, m] = piece[: dests // 2].astype(BF16)
                    left_ref[:, m] = piece[dests // 2 :].astype(BF16)


def block(me, first, mus, pivot_columns, previous, rows, pivot_inverse, orbitals, owners, dests, so_far):
    mu, nu, k = previous.shape
    n = pivot_columns.shape[2]
    occ = orbitals.shape[1]
    wide = 2 * occ // owners
    part_shape = (owners, dests, mus, n // dests, occ // owners)
    send_shape = (dests // 2,) + part_shape[2:]
    slab = lambda i, me: (first + jnp.minimum(i, mus - 1), 0, 0)
    whole = lambda i, me: (0, 0)
    in_specs = [
        pl.BlockSpec((1, nu, n), slab),
        pl.BlockSpec((1, nu, k), slab),
        pl.BlockSpec((n, k), whole),
        pl.BlockSpec((n, n), whole),
        pl.BlockSpec((nu, wide), lambda i, me: (0, jnp.maximum(i - mus, 0))),
    ]
    args = [pivot_columns, previous, rows, pivot_inverse, orbitals]
    aliases = {}
    if so_far is not None:
        in_specs.append(pl.BlockSpec(memory_space=pl.ANY))
        args.append(so_far)
        aliases = {len(args): 0}
    return pl.pallas_call(
        block_kernel,
        out_shape=(
            jax.ShapeDtypeStruct((mu, nu, n), BF16),
            jax.ShapeDtypeStruct(part_shape, F32),
            jax.ShapeDtypeStruct(send_shape, BF16),
            jax.ShapeDtypeStruct(send_shape, BF16),
        ),
        grid_spec=pltpu.PrefetchScalarGridSpec(
            num_scalar_prefetch=1,
            grid=(mus + occ // wide,),
            in_specs=in_specs,
            out_specs=(
                pl.BlockSpec((1, nu, n), slab),
                pl.BlockSpec(part_shape, lambda i, me: (0, 0, 0, 0, 0)),
                pl.BlockSpec(send_shape, lambda i, me: (0, 0, 0, 0)),
                pl.BlockSpec(send_shape, lambda i, me: (0, 0, 0, 0)),
            ),
            scratch_shapes=[pltpu.VMEM((mus * n, nu), BF16)],
        ),
        input_output_aliases=aliases,
        compiler_params=pltpu.CompilerParams(vmem_limit_bytes=28 << 20),
        cost_estimate=pl.CostEstimate(
            flops=2 * mus * nu * n * (k + n + occ),
            bytes_accessed=2 * mus * nu * (k + 2 * n) + 4 * mus * n * occ,
            transcendentals=0,
        ),
        name="block",
    )(me, *args)


def join_kernel(own_ref, came_ref, out_ref, *, second):
    half = came_ref.shape[0]
    mine, other = (slice(half, None), slice(0, half)) if second else (slice(0, half), slice(half, None))
    out_ref[mine] = (own_ref[0, mine] + came_ref[...].astype(F32)).astype(BF16)
    out_ref[other] = own_ref[0, other].astype(BF16)


def join(part, ahead, came, second):
    shape = part.shape[1:]
    return pl.pallas_call(
        functools.partial(join_kernel, second=second),
        grid=(1,),
        out_shape=jax.ShapeDtypeStruct(shape, BF16),
        in_specs=[
            pl.BlockSpec((1,) + shape, lambda i: (ahead, 0, 0, 0, 0)),
            pl.BlockSpec(came.shape, lambda i: (0, 0, 0, 0)),
        ],
        out_specs=pl.BlockSpec(shape, lambda i: (0, 0, 0, 0)),
        compiler_params=pltpu.CompilerParams(vmem_limit_bytes=6 << 20),
        cost_estimate=pl.CostEstimate(
            flops=came.size, bytes_accessed=12 * came.size, transcendentals=0
        ),
        name="join",
    )(part, came)


def reduce_to_owner(part, right, left):
    owners = part.shape[0]
    far = owners // 2

    def hop(x, way):
        return lax.ppermute(x, "grp", [(i, (i + way) % owners) for i in range(owners)])

    right, left = hop(right, 1), hop(left, -1)
    right, left = hop(join(part, far - 1, right, False), 1), hop(join(part, far + 1, left, True), -1)
    for ahead in range(far - 2, 0, -1):
        right, left = (
            hop((part[a].astype(F32) + x.astype(F32)).astype(BF16), way)
            for a, x, way in ((ahead, right, 1), (owners - ahead, left, -1))
        )
    return part, right, left


def finish_kernel(*refs):
    out_ref = refs[-1]
    mus = refs[0].shape[2]
    for s in range(len(refs) // 3):
        own, right, left = refs[3 * s : 3 * s + 3]
        total = own[0] + right[...].astype(F32) + left[...].astype(F32)
        out_ref[:, s * mus : (s + 1) * mus] = total


def finish(streams):
    dests, mus, keep, width = streams[0][0].shape[1:]
    out_shape = (dests, mus * len(streams), keep, width)
    zeros = lambda d: (lambda i: (0,) * d)
    own = pl.BlockSpec((1, dests, mus, keep, width), zeros(5))
    came = pl.BlockSpec((dests, mus, keep, width), zeros(4))
    return pl.pallas_call(
        finish_kernel,
        grid=(1,),
        out_shape=jax.ShapeDtypeStruct(out_shape, F32),
        in_specs=[own, came, came] * len(streams),
        out_specs=pl.BlockSpec(out_shape, zeros(4)),
        compiler_params=pltpu.CompilerParams(vmem_limit_bytes=10 << 20),
        cost_estimate=pl.CostEstimate(
            flops=2 * dests * mus * keep * width * len(streams),
            bytes_accessed=12 * dests * mus * keep * width * len(streams),
            transcendentals=0,
        ),
        name="finish",
    )(*[x for stream in streams for x in stream])


def final_kernel(half_ref, slab_ref, out_ref):
    rows, width = half_ref.shape
    mu = slab_ref.shape[0]
    keep = rows // mu
    slab_t = slab_ref[...].T
    slab_t = jnp.concatenate([slab_t, slab_t], axis=1)
    for p in range(0, keep, 2):
        pair = jnp.concatenate(
            [half_ref[pl.ds(q, mu, stride=keep), :] for q in (p, p + 1)], axis=1
        )
        high = pair.astype(BF16)
        low = (pair - high.astype(F32)).astype(BF16)
        both = jnp.dot(slab_t, jnp.concatenate([high, low], axis=0), preferred_element_type=F32)
        out_ref[p] = both[:, :width].astype(BF16)
        out_ref[p + 1] = both[:, width:].astype(BF16)


def final(half, slab):
    mu, occ = slab.shape
    rows, width = half.shape
    keep = rows // mu
    return pl.pallas_call(
        final_kernel,
        out_shape=jax.ShapeDtypeStruct((keep, occ, width), BF16),
        compiler_params=pltpu.CompilerParams(vmem_limit_bytes=16 << 20),
        cost_estimate=pl.CostEstimate(
            flops=4 * rows * width * occ,
            bytes_accessed=2 * keep * width * (2 * mu + occ),
            transcendentals=0,
        ),
        name="final",
    )(half, slab)


def exchange(x, axis):
    return lax.all_to_all(x, axis, split_axis=0, concat_axis=0, tiled=True)


def sum_rows(x):
    return jnp.sum(x.astype(F32), axis=0).astype(BF16)


def per_device(n_rows, n_grp, pivot_columns, previous, pivots, pivot_inverse, orbitals, slab_orbitals):
    mu, nu, k = previous.shape
    n = pivot_columns.shape[2]
    base = lax.axis_index("rows") * (mu * NBAS) + lax.axis_index("grp") * nu
    previous, orbitals = (
        pltpu.with_memory_space_constraint(x, pltpu.HBM) for x in (previous, orbitals)
    )
    picked = pick_rows(base.reshape(1).astype(jnp.int32), pivots, previous)
    mine = sum_rows(exchange(picked.reshape(n_rows, n // n_rows, k), "rows"))
    mine = sum_rows(exchange(jnp.broadcast_to(mine, (n_grp,) + mine.shape), "grp"))
    rows = exchange(jnp.broadcast_to(mine, (n_rows,) + mine.shape), "rows").reshape(n, k)
    me = lax.axis_index("grp").reshape(1).astype(jnp.int32)
    mus = mu // STREAMS
    new_vectors, streams = None, []
    for s in range(STREAMS):
        new_vectors, part, right, left = block(
            me, s * mus, mus, pivot_columns, previous, rows, pivot_inverse, orbitals,
            n_grp, n_rows, new_vectors,
        )
        streams.append(reduce_to_owner(part, right, left))
    half = exchange(finish(streams), "rows")
    return new_vectors, final(half.reshape(-1, half.shape[-1]), slab_orbitals)


def solution(mesh):
    in_specs = (P("rows", "grp", None), P("rows", "grp", None), P(), P(), P("grp", None), P())
    out_specs = (P("rows", "grp", None), P("rows", None, "grp"))
    body = functools.partial(per_device, mesh.shape["rows"], mesh.shape["grp"])
    return jax.shard_map(body, mesh=mesh, in_specs=in_specs, out_specs=out_specs, check_vma=False)
```

time: 149 us -> 122 us (0.82)
  waiting for transfers between devices: 47.8 us -> 14.3 us
  starting transfers between devices: 0.04 us -> 18.5 us
  between operations: 14.1 us -> 0.82 us
  blocking collectives: 63 us -> 69.5 us
  local copies, waits for them, and re-layouts: 5.19 us -> 0.71 us
    reduce_scatter x1 -> x0, waiting for transfers between devices: 47.8 us -> none  [per_device(): lax.psum_scatter(part.reshape(-1, width), 'grp', scatter_dimension=0, til...]
    ppermute x0 -> x16, starting transfers between devices: none -> 18.5 us  [hop(): lax.ppermute(x, 'grp', [(i, (i + way) % owners) for i in range(owners)])]
    ppermute x0 -> x16, waiting for transfers between devices: none -> 14.3 us  [hop(): lax.ppermute(x, 'grp', [(i, (i + way) % owners) for i in range(owners)])]
    all_to_all x4, blocking collectives: 63 us -> 69.5 us  [exchange(): return lax.all_to_all(x, axis, split_axis=0, concat_axis=0, tiled=True)]
    pallas_call x1, Pallas kernels: 5.55 us -> 0.32 us  [pick_rows(): pl.pallas_call(pick_kernel, out_shape=jax.ShapeDtypeStruct((n, k), BF16),...]
    pallas_call x1 -> x7, Pallas kernels: 10.2 us -> 15.1 us  [the longest x2 15 us: block(): pl.pallas_call(block_kernel, out_shape=(jax.ShapeDtypeStruct((mu, nu, n),...]
    unnamed x10 -> x8, local copies, waits for them, and re-layouts: 3.68 us -> 0.69 us
  transfers between devices with their start and end apart: 1 -> 16, of which waited for: 1 -> 6; matrix products, arithmetic and copies ran while one was open for 0% -> 0% of each run, Pallas kernels for 0% -> 0%
where the time goes in v2:
time: 122 us
  blocking collectives  69.5 us (57%)
  starting transfers between devices  18.5 us (15%)
  Pallas kernels  17.5 us (14%)
  waiting for transfers between devices  14.3 us (12%)
    all_to_all x4, blocking collectives, exchange(): return lax.all_to_all(x, axis, split_axis=0, concat_axis=0, tiled=True)  69.5 us
    ppermute x16, starting transfers between devices, hop(): lax.ppermute(x, 'grp', [(i, (i + way) % owners) for i in range(owners)])  18.5 us
    pallas_call x2, Pallas kernels, block(): pl.pallas_call(block_kernel, out_shape=(jax.ShapeDtypeStruct((mu, nu, n),...  15 us
    ppermute x16, waiting for transfers between devices, hop(): lax.ppermute(x, 'grp', [(i, (i + way) % owners) for i in range(owners)])  14.3 us
  transfers between devices with their start and end apart: 16, of which 6 were waited for; matrix products, arithmetic and copies ran while one was open for 0% of the time, Pallas kernels for 0%

profile of v2, /device:TPU:1, one launch (start us, length us, event | category | flops | bytes accessed | tf_op | source)
XLA Modules:
  0.0 121.7 jit_solution(6348574652525804111)
XLA Ops:
  0.6 0.7 copy-done.3
  1.3 0.3 pick_rows.1
  1.6 19.4 %all_to_all.20 = bf16[32,8,512]{2,1,0:T(8,128)(2,1)S(1)} all-to-all(bf16[32,8,512]{2,1,0:T(8,128)(2,1)S(1)} %bitcast.41), channel_id=1, replica_groups=mesh['rows'=32,'grp'=8] {'rows'}, dimensions={0} | all-to-all | bytes 524288 | tf_op jit(solution)/shard_map/all_to_all | solution.py:297
  21.1 14.5 %all_to_all.21 = bf16[8,8,512]{2,1,0:T(8,128)(2,1)S(1)} all-to-all(bf16[8,8,512]{2,1,0:T(8,128)(2,1)S(1)} %broadcast_in_dim.6), channel_id=1, replica_groups=mesh['rows'=32,'grp'=8] {'grp'}, dimensions={0} | all-to-all | bytes 131072 | tf_op jit(solution)/shard_map/all_to_all | solution.py:297
  35.6 13.9 %all_to_all.22 = bf16[32,8,512]{2,1,0:T(8,128)(2,1)S(1)} all-to-all(bf16[32,8,512]{2,1,0:T(8,128)(2,1)S(1)} %broadcast_in_dim.7), channel_id=1, replica_groups=mesh['rows'=32,'grp'=8] {'rows'}, dimensions={0} | all-to-all | bytes 524288 | tf_op jit(solution)/shard_map/all_to_all | solution.py:297
  49.5 7.5 %block.2 = (bf16[4,1280,256]{2,1,0:T(8,128)(2,1)}, f32[8,32,2,8,128]{4,3,2,1,0:T(8,128)S(1)}, bf16[16,2,8,128]{3,2,1,0:T(8,128)(2,1)S(1)}, bf16[16,2,8,128]{3,2,1,0:T(8,128)(2,1)S(1)}) custom-call(s32[1]{0:T(128)} %bitcast.me_ref, bf16[4,1280,256]{2,1,0:T(8,128)(2,1)S(1)} %copy-done, bf16[4,1280,512]{2,1,0:T(8,128)(2,1)} %prev_ref.5, ...), custom_call_target="tpu_custom_call" | custom-call | flops 2348810240 | bytes 7340032 | tf_op jit(solution)/shard_map/block/pallas_call | solution.py:157
  57.0 7.5 %block.3 = (bf16[4,1280,256]{2,1,0:T(8,128)(2,1)}, f32[8,32,2,8,128]{4,3,2,1,0:T(8,128)S(1)}, bf16[16,2,8,128]{3,2,1,0:T(8,128)(2,1)S(1)}, bf16[16,2,8,128]{3,2,1,0:T(8,128)(2,1)S(1)}) custom-call(s32[1]{0:T(128)} %bitcast.me_ref, bf16[4,1280,256]{2,1,0:T(8,128)(2,1)S(1)} %copy-done, ...), custom_call_target="tpu_custom_call", output_to_operand_aliasing={{0}: (6, {})} | custom-call | flops 2348810240 | bytes 7340032 | tf_op jit(solution)/shard_map/block/pallas_call | solution.py:157
  64.5 3.5 %collective-permute-done.12.came_ref = bf16[16,2,8,128]{3,2,1,0:T(8,128)(2,1)S(1)} collective-permute-done((bf16[16,2,8,128]{3,2,1,0:T(8,128)(2,1)S(1)}, bf16[16,2,8,128]{3,2,1,0:T(8,128)(2,1)S(1)}, u32[]{:S(2)}, u32[]{:S(2)}) %collective-permute-start.12) | collective-permute-done | bytes 65568 | tf_op jit(solution)/shard_map/ppermute | solution.py:219
  68.0 1.3 %collective-permute-start.13 = (bf16[32,2,8,128]{3,2,1,0:T(8,128)(2,1)S(1)}, bf16[32,2,8,128]{3,2,1,0:T(8,128)(2,1)S(1)}, u32[]{:S(2)}, u32[]{:S(2)}) collective-permute-start(bf16[32,2,8,128]{3,2,1,0:T(8,128)(2,1)S(1)} %join.7), channel_id=1, source_target_pairs={{0,7},{1,0},{2,1},{3,2},{4,3},{5,4},{6,5},{7,6},{8,15},{9,8},{10,9... | collective-permute-start | bytes 393224 | tf_op jit(solution)/shard_map/ppermute | solution.py:219
  69.4 0.2 collective-permute-start.8
  69.6 2.5 %collective-permute-start.4 = (bf16[16,2,8,128]{3,2,1,0:T(8,128)(2,1)S(1)}, bf16[16,2,8,128]{3,2,1,0:T(8,128)(2,1)S(1)}, u32[]{:S(2)}, u32[]{:S(2)}) collective-permute-start(bf16[16,2,8,128]{3,2,1,0:T(8,128)(2,1)S(1)} %get-tuple-element.14), channel_id=1, source_target_pairs={{0,7},{1,0},{2,1},{3,2},{4,3},{5,4},{6,5},{7,6},{8,15},{9,8},{10,9... | collective-permute-start | bytes 196616 | tf_op jit(solution)/shard_map/ppermute | solution.py:219
  72.1 1.6 %collective-permute-done.8.came_ref = bf16[16,2,8,128]{3,2,1,0:T(8,128)(2,1)S(1)} collective-permute-done((bf16[16,2,8,128]{3,2,1,0:T(8,128)(2,1)S(1)}, bf16[16,2,8,128]{3,2,1,0:T(8,128)(2,1)S(1)}, u32[]{:S(2)}, u32[]{:S(2)}) %collective-permute-start.8) | collective-permute-done | bytes 65568 | tf_op jit(solution)/shard_map/ppermute | solution.py:219
  73.9 2.8 %collective-permute-start.5 = (bf16[32,2,8,128]{3,2,1,0:T(8,128)(2,1)S(1)}, bf16[32,2,8,128]{3,2,1,0:T(8,128)(2,1)S(1)}, u32[]{:S(2)}, u32[]{:S(2)}) collective-permute-start(bf16[32,2,8,128]{3,2,1,0:T(8,128)(2,1)S(1)} %join.5), channel_id=1, source_target_pairs={{0,7},{1,0},{2,1},{3,2},{4,3},{5,4},{6,5},{7,6},{8,15},{9,8},{10,9... | collective-permute-start | bytes 393224 | tf_op jit(solution)/shard_map/ppermute | solution.py:219
  76.8 2.7 %collective-permute-start.14 = (bf16[32,2,8,128]{3,2,1,0:T(8,128)(2,1)S(1)}, bf16[32,2,8,128]{3,2,1,0:T(8,128)(2,1)S(1)}, u32[]{:S(2)}, u32[]{:S(2)}) collective-permute-start(bf16[32,2,8,128]{3,2,1,0:T(8,128)(2,1)S(1)} %fusion), channel_id=1, source_target_pairs={{0,7},{1,0},{2,1},{3,2},{4,3},{5,4},{6,5},{7,6},{8,15},{9,8},{10,9... | collective-permute-start | bytes 393224 | tf_op jit(solution)/shard_map/ppermute | solution.py:219
  79.5 2.2 %collective-permute-start.6 = (bf16[32,2,8,128]{3,2,1,0:T(8,128)(2,1)S(1)}, bf16[32,2,8,128]{3,2,1,0:T(8,128)(2,1)S(1)}, u32[]{:S(2)}, u32[]{:S(2)}) collective-permute-start(bf16[32,2,8,128]{3,2,1,0:T(8,128)(2,1)S(1)} %fusion.4), channel_id=1, source_target_pairs={{0,7},{1,0},{2,1},{3,2},{4,3},{5,4},{6,5},{7,6},{8,15},{9,8},{10,9... | collective-permute-start | bytes 393224 | tf_op jit(solution)/shard_map/ppermute | solution.py:219
  81.8 0.9 collective-permute-done.14
  82.7 0.3 collective-permute-start.10
  83.0 3.5 %collective-permute-start.15 = (bf16[32,2,8,128]{3,2,1,0:T(8,128)(2,1)S(1)}, bf16[32,2,8,128]{3,2,1,0:T(8,128)(2,1)S(1)}, u32[]{:S(2)}, u32[]{:S(2)}) collective-permute-start(bf16[32,2,8,128]{3,2,1,0:T(8,128)(2,1)S(1)} %get-tuple-element.18), channel_id=1, source_target_pairs={{0,7},{1,0},{2,1},{3,2},{4,3},{5,4},{6,5},{7,6},{8,15},{9,8},{10,9... | collective-permute-start | bytes 393224 | tf_op jit(solution)/shard_map/ppermute | solution.py:219
  86.6 2.7 %collective-permute-start.7 = (bf16[32,2,8,128]{3,2,1,0:T(8,128)(2,1)S(1)}, bf16[32,2,8,128]{3,2,1,0:T(8,128)(2,1)S(1)}, u32[]{:S(2)}, u32[]{:S(2)}) collective-permute-start(bf16[32,2,8,128]{3,2,1,0:T(8,128)(2,1)S(1)} %get-tuple-element.20), channel_id=1, source_target_pairs={{0,7},{1,0},{2,1},{3,2},{4,3},{5,4},{6,5},{7,6},{8,15},{9,8},{10,9... | collective-permute-start | bytes 393224 | tf_op jit(solution)/shard_map/ppermute | solution.py:219
  89.4 2.2 %collective-permute-done.2 = bf16[32,2,8,128]{3,2,1,0:T(8,128)(2,1)S(1)} collective-permute-done((bf16[32,2,8,128]{3,2,1,0:T(8,128)(2,1)S(1)}, bf16[32,2,8,128]{3,2,1,0:T(8,128)(2,1)S(1)}, u32[]{:S(2)}, u32[]{:S(2)}) %collective-permute-start.2) | collective-permute-done | bytes 131104 | tf_op jit(solution)/shard_map/ppermute | solution.py:219
  91.8 2.6 %collective-permute-done.11.refs_4_ = bf16[32,2,8,128]{3,2,1,0:T(8,128)(2,1)S(1)} collective-permute-done((bf16[32,2,8,128]{3,2,1,0:T(8,128)(2,1)S(1)}, bf16[32,2,8,128]{3,2,1,0:T(8,128)(2,1)S(1)}, u32[]{:S(2)}, u32[]{:S(2)}) %collective-permute-start.11) | collective-permute-done | bytes 131104 | tf_op jit(solution)/shard_map/ppermute | solution.py:219
  94.4 3.4 %collective-permute-done.3.refs_1_ = bf16[32,2,8,128]{3,2,1,0:T(8,128)(2,1)S(1)} collective-permute-done((bf16[32,2,8,128]{3,2,1,0:T(8,128)(2,1)S(1)}, bf16[32,2,8,128]{3,2,1,0:T(8,128)(2,1)S(1)}, u32[]{:S(2)}, u32[]{:S(2)}) %collective-permute-start.3) | collective-permute-done | bytes 131104 | tf_op jit(solution)/shard_map/ppermute | solution.py:219
  97.9 21.7 %all_to_all.23 = f32[32,4,8,128]{3,2,1,0:T(8,128)S(1)} all-to-all(f32[32,4,8,128]{3,2,1,0:T(8,128)S(1)} %finish.1), channel_id=1, replica_groups=mesh['rows'=32,'grp'=8] {'rows'}, dimensions={0} | all-to-all | bytes 1048576 | tf_op jit(solution)/shard_map/all_to_all | solution.py:297
  119.6 2.1 %final.1 = bf16[8,1024,128]{2,1,0:T(8,128)(2,1)} custom-call(f32[1024,128]{1,0:T(8,128)S(1)} %bitcast.40, bf16[128,1024]{1,0:T(8,128)(2,1)S(1)} %copy-done.2), custom_call_target="tpu_custom_call" | custom-call | flops 536870912 | bytes 2621440 | tf_op jit(solution)/shard_map/final/pallas_call | solution.py:283
  (39 shorter events, 1.0 us)
Async XLA Ops:
  0.6 0.7 copy-start.3
  1.3 48.2 %copy-start = (bf16[4,1280,256]{2,1,0:T(8,128)(2,1)S(1)}, bf16[4,1280,256]{2,1,0:T(8,128)(2,1)}, u32[]{:S(2)}) copy-start(bf16[4,1280,256]{2,1,0:T(8,128)(2,1)} %cols_ref.3) | copy-start | bytes 7864324
  1.3 48.2 %copy-start.1 = (bf16[256,256]{1,0:T(8,128)(2,1)S(1)}, bf16[256,256]{1,0:T(8,128)(2,1)}, u32[]{:S(2)}) copy-start(bf16[256,256]{1,0:T(8,128)(2,1)} %inv_ref.3) | copy-start | bytes 393220
  64.5 3.5 %collective-permute-start.12 = (bf16[16,2,8,128]{3,2,1,0:T(8,128)(2,1)S(1)}, bf16[16,2,8,128]{3,2,1,0:T(8,128)(2,1)S(1)}, u32[]{:S(2)}, u32[]{:S(2)}) collective-permute-start(bf16[16,2,8,128]{3,2,1,0:T(8,128)(2,1)S(1)} %get-tuple-element.17), channel_id=1, source_target_pairs={{0,7},{1,0},{2,1},{3,2},{4,3},{5,4},{6,5},{7,6},{8,15},{9,8},{10,9... | collective-permute-start | bytes 196616 | tf_op jit(solution)/shard_map/ppermute | solution.py:219
  68.0 8.7 %collective-permute-start.13 = (bf16[32,2,8,128]{3,2,1,0:T(8,128)(2,1)S(1)}, bf16[32,2,8,128]{3,2,1,0:T(8,128)(2,1)S(1)}, u32[]{:S(2)}, u32[]{:S(2)}) collective-permute-start(bf16[32,2,8,128]{3,2,1,0:T(8,128)(2,1)S(1)} %join.7), channel_id=1, source_target_pairs={{0,7},{1,0},{2,1},{3,2},{4,3},{5,4},{6,5},{7,6},{8,15},{9,8},{10,9... | collective-permute-start | bytes 393224 | tf_op jit(solution)/shard_map/ppermute | solution.py:219
  69.4 4.3 %collective-permute-start.8 = (bf16[16,2,8,128]{3,2,1,0:T(8,128)(2,1)S(1)}, bf16[16,2,8,128]{3,2,1,0:T(8,128)(2,1)S(1)}, u32[]{:S(2)}, u32[]{:S(2)}) collective-permute-start(bf16[16,2,8,128]{3,2,1,0:T(8,128)(2,1)S(1)} %get-tuple-element.16), channel_id=1, source_target_pairs={{0,1},{1,2},{2,3},{3,4},{4,5},{5,6},{6,7},{7,0},{8,9},{9,10},{10,1... | collective-permute-start | bytes 196616 | tf_op jit(solution)/shard_map/ppermute | solution.py:219
  69.6 4.2 %collective-permute-start.4 = (bf16[16,2,8,128]{3,2,1,0:T(8,128)(2,1)S(1)}, bf16[16,2,8,128]{3,2,1,0:T(8,128)(2,1)S(1)}, u32[]{:S(2)}, u32[]{:S(2)}) collective-permute-start(bf16[16,2,8,128]{3,2,1,0:T(8,128)(2,1)S(1)} %get-tuple-element.14), channel_id=1, source_target_pairs={{0,7},{1,0},{2,1},{3,2},{4,3},{5,4},{6,5},{7,6},{8,15},{9,8},{10,9... | collective-permute-start | bytes 196616 | tf_op jit(solution)/shard_map/ppermute | solution.py:219
  72.1 4.6 %collective-permute-start = (bf16[16,2,8,128]{3,2,1,0:T(8,128)(2,1)S(1)}, bf16[16,2,8,128]{3,2,1,0:T(8,128)(2,1)S(1)}, u32[]{:S(2)}, u32[]{:S(2)}) collective-permute-start(bf16[16,2,8,128]{3,2,1,0:T(8,128)(2,1)S(1)} %get-tuple-element.13), channel_id=1, source_target_pairs={{0,1},{1,2},{2,3},{3,4},{4,5},{5,6},{6,7},{7,0},{8,9},{9,10},{10,1... | collective-permute-start | bytes 196616 | tf_op jit(solution)/shard_map/ppermute | solution.py:219
  73.7 8.0 %collective-permute-start.9 = (bf16[32,2,8,128]{3,2,1,0:T(8,128)(2,1)S(1)}, bf16[32,2,8,128]{3,2,1,0:T(8,128)(2,1)S(1)}, u32[]{:S(2)}, u32[]{:S(2)}) collective-permute-start(bf16[32,2,8,128]{3,2,1,0:T(8,128)(2,1)S(1)} %join.6), channel_id=1, source_target_pairs={{0,1},{1,2},{2,3},{3,4},{4,5},{5,6},{6,7},{7,0},{8,9},{9,10},{10,1... | collective-permute-start | bytes 393224 | tf_op jit(solution)/shard_map/ppermute | solution.py:219
  73.9 5.7 %collective-permute-start.5 = (bf16[32,2,8,128]{3,2,1,0:T(8,128)(2,1)S(1)}, bf16[32,2,8,128]{3,2,1,0:T(8,128)(2,1)S(1)}, u32[]{:S(2)}, u32[]{:S(2)}) collective-permute-start(bf16[32,2,8,128]{3,2,1,0:T(8,128)(2,1)S(1)} %join.5), channel_id=1, source_target_pairs={{0,7},{1,0},{2,1},{3,2},{4,3},{5,4},{6,5},{7,6},{8,15},{9,8},{10,9... | collective-permute-start | bytes 393224 | tf_op jit(solution)/shard_map/ppermute | solution.py:219
  76.6 9.8 %collective-permute-start.1 = (bf16[32,2,8,128]{3,2,1,0:T(8,128)(2,1)S(1)}, bf16[32,2,8,128]{3,2,1,0:T(8,128)(2,1)S(1)}, u32[]{:S(2)}, u32[]{:S(2)}) collective-permute-start(bf16[32,2,8,128]{3,2,1,0:T(8,128)(2,1)S(1)} %join.4), channel_id=1, source_target_pairs={{0,1},{1,2},{2,3},{3,4},{4,5},{5,6},{6,7},{7,0},{8,9},{9,10},{10,1... | collective-permute-start | bytes 393224 | tf_op jit(solution)/shard_map/ppermute | solution.py:219
  76.8 5.9 %collective-permute-start.14 = (bf16[32,2,8,128]{3,2,1,0:T(8,128)(2,1)S(1)}, bf16[32,2,8,128]{3,2,1,0:T(8,128)(2,1)S(1)}, u32[]{:S(2)}, u32[]{:S(2)}) collective-permute-start(bf16[32,2,8,128]{3,2,1,0:T(8,128)(2,1)S(1)} %fusion), channel_id=1, source_target_pairs={{0,7},{1,0},{2,1},{3,2},{4,3},{5,4},{6,5},{7,6},{8,15},{9,8},{10,9... | collective-permute-start | bytes 393224 | tf_op jit(solution)/shard_map/ppermute | solution.py:219
  79.5 6.9 %collective-permute-start.6 = (bf16[32,2,8,128]{3,2,1,0:T(8,128)(2,1)S(1)}, bf16[32,2,8,128]{3,2,1,0:T(8,128)(2,1)S(1)}, u32[]{:S(2)}, u32[]{:S(2)}) collective-permute-start(bf16[32,2,8,128]{3,2,1,0:T(8,128)(2,1)S(1)} %fusion.4), channel_id=1, source_target_pairs={{0,7},{1,0},{2,1},{3,2},{4,3},{5,4},{6,5},{7,6},{8,15},{9,8},{10,9... | collective-permute-start | bytes 393224 | tf_op jit(solution)/shard_map/ppermute | solution.py:219
  82.7 6.6 %collective-permute-start.10 = (bf16[32,2,8,128]{3,2,1,0:T(8,128)(2,1)S(1)}, bf16[32,2,8,128]{3,2,1,0:T(8,128)(2,1)S(1)}, u32[]{:S(2)}, u32[]{:S(2)}) collective-permute-start(bf16[32,2,8,128]{3,2,1,0:T(8,128)(2,1)S(1)} %get-tuple-element.19), channel_id=1, source_target_pairs={{0,1},{1,2},{2,3},{3,4},{4,5},{5,6},{6,7},{7,0},{8,9},{9,10},{10,1... | collective-permute-start | bytes 393224 | tf_op jit(solution)/shard_map/ppermute | solution.py:219
  83.0 8.8 %collective-permute-start.15 = (bf16[32,2,8,128]{3,2,1,0:T(8,128)(2,1)S(1)}, bf16[32,2,8,128]{3,2,1,0:T(8,128)(2,1)S(1)}, u32[]{:S(2)}, u32[]{:S(2)}) collective-permute-start(bf16[32,2,8,128]{3,2,1,0:T(8,128)(2,1)S(1)} %get-tuple-element.18), channel_id=1, source_target_pairs={{0,7},{1,0},{2,1},{3,2},{4,3},{5,4},{6,5},{7,6},{8,15},{9,8},{10,9... | collective-permute-start | bytes 393224 | tf_op jit(solution)/shard_map/ppermute | solution.py:219
  86.5 5.1 %collective-permute-start.2 = (bf16[32,2,8,128]{3,2,1,0:T(8,128)(2,1)S(1)}, bf16[32,2,8,128]{3,2,1,0:T(8,128)(2,1)S(1)}, u32[]{:S(2)}, u32[]{:S(2)}) collective-permute-start(bf16[32,2,8,128]{3,2,1,0:T(8,128)(2,1)S(1)} %get-tuple-element.21), channel_id=1, source_target_pairs={{0,1},{1,2},{2,3},{3,4},{4,5},{5,6},{6,7},{7,0},{8,9},{9,10},{10,1... | collective-permute-start | bytes 393224 | tf_op jit(solution)/shard_map/ppermute | solution.py:219
  86.6 5.2 %collective-permute-start.7 = (bf16[32,2,8,128]{3,2,1,0:T(8,128)(2,1)S(1)}, bf16[32,2,8,128]{3,2,1,0:T(8,128)(2,1)S(1)}, u32[]{:S(2)}, u32[]{:S(2)}) collective-permute-start(bf16[32,2,8,128]{3,2,1,0:T(8,128)(2,1)S(1)} %get-tuple-element.20), channel_id=1, source_target_pairs={{0,7},{1,0},{2,1},{3,2},{4,3},{5,4},{6,5},{7,6},{8,15},{9,8},{10,9... | collective-permute-start | bytes 393224 | tf_op jit(solution)/shard_map/ppermute | solution.py:219
  89.3 5.1 %collective-permute-start.11 = (bf16[32,2,8,128]{3,2,1,0:T(8,128)(2,1)S(1)}, bf16[32,2,8,128]{3,2,1,0:T(8,128)(2,1)S(1)}, u32[]{:S(2)}, u32[]{:S(2)}) collective-permute-start(bf16[32,2,8,128]{3,2,1,0:T(8,128)(2,1)S(1)} %fusion.3), channel_id=1, source_target_pairs={{0,1},{1,2},{2,3},{3,4},{4,5},{5,6},{6,7},{7,0},{8,9},{9,10},{10,1... | collective-permute-start | bytes 393224 | tf_op jit(solution)/shard_map/ppermute | solution.py:219
  91.7 28.0 %copy-start.2 = (bf16[128,1024]{1,0:T(8,128)(2,1)S(1)}, bf16[128,1024]{1,0:T(8,128)(2,1)}, u32[]{:S(2)}) copy-start(bf16[128,1024]{1,0:T(8,128)(2,1)} %slab_ref.1) | copy-start | bytes 786436
  91.7 6.1 %collective-permute-start.3 = (bf16[32,2,8,128]{3,2,1,0:T(8,128)(2,1)S(1)}, bf16[32,2,8,128]{3,2,1,0:T(8,128)(2,1)S(1)}, u32[]{:S(2)}, u32[]{:S(2)}) collective-permute-start(bf16[32,2,8,128]{3,2,1,0:T(8,128)(2,1)S(1)} %fusion.7), channel_id=1, source_target_pairs={{0,1},{1,2},{2,3},{3,4},{4,5},{5,6},{6,7},{7,0},{8,9},{9,10},{10,1... | collective-permute-start | bytes 393224 | tf_op jit(solution)/shard_map/ppermute | solution.py:219

commit v3 on v2

v3 whole, which is shorter than its diff:
```python
import functools

import jax
import jax.numpy as jnp
from jax import lax
from jax.experimental import pallas as pl
from jax.experimental.pallas import tpu as pltpu
from jax.sharding import PartitionSpec as P

NBAS = 10240
F32 = jnp.float32
BF16 = jnp.bfloat16


def pick_kernel(base_ref, piv_ref, prev_ref, out_ref, acc_ref, slots, sems, where_ref):
    mu, nu, _ = prev_ref.shape
    depth, group, _ = slots.shape
    n = acc_ref.shape[0]
    acc_ref[...] = jnp.zeros_like(acc_ref)
    offset = piv_ref[...] - base_ref[0]
    local = jnp.full_like(offset, -1)
    for m in range(mu):
        inside = offset - m * NBAS
        local = jnp.where((inside >= 0) & (inside < nu), inside + m * nu, local)
    order = lax.broadcasted_iota(jnp.int32, local.shape, 0) * local.shape[1] + lax.broadcasted_iota(
        jnp.int32, local.shape, 1
    )
    total = jnp.sum((local >= 0).astype(jnp.int32))

    def find(count, last):
        p = jnp.min(jnp.where((local >= 0) & (order > last), order, n))
        where_ref[0, count] = p
        where_ref[1, count] = jnp.max(jnp.where(order == p, local, -1))
        return p

    lax.fori_loop(0, total, find, jnp.int32(-1))

    def fetch(row, slot):
        m = jnp.int32(0)
        for step in range(1, mu):
            m += (row >= step * nu).astype(jnp.int32)
        start = pl.multiple_of((row - m * nu) // group * group, group)
        return pltpu.make_async_copy(
            prev_ref.at[m, pl.ds(start, group)], slots.at[slot], sems.at[slot]
        )

    def batch(b, _):
        first = b * depth
        size = jnp.minimum(total - first, depth)

        def begin(i, _):
            fetch(where_ref[1, first + i], i).start()
            return 0

        def end(i, _):
            row = where_ref[1, first + i]
            fetch(row, i).wait()
            rows = slots[i].astype(F32)
            keep = lax.broadcasted_iota(jnp.int32, rows.shape, 0) == row % group
            picked = jnp.sum(jnp.where(keep, rows, 0.0), axis=0, keepdims=True)
            acc_ref[pl.ds(where_ref[0, first + i], 1), :] = picked
            return 0

        lax.fori_loop(0, size, begin, 0)
        lax.fori_loop(0, size, end, 0)
        return 0

    lax.fori_loop(0, (total + depth - 1) // depth, batch, 0)
    out_ref[...] = acc_ref[...].astype(BF16)


def pick_rows(base, pivots, previous):
    mu, nu, k = previous.shape
    n = pivots.shape[0]
    lanes = 128
    return pl.pallas_call(
        pick_kernel,
        out_shape=jax.ShapeDtypeStruct((n, k), BF16),
        in_specs=[
            pl.BlockSpec(memory_space=pltpu.SMEM),
            pl.BlockSpec(memory_space=pltpu.VMEM),
            pl.BlockSpec(memory_space=pltpu.HBM),
        ],
        out_specs=pl.BlockSpec(memory_space=pltpu.VMEM),
        scratch_shapes=[
            pltpu.VMEM((n, k), F32),
            pltpu.VMEM((16, 16, k), BF16),
            pltpu.SemaphoreType.DMA((16,)),
            pltpu.SMEM((2, n), jnp.int32),
        ],
        compiler_params=pltpu.CompilerParams(vmem_limit_bytes=4 << 20),
        cost_estimate=pl.CostEstimate(flops=n * k, bytes_accessed=2 * n * k, transcendentals=0),
        name="pick_rows",
    )(base, pivots.reshape(n // lanes, lanes), previous)


def vectors_kernel(cols_ref, prev_ref, rows_ref, inv_ref, new_ref, turned_ref):
    contract = (((1,), (1,)), ((), ()))
    correction = lax.dot_general(prev_ref[0], rows_ref[...], contract, preferred_element_type=F32)
    residual = (cols_ref[0].astype(F32) - correction).astype(BF16)
    inv = inv_ref[...]
    row, column = (lax.broadcasted_iota(jnp.int32, inv.shape, d) for d in (0, 1))
    upper = jnp.where(row > column, 0.0, inv.astype(F32)).astype(BF16)
    new = jnp.dot(residual, upper, preferred_element_type=F32).astype(BF16)
    new_ref[0] = new
    turned_ref[0] = new.T


def vectors(pivot_columns, previous, rows, pivot_inverse):
    mu, nu, k = previous.shape
    n = pivot_columns.shape[2]
    slab = lambda m: (m, 0, 0)
    whole = lambda m: (0, 0)
    return pl.pallas_call(
        vectors_kernel,
        grid=(mu,),
        out_shape=(
            jax.ShapeDtypeStruct((mu, nu, n), BF16),
            jax.ShapeDtypeStruct((mu, n, nu), BF16),
        ),
        in_specs=[
            pl.BlockSpec((1, nu, n), slab),
            pl.BlockSpec((1, nu, k), slab),
            pl.BlockSpec((n, k), whole),
            pl.BlockSpec((n, n), whole),
        ],
        out_specs=(pl.BlockSpec((1, nu, n), slab), pl.BlockSpec((1, n, nu), slab)),
        compiler_params=pltpu.CompilerParams(vmem_limit_bytes=20 << 20),
        cost_estimate=pl.CostEstimate(
            flops=2 * mu * nu * n * (k + n),
            bytes_accessed=2 * mu * nu * (k + 3 * n),
            transcendentals=0,
        ),
        name="vectors",
    )(pivot_columns, previous, rows, pivot_inverse)


def parts_kernel(me_ref, turned_ref, orb_ref, *out_refs, ahead, owners):
    mu, n, nu = turned_ref.shape
    width = orb_ref.shape[1] // owners
    keep, last = out_refs[0].shape[-2:]
    columns = []
    for a in ahead:
        start = pl.multiple_of(lax.rem(me_ref[0] + a, owners) * width, width)
        columns.append(orb_ref[:, pl.ds(start, width)])
    columns = columns[0] if len(columns) == 1 else jnp.concatenate(columns, axis=1)
    for m in range(mu):
        part = jnp.dot(turned_ref[m], columns, preferred_element_type=F32)
        if len(out_refs) == 2:
            half = n // 2
            for h, out_ref in enumerate(out_refs):
                piece = part[h * half : (h + 1) * half].reshape(half // keep, keep, last)
                out_ref[:, m] = piece.astype(out_ref.dtype)
        else:
            for q in range(len(ahead)):
                piece = part[:, q * width : (q + 1) * width].reshape(n // keep, keep, width)
                out_refs[0][q, :, m] = piece


def parts(me, turned, orbitals, ahead, owners, dests, send=False):
    mu, n, nu = turned.shape
    width = orbitals.shape[1] // owners
    if send:
        shape = (dests // 2, mu, n // dests, width)
        out_shape = (jax.ShapeDtypeStruct(shape, BF16),) * 2
    else:
        shape = (len(ahead), dests, mu, n // dests, width)
        out_shape = jax.ShapeDtypeStruct(shape, F32)
    vmem = pl.BlockSpec(memory_space=pltpu.VMEM)
    return pl.pallas_call(
        functools.partial(parts_kernel, ahead=ahead, owners=owners),
        out_shape=out_shape,
        in_specs=[pl.BlockSpec(memory_space=pltpu.SMEM), vmem, vmem],
        out_specs=(vmem, vmem) if send else vmem,
        compiler_params=pltpu.CompilerParams(vmem_limit_bytes=20 << 20),
        cost_estimate=pl.CostEstimate(
            flops=2 * mu * n * nu * width * len(ahead),
            bytes_accessed=2 * mu * n * nu,
            transcendentals=0,
        ),
        name="parts",
    )(me, turned, orbitals)


def join_kernel(own_ref, came_ref, out_ref, *, second):
    half = came_ref.shape[0]
    mine, other = (slice(half, None), slice(0, half)) if second else (slice(0, half), slice(half, None))
    out_ref[mine] = (own_ref[0, mine] + came_ref[...].astype(F32)).astype(BF16)
    out_ref[other] = own_ref[0, other].astype(BF16)


def join(part, which, came, second):
    shape = part.shape[1:]
    return pl.pallas_call(
        functools.partial(join_kernel, second=second),
        grid=(1,),
        out_shape=jax.ShapeDtypeStruct(shape, BF16),
        in_specs=[
            pl.BlockSpec((1,) + shape, lambda i: (which, 0, 0, 0, 0)),
            pl.BlockSpec(came.shape, lambda i: (0, 0, 0, 0)),
        ],
        out_specs=pl.BlockSpec(shape, lambda i: (0, 0, 0, 0)),
        compiler_params=pltpu.CompilerParams(vmem_limit_bytes=6 << 20),
        cost_estimate=pl.CostEstimate(
            flops=came.size, bytes_accessed=12 * came.size, transcendentals=0
        ),
        name="join",
    )(part, came)


def reduce_to_owner(me, turned, orbitals, owners, dests):
    far = owners // 2

    def hop(x, way):
        return lax.ppermute(x, "grp", [(i, (i + way) % owners) for i in range(owners)])

    def own(ahead, **more):
        return parts(me, turned, orbitals, ahead, owners, dests, **more)

    right, left = own((far,), send=True)
    right, left = hop(right, 1), hop(left, -1)
    near = own((far - 1, far + 1))
    right, left = hop(join(near, 0, right, False), 1), hop(join(near, 1, left, True), -1)
    for ahead in range(far - 2, 0, -1):
        near = own((ahead, owners - ahead))
        right, left = (
            hop((near[q] + x.astype(F32)).astype(BF16), way)
            for q, (x, way) in enumerate(((right, 1), (left, -1)))
        )
    return own((0,))[0] + right.astype(F32) + left.astype(F32)


def final_kernel(half_ref, slab_ref, out_ref):
    rows, width = half_ref.shape
    mu = slab_ref.shape[0]
    keep = rows // mu
    slab_t = slab_ref[...].T
    slab_t = jnp.concatenate([slab_t, slab_t], axis=1)
    for p in range(0, keep, 2):
        pair = jnp.concatenate(
            [half_ref[pl.ds(q, mu, stride=keep), :] for q in (p, p + 1)], axis=1
        )
        high = pair.astype(BF16)
        low = (pair - high.astype(F32)).astype(BF16)
        both = jnp.dot(slab_t, jnp.concatenate([high, low], axis=0), preferred_element_type=F32)
        out_ref[p] = both[:, :width].astype(BF16)
        out_ref[p + 1] = both[:, width:].astype(BF16)


def final(half, slab):
    mu, occ = slab.shape
    rows, width = half.shape
    keep = rows // mu
    return pl.pallas_call(
        final_kernel,
        out_shape=jax.ShapeDtypeStruct((keep, occ, width), BF16),
        compiler_params=pltpu.CompilerParams(vmem_limit_bytes=16 << 20),
        cost_estimate=pl.CostEstimate(
            flops=4 * rows * width * occ,
            bytes_accessed=2 * keep * width * (2 * mu + occ),
            transcendentals=0,
        ),
        name="final",
    )(half, slab)


def exchange(x, axis):
    return lax.all_to_all(x, axis, split_axis=0, concat_axis=0, tiled=True)


def sum_rows(x):
    return jnp.sum(x.astype(F32), axis=0).astype(BF16)


def per_device(n_rows, n_grp, pivot_columns, previous, pivots, pivot_inverse, orbitals, slab_orbitals):
    mu, nu, k = previous.shape
    n = pivot_columns.shape[2]
    base = lax.axis_index("rows") * (mu * NBAS) + lax.axis_index("grp") * nu
    previous = pltpu.with_memory_space_constraint(previous, pltpu.HBM)
    picked = pick_rows(base.reshape(1).astype(jnp.int32), pivots, previous)
    mine = sum_rows(exchange(picked.reshape(n_rows, n // n_rows, k), "rows"))
    mine = sum_rows(exchange(jnp.broadcast_to(mine, (n_grp,) + mine.shape), "grp"))
    rows = exchange(jnp.broadcast_to(mine, (n_rows,) + mine.shape), "rows").reshape(n, k)
    me = lax.axis_index("grp").reshape(1).astype(jnp.int32)
    new_vectors, turned = vectors(pivot_columns, previous, rows, pivot_inverse)
    half = exchange(reduce_to_owner(me, turned, orbitals, n_grp, n_rows), "rows")
    return new_vectors, final(half.reshape(-1, half.shape[-1]), slab_orbitals)


def solution(mesh):
    in_specs = (P("rows", "grp", None), P("rows", "grp", None), P(), P(), P("grp", None), P())
    out_specs = (P("rows", "grp", None), P("rows", None, "grp"))
    body = functools.partial(per_device, mesh.shape["rows"], mesh.shape["grp"])
    return jax.shard_map(body, mesh=mesh, in_specs=in_specs, out_specs=out_specs, check_vma=False)
```

time: 122 us -> 107 us (0.88)
  starting transfers between devices: 18.5 us -> 8.65 us
  blocking collectives: 69.5 us -> 65.6 us
  Pallas kernels: 17.5 us -> 14.7 us
  waiting for transfers between devices: 14.3 us -> 15.6 us
    ppermute x16 -> x8, starting transfers between devices: 18.5 us -> 8.65 us  [hop(): lax.ppermute(x, 'grp', [(i, (i + way) % owners) for i in range(owners)])]
    pallas_call x3 -> x6, Pallas kernels: 15 us -> 10.8 us  [the longest x1 6.53 us: vectors(): pl.pallas_call(vectors_kernel, grid=(mu,), out_shape=(jax.ShapeDtypeStruc...]
    all_to_all x4, blocking collectives: 69.5 us -> 65.6 us  [exchange(): return lax.all_to_all(x, axis, split_axis=0, concat_axis=0, tiled=True)]
    pallas_call x1, Pallas kernels: 0.32 us -> 1.73 us  [pick_rows(): pl.pallas_call(pick_kernel, out_shape=jax.ShapeDtypeStruct((n, k), BF16),...]
    ppermute x16 -> x8, waiting for transfers between devices: 14.3 us -> 15.6 us  [hop(): lax.ppermute(x, 'grp', [(i, (i + way) % owners) for i in range(owners)])]
  transfers between devices with their start and end apart: 16 -> 8, of which waited for: 6 -> 5; matrix products, arithmetic and copies ran while one was open for 0% -> 0% of each run, Pallas kernels for 0% -> 3%
where the time goes in v3:
time: 107 us
  blocking collectives  65.6 us (61%)
  waiting for transfers between devices  15.6 us (15%)
  Pallas kernels  14.7 us (14%)
  starting transfers between devices  8.65 us (8%)
    all_to_all x4, blocking collectives, exchange(): return lax.all_to_all(x, axis, split_axis=0, concat_axis=0, tiled=True)  65.6 us
    ppermute x8, waiting for transfers between devices, hop(): lax.ppermute(x, 'grp', [(i, (i + way) % owners) for i in range(owners)])  15.6 us
    ppermute x8, starting transfers between devices, hop(): lax.ppermute(x, 'grp', [(i, (i + way) % owners) for i in range(owners)])  8.65 us
    pallas_call x1, Pallas kernels, vectors(): pl.pallas_call(vectors_kernel, grid=(mu,), out_shape=(jax.ShapeDtypeStruc...  6.53 us
    pallas_call x5, Pallas kernels, parts(): pl.pallas_call(functools.partial(parts_kernel, ahead=ahead, owners=owners...  4.3 us
  transfers between devices with their start and end apart: 8, of which 5 were waited for; matrix products, arithmetic and copies ran while one was open for 0% of the time, Pallas kernels for 3%

profile of v3, /device:TPU:1, one launch (start us, length us, event | category | flops | bytes accessed | tf_op | source)
XLA Modules:
  0.0 106.5 jit_solution(15848560216217975216)
XLA Ops:
  0.6 0.7 copy-done.4
  1.3 1.7 %pick_rows.1 = bf16[256,512]{1,0:T(8,128)(2,1)S(1)} custom-call(s32[1]{0:T(128)} %bitcast.base_ref, s32[2,128]{1,0:T(2,128)S(1)} %bitcast.37, bf16[4,1280,512]{2,1,0:T(8,128)(2,1)} %prev_ref.3), custom_call_target="tpu_custom_call" | custom-call | flops 131072 | bytes 262144 | tf_op jit(solution)/shard_map/pick_rows/pallas_call | solution.py:76
  3.1 17.3 %all_to_all.20 = bf16[32,8,512]{2,1,0:T(8,128)(2,1)S(1)} all-to-all(bf16[32,8,512]{2,1,0:T(8,128)(2,1)S(1)} %bitcast.36), channel_id=1, replica_groups=mesh['rows'=32,'grp'=8] {'rows'}, dimensions={0} | all-to-all | bytes 524288 | tf_op jit(solution)/shard_map/all_to_all | solution.py:268
  20.4 15.1 %all_to_all.21 = bf16[8,8,512]{2,1,0:T(8,128)(2,1)S(1)} all-to-all(bf16[8,8,512]{2,1,0:T(8,128)(2,1)S(1)} %broadcast_in_dim.6), channel_id=1, replica_groups=mesh['rows'=32,'grp'=8] {'grp'}, dimensions={0} | all-to-all | bytes 131072 | tf_op jit(solution)/shard_map/all_to_all | solution.py:268
  35.5 13.9 %all_to_all.22 = bf16[32,8,512]{2,1,0:T(8,128)(2,1)S(1)} all-to-all(bf16[32,8,512]{2,1,0:T(8,128)(2,1)S(1)} %broadcast_in_dim.7), channel_id=1, replica_groups=mesh['rows'=32,'grp'=8] {'rows'}, dimensions={0} | all-to-all | bytes 524288 | tf_op jit(solution)/shard_map/all_to_all | solution.py:268
  49.5 6.5 %vectors.1 = (bf16[4,1280,256]{2,1,0:T(8,128)(2,1)}, bf16[4,256,1280]{2,1,0:T(8,128)(2,1)S(1)}) custom-call(bf16[4,1280,256]{2,1,0:T(8,128)(2,1)S(1)} %copy-done.1, bf16[4,1280,512]{2,1,0:T(8,128)(2,1)} %prev_ref.3, bf16[256,512]{1,0:T(8,128)(2,1)S(1)} %bitcast.35, bf16[256,256]{1,0:T(8,128)(2,1)S(1)} %copy-done.3), custom_call_target="tpu_custom_call" | custom-call | flops 2013265920 | bytes 13107200 | tf_op jit(solution)/shard_map/vectors/pallas_call | solution.py:114
  56.0 0.9 parts.9
  57.0 1.5 %collective-permute-start = (bf16[16,4,8,128]{3,2,1,0:T(8,128)(2,1)S(1)}, bf16[16,4,8,128]{3,2,1,0:T(8,128)(2,1)S(1)}, u32[]{:S(2)}, u32[]{:S(2)}) collective-permute-start(bf16[16,4,8,128]{3,2,1,0:T(8,128)(2,1)S(1)} %get-tuple-element.8), channel_id=1, source_target_pairs={{0,1},{1,2},{2,3},{3,4},{4,5},{5,6},{6,7},{7,0},{8,9},{9,10},{10,1... | collective-permute-start | bytes 393224 | tf_op jit(solution)/shard_map/ppermute | solution.py:215
  58.4 0.9 parts.8.own_ref
  59.3 2.6 %collective-permute-done.4.came_ref = bf16[16,4,8,128]{3,2,1,0:T(8,128)(2,1)S(1)} collective-permute-done((bf16[16,4,8,128]{3,2,1,0:T(8,128)(2,1)S(1)}, bf16[16,4,8,128]{3,2,1,0:T(8,128)(2,1)S(1)}, u32[]{:S(2)}, u32[]{:S(2)}) %collective-permute-start.4) | collective-permute-done | bytes 131104 | tf_op jit(solution)/shard_map/ppermute | solution.py:215
  61.9 1.4 %collective-permute-start.5 = (bf16[32,4,8,128]{3,2,1,0:T(8,128)(2,1)S(1)}, bf16[32,4,8,128]{3,2,1,0:T(8,128)(2,1)S(1)}, u32[]{:S(2)}, u32[]{:S(2)}) collective-permute-start(bf16[32,4,8,128]{3,2,1,0:T(8,128)(2,1)S(1)} %join.3), channel_id=1, source_target_pairs={{0,7},{1,0},{2,1},{3,2},{4,3},{5,4},{6,5},{7,6},{8,15},{9,8},{10,9... | collective-permute-start | bytes 786440 | tf_op jit(solution)/shard_map/ppermute | solution.py:215
  63.3 0.3 collective-permute-start.1
  63.6 0.9 parts.7
  64.4 4.4 %collective-permute-done.5 = bf16[32,4,8,128]{3,2,1,0:T(8,128)(2,1)S(1)} collective-permute-done((bf16[32,4,8,128]{3,2,1,0:T(8,128)(2,1)S(1)}, bf16[32,4,8,128]{3,2,1,0:T(8,128)(2,1)S(1)}, u32[]{:S(2)}, u32[]{:S(2)}) %collective-permute-start.5) | collective-permute-done | bytes 262176 | tf_op jit(solution)/shard_map/ppermute | solution.py:215
  68.8 2.4 %collective-permute-done.1 = bf16[32,4,8,128]{3,2,1,0:T(8,128)(2,1)S(1)} collective-permute-done((bf16[32,4,8,128]{3,2,1,0:T(8,128)(2,1)S(1)}, bf16[32,4,8,128]{3,2,1,0:T(8,128)(2,1)S(1)}, u32[]{:S(2)}, u32[]{:S(2)}) %collective-permute-start.1) | collective-permute-done | bytes 262176 | tf_op jit(solution)/shard_map/ppermute | solution.py:215
  71.2 0.2 fusion.5
  71.4 2.7 %collective-permute-start.6 = (bf16[32,4,8,128]{3,2,1,0:T(8,128)(2,1)S(1)}, bf16[32,4,8,128]{3,2,1,0:T(8,128)(2,1)S(1)}, u32[]{:S(2)}, u32[]{:S(2)}) collective-permute-start(bf16[32,4,8,128]{3,2,1,0:T(8,128)(2,1)S(1)} %get-tuple-element.13), channel_id=1, source_target_pairs={{0,7},{1,0},{2,1},{3,2},{4,3},{5,4},{6,5},{7,6},{8,15},{9,8},{10,9... | collective-permute-start | bytes 786440 | tf_op jit(solution)/shard_map/ppermute | solution.py:215
  74.1 0.9 parts.6
  75.0 3.3 %collective-permute-done.2 = bf16[32,4,8,128]{3,2,1,0:T(8,128)(2,1)S(1)} collective-permute-done((bf16[32,4,8,128]{3,2,1,0:T(8,128)(2,1)S(1)}, bf16[32,4,8,128]{3,2,1,0:T(8,128)(2,1)S(1)}, u32[]{:S(2)}, u32[]{:S(2)}) %collective-permute-start.2) | collective-permute-done | bytes 262176 | tf_op jit(solution)/shard_map/ppermute | solution.py:215
  78.6 2.7 %collective-permute-start.7 = (bf16[32,4,8,128]{3,2,1,0:T(8,128)(2,1)S(1)}, bf16[32,4,8,128]{3,2,1,0:T(8,128)(2,1)S(1)}, u32[]{:S(2)}, u32[]{:S(2)}) collective-permute-start(bf16[32,4,8,128]{3,2,1,0:T(8,128)(2,1)S(1)} %get-tuple-element.11), channel_id=1, source_target_pairs={{0,7},{1,0},{2,1},{3,2},{4,3},{5,4},{6,5},{7,6},{8,15},{9,8},{10,9... | collective-permute-start | bytes 786440 | tf_op jit(solution)/shard_map/ppermute | solution.py:215
  81.2 0.9 parts.5
  82.1 2.9 %collective-permute-done.3 = bf16[32,4,8,128]{3,2,1,0:T(8,128)(2,1)S(1)} collective-permute-done((bf16[32,4,8,128]{3,2,1,0:T(8,128)(2,1)S(1)}, bf16[32,4,8,128]{3,2,1,0:T(8,128)(2,1)S(1)}, u32[]{:S(2)}, u32[]{:S(2)}) %collective-permute-start.3) | collective-permute-done | bytes 262176 | tf_op jit(solution)/shard_map/ppermute | solution.py:215
  85.1 19.3 %all_to_all.23 = f32[32,4,8,128]{3,2,1,0:T(8,128)S(1)} all-to-all(f32[32,4,8,128]{3,2,1,0:T(8,128)S(1)} %fusion.8), channel_id=1, replica_groups=mesh['rows'=32,'grp'=8] {'rows'}, dimensions={0} | all-to-all | bytes 1048576 | tf_op jit(solution)/shard_map/all_to_all | solution.py:268
  104.4 2.1 %final.1 = bf16[8,1024,128]{2,1,0:T(8,128)(2,1)} custom-call(f32[1024,128]{1,0:T(8,128)S(1)} %bitcast.34, bf16[128,1024]{1,0:T(8,128)(2,1)S(1)} %copy-done.2), custom_call_target="tpu_custom_call" | custom-call | flops 536870912 | bytes 2621440 | tf_op jit(solution)/shard_map/final/pallas_call | solution.py:254
  (23 shorter events, 0.7 us)
Async XLA Ops:
  0.6 0.7 copy-start.4
  1.3 48.1 %copy-start.1 = (bf16[4,1280,256]{2,1,0:T(8,128)(2,1)S(1)}, bf16[4,1280,256]{2,1,0:T(8,128)(2,1)}, u32[]{:S(2)}) copy-start(bf16[4,1280,256]{2,1,0:T(8,128)(2,1)} %cols_ref.1) | copy-start | bytes 7864324
  1.3 48.1 %copy-start.3 = (bf16[256,256]{1,0:T(8,128)(2,1)S(1)}, bf16[256,256]{1,0:T(8,128)(2,1)}, u32[]{:S(2)}) copy-start(bf16[256,256]{1,0:T(8,128)(2,1)} %inv_ref.1) | copy-start | bytes 393220
  49.5 6.5 %copy-start = (bf16[1280,1024]{1,0:T(8,128)(2,1)S(1)}, bf16[1280,1024]{1,0:T(8,128)(2,1)}, u32[]{:S(2)}) copy-start(bf16[1280,1024]{1,0:T(8,128)(2,1)} %orb_ref.9) | copy-start | bytes 7864324
  56.9 5.0 %collective-permute-start.4 = (bf16[16,4,8,128]{3,2,1,0:T(8,128)(2,1)S(1)}, bf16[16,4,8,128]{3,2,1,0:T(8,128)(2,1)S(1)}, u32[]{:S(2)}, u32[]{:S(2)}) collective-permute-start(bf16[16,4,8,128]{3,2,1,0:T(8,128)(2,1)S(1)} %get-tuple-element.9), channel_id=1, source_target_pairs={{0,7},{1,0},{2,1},{3,2},{4,3},{5,4},{6,5},{7,6},{8,15},{9,8},{10,9... | collective-permute-start | bytes 393224 | tf_op jit(solution)/shard_map/ppermute | solution.py:215
  57.0 6.3 %collective-permute-start = (bf16[16,4,8,128]{3,2,1,0:T(8,128)(2,1)S(1)}, bf16[16,4,8,128]{3,2,1,0:T(8,128)(2,1)S(1)}, u32[]{:S(2)}, u32[]{:S(2)}) collective-permute-start(bf16[16,4,8,128]{3,2,1,0:T(8,128)(2,1)S(1)} %get-tuple-element.8), channel_id=1, source_target_pairs={{0,1},{1,2},{2,3},{3,4},{4,5},{5,6},{6,7},{7,0},{8,9},{9,10},{10,1... | collective-permute-start | bytes 393224 | tf_op jit(solution)/shard_map/ppermute | solution.py:215
  61.9 6.9 %collective-permute-start.5 = (bf16[32,4,8,128]{3,2,1,0:T(8,128)(2,1)S(1)}, bf16[32,4,8,128]{3,2,1,0:T(8,128)(2,1)S(1)}, u32[]{:S(2)}, u32[]{:S(2)}) collective-permute-start(bf16[32,4,8,128]{3,2,1,0:T(8,128)(2,1)S(1)} %join.3), channel_id=1, source_target_pairs={{0,7},{1,0},{2,1},{3,2},{4,3},{5,4},{6,5},{7,6},{8,15},{9,8},{10,9... | collective-permute-start | bytes 786440 | tf_op jit(solution)/shard_map/ppermute | solution.py:215
  63.3 7.9 %collective-permute-start.1 = (bf16[32,4,8,128]{3,2,1,0:T(8,128)(2,1)S(1)}, bf16[32,4,8,128]{3,2,1,0:T(8,128)(2,1)S(1)}, u32[]{:S(2)}, u32[]{:S(2)}) collective-permute-start(bf16[32,4,8,128]{3,2,1,0:T(8,128)(2,1)S(1)} %join.2), channel_id=1, source_target_pairs={{0,1},{1,2},{2,3},{3,4},{4,5},{5,6},{6,7},{7,0},{8,9},{9,10},{10,1... | collective-permute-start | bytes 786440 | tf_op jit(solution)/shard_map/ppermute | solution.py:215
  71.3 7.0 %collective-permute-start.2 = (bf16[32,4,8,128]{3,2,1,0:T(8,128)(2,1)S(1)}, bf16[32,4,8,128]{3,2,1,0:T(8,128)(2,1)S(1)}, u32[]{:S(2)}, u32[]{:S(2)}) collective-permute-start(bf16[32,4,8,128]{3,2,1,0:T(8,128)(2,1)S(1)} %get-tuple-element.12), channel_id=1, source_target_pairs={{0,1},{1,2},{2,3},{3,4},{4,5},{5,6},{6,7},{7,0},{8,9},{9,10},{10,1... | collective-permute-start | bytes 786440 | tf_op jit(solution)/shard_map/ppermute | solution.py:215
  71.4 6.9 %collective-permute-start.6 = (bf16[32,4,8,128]{3,2,1,0:T(8,128)(2,1)S(1)}, bf16[32,4,8,128]{3,2,1,0:T(8,128)(2,1)S(1)}, u32[]{:S(2)}, u32[]{:S(2)}) collective-permute-start(bf16[32,4,8,128]{3,2,1,0:T(8,128)(2,1)S(1)} %get-tuple-element.13), channel_id=1, source_target_pairs={{0,7},{1,0},{2,1},{3,2},{4,3},{5,4},{6,5},{7,6},{8,15},{9,8},{10,9... | collective-permute-start | bytes 786440 | tf_op jit(solution)/shard_map/ppermute | solution.py:215
  78.5 6.5 %collective-permute-start.3 = (bf16[32,4,8,128]{3,2,1,0:T(8,128)(2,1)S(1)}, bf16[32,4,8,128]{3,2,1,0:T(8,128)(2,1)S(1)}, u32[]{:S(2)}, u32[]{:S(2)}) collective-permute-start(bf16[32,4,8,128]{3,2,1,0:T(8,128)(2,1)S(1)} %get-tuple-element.10), channel_id=1, source_target_pairs={{0,1},{1,2},{2,3},{3,4},{4,5},{5,6},{6,7},{7,0},{8,9},{9,10},{10,1... | collective-permute-start | bytes 786440 | tf_op jit(solution)/shard_map/ppermute | solution.py:215
  78.6 6.4 %collective-permute-start.7 = (bf16[32,4,8,128]{3,2,1,0:T(8,128)(2,1)S(1)}, bf16[32,4,8,128]{3,2,1,0:T(8,128)(2,1)S(1)}, u32[]{:S(2)}, u32[]{:S(2)}) collective-permute-start(bf16[32,4,8,128]{3,2,1,0:T(8,128)(2,1)S(1)} %get-tuple-element.11), channel_id=1, source_target_pairs={{0,7},{1,0},{2,1},{3,2},{4,3},{5,4},{6,5},{7,6},{8,15},{9,8},{10,9... | collective-permute-start | bytes 786440 | tf_op jit(solution)/shard_map/ppermute | solution.py:215
  82.1 22.3 %copy-start.2 = (bf16[128,1024]{1,0:T(8,128)(2,1)S(1)}, bf16[128,1024]{1,0:T(8,128)(2,1)}, u32[]{:S(2)}) copy-start(bf16[128,1024]{1,0:T(8,128)(2,1)} %slab_ref.1) | copy-start | bytes 786436

commit v4 on v3

--- a/solution.py
+++ b/solution.py
@@ -10,55 +10,59 @@
 NBAS = 10240
 F32 = jnp.float32
 BF16 = jnp.bfloat16
-
-
-def pick_kernel(base_ref, piv_ref, prev_ref, out_ref, acc_ref, slots, sems, where_ref):
+SLOTS = 24
+
+
+def pick_kernel(where_from_ref, piv_ref, prev_ref, out_ref, acc_ref, held, sems, todo_ref):
     mu, nu, _ = prev_ref.shape
-    depth, group, _ = slots.shape
-    n = acc_ref.shape[0]
+    depth, group, _ = held.shape
+    line, base, round_index = (where_from_ref[i] for i in range(3))
+    n = todo_ref.shape[1]
+    slots = acc_ref.shape[0]
     acc_ref[...] = jnp.zeros_like(acc_ref)
-    offset = piv_ref[...] - base_ref[0]
-    local = jnp.full_like(offset, -1)
+    pivots = piv_ref[...]
+    order = lax.broadcasted_iota(jnp.int32, pivots.shape, 0) * pivots.shape[1]
+    order += lax.broadcasted_iota(jnp.int32, pivots.shape, 1)
+    in_line = (pivots >= line) & (pivots < line + mu * NBAS)
+    local = jnp.full_like(pivots, -1)
     for m in range(mu):
-        inside = offset - m * NBAS
+        inside = pivots - base - m * NBAS
         local = jnp.where((inside >= 0) & (inside < nu), inside + m * nu, local)
-    order = lax.broadcasted_iota(jnp.int32, local.shape, 0) * local.shape[1] + lax.broadcasted_iota(
-        jnp.int32, local.shape, 1
-    )
-    total = jnp.sum((local >= 0).astype(jnp.int32))
-
-    def find(count, last):
+    owned = jnp.sum((local >= 0).astype(jnp.int32))
+
+    def find(i, carry):
+        last, count = carry
         p = jnp.min(jnp.where((local >= 0) & (order > last), order, n))
-        where_ref[0, count] = p
-        where_ref[1, count] = jnp.max(jnp.where(order == p, local, -1))
-        return p
-
-    lax.fori_loop(0, total, find, jnp.int32(-1))
-
-    def fetch(row, slot):
+        rank = jnp.sum((in_line & (order < p)).astype(jnp.int32))
+        slot = rank - round_index * slots
+        todo_ref[0, count] = slot
+        todo_ref[1, count] = jnp.max(jnp.where(order == p, local, -1))
+        return p, count + ((slot >= 0) & (slot < slots)).astype(jnp.int32)
+
+    _, total = lax.fori_loop(0, owned, find, (jnp.int32(-1), jnp.int32(0)))
+
+    def fetch(row, i):
         m = jnp.int32(0)
         for step in range(1, mu):
             m += (row >= step * nu).astype(jnp.int32)
         start = pl.multiple_of((row - m * nu) // group * group, group)
-        return pltpu.make_async_copy(
-            prev_ref.at[m, pl.ds(start, group)], slots.at[slot], sems.at[slot]
-        )
+        return pltpu.make_async_copy(prev_ref.at[m, pl.ds(start, group)], held.at[i], sems.at[i])
 
     def batch(b, _):
         first = b * depth
         size = jnp.minimum(total - first, depth)
 
         def begin(i, _):
-            fetch(where_ref[1, first + i], i).start()
+            fetch(todo_ref[1, first + i], i).start()
             return 0
 
         def end(i, _):
-            row = where_ref[1, first + i]
+            row = todo_ref[1, first + i]
             fetch(row, i).wait()
-            rows = slots[i].astype(F32)
+            rows = held[i].astype(F32)
             keep = lax.broadcasted_iota(jnp.int32, rows.shape, 0) == row % group
             picked = jnp.sum(jnp.where(keep, rows, 0.0), axis=0, keepdims=True)
-            acc_ref[pl.ds(where_ref[0, first + i], 1), :] = picked
+            acc_ref[pl.ds(todo_ref[0, first + i], 1), :] = picked
             return 0
 
         lax.fori_loop(0, size, begin, 0)
@@ -69,13 +73,13 @@
     out_ref[...] = acc_ref[...].astype(BF16)
 
 
-def pick_rows(base, pivots, previous):
+def pick_rows(where_from, pivots, previous):
     mu, nu, k = previous.shape
     n = pivots.shape[0]
     lanes = 128
     return pl.pallas_call(
         pick_kernel,
-        out_shape=jax.ShapeDtypeStruct((n, k), BF16),
+        out_shape=jax.ShapeDtypeStruct((SLOTS, k), BF16),
         in_specs=[
             pl.BlockSpec(memory_space=pltpu.SMEM),
             pl.BlockSpec(memory_space=pltpu.VMEM),
@@ -83,20 +87,72 @@
         ],
         out_specs=pl.BlockSpec(memory_space=pltpu.VMEM),
         scratch_shapes=[
-            pltpu.VMEM((n, k), F32),
+            pltpu.VMEM((SLOTS, k), F32),
             pltpu.VMEM((16, 16, k), BF16),
             pltpu.SemaphoreType.DMA((16,)),
-            pltpu.SMEM((2, n), jnp.int32),
+            pltpu.SMEM((2, n + 1), jnp.int32),
         ],
         compiler_params=pltpu.CompilerParams(vmem_limit_bytes=4 << 20),
         cost_estimate=pl.CostEstimate(flops=n * k, bytes_accessed=2 * n * k, transcendentals=0),
         name="pick_rows",
-    )(base, pivots.reshape(n // lanes, lanes), previous)
-
-
-def vectors_kernel(cols_ref, prev_ref, rows_ref, inv_ref, new_ref, turned_ref):
+    )(where_from, pivots.reshape(n // lanes, lanes), previous)
+
+
+def select_kernel(round_ref, piv_ref, slots_ref, so_far_ref, out_ref, *, per_line):
+    total, _ = slots_ref.shape
+    n = piv_ref.shape[1]
+    along = jnp.broadcast_to(piv_ref[...].astype(F32), (n, n))
+    lines_along = jnp.floor((along + 0.5) * (1.0 / per_line))
+    lines = lines_along.T
+    earlier = lax.broadcasted_iota(jnp.int32, (n, n), 1) < lax.broadcasted_iota(jnp.int32, (n, n), 0)
+    same = jnp.where((lines_along == lines) & earlier, 1.0, 0.0)
+    rank = jnp.sum(same, axis=1, keepdims=True) - (round_ref[0] * SLOTS).astype(F32)
+    mine = (rank >= 0.0) & (rank < SLOTS)
+    index = jnp.where(mine, lines[:, :1] * SLOTS + rank, -1.0).astype(jnp.int32)
+    hot = index == lax.broadcasted_iota(jnp.int32, (n, total), 1)
+    hot = jnp.where(hot, 1.0, 0.0).astype(BF16)
+    picked = jnp.dot(hot, slots_ref[...], preferred_element_type=F32)
+    out_ref[...] = (picked + so_far_ref[...].astype(F32)).astype(BF16)
+
+
+def select_rows(round_index, pivots, slots, so_far, per_line):
+    total, width = slots.shape
+    n = pivots.shape[0]
+    vmem = pl.BlockSpec(memory_space=pltpu.VMEM)
+    return pl.pallas_call(
+        functools.partial(select_kernel, per_line=per_line),
+        out_shape=jax.ShapeDtypeStruct((n, width), BF16),
+        in_specs=[pl.BlockSpec(memory_space=pltpu.SMEM), vmem, vmem, vmem],
+        out_specs=vmem,
+        compiler_params=pltpu.CompilerParams(vmem_limit_bytes=8 << 20),
+        cost_estimate=pl.CostEstimate(
+            flops=2 * n * total * width, bytes_accessed=2 * total * width, transcendentals=0
+        ),
+        name="select_rows",
+    )(round_index, pivots.reshape(1, n), slots, so_far)
+
+
+def vectors_kernel(
+    core_ref, cols_ref, prev_ref, mine_ref, other_ref, inv_ref, new_ref, turned_ref, came, load
+):
+    m = pl.program_id(0)
+
+    def load_of(m):
+        return pltpu.make_async_copy(prev_ref.at[m], came.at[m], load.at[m])
+
+    @pl.when(m == 0)
+    def _():
+        for other_m in range(came.shape[0]):
+            load_of(other_m).start()
+
+    load_of(m).wait()
+    mine, other = mine_ref[...].astype(F32), other_ref[...].astype(F32)
+    first = core_ref[0] == 0
+    rows = jnp.concatenate(
+        [jnp.where(first, mine, other), jnp.where(first, other, mine)], axis=1
+    ).astype(BF16)
     contract = (((1,), (1,)), ((), ()))
-    correction = lax.dot_general(prev_ref[0], rows_ref[...], contract, preferred_element_type=F32)
+    correction = lax.dot_general(came[m], rows, contract, preferred_element_type=F32)
     residual = (cols_ref[0].astype(F32) - correction).astype(BF16)
     inv = inv_ref[...]
     row, column = (lax.broadcasted_iota(jnp.int32, inv.shape, d) for d in (0, 1))
@@ -106,7 +162,7 @@
     turned_ref[0] = new.T
 
 
-def vectors(pivot_columns, previous, rows, pivot_inverse):
+def vectors(core, pivot_columns, previous, mine, other, pivot_inverse):
     mu, nu, k = previous.shape
     n = pivot_columns.shape[2]
     slab = lambda m: (m, 0, 0)
@@ -119,20 +175,23 @@
             jax.ShapeDtypeStruct((mu, n, nu), BF16),
         ),
         in_specs=[
+            pl.BlockSpec(memory_space=pltpu.SMEM),
             pl.BlockSpec((1, nu, n), slab),
-            pl.BlockSpec((1, nu, k), slab),
-            pl.BlockSpec((n, k), whole),
+            pl.BlockSpec(memory_space=pltpu.HBM),
+            pl.BlockSpec((n, k // 2), whole),
+            pl.BlockSpec((n, k // 2), whole),
             pl.BlockSpec((n, n), whole),
         ],
         out_specs=(pl.BlockSpec((1, nu, n), slab), pl.BlockSpec((1, n, nu), slab)),
-        compiler_params=pltpu.CompilerParams(vmem_limit_bytes=20 << 20),
+        scratch_shapes=[pltpu.VMEM((mu, nu, k), BF16), pltpu.SemaphoreType.DMA((mu,))],
+        compiler_params=pltpu.CompilerParams(vmem_limit_bytes=24 << 20),
         cost_estimate=pl.CostEstimate(
             flops=2 * mu * nu * n * (k + n),
             bytes_accessed=2 * mu * nu * (k + 3 * n),
             transcendentals=0,
         ),
         name="vectors",
-    )(pivot_columns, previous, rows, pivot_inverse)
+    )(core, pivot_columns, previous, mine, other, pivot_inverse)
 
 
 def parts_kernel(me_ref, turned_ref, orb_ref, *out_refs, ahead, owners):
@@ -272,17 +331,41 @@
     return jnp.sum(x.astype(F32), axis=0).astype(BF16)
 
 
+def pivot_halves(n_rows, n_grp, pivots, previous):
+    mu, nu, k = previous.shape
+    n = pivots.shape[0]
+    half = k // 2
+    per_line = mu * NBAS
+    line = lax.axis_index("rows") * per_line
+    base = line + lax.axis_index("grp") * nu
+    line, base = line.astype(jnp.int32), base.astype(jnp.int32)
+
+    def one_round(index, so_far):
+        index = jnp.asarray(index, jnp.int32)
+        picked = pick_rows(jnp.stack([line, base, index]), pivots, previous)
+        line_slots = sum_rows(exchange(jnp.broadcast_to(picked, (n_grp,) + picked.shape), "grp"))
+        both = jnp.stack([line_slots[:, :half], line_slots[:, half:]])
+        copies = jnp.broadcast_to(both, (n_rows // 2,) + both.shape)
+        slots = exchange(copies.reshape(n_rows, SLOTS, half), "rows")
+        return select_rows(
+            index.reshape(1), pivots, slots.reshape(n_rows * SLOTS, half), so_far, per_line
+        )
+
+    lines = pivots // per_line
+    most = jnp.max(jnp.sum(lines[:, None] == jnp.arange(n_rows)[None, :], axis=0))
+    rounds = (most + SLOTS - 1) // SLOTS
+    mine = one_round(0, jnp.zeros((n, half), BF16))
+    mine = lax.fori_loop(1, rounds, one_round, mine)
+    other = lax.ppermute(mine, "rows", [(i, i ^ 1) for i in range(n_rows)])
+    return mine, other
+
+
 def per_device(n_rows, n_grp, pivot_columns, previous, pivots, pivot_inverse, orbitals, slab_orbitals):
-    mu, nu, k = previous.shape
-    n = pivot_columns.shape[2]
-    base = lax.axis_index("rows") * (mu * NBAS) + lax.axis_index("grp") * nu
     previous = pltpu.with_memory_space_constraint(previous, pltpu.HBM)
-    picked = pick_rows(base.reshape(1).astype(jnp.int32), pivots, previous)
-    mine = sum_rows(exchange(picked.reshape(n_rows, n // n_rows, k), "rows"))
-    mine = sum_rows(exchange(jnp.broadcast_to(mine, (n_grp,) + mine.shape), "grp"))
-    rows = exchange(jnp.broadcast_to(mine, (n_rows,) + mine.shape), "rows").reshape(n, k)
+    mine, other = pivot_halves(n_rows, n_grp, pivots, previous)
+    core = (lax.axis_index("rows") % 2).reshape(1).astype(jnp.int32)
     me = lax.axis_index("grp").reshape(1).astype(jnp.int32)
-    new_vectors, turned = vectors(pivot_columns, previous, rows, pivot_inverse)
+    new_vectors, turned = vectors(core, pivot_columns, previous, mine, other, pivot_inverse)
     half = exchange(reduce_to_owner(me, turned, orbitals, n_grp, n_rows), "rows")
     return new_vectors, final(half.reshape(-1, half.shape[-1]), slab_orbitals)
 

time: 107 us -> 102 us (0.953)
  blocking collectives: 65.6 us -> 37.1 us
  waiting for transfers between devices: 15.6 us -> 27.1 us
  starting transfers between devices: 8.65 us -> 19.3 us
    all_to_all x4 -> x2, blocking collectives: 65.6 us -> 37.1 us  [exchange(): return lax.all_to_all(x, axis, split_axis=0, concat_axis=0, tiled=True)]
    all_to_all x0 -> x1, starting transfers between devices: none -> 10.4 us  [exchange(): return lax.all_to_all(x, axis, split_axis=0, concat_axis=0, tiled=True)]
    all_to_all x0 -> x1, waiting for transfers between devices: none -> 8.85 us  [exchange(): return lax.all_to_all(x, axis, split_axis=0, concat_axis=0, tiled=True)]
    ppermute x8, waiting for transfers between devices: 15.6 us -> 17 us  [hop(): lax.ppermute(x, 'grp', [(i, (i + way) % owners) for i in range(owners)])]
    ppermute x0 -> x1, waiting for transfers between devices: none -> 1.32 us  [pivot_halves(): other = lax.ppermute(mine, 'rows', [(i, i ^ 1) for i in range(n_rows)])]
  transfers between devices with their start and end apart: 8 -> 10, of which waited for: 5 -> 7; matrix products, arithmetic and copies ran while one was open for 0% -> 1% of each run, Pallas kernels for 3% -> 3%
where the time goes in v4:
time: 102 us; the launch traced here: 101 us
  blocking collectives  37.1 us (36%)
  waiting for transfers between devices  27.1 us (27%)
  starting transfers between devices  19.3 us (19%)
  Pallas kernels  13.9 us (14%)
  between operations  1.54 us (2%)
  other arithmetic  1.29 us (1%)
  local copies, waits for them, and re-layouts  1.09 us (1%)
    all_to_all x2, blocking collectives, exchange(): return lax.all_to_all(x, axis, split_axis=0, concat_axis=0, tiled=True)  37.1 us
    ppermute x8, waiting for transfers between devices, hop(): lax.ppermute(x, 'grp', [(i, (i + way) % owners) for i in range(owners)])  17 us
    all_to_all x1, starting transfers between devices, exchange(): return lax.all_to_all(x, axis, split_axis=0, concat_axis=0, tiled=True)  10.4 us
    all_to_all x1, waiting for transfers between devices, exchange(): return lax.all_to_all(x, axis, split_axis=0, concat_axis=0, tiled=True)  8.85 us
    ppermute x8, starting transfers between devices, hop(): lax.ppermute(x, 'grp', [(i, (i + way) % owners) for i in range(owners)])  8.83 us
    pallas_call x1, Pallas kernels, vectors(): pl.pallas_call(vectors_kernel, grid=(mu,), out_shape=(jax.ShapeDtypeStruc...  5.87 us
    pallas_call x5, Pallas kernels, parts(): pl.pallas_call(functools.partial(parts_kernel, ahead=ahead, owners=owners...  4.3 us
    pallas_call x1, Pallas kernels, final(): pl.pallas_call(final_kernel, out_shape=jax.ShapeDtypeStruct((keep, occ, w...  2.07 us
  transfers between devices with their start and end apart: 10, of which 7 were waited for; matrix products, arithmetic and copies ran while one was open for 1% of the time, Pallas kernels for 3%

profile of v4, /device:TPU:1, one launch (start us, length us, event | category | flops | bytes accessed | tf_op | source)
XLA Modules:
  0.0 101.4 jit_solution(6845403382418025871)
XLA Ops:
  0.7 1.1 %pick_rows.5 = bf16[24,512]{1,0:T(8,128)(2,1)S(1)} custom-call(s32[3]{0:T(128)S(1)} %pad_add_fusion.1.where_from_ref, s32[2,128]{1,0:T(2,128)} %bitcast.71, bf16[4,1280,512]{2,1,0:T(8,128)(2,1)} %prev_ref.3), custom_call_target="tpu_custom_call" | custom-call | flops 131072 | bytes 262144 | tf_op jit(solution)/shard_map/pick_rows/pallas_call | solution.py:80
  1.8 18.6 %all_to_all.33 = bf16[8,24,512]{2,1,0:T(8,128)(2,1)S(1)} all-to-all(bf16[8,24,512]{2,1,0:T(8,128)(2,1)S(1)} %broadcast_in_dim.23), channel_id=1, replica_groups=mesh['rows'=32,'grp'=8] {'grp'}, dimensions={0} | all-to-all | bytes 393216 | tf_op jit(solution)/shard_map/all_to_all | solution.py:327
  20.5 0.8 broadcast_in_dim.24
  21.3 10.4 %all-to-all-start.3 = ((bf16[32,24,256]{2,1,0:T(8,128)(2,1)}), bf16[32,24,256]{2,1,0:T(8,128)(2,1)S(1)}, u32[]{:S(2)}, u32[]{:S(2)}) async-start(bf16[32,24,256]{2,1,0:T(8,128)(2,1)} %bitcast.16), calls=%async_computation.3 | async-start | bytes 786432 | tf_op jit(solution)/shard_map/all_to_all | solution.py:327
  31.8 0.6 reduce_max.9
  33.1 8.8 %all-to-all-done.3 = bf16[32,24,256]{2,1,0:T(8,128)(2,1)S(1)} async-done(((bf16[32,24,256]{2,1,0:T(8,128)(2,1)}), bf16[32,24,256]{2,1,0:T(8,128)(2,1)S(1)}, u32[]{:S(2)}, u32[]{:S(2)}) %all-to-all-start.3) | async-done | bytes 393248 | tf_op jit(solution)/shard_map/all_to_all | solution.py:327
  42.7 1.3 %collective-permute-done.other_ref = bf16[256,256]{1,0:T(8,128)(2,1)S(1)} collective-permute-done((bf16[256,256]{1,0:T(8,128)(2,1)S(1)}, bf16[256,256]{1,0:T(8,128)(2,1)S(1)}, u32[]{:S(2)}, u32[]{:S(2)}) %collective-permute-start) | collective-permute-done | bytes 131104 | tf_op jit(solution)/shard_map/ppermute | solution.py:359
  44.3 5.9 %vectors.1 = (bf16[4,1280,256]{2,1,0:T(8,128)(2,1)}, bf16[4,256,1280]{2,1,0:T(8,128)(2,1)S(1)}) custom-call(s32[1]{0:T(128)} %bitcast.9.core_ref, bf16[4,1280,256]{2,1,0:T(8,128)(2,1)S(1)} %copy-done.1, bf16[4,1280,512]{2,1,0:T(8,128)(2,1)} %get-tuple-element.206, bf16[256,256]{1,0:T(8,128)(2,1)S(1)} %get-tuple-element.95.mine_ref, ...), custom_call_target="tpu_custom_call" | custom-call | flops 2013265920 | bytes 13107200 | tf_op jit(solution)/shard_map/vectors/pallas_call | solution.py:170
  50.2 0.9 parts.9
  51.1 1.5 %collective-permute-start.1 = (bf16[16,4,8,128]{3,2,1,0:T(8,128)(2,1)S(1)}, bf16[16,4,8,128]{3,2,1,0:T(8,128)(2,1)S(1)}, u32[]{:S(2)}, u32[]{:S(2)}) collective-permute-start(bf16[16,4,8,128]{3,2,1,0:T(8,128)(2,1)S(1)} %get-tuple-element.98), channel_id=1, source_target_pairs={{0,1},{1,2},{2,3},{3,4},{4,5},{5,6},{6,7},{7,0},{8,9},{9,10},{10,1... | collective-permute-start | bytes 393224 | tf_op jit(solution)/shard_map/ppermute | solution.py:274
  52.6 0.9 parts.8.own_ref
  53.5 2.9 %collective-permute-done.5.came_ref = bf16[16,4,8,128]{3,2,1,0:T(8,128)(2,1)S(1)} collective-permute-done((bf16[16,4,8,128]{3,2,1,0:T(8,128)(2,1)S(1)}, bf16[16,4,8,128]{3,2,1,0:T(8,128)(2,1)S(1)}, u32[]{:S(2)}, u32[]{:S(2)}) %collective-permute-start.5) | collective-permute-done | bytes 131104 | tf_op jit(solution)/shard_map/ppermute | solution.py:274
  56.4 1.5 %collective-permute-start.6 = (bf16[32,4,8,128]{3,2,1,0:T(8,128)(2,1)S(1)}, bf16[32,4,8,128]{3,2,1,0:T(8,128)(2,1)S(1)}, u32[]{:S(2)}, u32[]{:S(2)}) collective-permute-start(bf16[32,4,8,128]{3,2,1,0:T(8,128)(2,1)S(1)} %join.3), channel_id=1, source_target_pairs={{0,7},{1,0},{2,1},{3,2},{4,3},{5,4},{6,5},{7,6},{8,15},{9,8},{10,9... | collective-permute-start | bytes 786440 | tf_op jit(solution)/shard_map/ppermute | solution.py:274
  58.1 0.9 parts.7
  58.9 4.7 %collective-permute-done.6 = bf16[32,4,8,128]{3,2,1,0:T(8,128)(2,1)S(1)} collective-permute-done((bf16[32,4,8,128]{3,2,1,0:T(8,128)(2,1)S(1)}, bf16[32,4,8,128]{3,2,1,0:T(8,128)(2,1)S(1)}, u32[]{:S(2)}, u32[]{:S(2)}) %collective-permute-start.6) | collective-permute-done | bytes 262176 | tf_op jit(solution)/shard_map/ppermute | solution.py:274
  63.7 2.6 %collective-permute-done.2 = bf16[32,4,8,128]{3,2,1,0:T(8,128)(2,1)S(1)} collective-permute-done((bf16[32,4,8,128]{3,2,1,0:T(8,128)(2,1)S(1)}, bf16[32,4,8,128]{3,2,1,0:T(8,128)(2,1)S(1)}, u32[]{:S(2)}, u32[]{:S(2)}) %collective-permute-start.2) | collective-permute-done | bytes 262176 | tf_op jit(solution)/shard_map/ppermute | solution.py:274
  66.5 2.7 %collective-permute-start.7 = (bf16[32,4,8,128]{3,2,1,0:T(8,128)(2,1)S(1)}, bf16[32,4,8,128]{3,2,1,0:T(8,128)(2,1)S(1)}, u32[]{:S(2)}, u32[]{:S(2)}) collective-permute-start(bf16[32,4,8,128]{3,2,1,0:T(8,128)(2,1)S(1)} %get-tuple-element.119), channel_id=1, source_target_pairs={{0,7},{1,0},{2,1},{3,2},{4,3},{5,4},{6,5},{7,6},{8,15},{9,8},{10,9... | collective-permute-start | bytes 786440 | tf_op jit(solution)/shard_map/ppermute | solution.py:274
  69.2 0.9 parts.6
  70.1 3.8 %collective-permute-done.3 = bf16[32,4,8,128]{3,2,1,0:T(8,128)(2,1)S(1)} collective-permute-done((bf16[32,4,8,128]{3,2,1,0:T(8,128)(2,1)S(1)}, bf16[32,4,8,128]{3,2,1,0:T(8,128)(2,1)S(1)}, u32[]{:S(2)}, u32[]{:S(2)}) %collective-permute-start.3) | collective-permute-done | bytes 262176 | tf_op jit(solution)/shard_map/ppermute | solution.py:274
  74.3 2.7 %collective-permute-start.8 = (bf16[32,4,8,128]{3,2,1,0:T(8,128)(2,1)S(1)}, bf16[32,4,8,128]{3,2,1,0:T(8,128)(2,1)S(1)}, u32[]{:S(2)}, u32[]{:S(2)}) collective-permute-start(bf16[32,4,8,128]{3,2,1,0:T(8,128)(2,1)S(1)} %get-tuple-element.117), channel_id=1, source_target_pairs={{0,7},{1,0},{2,1},{3,2},{4,3},{5,4},{6,5},{7,6},{8,15},{9,8},{10,9... | collective-permute-start | bytes 786440 | tf_op jit(solution)/shard_map/ppermute | solution.py:274
  77.0 0.8 parts.5
  77.9 2.9 %collective-permute-done.4 = bf16[32,4,8,128]{3,2,1,0:T(8,128)(2,1)S(1)} collective-permute-done((bf16[32,4,8,128]{3,2,1,0:T(8,128)(2,1)S(1)}, bf16[32,4,8,128]{3,2,1,0:T(8,128)(2,1)S(1)}, u32[]{:S(2)}, u32[]{:S(2)}) %collective-permute-start.4) | collective-permute-done | bytes 262176 | tf_op jit(solution)/shard_map/ppermute | solution.py:274
  80.9 18.4 %all_to_all.34 = f32[32,4,8,128]{3,2,1,0:T(8,128)S(1)} all-to-all(f32[32,4,8,128]{3,2,1,0:T(8,128)S(1)} %fusion.8), channel_id=1, replica_groups=mesh['rows'=32,'grp'=8] {'rows'}, dimensions={0} | all-to-all | bytes 1048576 | tf_op jit(solution)/shard_map/all_to_all | solution.py:327
  99.3 2.1 %final.1 = bf16[8,1024,128]{2,1,0:T(8,128)(2,1)} custom-call(f32[1024,128]{1,0:T(8,128)S(1)} %bitcast.69, bf16[128,1024]{1,0:T(8,128)(2,1)S(1)} %copy-done.2), custom_call_target="tpu_custom_call" | custom-call | flops 536870912 | bytes 2621440 | tf_op jit(solution)/shard_map/final/pallas_call | solution.py:313
  (33 shorter events, 2.3 us)
Async XLA Ops:
  0.7 31.0 %copy-start.4 = (s32[256]{0:T(256)S(1)}, s32[256]{0:T(256)}, u32[]{:S(2)}) copy-start(s32[256]{0:T(256)} %param.10) | copy-start | bytes 3076
  21.3 20.7 %all-to-all-start.3 = ((bf16[32,24,256]{2,1,0:T(8,128)(2,1)}), bf16[32,24,256]{2,1,0:T(8,128)(2,1)S(1)}, u32[]{:S(2)}, u32[]{:S(2)}) async-start(bf16[32,24,256]{2,1,0:T(8,128)(2,1)} %bitcast.16), calls=%async_computation.3 | async-start | bytes 786432 | tf_op jit(solution)/shard_map/all_to_all | solution.py:327
  42.5 1.7 %copy-start.1 = (bf16[4,1280,256]{2,1,0:T(8,128)(2,1)S(1)}, bf16[4,1280,256]{2,1,0:T(8,128)(2,1)}, u32[]{:S(2)}) copy-start(bf16[4,1280,256]{2,1,0:T(8,128)(2,1)} %cols_ref.1) | copy-start | bytes 7864324
  42.6 1.7 %copy-start.3 = (bf16[256,256]{1,0:T(8,128)(2,1)S(1)}, bf16[256,256]{1,0:T(8,128)(2,1)}, u32[]{:S(2)}) copy-start(bf16[256,256]{1,0:T(8,128)(2,1)} %inv_ref.1) | copy-start | bytes 393220
  42.6 1.4 %collective-permute-start = (bf16[256,256]{1,0:T(8,128)(2,1)S(1)}, bf16[256,256]{1,0:T(8,128)(2,1)S(1)}, u32[]{:S(2)}, u32[]{:S(2)}) collective-permute-start(bf16[256,256]{1,0:T(8,128)(2,1)S(1)} %get-tuple-element.95.mine_ref), channel_id=1, source_target_pairs={{0,8},{8,0},{16,24},{24,16},{32,40},{40,32},{48,56},{56,48},{64,72... | collective-permute-start | bytes 393224 | tf_op jit(solution)/shard_map/ppermute | solution.py:359
  44.3 5.9 %copy-start = (bf16[1280,1024]{1,0:T(8,128)(2,1)S(1)}, bf16[1280,1024]{1,0:T(8,128)(2,1)}, u32[]{:S(2)}) copy-start(bf16[1280,1024]{1,0:T(8,128)(2,1)} %orb_ref.9) | copy-start | bytes 7864324
  51.1 5.3 %collective-permute-start.5 = (bf16[16,4,8,128]{3,2,1,0:T(8,128)(2,1)S(1)}, bf16[16,4,8,128]{3,2,1,0:T(8,128)(2,1)S(1)}, u32[]{:S(2)}, u32[]{:S(2)}) collective-permute-start(bf16[16,4,8,128]{3,2,1,0:T(8,128)(2,1)S(1)} %get-tuple-element.99), channel_id=1, source_target_pairs={{0,7},{1,0},{2,1},{3,2},{4,3},{5,4},{6,5},{7,6},{8,15},{9,8},{10,9... | collective-permute-start | bytes 393224 | tf_op jit(solution)/shard_map/ppermute | solution.py:274
  51.1 6.7 %collective-permute-start.1 = (bf16[16,4,8,128]{3,2,1,0:T(8,128)(2,1)S(1)}, bf16[16,4,8,128]{3,2,1,0:T(8,128)(2,1)S(1)}, u32[]{:S(2)}, u32[]{:S(2)}) collective-permute-start(bf16[16,4,8,128]{3,2,1,0:T(8,128)(2,1)S(1)} %get-tuple-element.98), channel_id=1, source_target_pairs={{0,1},{1,2},{2,3},{3,4},{4,5},{5,6},{6,7},{7,0},{8,9},{9,10},{10,1... | collective-permute-start | bytes 393224 | tf_op jit(solution)/shard_map/ppermute | solution.py:274
  56.4 7.3 %collective-permute-start.6 = (bf16[32,4,8,128]{3,2,1,0:T(8,128)(2,1)S(1)}, bf16[32,4,8,128]{3,2,1,0:T(8,128)(2,1)S(1)}, u32[]{:S(2)}, u32[]{:S(2)}) collective-permute-start(bf16[32,4,8,128]{3,2,1,0:T(8,128)(2,1)S(1)} %join.3), channel_id=1, source_target_pairs={{0,7},{1,0},{2,1},{3,2},{4,3},{5,4},{6,5},{7,6},{8,15},{9,8},{10,9... | collective-permute-start | bytes 786440 | tf_op jit(solution)/shard_map/ppermute | solution.py:274
  57.9 8.4 %collective-permute-start.2 = (bf16[32,4,8,128]{3,2,1,0:T(8,128)(2,1)S(1)}, bf16[32,4,8,128]{3,2,1,0:T(8,128)(2,1)S(1)}, u32[]{:S(2)}, u32[]{:S(2)}) collective-permute-start(bf16[32,4,8,128]{3,2,1,0:T(8,128)(2,1)S(1)} %join.2), channel_id=1, source_target_pairs={{0,1},{1,2},{2,3},{3,4},{4,5},{5,6},{6,7},{7,0},{8,9},{9,10},{10,1... | collective-permute-start | bytes 786440 | tf_op jit(solution)/shard_map/ppermute | solution.py:274
  66.5 7.4 %collective-permute-start.3 = (bf16[32,4,8,128]{3,2,1,0:T(8,128)(2,1)S(1)}, bf16[32,4,8,128]{3,2,1,0:T(8,128)(2,1)S(1)}, u32[]{:S(2)}, u32[]{:S(2)}) collective-permute-start(bf16[32,4,8,128]{3,2,1,0:T(8,128)(2,1)S(1)} %get-tuple-element.118), channel_id=1, source_target_pairs={{0,1},{1,2},{2,3},{3,4},{4,5},{5,6},{6,7},{7,0},{8,9},{9,10},{10,1... | collective-permute-start | bytes 786440 | tf_op jit(solution)/shard_map/ppermute | solution.py:274
  66.5 7.4 %collective-permute-start.7 = (bf16[32,4,8,128]{3,2,1,0:T(8,128)(2,1)S(1)}, bf16[32,4,8,128]{3,2,1,0:T(8,128)(2,1)S(1)}, u32[]{:S(2)}, u32[]{:S(2)}) collective-permute-start(bf16[32,4,8,128]{3,2,1,0:T(8,128)(2,1)S(1)} %get-tuple-element.119), channel_id=1, source_target_pairs={{0,7},{1,0},{2,1},{3,2},{4,3},{5,4},{6,5},{7,6},{8,15},{9,8},{10,9... | collective-permute-start | bytes 786440 | tf_op jit(solution)/shard_map/ppermute | solution.py:274
  74.1 6.7 %collective-permute-start.4 = (bf16[32,4,8,128]{3,2,1,0:T(8,128)(2,1)S(1)}, bf16[32,4,8,128]{3,2,1,0:T(8,128)(2,1)S(1)}, u32[]{:S(2)}, u32[]{:S(2)}) collective-permute-start(bf16[32,4,8,128]{3,2,1,0:T(8,128)(2,1)S(1)} %get-tuple-element.116), channel_id=1, source_target_pairs={{0,1},{1,2},{2,3},{3,4},{4,5},{5,6},{6,7},{7,0},{8,9},{9,10},{10,1... | collective-permute-start | bytes 786440 | tf_op jit(solution)/shard_map/ppermute | solution.py:274
  74.3 6.4 %collective-permute-start.8 = (bf16[32,4,8,128]{3,2,1,0:T(8,128)(2,1)S(1)}, bf16[32,4,8,128]{3,2,1,0:T(8,128)(2,1)S(1)}, u32[]{:S(2)}, u32[]{:S(2)}) collective-permute-start(bf16[32,4,8,128]{3,2,1,0:T(8,128)(2,1)S(1)} %get-tuple-element.117), channel_id=1, source_target_pairs={{0,7},{1,0},{2,1},{3,2},{4,3},{5,4},{6,5},{7,6},{8,15},{9,8},{10,9... | collective-permute-start | bytes 786440 | tf_op jit(solution)/shard_map/ppermute | solution.py:274
  77.8 21.4 %copy-start.2 = (bf16[128,1024]{1,0:T(8,128)(2,1)S(1)}, bf16[128,1024]{1,0:T(8,128)(2,1)}, u32[]{:S(2)}) copy-start(bf16[128,1024]{1,0:T(8,128)(2,1)} %slab_ref.1) | copy-start | bytes 786436

commit v5 on v4

--- a/solution.py
+++ b/solution.py
@@ -98,7 +98,7 @@
     )(where_from, pivots.reshape(n // lanes, lanes), previous)
 
 
-def select_kernel(round_ref, piv_ref, slots_ref, so_far_ref, out_ref, *, per_line):
+def select_kernel(round_ref, piv_ref, slots_ref, so_far_ref, out_ref, rounds_ref, *, per_line):
     total, _ = slots_ref.shape
     n = piv_ref.shape[1]
     along = jnp.broadcast_to(piv_ref[...].astype(F32), (n, n))
@@ -106,7 +106,9 @@
     lines = lines_along.T
     earlier = lax.broadcasted_iota(jnp.int32, (n, n), 1) < lax.broadcasted_iota(jnp.int32, (n, n), 0)
     same = jnp.where((lines_along == lines) & earlier, 1.0, 0.0)
-    rank = jnp.sum(same, axis=1, keepdims=True) - (round_ref[0] * SLOTS).astype(F32)
+    rank = jnp.sum(same, axis=1, keepdims=True)
+    rounds_ref[0] = jnp.max(rank).astype(jnp.int32) // SLOTS + 1
+    rank = rank - (round_ref[0] * SLOTS).astype(F32)
     mine = (rank >= 0.0) & (rank < SLOTS)
     index = jnp.where(mine, lines[:, :1] * SLOTS + rank, -1.0).astype(jnp.int32)
     hot = index == lax.broadcasted_iota(jnp.int32, (n, total), 1)
@@ -121,9 +123,12 @@
     vmem = pl.BlockSpec(memory_space=pltpu.VMEM)
     return pl.pallas_call(
         functools.partial(select_kernel, per_line=per_line),
-        out_shape=jax.ShapeDtypeStruct((n, width), BF16),
+        out_shape=(
+            jax.ShapeDtypeStruct((n, width), BF16),
+            jax.ShapeDtypeStruct((1,), jnp.int32),
+        ),
         in_specs=[pl.BlockSpec(memory_space=pltpu.SMEM), vmem, vmem, vmem],
-        out_specs=vmem,
+        out_specs=(vmem, pl.BlockSpec(memory_space=pltpu.SMEM)),
         compiler_params=pltpu.CompilerParams(vmem_limit_bytes=8 << 20),
         cost_estimate=pl.CostEstimate(
             flops=2 * n * total * width, bytes_accessed=2 * total * width, transcendentals=0
@@ -132,58 +137,95 @@
     )(round_index, pivots.reshape(1, n), slots, so_far)
 
 
+def spread_kernel(came_ref, out_ref):
+    total = jnp.sum(came_ref[...].astype(F32), axis=0).astype(BF16)
+    half = out_ref.shape[2]
+    for c in range(2):
+        piece = total[:, c * half : (c + 1) * half]
+
+        @pl.loop(0, out_ref.shape[0] // 2)
+        def _(chip):
+            out_ref[2 * chip + c] = piece
+
+
+def spread(came, n_rows):
+    n_grp, slots, k = came.shape
+    vmem = pl.BlockSpec(memory_space=pltpu.VMEM)
+    return pl.pallas_call(
+        spread_kernel,
+        out_shape=jax.ShapeDtypeStruct((n_rows, slots, k // 2), BF16),
+        in_specs=[vmem],
+        out_specs=vmem,
+        compiler_params=pltpu.CompilerParams(vmem_limit_bytes=4 << 20),
+        cost_estimate=pl.CostEstimate(
+            flops=n_grp * slots * k, bytes_accessed=n_rows * slots * k, transcendentals=0
+        ),
+        name="spread",
+    )(came)
+
+
 def vectors_kernel(
-    core_ref, cols_ref, prev_ref, mine_ref, other_ref, inv_ref, new_ref, turned_ref, came, load
+    core_ref, cols_ref, prev_ref, mine_ref, other_ref, inv_ref, new_ref, turned_ref, came, made, load, store
 ):
-    m = pl.program_id(0)
+    mu = came.shape[0]
 
     def load_of(m):
         return pltpu.make_async_copy(prev_ref.at[m], came.at[m], load.at[m])
 
-    @pl.when(m == 0)
-    def _():
-        for other_m in range(came.shape[0]):
-            load_of(other_m).start()
-
-    load_of(m).wait()
-    mine, other = mine_ref[...].astype(F32), other_ref[...].astype(F32)
-    first = core_ref[0] == 0
-    rows = jnp.concatenate(
-        [jnp.where(first, mine, other), jnp.where(first, other, mine)], axis=1
-    ).astype(BF16)
-    contract = (((1,), (1,)), ((), ()))
-    correction = lax.dot_general(came[m], rows, contract, preferred_element_type=F32)
-    residual = (cols_ref[0].astype(F32) - correction).astype(BF16)
-    inv = inv_ref[...]
-    row, column = (lax.broadcasted_iota(jnp.int32, inv.shape, d) for d in (0, 1))
-    upper = jnp.where(row > column, 0.0, inv.astype(F32)).astype(BF16)
-    new = jnp.dot(residual, upper, preferred_element_type=F32).astype(BF16)
-    new_ref[0] = new
-    turned_ref[0] = new.T
+    def store_of(m):
+        return pltpu.make_async_copy(made.at[m], new_ref.at[m], store.at[m])
+
+    for m in range(mu):
+        load_of(m).start()
+
+    @pl.loop(0, mu)
+    def _(m):
+        load_of(m).wait()
+        mine, other = mine_ref[...].astype(F32), other_ref[...].astype(F32)
+        first = core_ref[0] == 0
+        rows = jnp.concatenate(
+            [jnp.where(first, mine, other), jnp.where(first, other, mine)], axis=1
+        ).astype(BF16)
+        contract = (((1,), (1,)), ((), ()))
+        correction = lax.dot_general(came[m], rows, contract, preferred_element_type=F32)
+        residual = (cols_ref[m].astype(F32) - correction).astype(BF16)
+        inv = inv_ref[...]
+        row, column = (lax.broadcasted_iota(jnp.int32, inv.shape, d) for d in (0, 1))
+        upper = jnp.where(row > column, 0.0, inv.astype(F32)).astype(BF16)
+        new = jnp.dot(residual, upper, preferred_element_type=F32).astype(BF16)
+        made[m] = new
+        store_of(m).start()
+        turned_ref[m] = new.T
+
+    for m in range(mu):
+        store_of(m).wait()
 
 
 def vectors(core, pivot_columns, previous, mine, other, pivot_inverse):
     mu, nu, k = previous.shape
     n = pivot_columns.shape[2]
-    slab = lambda m: (m, 0, 0)
-    whole = lambda m: (0, 0)
+    vmem = pl.BlockSpec(memory_space=pltpu.VMEM)
     return pl.pallas_call(
         vectors_kernel,
-        grid=(mu,),
         out_shape=(
             jax.ShapeDtypeStruct((mu, nu, n), BF16),
             jax.ShapeDtypeStruct((mu, n, nu), BF16),
         ),
         in_specs=[
             pl.BlockSpec(memory_space=pltpu.SMEM),
-            pl.BlockSpec((1, nu, n), slab),
+            vmem,
             pl.BlockSpec(memory_space=pltpu.HBM),
-            pl.BlockSpec((n, k // 2), whole),
-            pl.BlockSpec((n, k // 2), whole),
-            pl.BlockSpec((n, n), whole),
+            vmem,
+            vmem,
+            vmem,
         ],
-        out_specs=(pl.BlockSpec((1, nu, n), slab), pl.BlockSpec((1, n, nu), slab)),
-        scratch_shapes=[pltpu.VMEM((mu, nu, k), BF16), pltpu.SemaphoreType.DMA((mu,))],
+        out_specs=(pl.BlockSpec(memory_space=pl.ANY), vmem),
+        scratch_shapes=[
+            pltpu.VMEM((mu, nu, k), BF16),
+            pltpu.VMEM((mu, nu, n), BF16),
+            pltpu.SemaphoreType.DMA((mu,)),
+            pltpu.SemaphoreType.DMA((mu,)),
+        ],
         compiler_params=pltpu.CompilerParams(vmem_limit_bytes=24 << 20),
         cost_estimate=pl.CostEstimate(
             flops=2 * mu * nu * n * (k + n),
@@ -289,30 +331,41 @@
     return own((0,))[0] + right.astype(F32) + left.astype(F32)
 
 
-def final_kernel(half_ref, slab_ref, out_ref):
+def final_kernel(half_ref, slab_ref, out_ref, turned_ref):
     rows, width = half_ref.shape
     mu = slab_ref.shape[0]
     keep = rows // mu
-    slab_t = slab_ref[...].T
-    slab_t = jnp.concatenate([slab_t, slab_t], axis=1)
-    for p in range(0, keep, 2):
-        pair = jnp.concatenate(
-            [half_ref[pl.ds(q, mu, stride=keep), :] for q in (p, p + 1)], axis=1
-        )
-        high = pair.astype(BF16)
-        low = (pair - high.astype(F32)).astype(BF16)
-        both = jnp.dot(slab_t, jnp.concatenate([high, low], axis=0), preferred_element_type=F32)
-        out_ref[p] = both[:, :width].astype(BF16)
-        out_ref[p + 1] = both[:, width:].astype(BF16)
+
+    @pl.when(pl.program_id(0) == 0)
+    def _():
+        slab_t = slab_ref[...].T
+        turned_ref[...] = jnp.concatenate([slab_t, slab_t], axis=1)
+
+    first = pl.program_id(0) * 2
+    pair = jnp.concatenate(
+        [half_ref[pl.ds(first + q, mu, stride=keep), :] for q in (0, 1)], axis=1
+    )
+    high = pair.astype(BF16)
+    low = (pair - high.astype(F32)).astype(BF16)
+    both = jnp.dot(
+        turned_ref[...], jnp.concatenate([high, low], axis=0), preferred_element_type=F32
+    )
+    out_ref[0] = both[:, :width].astype(BF16)
+    out_ref[1] = both[:, width:].astype(BF16)
 
 
 def final(half, slab):
     mu, occ = slab.shape
     rows, width = half.shape
     keep = rows // mu
+    whole = lambda i: (0, 0)
     return pl.pallas_call(
         final_kernel,
+        grid=(keep // 2,),
         out_shape=jax.ShapeDtypeStruct((keep, occ, width), BF16),
+        in_specs=[pl.BlockSpec((rows, width), whole), pl.BlockSpec((mu, occ), whole)],
+        out_specs=pl.BlockSpec((2, occ, width), lambda i: (i, 0, 0)),
+        scratch_shapes=[pltpu.VMEM((occ, 2 * mu), BF16)],
         compiler_params=pltpu.CompilerParams(vmem_limit_bytes=16 << 20),
         cost_estimate=pl.CostEstimate(
             flops=4 * rows * width * occ,
@@ -325,10 +378,6 @@
 
 def exchange(x, axis):
     return lax.all_to_all(x, axis, split_axis=0, concat_axis=0, tiled=True)
-
-
-def sum_rows(x):
-    return jnp.sum(x.astype(F32), axis=0).astype(BF16)
 
 
 def pivot_halves(n_rows, n_grp, pivots, previous):
@@ -343,19 +392,15 @@
     def one_round(index, so_far):
         index = jnp.asarray(index, jnp.int32)
         picked = pick_rows(jnp.stack([line, base, index]), pivots, previous)
-        line_slots = sum_rows(exchange(jnp.broadcast_to(picked, (n_grp,) + picked.shape), "grp"))
-        both = jnp.stack([line_slots[:, :half], line_slots[:, half:]])
-        copies = jnp.broadcast_to(both, (n_rows // 2,) + both.shape)
-        slots = exchange(copies.reshape(n_rows, SLOTS, half), "rows")
+        came = exchange(jnp.broadcast_to(picked, (n_grp,) + picked.shape), "grp")
+        slots = exchange(spread(came, n_rows), "rows")
         return select_rows(
             index.reshape(1), pivots, slots.reshape(n_rows * SLOTS, half), so_far, per_line
         )
 
-    lines = pivots // per_line
-    most = jnp.max(jnp.sum(lines[:, None] == jnp.arange(n_rows)[None, :], axis=0))
-    rounds = (most + SLOTS - 1) // SLOTS
-    mine = one_round(0, jnp.zeros((n, half), BF16))
-    mine = lax.fori_loop(1, rounds, one_round, mine)
+    mine, rounds = one_round(0, jnp.zeros((n, half), BF16))
+    start, mine, rounds = lax.optimization_barrier((jnp.int32(1), mine, rounds))
+    mine = lax.fori_loop(start, rounds[0], lambda i, rows: one_round(i, rows)[0], mine)
     other = lax.ppermute(mine, "rows", [(i, i ^ 1) for i in range(n_rows)])
     return mine, other
 

time: 102 us -> 102 us (level)
  blocking collectives: 37.1 us -> 57.4 us
  starting transfers between devices: 19.3 us -> 8.92 us
  waiting for transfers between devices: 27.1 us -> 17.5 us
  Pallas kernels: 13.9 us -> 16.1 us
  local copies, waits for them, and re-layouts: 1.09 us -> 0.05 us
    all_to_all x2 -> x3, blocking collectives: 37.1 us -> 57.4 us  [exchange(): return lax.all_to_all(x, axis, split_axis=0, concat_axis=0, tiled=True)]
    all_to_all x1 -> x0, starting transfers between devices: 10.4 us -> none  [exchange(): return lax.all_to_all(x, axis, split_axis=0, concat_axis=0, tiled=True)]
    all_to_all x1 -> x0, waiting for transfers between devices: 8.85 us -> none  [exchange(): return lax.all_to_all(x, axis, split_axis=0, concat_axis=0, tiled=True)]
    pallas_call x1, Pallas kernels: 1.06 us -> 2.21 us  [pick_rows(): pl.pallas_call(pick_kernel, out_shape=jax.ShapeDtypeStruct((SLOTS, k), BF...]
    pallas_call x2 -> x3, Pallas kernels: 7.94 us -> 8.69 us  [the longest x1 5.85 us: vectors(): pl.pallas_call(vectors_kernel, out_shape=(jax.ShapeDtypeStruct((mu, nu, n...]
  transfers between devices with their start and end apart: 10 -> 9, of which waited for: 7 -> 6; matrix products, arithmetic and copies ran while one was open for 1% -> 0% of each run, Pallas kernels for 3% -> 3%
where the time goes in v5:
time: 102 us
  blocking collectives  57.4 us (56%)
  waiting for transfers between devices  17.5 us (17%)
  Pallas kernels  16.1 us (16%)
  starting transfers between devices  8.92 us (9%)
    all_to_all x3, blocking collectives, exchange(): return lax.all_to_all(x, axis, split_axis=0, concat_axis=0, tiled=True)  57.4 us
    ppermute x8, waiting for transfers between devices, hop(): lax.ppermute(x, 'grp', [(i, (i + way) % owners) for i in range(owners)])  16.2 us
    ppermute x8, starting transfers between devices, hop(): lax.ppermute(x, 'grp', [(i, (i + way) % owners) for i in range(owners)])  8.83 us
    pallas_call x1, Pallas kernels, vectors(): pl.pallas_call(vectors_kernel, out_shape=(jax.ShapeDtypeStruct((mu, nu, n...  5.85 us
    pallas_call x5, Pallas kernels, parts(): pl.pallas_call(functools.partial(parts_kernel, ahead=ahead, owners=owners...  4.31 us
    pallas_call x1, Pallas kernels, final(): pl.pallas_call(final_kernel, grid=(keep // 2,), out_shape=jax.ShapeDtypeS...  2.63 us
    pallas_call x1, Pallas kernels, pick_rows(): pl.pallas_call(pick_kernel, out_shape=jax.ShapeDtypeStruct((SLOTS, k), BF...  2.21 us
  transfers between devices with their start and end apart: 9, of which 6 were waited for; matrix products, arithmetic and copies ran while one was open for 0% of the time, Pallas kernels for 3%

profile of v5, /device:TPU:1, one launch (start us, length us, event | category | flops | bytes accessed | tf_op | source)
XLA Modules:
  0.0 102.2 jit_solution(9422613810558245821)
XLA Ops:
  0.7 2.2 %pick_rows.2 = bf16[24,512]{1,0:T(8,128)(2,1)S(1)} custom-call(s32[3]{0:T(128)S(1)} %pad_add_fusion.1.where_from_ref, s32[2,128]{1,0:T(2,128)} %bitcast.58, bf16[4,1280,512]{2,1,0:T(8,128)(2,1)} %prev_ref.3), custom_call_target="tpu_custom_call" | custom-call | flops 131072 | bytes 262144 | tf_op jit(solution)/shard_map/pick_rows/pallas_call | solution.py:80
  3.0 20.7 %all_to_all.27.came_ref = bf16[8,24,512]{2,1,0:T(8,128)(2,1)S(1)} all-to-all(bf16[8,24,512]{2,1,0:T(8,128)(2,1)S(1)} %broadcast_in_dim.9), channel_id=1, replica_groups=mesh['rows'=32,'grp'=8] {'grp'}, dimensions={0} | all-to-all | bytes 393216 | tf_op jit(solution)/shard_map/all_to_all | solution.py:380
  23.8 18.0 %all_to_all.28 = bf16[32,24,256]{2,1,0:T(8,128)(2,1)S(1)} all-to-all(bf16[32,24,256]{2,1,0:T(8,128)(2,1)S(1)} %spread.2), channel_id=1, replica_groups=mesh['rows'=32,'grp'=8] {'rows'}, dimensions={0} | all-to-all | bytes 786432 | tf_op jit(solution)/shard_map/all_to_all | solution.py:380
  41.8 0.9 select_rows.2
  42.7 0.8 while.10
  43.7 1.3 %collective-permute-done.other_ref = bf16[256,256]{1,0:T(8,128)(2,1)S(1)} collective-permute-done((bf16[256,256]{1,0:T(8,128)(2,1)S(1)}, bf16[256,256]{1,0:T(8,128)(2,1)S(1)}, u32[]{:S(2)}, u32[]{:S(2)}) %collective-permute-start) | collective-permute-done | bytes 131104 | tf_op jit(solution)/shard_map/ppermute | solution.py:404
  45.0 5.9 %vectors.1 = (bf16[4,1280,256]{2,1,0:T(8,128)(2,1)}, bf16[4,256,1280]{2,1,0:T(8,128)(2,1)S(1)}) custom-call(s32[1]{0:T(128)} %bitcast.6.core_ref, bf16[4,1280,256]{2,1,0:T(8,128)(2,1)S(1)} %copy-done.1, bf16[4,1280,512]{2,1,0:T(8,128)(2,1)} %get-tuple-element.156, bf16[256,256]{1,0:T(8,128)(2,1)S(1)} %get-tuple-element.55.mine_ref, ...), custom_call_target="tpu_custom_call" | custom-call | flops 2013265920 | bytes 13107200 | tf_op jit(solution)/shard_map/vectors/pallas_call | solution.py:208
  50.9 0.9 parts.9
  51.9 1.5 %collective-permute-start.1 = (bf16[16,4,8,128]{3,2,1,0:T(8,128)(2,1)S(1)}, bf16[16,4,8,128]{3,2,1,0:T(8,128)(2,1)S(1)}, u32[]{:S(2)}, u32[]{:S(2)}) collective-permute-start(bf16[16,4,8,128]{3,2,1,0:T(8,128)(2,1)S(1)} %get-tuple-element.58), channel_id=1, source_target_pairs={{0,1},{1,2},{2,3},{3,4},{4,5},{5,6},{6,7},{7,0},{8,9},{9,10},{10,1... | collective-permute-start | bytes 393224 | tf_op jit(solution)/shard_map/ppermute | solution.py:316
  53.3 0.9 parts.8.own_ref
  54.2 2.6 %collective-permute-done.5.came_ref = bf16[16,4,8,128]{3,2,1,0:T(8,128)(2,1)S(1)} collective-permute-done((bf16[16,4,8,128]{3,2,1,0:T(8,128)(2,1)S(1)}, bf16[16,4,8,128]{3,2,1,0:T(8,128)(2,1)S(1)}, u32[]{:S(2)}, u32[]{:S(2)}) %collective-permute-start.5) | collective-permute-done | bytes 131104 | tf_op jit(solution)/shard_map/ppermute | solution.py:316
  56.8 1.5 %collective-permute-start.6 = (bf16[32,4,8,128]{3,2,1,0:T(8,128)(2,1)S(1)}, bf16[32,4,8,128]{3,2,1,0:T(8,128)(2,1)S(1)}, u32[]{:S(2)}, u32[]{:S(2)}) collective-permute-start(bf16[32,4,8,128]{3,2,1,0:T(8,128)(2,1)S(1)} %join.3), channel_id=1, source_target_pairs={{0,7},{1,0},{2,1},{3,2},{4,3},{5,4},{6,5},{7,6},{8,15},{9,8},{10,9... | collective-permute-start | bytes 786440 | tf_op jit(solution)/shard_map/ppermute | solution.py:316
  58.5 0.9 parts.7
  59.4 4.4 %collective-permute-done.6 = bf16[32,4,8,128]{3,2,1,0:T(8,128)(2,1)S(1)} collective-permute-done((bf16[32,4,8,128]{3,2,1,0:T(8,128)(2,1)S(1)}, bf16[32,4,8,128]{3,2,1,0:T(8,128)(2,1)S(1)}, u32[]{:S(2)}, u32[]{:S(2)}) %collective-permute-start.6) | collective-permute-done | bytes 262176 | tf_op jit(solution)/shard_map/ppermute | solution.py:316
  63.8 2.7 %collective-permute-done.2 = bf16[32,4,8,128]{3,2,1,0:T(8,128)(2,1)S(1)} collective-permute-done((bf16[32,4,8,128]{3,2,1,0:T(8,128)(2,1)S(1)}, bf16[32,4,8,128]{3,2,1,0:T(8,128)(2,1)S(1)}, u32[]{:S(2)}, u32[]{:S(2)}) %collective-permute-start.2) | collective-permute-done | bytes 262176 | tf_op jit(solution)/shard_map/ppermute | solution.py:316
  66.8 2.7 %collective-permute-start.7 = (bf16[32,4,8,128]{3,2,1,0:T(8,128)(2,1)S(1)}, bf16[32,4,8,128]{3,2,1,0:T(8,128)(2,1)S(1)}, u32[]{:S(2)}, u32[]{:S(2)}) collective-permute-start(bf16[32,4,8,128]{3,2,1,0:T(8,128)(2,1)S(1)} %get-tuple-element.77), channel_id=1, source_target_pairs={{0,7},{1,0},{2,1},{3,2},{4,3},{5,4},{6,5},{7,6},{8,15},{9,8},{10,9... | collective-permute-start | bytes 786440 | tf_op jit(solution)/shard_map/ppermute | solution.py:316
  69.4 0.9 parts.6
  70.3 3.5 %collective-permute-done.3 = bf16[32,4,8,128]{3,2,1,0:T(8,128)(2,1)S(1)} collective-permute-done((bf16[32,4,8,128]{3,2,1,0:T(8,128)(2,1)S(1)}, bf16[32,4,8,128]{3,2,1,0:T(8,128)(2,1)S(1)}, u32[]{:S(2)}, u32[]{:S(2)}) %collective-permute-start.3) | collective-permute-done | bytes 262176 | tf_op jit(solution)/shard_map/ppermute | solution.py:316
  74.0 0.3 collective-permute-start.4
  74.3 2.7 %collective-permute-start.8 = (bf16[32,4,8,128]{3,2,1,0:T(8,128)(2,1)S(1)}, bf16[32,4,8,128]{3,2,1,0:T(8,128)(2,1)S(1)}, u32[]{:S(2)}, u32[]{:S(2)}) collective-permute-start(bf16[32,4,8,128]{3,2,1,0:T(8,128)(2,1)S(1)} %get-tuple-element.75), channel_id=1, source_target_pairs={{0,7},{1,0},{2,1},{3,2},{4,3},{5,4},{6,5},{7,6},{8,15},{9,8},{10,9... | collective-permute-start | bytes 786440 | tf_op jit(solution)/shard_map/ppermute | solution.py:316
  76.9 0.9 parts.5
  77.8 2.9 %collective-permute-done.4 = bf16[32,4,8,128]{3,2,1,0:T(8,128)(2,1)S(1)} collective-permute-done((bf16[32,4,8,128]{3,2,1,0:T(8,128)(2,1)S(1)}, bf16[32,4,8,128]{3,2,1,0:T(8,128)(2,1)S(1)}, u32[]{:S(2)}, u32[]{:S(2)}) %collective-permute-start.4) | collective-permute-done | bytes 262176 | tf_op jit(solution)/shard_map/ppermute | solution.py:316
  80.8 18.7 %all_to_all.29 = f32[32,4,8,128]{3,2,1,0:T(8,128)S(1)} all-to-all(f32[32,4,8,128]{3,2,1,0:T(8,128)S(1)} %fusion.8), channel_id=1, replica_groups=mesh['rows'=32,'grp'=8] {'rows'}, dimensions={0} | all-to-all | bytes 1048576 | tf_op jit(solution)/shard_map/all_to_all | solution.py:380
  99.5 2.6 %final.1 = bf16[8,1024,128]{2,1,0:T(8,128)(2,1)} custom-call(f32[1024,128]{1,0:T(8,128)S(1)} %bitcast.56, bf16[128,1024]{1,0:T(8,128)(2,1)S(1)} %copy-done.2), custom_call_target="tpu_custom_call" | custom-call | flops 536870912 | bytes 2621440 | tf_op jit(solution)/shard_map/final/pallas_call | solution.py:362
  (26 shorter events, 1.2 us)
Async XLA Ops:
  0.7 41.1 %copy-start.4 = (s32[256]{0:T(256)S(1)}, s32[256]{0:T(256)}, u32[]{:S(2)}) copy-start(s32[256]{0:T(256)} %param.10) | copy-start | bytes 3076
  42.7 2.3 %copy-start.1 = (bf16[4,1280,256]{2,1,0:T(8,128)(2,1)S(1)}, bf16[4,1280,256]{2,1,0:T(8,128)(2,1)}, u32[]{:S(2)}) copy-start(bf16[4,1280,256]{2,1,0:T(8,128)(2,1)} %cols_ref.1) | copy-start | bytes 7864324
  42.7 2.3 %copy-start.3 = (bf16[256,256]{1,0:T(8,128)(2,1)S(1)}, bf16[256,256]{1,0:T(8,128)(2,1)}, u32[]{:S(2)}) copy-start(bf16[256,256]{1,0:T(8,128)(2,1)} %inv_ref.1) | copy-start | bytes 393220
  43.6 1.4 %collective-permute-start = (bf16[256,256]{1,0:T(8,128)(2,1)S(1)}, bf16[256,256]{1,0:T(8,128)(2,1)S(1)}, u32[]{:S(2)}, u32[]{:S(2)}) collective-permute-start(bf16[256,256]{1,0:T(8,128)(2,1)S(1)} %get-tuple-element.55.mine_ref), channel_id=1, source_target_pairs={{0,8},{8,0},{16,24},{24,16},{32,40},{40,32},{48,56},{56,48},{64,72... | collective-permute-start | bytes 393224 | tf_op jit(solution)/shard_map/ppermute | solution.py:404
  45.0 5.9 %copy-start = (bf16[1280,1024]{1,0:T(8,128)(2,1)S(1)}, bf16[1280,1024]{1,0:T(8,128)(2,1)}, u32[]{:S(2)}) copy-start(bf16[1280,1024]{1,0:T(8,128)(2,1)} %orb_ref.9) | copy-start | bytes 7864324
  51.8 5.0 %collective-permute-start.5 = (bf16[16,4,8,128]{3,2,1,0:T(8,128)(2,1)S(1)}, bf16[16,4,8,128]{3,2,1,0:T(8,128)(2,1)S(1)}, u32[]{:S(2)}, u32[]{:S(2)}) collective-permute-start(bf16[16,4,8,128]{3,2,1,0:T(8,128)(2,1)S(1)} %get-tuple-element.59), channel_id=1, source_target_pairs={{0,7},{1,0},{2,1},{3,2},{4,3},{5,4},{6,5},{7,6},{8,15},{9,8},{10,9... | collective-permute-start | bytes 393224 | tf_op jit(solution)/shard_map/ppermute | solution.py:316
  51.9 6.5 %collective-permute-start.1 = (bf16[16,4,8,128]{3,2,1,0:T(8,128)(2,1)S(1)}, bf16[16,4,8,128]{3,2,1,0:T(8,128)(2,1)S(1)}, u32[]{:S(2)}, u32[]{:S(2)}) collective-permute-start(bf16[16,4,8,128]{3,2,1,0:T(8,128)(2,1)S(1)} %get-tuple-element.58), channel_id=1, source_target_pairs={{0,1},{1,2},{2,3},{3,4},{4,5},{5,6},{6,7},{7,0},{8,9},{9,10},{10,1... | collective-permute-start | bytes 393224 | tf_op jit(solution)/shard_map/ppermute | solution.py:316
  56.8 6.9 %collective-permute-start.6 = (bf16[32,4,8,128]{3,2,1,0:T(8,128)(2,1)S(1)}, bf16[32,4,8,128]{3,2,1,0:T(8,128)(2,1)S(1)}, u32[]{:S(2)}, u32[]{:S(2)}) collective-permute-start(bf16[32,4,8,128]{3,2,1,0:T(8,128)(2,1)S(1)} %join.3), channel_id=1, source_target_pairs={{0,7},{1,0},{2,1},{3,2},{4,3},{5,4},{6,5},{7,6},{8,15},{9,8},{10,9... | collective-permute-start | bytes 786440 | tf_op jit(solution)/shard_map/ppermute | solution.py:316
  58.4 8.1 %collective-permute-start.2 = (bf16[32,4,8,128]{3,2,1,0:T(8,128)(2,1)S(1)}, bf16[32,4,8,128]{3,2,1,0:T(8,128)(2,1)S(1)}, u32[]{:S(2)}, u32[]{:S(2)}) collective-permute-start(bf16[32,4,8,128]{3,2,1,0:T(8,128)(2,1)S(1)} %join.2), channel_id=1, source_target_pairs={{0,1},{1,2},{2,3},{3,4},{4,5},{5,6},{6,7},{7,0},{8,9},{9,10},{10,1... | collective-permute-start | bytes 786440 | tf_op jit(solution)/shard_map/ppermute | solution.py:316
  66.7 7.2 %collective-permute-start.3 = (bf16[32,4,8,128]{3,2,1,0:T(8,128)(2,1)S(1)}, bf16[32,4,8,128]{3,2,1,0:T(8,128)(2,1)S(1)}, u32[]{:S(2)}, u32[]{:S(2)}) collective-permute-start(bf16[32,4,8,128]{3,2,1,0:T(8,128)(2,1)S(1)} %get-tuple-element.76), channel_id=1, source_target_pairs={{0,1},{1,2},{2,3},{3,4},{4,5},{5,6},{6,7},{7,0},{8,9},{9,10},{10,1... | collective-permute-start | bytes 786440 | tf_op jit(solution)/shard_map/ppermute | solution.py:316
  66.8 7.1 %collective-permute-start.7 = (bf16[32,4,8,128]{3,2,1,0:T(8,128)(2,1)S(1)}, bf16[32,4,8,128]{3,2,1,0:T(8,128)(2,1)S(1)}, u32[]{:S(2)}, u32[]{:S(2)}) collective-permute-start(bf16[32,4,8,128]{3,2,1,0:T(8,128)(2,1)S(1)} %get-tuple-element.77), channel_id=1, source_target_pairs={{0,7},{1,0},{2,1},{3,2},{4,3},{5,4},{6,5},{7,6},{8,15},{9,8},{10,9... | collective-permute-start | bytes 786440 | tf_op jit(solution)/shard_map/ppermute | solution.py:316
  74.0 6.7 %collective-permute-start.4 = (bf16[32,4,8,128]{3,2,1,0:T(8,128)(2,1)S(1)}, bf16[32,4,8,128]{3,2,1,0:T(8,128)(2,1)S(1)}, u32[]{:S(2)}, u32[]{:S(2)}) collective-permute-start(bf16[32,4,8,128]{3,2,1,0:T(8,128)(2,1)S(1)} %get-tuple-element.74), channel_id=1, source_target_pairs={{0,1},{1,2},{2,3},{3,4},{4,5},{5,6},{6,7},{7,0},{8,9},{9,10},{10,1... | collective-permute-start | bytes 786440 | tf_op jit(solution)/shard_map/ppermute | solution.py:316
  74.3 6.4 %collective-permute-start.8 = (bf16[32,4,8,128]{3,2,1,0:T(8,128)(2,1)S(1)}, bf16[32,4,8,128]{3,2,1,0:T(8,128)(2,1)S(1)}, u32[]{:S(2)}, u32[]{:S(2)}) collective-permute-start(bf16[32,4,8,128]{3,2,1,0:T(8,128)(2,1)S(1)} %get-tuple-element.75), channel_id=1, source_target_pairs={{0,7},{1,0},{2,1},{3,2},{4,3},{5,4},{6,5},{7,6},{8,15},{9,8},{10,9... | collective-permute-start | bytes 786440 | tf_op jit(solution)/shard_map/ppermute | solution.py:316
  77.8 21.7 %copy-start.2 = (bf16[128,1024]{1,0:T(8,128)(2,1)S(1)}, bf16[128,1024]{1,0:T(8,128)(2,1)}, u32[]{:S(2)}) copy-start(bf16[128,1024]{1,0:T(8,128)(2,1)} %slab_ref.1) | copy-start | bytes 786436

commit v6 on v5

--- a/solution.py
+++ b/solution.py
@@ -164,30 +164,49 @@
     )(came)
 
 
+def preload_kernel(prev_ref, after_ref, out_ref, sems):
+    copies = [
+        pltpu.make_async_copy(prev_ref.at[m], out_ref.at[m], sems.at[m])
+        for m in range(prev_ref.shape[0])
+    ]
+    for copy in copies:
+        copy.start()
+    for copy in copies:
+        copy.wait()
+
+
+def preload(previous, after):
+    return pl.pallas_call(
+        preload_kernel,
+        out_shape=jax.ShapeDtypeStruct(previous.shape, previous.dtype),
+        in_specs=[pl.BlockSpec(memory_space=pltpu.HBM), pl.BlockSpec(memory_space=pl.ANY)],
+        out_specs=pl.BlockSpec(memory_space=pltpu.VMEM),
+        scratch_shapes=[pltpu.SemaphoreType.DMA((previous.shape[0],))],
+        compiler_params=pltpu.CompilerParams(vmem_limit_bytes=8 << 20),
+        cost_estimate=pl.CostEstimate(
+            flops=0, bytes_accessed=2 * previous.size, transcendentals=0
+        ),
+        name="preload",
+    )(previous, after)
+
+
 def vectors_kernel(
-    core_ref, cols_ref, prev_ref, mine_ref, other_ref, inv_ref, new_ref, turned_ref, came, made, load, store
+    core_ref, cols_ref, prev_ref, mine_ref, other_ref, inv_ref, new_ref, turned_ref, made, store
 ):
-    mu = came.shape[0]
-
-    def load_of(m):
-        return pltpu.make_async_copy(prev_ref.at[m], came.at[m], load.at[m])
+    mu = prev_ref.shape[0]
 
     def store_of(m):
         return pltpu.make_async_copy(made.at[m], new_ref.at[m], store.at[m])
 
-    for m in range(mu):
-        load_of(m).start()
-
     @pl.loop(0, mu)
     def _(m):
-        load_of(m).wait()
         mine, other = mine_ref[...].astype(F32), other_ref[...].astype(F32)
         first = core_ref[0] == 0
         rows = jnp.concatenate(
             [jnp.where(first, mine, other), jnp.where(first, other, mine)], axis=1
         ).astype(BF16)
         contract = (((1,), (1,)), ((), ()))
-        correction = lax.dot_general(came[m], rows, contract, preferred_element_type=F32)
+        correction = lax.dot_general(prev_ref[m], rows, contract, preferred_element_type=F32)
         residual = (cols_ref[m].astype(F32) - correction).astype(BF16)
         inv = inv_ref[...]
         row, column = (lax.broadcasted_iota(jnp.int32, inv.shape, d) for d in (0, 1))
@@ -211,21 +230,9 @@
             jax.ShapeDtypeStruct((mu, nu, n), BF16),
             jax.ShapeDtypeStruct((mu, n, nu), BF16),
         ),
-        in_specs=[
-            pl.BlockSpec(memory_space=pltpu.SMEM),
-            vmem,
-            pl.BlockSpec(memory_space=pltpu.HBM),
-            vmem,
-            vmem,
-            vmem,
-        ],
+        in_specs=[pl.BlockSpec(memory_space=pltpu.SMEM), vmem, vmem, vmem, vmem, vmem],
         out_specs=(pl.BlockSpec(memory_space=pl.ANY), vmem),
-        scratch_shapes=[
-            pltpu.VMEM((mu, nu, k), BF16),
-            pltpu.VMEM((mu, nu, n), BF16),
-            pltpu.SemaphoreType.DMA((mu,)),
-            pltpu.SemaphoreType.DMA((mu,)),
-        ],
+        scratch_shapes=[pltpu.VMEM((mu, nu, n), BF16), pltpu.SemaphoreType.DMA((mu,))],
         compiler_params=pltpu.CompilerParams(vmem_limit_bytes=24 << 20),
         cost_estimate=pl.CostEstimate(
             flops=2 * mu * nu * n * (k + n),
@@ -331,41 +338,30 @@
     return own((0,))[0] + right.astype(F32) + left.astype(F32)
 
 
-def final_kernel(half_ref, slab_ref, out_ref, turned_ref):
+def final_kernel(half_ref, slab_ref, out_ref):
     rows, width = half_ref.shape
     mu = slab_ref.shape[0]
     keep = rows // mu
-
-    @pl.when(pl.program_id(0) == 0)
-    def _():
-        slab_t = slab_ref[...].T
-        turned_ref[...] = jnp.concatenate([slab_t, slab_t], axis=1)
-
-    first = pl.program_id(0) * 2
-    pair = jnp.concatenate(
-        [half_ref[pl.ds(first + q, mu, stride=keep), :] for q in (0, 1)], axis=1
-    )
-    high = pair.astype(BF16)
-    low = (pair - high.astype(F32)).astype(BF16)
-    both = jnp.dot(
-        turned_ref[...], jnp.concatenate([high, low], axis=0), preferred_element_type=F32
-    )
-    out_ref[0] = both[:, :width].astype(BF16)
-    out_ref[1] = both[:, width:].astype(BF16)
+    slab_t = slab_ref[...].T
+    slab_t = jnp.concatenate([slab_t, slab_t], axis=1)
+    for p in range(0, keep, 2):
+        pair = jnp.concatenate(
+            [half_ref[pl.ds(q, mu, stride=keep), :] for q in (p, p + 1)], axis=1
+        )
+        high = pair.astype(BF16)
+        low = (pair - high.astype(F32)).astype(BF16)
+        both = jnp.dot(slab_t, jnp.concatenate([high, low], axis=0), preferred_element_type=F32)
+        out_ref[p] = both[:, :width].astype(BF16)
+        out_ref[p + 1] = both[:, width:].astype(BF16)
 
 
 def final(half, slab):
     mu, occ = slab.shape
     rows, width = half.shape
     keep = rows // mu
-    whole = lambda i: (0, 0)
     return pl.pallas_call(
         final_kernel,
-        grid=(keep // 2,),
         out_shape=jax.ShapeDtypeStruct((keep, occ, width), BF16),
-        in_specs=[pl.BlockSpec((rows, width), whole), pl.BlockSpec((mu, occ), whole)],
-        out_specs=pl.BlockSpec((2, occ, width), lambda i: (i, 0, 0)),
-        scratch_shapes=[pltpu.VMEM((occ, 2 * mu), BF16)],
         compiler_params=pltpu.CompilerParams(vmem_limit_bytes=16 << 20),
         cost_estimate=pl.CostEstimate(
             flops=4 * rows * width * occ,
@@ -406,11 +402,12 @@
 
 
 def per_device(n_rows, n_grp, pivot_columns, previous, pivots, pivot_inverse, orbitals, slab_orbitals):
-    previous = pltpu.with_memory_space_constraint(previous, pltpu.HBM)
-    mine, other = pivot_halves(n_rows, n_grp, pivots, previous)
+    in_hbm = pltpu.with_memory_space_constraint(previous, pltpu.HBM)
+    mine, other = pivot_halves(n_rows, n_grp, pivots, in_hbm)
     core = (lax.axis_index("rows") % 2).reshape(1).astype(jnp.int32)
     me = lax.axis_index("grp").reshape(1).astype(jnp.int32)
-    new_vectors, turned = vectors(core, pivot_columns, previous, mine, other, pivot_inverse)
+    close = preload(in_hbm, mine)
+    new_vectors, turned = vectors(core, pivot_columns, close, mine, other, pivot_inverse)
     half = exchange(reduce_to_owner(me, turned, orbitals, n_grp, n_rows), "rows")
     return new_vectors, final(half.reshape(-1, half.shape[-1]), slab_orbitals)
 

time: 102 us -> 102 us (level)
  waiting for transfers between devices: 17.5 us -> 12.4 us
  starting transfers between devices: 8.92 us -> 11.3 us
  blocking collectives: 57.4 us -> 59.5 us
    ppermute x8, waiting for transfers between devices: 16.2 us -> 12.4 us  [hop(): lax.ppermute(x, 'grp', [(i, (i + way) % owners) for i in range(owners)])]
    ppermute x8, starting transfers between devices: 8.83 us -> 11.2 us  [hop(): lax.ppermute(x, 'grp', [(i, (i + way) % owners) for i in range(owners)])]
    pallas_call x1 -> x2, Pallas kernels: 2.63 us -> 4.76 us  [the longest x1 2.69 us: preload(): pl.pallas_call(preload_kernel, out_shape=jax.ShapeDtypeStruct(previous.sh...]
    all_to_all x3, blocking collectives: 57.4 us -> 59.5 us  [exchange(): return lax.all_to_all(x, axis, split_axis=0, concat_axis=0, tiled=True)]
    pallas_call x1, Pallas kernels: 5.85 us -> 4.35 us  [vectors(): pl.pallas_call(vectors_kernel, out_shape=(jax.ShapeDtypeStruct((mu, nu, n...]
    ppermute x1, waiting for transfers between devices: 1.32 us -> 0.01 us  [pivot_halves(): other = lax.ppermute(mine, 'rows', [(i, i ^ 1) for i in range(n_rows)])]
    pallas_call x1, Pallas kernels: 2.21 us -> 1.06 us  [pick_rows(): pl.pallas_call(pick_kernel, out_shape=jax.ShapeDtypeStruct((SLOTS, k), BF...]
  transfers between devices with their start and end apart: 9 -> 9, of which waited for: 6 -> 4; matrix products, arithmetic and copies ran while one was open for 0% -> 0% of each run, Pallas kernels for 3% -> 6%
where the time goes in v6:
time: 102 us; the launch traced here: 101 us
  blocking collectives  59.5 us (58%)
  Pallas kernels  15.6 us (15%)
  waiting for transfers between devices  12.4 us (12%)
  starting transfers between devices  11.3 us (11%)
    all_to_all x3, blocking collectives, exchange(): return lax.all_to_all(x, axis, split_axis=0, concat_axis=0, tiled=True)  59.5 us
    ppermute x8, waiting for transfers between devices, hop(): lax.ppermute(x, 'grp', [(i, (i + way) % owners) for i in range(owners)])  12.4 us
    ppermute x8, starting transfers between devices, hop(): lax.ppermute(x, 'grp', [(i, (i + way) % owners) for i in range(owners)])  11.2 us
    pallas_call x1, Pallas kernels, vectors(): pl.pallas_call(vectors_kernel, out_shape=(jax.ShapeDtypeStruct((mu, nu, n...  4.35 us
    pallas_call x5, Pallas kernels, parts(): pl.pallas_call(functools.partial(parts_kernel, ahead=ahead, owners=owners...  4.3 us
    pallas_call x1, Pallas kernels, preload(): pl.pallas_call(preload_kernel, out_shape=jax.ShapeDtypeStruct(previous.sh...  2.69 us
    pallas_call x1, Pallas kernels, final(): pl.pallas_call(final_kernel, out_shape=jax.ShapeDtypeStruct((keep, occ, w...  2.08 us
  transfers between devices with their start and end apart: 9, of which 4 were waited for; matrix products, arithmetic and copies ran while one was open for 0% of the time, Pallas kernels for 6%

profile of v6, /device:TPU:1, one launch (start us, length us, event | category | flops | bytes accessed | tf_op | source)
XLA Modules:
  0.0 101.5 jit_solution(11720563673036927335)
XLA Ops:
  0.7 1.1 %pick_rows.2 = bf16[24,512]{1,0:T(8,128)(2,1)S(1)} custom-call(s32[3]{0:T(128)S(1)} %pad_add_fusion.1.where_from_ref, s32[2,128]{1,0:T(2,128)} %bitcast.58, bf16[4,1280,512]{2,1,0:T(8,128)(2,1)} %prev_ref.3), custom_call_target="tpu_custom_call" | custom-call | flops 131072 | bytes 262144 | tf_op jit(solution)/shard_map/pick_rows/pallas_call | solution.py:80
  1.8 19.2 %all_to_all.27.came_ref = bf16[8,24,512]{2,1,0:T(8,128)(2,1)S(1)} all-to-all(bf16[8,24,512]{2,1,0:T(8,128)(2,1)S(1)} %broadcast_in_dim.9), channel_id=1, replica_groups=mesh['rows'=32,'grp'=8] {'grp'}, dimensions={0} | all-to-all | bytes 393216 | tf_op jit(solution)/shard_map/all_to_all | solution.py:376
  21.2 19.9 %all_to_all.28 = bf16[32,24,256]{2,1,0:T(8,128)(2,1)S(1)} all-to-all(bf16[32,24,256]{2,1,0:T(8,128)(2,1)S(1)} %spread.2), channel_id=1, replica_groups=mesh['rows'=32,'grp'=8] {'rows'}, dimensions={0} | all-to-all | bytes 786432 | tf_op jit(solution)/shard_map/all_to_all | solution.py:376
  41.2 0.9 select_rows.2
  42.1 0.7 while.10
  42.9 2.7 %preload.1.prev_ref = bf16[4,1280,512]{2,1,0:T(8,128)(2,1)S(1)} custom-call(bf16[4,1280,512]{2,1,0:T(8,128)(2,1)} %get-tuple-element.156, bf16[256,256]{1,0:T(8,128)(2,1)S(1)} %get-tuple-element.55.after_ref.mine_ref), custom_call_target="tpu_custom_call" | custom-call | bytes 5242880 | tf_op jit(solution)/shard_map/preload/pallas_call | solution.py:179
  45.6 0.6 copy-done.1
  46.2 4.4 %vectors.1 = (bf16[4,1280,256]{2,1,0:T(8,128)(2,1)}, bf16[4,256,1280]{2,1,0:T(8,128)(2,1)S(1)}) custom-call(s32[1]{0:T(128)} %bitcast.6.core_ref, bf16[4,1280,256]{2,1,0:T(8,128)(2,1)S(1)} %copy-done.1, bf16[4,1280,512]{2,1,0:T(8,128)(2,1)S(1)} %preload.1.prev_ref, bf16[256,256]{1,0:T(8,128)(2,1)S(1)} %get-tuple-element.55.after_ref.mine_ref, ...), custom_call_target="tpu_custom_call" | custom-call | flops 2013265920 | bytes 13107200 | tf_op jit(solution)/shard_map/vectors/pallas_call | solution.py:227
  50.6 0.9 parts.9
  51.4 0.4 collective-permute-start.1
  51.8 2.4 %collective-permute-start.5 = (bf16[16,4,8,128]{3,2,1,0:T(8,128)(2,1)S(1)}, bf16[16,4,8,128]{3,2,1,0:T(8,128)(2,1)S(1)}, u32[]{:S(2)}, u32[]{:S(2)}) collective-permute-start(bf16[16,4,8,128]{3,2,1,0:T(8,128)(2,1)S(1)} %get-tuple-element.59), channel_id=1, source_target_pairs={{0,7},{1,0},{2,1},{3,2},{4,3},{5,4},{6,5},{7,6},{8,15},{9,8},{10,9... | collective-permute-start | bytes 393224 | tf_op jit(solution)/shard_map/ppermute | solution.py:323
  54.2 0.9 parts.8.own_ref
  55.1 2.2 %collective-permute-done.1.came_ref = bf16[16,4,8,128]{3,2,1,0:T(8,128)(2,1)S(1)} collective-permute-done((bf16[16,4,8,128]{3,2,1,0:T(8,128)(2,1)S(1)}, bf16[16,4,8,128]{3,2,1,0:T(8,128)(2,1)S(1)}, u32[]{:S(2)}, u32[]{:S(2)}) %collective-permute-start.1) | collective-permute-done | bytes 131104 | tf_op jit(solution)/shard_map/ppermute | solution.py:323
  57.5 2.7 %collective-permute-start.6 = (bf16[32,4,8,128]{3,2,1,0:T(8,128)(2,1)S(1)}, bf16[32,4,8,128]{3,2,1,0:T(8,128)(2,1)S(1)}, u32[]{:S(2)}, u32[]{:S(2)}) collective-permute-start(bf16[32,4,8,128]{3,2,1,0:T(8,128)(2,1)S(1)} %join.3), channel_id=1, source_target_pairs={{0,7},{1,0},{2,1},{3,2},{4,3},{5,4},{6,5},{7,6},{8,15},{9,8},{10,9... | collective-permute-start | bytes 786440 | tf_op jit(solution)/shard_map/ppermute | solution.py:323
  60.2 0.9 parts.7
  61.1 4.0 %collective-permute-done.2 = bf16[32,4,8,128]{3,2,1,0:T(8,128)(2,1)S(1)} collective-permute-done((bf16[32,4,8,128]{3,2,1,0:T(8,128)(2,1)S(1)}, bf16[32,4,8,128]{3,2,1,0:T(8,128)(2,1)S(1)}, u32[]{:S(2)}, u32[]{:S(2)}) %collective-permute-start.2) | collective-permute-done | bytes 262176 | tf_op jit(solution)/shard_map/ppermute | solution.py:323
  65.4 2.7 %collective-permute-start.7 = (bf16[32,4,8,128]{3,2,1,0:T(8,128)(2,1)S(1)}, bf16[32,4,8,128]{3,2,1,0:T(8,128)(2,1)S(1)}, u32[]{:S(2)}, u32[]{:S(2)}) collective-permute-start(bf16[32,4,8,128]{3,2,1,0:T(8,128)(2,1)S(1)} %get-tuple-element.77), channel_id=1, source_target_pairs={{0,7},{1,0},{2,1},{3,2},{4,3},{5,4},{6,5},{7,6},{8,15},{9,8},{10,9... | collective-permute-start | bytes 786440 | tf_op jit(solution)/shard_map/ppermute | solution.py:323
  68.0 0.9 parts.6
  68.9 3.2 %collective-permute-done.3 = bf16[32,4,8,128]{3,2,1,0:T(8,128)(2,1)S(1)} collective-permute-done((bf16[32,4,8,128]{3,2,1,0:T(8,128)(2,1)S(1)}, bf16[32,4,8,128]{3,2,1,0:T(8,128)(2,1)S(1)}, u32[]{:S(2)}, u32[]{:S(2)}) %collective-permute-start.3) | collective-permute-done | bytes 262176 | tf_op jit(solution)/shard_map/ppermute | solution.py:323
  72.5 2.7 %collective-permute-start.8 = (bf16[32,4,8,128]{3,2,1,0:T(8,128)(2,1)S(1)}, bf16[32,4,8,128]{3,2,1,0:T(8,128)(2,1)S(1)}, u32[]{:S(2)}, u32[]{:S(2)}) collective-permute-start(bf16[32,4,8,128]{3,2,1,0:T(8,128)(2,1)S(1)} %get-tuple-element.75), channel_id=1, source_target_pairs={{0,7},{1,0},{2,1},{3,2},{4,3},{5,4},{6,5},{7,6},{8,15},{9,8},{10,9... | collective-permute-start | bytes 786440 | tf_op jit(solution)/shard_map/ppermute | solution.py:323
  75.2 0.8 parts.5
  76.1 2.9 %collective-permute-done.4 = bf16[32,4,8,128]{3,2,1,0:T(8,128)(2,1)S(1)} collective-permute-done((bf16[32,4,8,128]{3,2,1,0:T(8,128)(2,1)S(1)}, bf16[32,4,8,128]{3,2,1,0:T(8,128)(2,1)S(1)}, u32[]{:S(2)}, u32[]{:S(2)}) %collective-permute-start.4) | collective-permute-done | bytes 262176 | tf_op jit(solution)/shard_map/ppermute | solution.py:323
  79.1 20.3 %all_to_all.29 = f32[32,4,8,128]{3,2,1,0:T(8,128)S(1)} all-to-all(f32[32,4,8,128]{3,2,1,0:T(8,128)S(1)} %fusion.8), channel_id=1, replica_groups=mesh['rows'=32,'grp'=8] {'rows'}, dimensions={0} | all-to-all | bytes 1048576 | tf_op jit(solution)/shard_map/all_to_all | solution.py:376
  99.4 2.1 %final.1 = bf16[8,1024,128]{2,1,0:T(8,128)(2,1)} custom-call(f32[1024,128]{1,0:T(8,128)S(1)} %bitcast.56, bf16[128,1024]{1,0:T(8,128)(2,1)S(1)} %copy-done.2), custom_call_target="tpu_custom_call" | custom-call | flops 536870912 | bytes 2621440 | tf_op jit(solution)/shard_map/final/pallas_call | solution.py:362
  (27 shorter events, 1.3 us)
Async XLA Ops:
  0.7 40.5 %copy-start.4 = (s32[256]{0:T(256)S(1)}, s32[256]{0:T(256)}, u32[]{:S(2)}) copy-start(s32[256]{0:T(256)} %param.10) | copy-start | bytes 3076
  42.8 2.8 %collective-permute-start = (bf16[256,256]{1,0:T(8,128)(2,1)S(1)}, bf16[256,256]{1,0:T(8,128)(2,1)S(1)}, u32[]{:S(2)}, u32[]{:S(2)}) collective-permute-start(bf16[256,256]{1,0:T(8,128)(2,1)S(1)} %get-tuple-element.55.after_ref.mine_ref), channel_id=1, source_target_pairs={{0,8},{8,0},{16,24},{24,16},{32,40},{40,32},{48,56},{56,48},{64,72... | collective-permute-start | bytes 393224 | tf_op jit(solution)/shard_map/ppermute | solution.py:400
  42.9 3.3 %copy-start.1 = (bf16[4,1280,256]{2,1,0:T(8,128)(2,1)S(1)}, bf16[4,1280,256]{2,1,0:T(8,128)(2,1)}, u32[]{:S(2)}) copy-start(bf16[4,1280,256]{2,1,0:T(8,128)(2,1)} %cols_ref.1) | copy-start | bytes 7864324
  42.9 3.3 %copy-start.3 = (bf16[256,256]{1,0:T(8,128)(2,1)S(1)}, bf16[256,256]{1,0:T(8,128)(2,1)}, u32[]{:S(2)}) copy-start(bf16[256,256]{1,0:T(8,128)(2,1)} %inv_ref.1) | copy-start | bytes 393220
  46.2 4.4 %copy-start = (bf16[1280,1024]{1,0:T(8,128)(2,1)S(1)}, bf16[1280,1024]{1,0:T(8,128)(2,1)}, u32[]{:S(2)}) copy-start(bf16[1280,1024]{1,0:T(8,128)(2,1)} %orb_ref.9) | copy-start | bytes 7864324
  51.4 5.9 %collective-permute-start.1 = (bf16[16,4,8,128]{3,2,1,0:T(8,128)(2,1)S(1)}, bf16[16,4,8,128]{3,2,1,0:T(8,128)(2,1)S(1)}, u32[]{:S(2)}, u32[]{:S(2)}) collective-permute-start(bf16[16,4,8,128]{3,2,1,0:T(8,128)(2,1)S(1)} %get-tuple-element.58), channel_id=1, source_target_pairs={{0,1},{1,2},{2,3},{3,4},{4,5},{5,6},{6,7},{7,0},{8,9},{9,10},{10,1... | collective-permute-start | bytes 393224 | tf_op jit(solution)/shard_map/ppermute | solution.py:323
  51.8 5.6 %collective-permute-start.5 = (bf16[16,4,8,128]{3,2,1,0:T(8,128)(2,1)S(1)}, bf16[16,4,8,128]{3,2,1,0:T(8,128)(2,1)S(1)}, u32[]{:S(2)}, u32[]{:S(2)}) collective-permute-start(bf16[16,4,8,128]{3,2,1,0:T(8,128)(2,1)S(1)} %get-tuple-element.59), channel_id=1, source_target_pairs={{0,7},{1,0},{2,1},{3,2},{4,3},{5,4},{6,5},{7,6},{8,15},{9,8},{10,9... | collective-permute-start | bytes 393224 | tf_op jit(solution)/shard_map/ppermute | solution.py:323
  57.3 7.8 %collective-permute-start.2 = (bf16[32,4,8,128]{3,2,1,0:T(8,128)(2,1)S(1)}, bf16[32,4,8,128]{3,2,1,0:T(8,128)(2,1)S(1)}, u32[]{:S(2)}, u32[]{:S(2)}) collective-permute-start(bf16[32,4,8,128]{3,2,1,0:T(8,128)(2,1)S(1)} %join.2), channel_id=1, source_target_pairs={{0,1},{1,2},{2,3},{3,4},{4,5},{5,6},{6,7},{7,0},{8,9},{9,10},{10,1... | collective-permute-start | bytes 786440 | tf_op jit(solution)/shard_map/ppermute | solution.py:323
  57.5 7.6 %collective-permute-start.6 = (bf16[32,4,8,128]{3,2,1,0:T(8,128)(2,1)S(1)}, bf16[32,4,8,128]{3,2,1,0:T(8,128)(2,1)S(1)}, u32[]{:S(2)}, u32[]{:S(2)}) collective-permute-start(bf16[32,4,8,128]{3,2,1,0:T(8,128)(2,1)S(1)} %join.3), channel_id=1, source_target_pairs={{0,7},{1,0},{2,1},{3,2},{4,3},{5,4},{6,5},{7,6},{8,15},{9,8},{10,9... | collective-permute-start | bytes 786440 | tf_op jit(solution)/shard_map/ppermute | solution.py:323
  65.3 6.8 %collective-permute-start.3 = (bf16[32,4,8,128]{3,2,1,0:T(8,128)(2,1)S(1)}, bf16[32,4,8,128]{3,2,1,0:T(8,128)(2,1)S(1)}, u32[]{:S(2)}, u32[]{:S(2)}) collective-permute-start(bf16[32,4,8,128]{3,2,1,0:T(8,128)(2,1)S(1)} %get-tuple-element.76), channel_id=1, source_target_pairs={{0,1},{1,2},{2,3},{3,4},{4,5},{5,6},{6,7},{7,0},{8,9},{9,10},{10,1... | collective-permute-start | bytes 786440 | tf_op jit(solution)/shard_map/ppermute | solution.py:323
  65.4 6.8 %collective-permute-start.7 = (bf16[32,4,8,128]{3,2,1,0:T(8,128)(2,1)S(1)}, bf16[32,4,8,128]{3,2,1,0:T(8,128)(2,1)S(1)}, u32[]{:S(2)}, u32[]{:S(2)}) collective-permute-start(bf16[32,4,8,128]{3,2,1,0:T(8,128)(2,1)S(1)} %get-tuple-element.77), channel_id=1, source_target_pairs={{0,7},{1,0},{2,1},{3,2},{4,3},{5,4},{6,5},{7,6},{8,15},{9,8},{10,9... | collective-permute-start | bytes 786440 | tf_op jit(solution)/shard_map/ppermute | solution.py:323
  72.3 6.7 %collective-permute-start.4 = (bf16[32,4,8,128]{3,2,1,0:T(8,128)(2,1)S(1)}, bf16[32,4,8,128]{3,2,1,0:T(8,128)(2,1)S(1)}, u32[]{:S(2)}, u32[]{:S(2)}) collective-permute-start(bf16[32,4,8,128]{3,2,1,0:T(8,128)(2,1)S(1)} %get-tuple-element.74), channel_id=1, source_target_pairs={{0,1},{1,2},{2,3},{3,4},{4,5},{5,6},{6,7},{7,0},{8,9},{9,10},{10,1... | collective-permute-start | bytes 786440 | tf_op jit(solution)/shard_map/ppermute | solution.py:323
  72.5 6.4 %collective-permute-start.8 = (bf16[32,4,8,128]{3,2,1,0:T(8,128)(2,1)S(1)}, bf16[32,4,8,128]{3,2,1,0:T(8,128)(2,1)S(1)}, u32[]{:S(2)}, u32[]{:S(2)}) collective-permute-start(bf16[32,4,8,128]{3,2,1,0:T(8,128)(2,1)S(1)} %get-tuple-element.75), channel_id=1, source_target_pairs={{0,7},{1,0},{2,1},{3,2},{4,3},{5,4},{6,5},{7,6},{8,15},{9,8},{10,9... | collective-permute-start | bytes 786440 | tf_op jit(solution)/shard_map/ppermute | solution.py:323
  76.1 23.3 %copy-start.2 = (bf16[128,1024]{1,0:T(8,128)(2,1)S(1)}, bf16[128,1024]{1,0:T(8,128)(2,1)}, u32[]{:S(2)}) copy-start(bf16[128,1024]{1,0:T(8,128)(2,1)} %slab_ref.1) | copy-start | bytes 786436

commit v7 on v6

--- a/solution.py
+++ b/solution.py
@@ -10,36 +10,28 @@
 NBAS = 10240
 F32 = jnp.float32
 BF16 = jnp.bfloat16
+DEPTH = 8
 SLOTS = 24
-
-
-def pick_kernel(where_from_ref, piv_ref, prev_ref, out_ref, acc_ref, held, sems, todo_ref):
+PARTS = 3
+
+
+def pick_kernel(where_from_ref, piv_ref, prev_ref, out_ref, acc_ref, held, sems, rows_ref):
     mu, nu, _ = prev_ref.shape
     depth, group, _ = held.shape
-    line, base, round_index = (where_from_ref[i] for i in range(3))
-    n = todo_ref.shape[1]
-    slots = acc_ref.shape[0]
+    base, turn = where_from_ref[1], where_from_ref[2]
     acc_ref[...] = jnp.zeros_like(acc_ref)
     pivots = piv_ref[...]
     order = lax.broadcasted_iota(jnp.int32, pivots.shape, 0) * pivots.shape[1]
     order += lax.broadcasted_iota(jnp.int32, pivots.shape, 1)
-    in_line = (pivots >= line) & (pivots < line + mu * NBAS)
-    local = jnp.full_like(pivots, -1)
+    many = 1 << (mu * nu - 1).bit_length()
+    last = many * pivots.size
+    keys = jnp.full_like(pivots, last)
     for m in range(mu):
         inside = pivots - base - m * NBAS
-        local = jnp.where((inside >= 0) & (inside < nu), inside + m * nu, local)
-    owned = jnp.sum((local >= 0).astype(jnp.int32))
-
-    def find(i, carry):
-        last, count = carry
-        p = jnp.min(jnp.where((local >= 0) & (order > last), order, n))
-        rank = jnp.sum((in_line & (order < p)).astype(jnp.int32))
-        slot = rank - round_index * slots
-        todo_ref[0, count] = slot
-        todo_ref[1, count] = jnp.max(jnp.where(order == p, local, -1))
-        return p, count + ((slot >= 0) & (slot < slots)).astype(jnp.int32)
-
-    _, total = lax.fori_loop(0, owned, find, (jnp.int32(-1), jnp.int32(0)))
+        keys = jnp.where((inside >= 0) & (inside < nu), order * many + inside + m * nu, keys)
+    owned = jnp.sum((keys < last).astype(jnp.int32))
+    skip = turn * depth
+    total = jnp.clip(owned - skip, 0, depth)
 
     def fetch(row, i):
         m = jnp.int32(0)
@@ -48,38 +40,38 @@
         start = pl.multiple_of((row - m * nu) // group * group, group)
         return pltpu.make_async_copy(prev_ref.at[m, pl.ds(start, group)], held.at[i], sems.at[i])
 
-    def batch(b, _):
-        first = b * depth
-        size = jnp.minimum(total - first, depth)
-
-        def begin(i, _):
-            fetch(todo_ref[1, first + i], i).start()
-            return 0
-
-        def end(i, _):
-            row = todo_ref[1, first + i]
-            fetch(row, i).wait()
-            rows = held[i].astype(F32)
-            keep = lax.broadcasted_iota(jnp.int32, rows.shape, 0) == row % group
-            picked = jnp.sum(jnp.where(keep, rows, 0.0), axis=0, keepdims=True)
-            acc_ref[pl.ds(todo_ref[0, first + i], 1), :] = picked
-            return 0
-
-        lax.fori_loop(0, size, begin, 0)
-        lax.fori_loop(0, size, end, 0)
+    def find(i, key):
+        key = jnp.min(jnp.where(keys > key, keys, last))
+
+        @pl.when(i >= skip)
+        def _():
+            row = key & (many - 1)
+            rows_ref[i - skip] = row
+            fetch(row, i - skip).start()
+
+        return key
+
+    lax.fori_loop(0, skip + total, find, jnp.int32(-1))
+
+    def place(i, _):
+        row = rows_ref[i]
+        fetch(row, i).wait()
+        rows = held[i].astype(F32)
+        keep = lax.broadcasted_iota(jnp.int32, rows.shape, 0) == row % group
+        acc_ref[pl.ds(i, 1), :] = jnp.sum(jnp.where(keep, rows, 0.0), axis=0, keepdims=True)
         return 0
 
-    lax.fori_loop(0, (total + depth - 1) // depth, batch, 0)
+    lax.fori_loop(0, total, place, 0)
     out_ref[...] = acc_ref[...].astype(BF16)
 
 
 def pick_rows(where_from, pivots, previous):
-    mu, nu, k = previous.shape
     n = pivots.shape[0]
+    k = previous.shape[2]
     lanes = 128
     return pl.pallas_call(
         pick_kernel,
-        out_shape=jax.ShapeDtypeStruct((SLOTS, k), BF16),
+        out_shape=jax.ShapeDtypeStruct((DEPTH, k), BF16),
         in_specs=[
             pl.BlockSpec(memory_space=pltpu.SMEM),
             pl.BlockSpec(memory_space=pltpu.VMEM),
@@ -87,10 +79,10 @@
         ],
         out_specs=pl.BlockSpec(memory_space=pltpu.VMEM),
         scratch_shapes=[
-            pltpu.VMEM((SLOTS, k), F32),
-            pltpu.VMEM((16, 16, k), BF16),
-            pltpu.SemaphoreType.DMA((16,)),
-            pltpu.SMEM((2, n + 1), jnp.int32),
+            pltpu.VMEM((DEPTH, k), F32),
+            pltpu.VMEM((DEPTH, 16, k), BF16),
+            pltpu.SemaphoreType.DMA((DEPTH,)),
+            pltpu.SMEM((DEPTH,), jnp.int32),
         ],
         compiler_params=pltpu.CompilerParams(vmem_limit_bytes=4 << 20),
         cost_estimate=pl.CostEstimate(flops=n * k, bytes_accessed=2 * n * k, transcendentals=0),
@@ -98,31 +90,43 @@
     )(where_from, pivots.reshape(n // lanes, lanes), previous)
 
 
-def select_kernel(round_ref, piv_ref, slots_ref, so_far_ref, out_ref, rounds_ref, *, per_line):
+def whole_part(x, by):
+    return jnp.floor((x + 0.5) * (1.0 / by))
+
+
+def select_kernel(round_ref, piv_ref, slots_ref, so_far_ref, out_ref, rounds_ref, *, per_line, nu, owners):
     total, _ = slots_ref.shape
     n = piv_ref.shape[1]
-    along = jnp.broadcast_to(piv_ref[...].astype(F32), (n, n))
-    lines_along = jnp.floor((along + 0.5) * (1.0 / per_line))
-    lines = lines_along.T
-    earlier = lax.broadcasted_iota(jnp.int32, (n, n), 1) < lax.broadcasted_iota(jnp.int32, (n, n), 0)
-    same = jnp.where((lines_along == lines) & earlier, 1.0, 0.0)
-    rank = jnp.sum(same, axis=1, keepdims=True)
-    rounds_ref[0] = jnp.max(rank).astype(jnp.int32) // SLOTS + 1
-    rank = rank - (round_ref[0] * SLOTS).astype(F32)
-    mine = (rank >= 0.0) & (rank < SLOTS)
-    index = jnp.where(mine, lines[:, :1] * SLOTS + rank, -1.0).astype(jnp.int32)
+    pivot = piv_ref[...].astype(F32)
+    line = whole_part(pivot, per_line)
+    inside = pivot - line * per_line
+    inside = inside - whole_part(inside, NBAS) * NBAS
+    device = jnp.broadcast_to(line * owners + whole_part(inside, nu), (n, n))
+    mine = device.T
+    before = lax.broadcasted_iota(jnp.int32, (n, n), 1) < lax.broadcasted_iota(jnp.int32, (n, n), 0)
+    rank = jnp.sum(jnp.where((device == mine) & before, 1.0, 0.0), axis=1, keepdims=True)
+    turn = whole_part(rank, DEPTH)
+    turns = jnp.broadcast_to(turn, (n, n))
+    my_line = whole_part(mine, owners)
+    ahead = (device >= my_line * owners) & (device < mine) & (turns.T == turns)
+    place = jnp.sum(jnp.where(ahead, 1.0, 0.0), axis=1, keepdims=True) + rank - turn * DEPTH
+    part = whole_part(place, SLOTS)
+    when = turn * PARTS + part
+    rounds_ref[0] = jnp.max(when).astype(jnp.int32) + 1
+    index = my_line[:, :1] * SLOTS + place - part * SLOTS
+    index = jnp.where(when == round_ref[0].astype(F32), index, -1.0).astype(jnp.int32)
     hot = index == lax.broadcasted_iota(jnp.int32, (n, total), 1)
     hot = jnp.where(hot, 1.0, 0.0).astype(BF16)
     picked = jnp.dot(hot, slots_ref[...], preferred_element_type=F32)
     out_ref[...] = (picked + so_far_ref[...].astype(F32)).astype(BF16)
 
 
-def select_rows(round_index, pivots, slots, so_far, per_line):
+def select_rows(round_index, pivots, slots, so_far, per_line, nu, owners):
     total, width = slots.shape
     n = pivots.shape[0]
     vmem = pl.BlockSpec(memory_space=pltpu.VMEM)
     return pl.pallas_call(
-        functools.partial(select_kernel, per_line=per_line),
+        functools.partial(select_kernel, per_line=per_line, nu=nu, owners=owners),
         out_shape=(
             jax.ShapeDtypeStruct((n, width), BF16),
             jax.ShapeDtypeStruct((1,), jnp.int32),
@@ -137,76 +141,95 @@
     )(round_index, pivots.reshape(1, n), slots, so_far)
 
 
-def spread_kernel(came_ref, out_ref):
-    total = jnp.sum(came_ref[...].astype(F32), axis=0).astype(BF16)
+def spread_kernel(where_from_ref, piv_ref, came_ref, out_ref, *, mu, nu):
+    owners, depth, k = came_ref.shape
+    n = piv_ref.shape[1]
+    line, turn, part = (where_from_ref[i] for i in (0, 2, 3))
+    offset = jnp.broadcast_to(piv_ref[...] - line, (owners, n))
+    low = lax.broadcasted_iota(jnp.int32, (owners, n), 0) * nu
+    count = jnp.zeros((owners, n), F32)
+    for m in range(mu):
+        inside = offset - m * NBAS - low
+        count += jnp.where((inside >= 0) & (inside < nu), 1.0, 0.0)
+    count = jnp.sum(count, axis=1, keepdims=True) - (turn * depth).astype(F32)
+    count = jnp.clip(count, 0.0, depth)
+    wide = (owners, owners * depth)
+    slot = lax.broadcasted_iota(jnp.int32, wide, 1) - lax.broadcasted_iota(jnp.int32, wide, 0) * depth
+    here = (slot >= 0) & (slot < depth)
+    start = jnp.sum(jnp.where(slot >= depth, count, 0.0), axis=0, keepdims=True)
+    used = jnp.sum(jnp.where(here & (slot.astype(F32) < count), 1.0, 0.0), axis=0, keepdims=True)
+    place = start + jnp.sum(jnp.where(here, slot.astype(F32), 0.0), axis=0, keepdims=True)
+    place = place - (part * SLOTS).astype(F32)
+    packed = lax.broadcasted_iota(jnp.int32, (SLOTS, wide[1]), 0).astype(F32)
+    hot = jnp.where((packed == place) & (used > 0.0), 1.0, 0.0).astype(BF16)
+    rows = came_ref[...].astype(F32).reshape(wide[1], k).astype(BF16)
+    rows = jnp.dot(hot, rows, preferred_element_type=F32).astype(BF16)
     half = out_ref.shape[2]
     for c in range(2):
-        piece = total[:, c * half : (c + 1) * half]
+        piece = rows[:, c * half : (c + 1) * half]
 
         @pl.loop(0, out_ref.shape[0] // 2)
         def _(chip):
             out_ref[2 * chip + c] = piece
 
 
-def spread(came, n_rows):
-    n_grp, slots, k = came.shape
+def spread(where_from, pivots, came, n_rows, mu, nu):
+    k = came.shape[2]
+    n = pivots.shape[0]
     vmem = pl.BlockSpec(memory_space=pltpu.VMEM)
     return pl.pallas_call(
-        spread_kernel,
-        out_shape=jax.ShapeDtypeStruct((n_rows, slots, k // 2), BF16),
-        in_specs=[vmem],
+        functools.partial(spread_kernel, mu=mu, nu=nu),
+        out_shape=jax.ShapeDtypeStruct((n_rows, SLOTS, k // 2), BF16),
+        in_specs=[pl.BlockSpec(memory_space=pltpu.SMEM), vmem, vmem],
         out_specs=vmem,
         compiler_params=pltpu.CompilerParams(vmem_limit_bytes=4 << 20),
         cost_estimate=pl.CostEstimate(
-            flops=n_grp * slots * k, bytes_accessed=n_rows * slots * k, transcendentals=0
+            flops=came.size, bytes_accessed=n_rows * SLOTS * k, transcendentals=0
         ),
         name="spread",
-    )(came)
-
-
-def preload_kernel(prev_ref, after_ref, out_ref, sems):
-    copies = [
-        pltpu.make_async_copy(prev_ref.at[m], out_ref.at[m], sems.at[m])
-        for m in range(prev_ref.shape[0])
-    ]
-    for copy in copies:
-        copy.start()
-    for copy in copies:
-        copy.wait()
+    )(where_from, pivots.reshape(1, n), came)
+
+
+def preload_kernel(prev_ref, after_ref, out_ref, sem):
+    copy = pltpu.make_async_copy(prev_ref.at[0], out_ref, sem)
+    copy.start()
+    copy.wait()
 
 
 def preload(previous, after):
     return pl.pallas_call(
         preload_kernel,
-        out_shape=jax.ShapeDtypeStruct(previous.shape, previous.dtype),
+        out_shape=jax.ShapeDtypeStruct(previous.shape[1:], previous.dtype),
         in_specs=[pl.BlockSpec(memory_space=pltpu.HBM), pl.BlockSpec(memory_space=pl.ANY)],
         out_specs=pl.BlockSpec(memory_space=pltpu.VMEM),
-        scratch_shapes=[pltpu.SemaphoreType.DMA((previous.shape[0],))],
-        compiler_params=pltpu.CompilerParams(vmem_limit_bytes=8 << 20),
-        cost_estimate=pl.CostEstimate(
-            flops=0, bytes_accessed=2 * previous.size, transcendentals=0
+        scratch_shapes=[pltpu.SemaphoreType.DMA],
+        compiler_params=pltpu.CompilerParams(vmem_limit_bytes=4 << 20),
+        cost_estimate=pl.CostEstimate(
+            flops=0, bytes_accessed=previous.size // 2, transcendentals=0
         ),
         name="preload",
     )(previous, after)
 
 
 def vectors_kernel(
-    core_ref, cols_ref, prev_ref, mine_ref, other_ref, inv_ref, new_ref, turned_ref, made, store
+    core_ref, cols_ref, close_ref, prev_ref, mine_ref, other_ref, inv_ref, new_ref, turned_ref, came, made, load, store
 ):
-    mu = prev_ref.shape[0]
+    mu = cols_ref.shape[0]
+
+    def load_of(m):
+        return pltpu.make_async_copy(prev_ref.at[m], came.at[m - 1], load.at[m - 1])
 
     def store_of(m):
         return pltpu.make_async_copy(made.at[m], new_ref.at[m], store.at[m])
 
-    @pl.loop(0, mu)
-    def _(m):
+    def step(m, prev):
         mine, other = mine_ref[...].astype(F32), other_ref[...].astype(F32)
         first = core_ref[0] == 0
         rows = jnp.concatenate(
             [jnp.where(first, mine, other), jnp.where(first, other, mine)], axis=1
         ).astype(BF16)
         contract = (((1,), (1,)), ((), ()))
-        correction = lax.dot_general(prev_ref[m], rows, contract, preferred_element_type=F32)
+        correction = lax.dot_general(prev, rows, contract, preferred_element_type=F32)
         residual = (cols_ref[m].astype(F32) - correction).astype(BF16)
         inv = inv_ref[...]
         row, column = (lax.broadcasted_iota(jnp.int32, inv.shape, d) for d in (0, 1))
@@ -216,23 +239,42 @@
         store_of(m).start()
         turned_ref[m] = new.T
 
+    load_of(1).start()
+    step(0, close_ref[...])
+
+    @pl.loop(1, mu)
+    def _(m):
+        load_of(m).wait()
+
+        @pl.when(m + 1 < mu)
+        def _():
+            load_of(m + 1).start()
+
+        step(m, came[m - 1])
+
     for m in range(mu):
         store_of(m).wait()
 
 
-def vectors(core, pivot_columns, previous, mine, other, pivot_inverse):
+def vectors(core, pivot_columns, close, previous, mine, other, pivot_inverse):
     mu, nu, k = previous.shape
     n = pivot_columns.shape[2]
     vmem = pl.BlockSpec(memory_space=pltpu.VMEM)
+    hbm = pl.BlockSpec(memory_space=pltpu.HBM)
     return pl.pallas_call(
         vectors_kernel,
         out_shape=(
             jax.ShapeDtypeStruct((mu, nu, n), BF16),
             jax.ShapeDtypeStruct((mu, n, nu), BF16),
         ),
-        in_specs=[pl.BlockSpec(memory_space=pltpu.SMEM), vmem, vmem, vmem, vmem, vmem],
+        in_specs=[pl.BlockSpec(memory_space=pltpu.SMEM), vmem, vmem, hbm, vmem, vmem, vmem],
         out_specs=(pl.BlockSpec(memory_space=pl.ANY), vmem),
-        scratch_shapes=[pltpu.VMEM((mu, nu, n), BF16), pltpu.SemaphoreType.DMA((mu,))],
+        scratch_shapes=[
+            pltpu.VMEM((mu - 1, nu, k), BF16),
+            pltpu.VMEM((mu, nu, n), BF16),
+            pltpu.SemaphoreType.DMA((mu - 1,)),
+            pltpu.SemaphoreType.DMA((mu,)),
+        ],
         compiler_params=pltpu.CompilerParams(vmem_limit_bytes=24 << 20),
         cost_estimate=pl.CostEstimate(
             flops=2 * mu * nu * n * (k + n),
@@ -240,7 +282,7 @@
             transcendentals=0,
         ),
         name="vectors",
-    )(core, pivot_columns, previous, mine, other, pivot_inverse)
+    )(core, pivot_columns, close, previous, mine, other, pivot_inverse)
 
 
 def parts_kernel(me_ref, turned_ref, orb_ref, *out_refs, ahead, owners):
@@ -387,12 +429,13 @@
 
     def one_round(index, so_far):
         index = jnp.asarray(index, jnp.int32)
-        picked = pick_rows(jnp.stack([line, base, index]), pivots, previous)
+        turn, part = index // PARTS, index % PARTS
+        where_from = jnp.stack([line, base, turn, part])
+        picked = pick_rows(where_from, pivots, previous)
         came = exchange(jnp.broadcast_to(picked, (n_grp,) + picked.shape), "grp")
-        slots = exchange(spread(came, n_rows), "rows")
-        return select_rows(
-            index.reshape(1), pivots, slots.reshape(n_rows * SLOTS, half), so_far, per_line
-        )
+        messages = spread(where_from, pivots, came, n_rows, mu, nu)
+        slots = exchange(messages, "rows").reshape(n_rows * SLOTS, half)
+        return select_rows(index.reshape(1), pivots, slots, so_far, per_line, nu, n_grp)
 
     mine, rounds = one_round(0, jnp.zeros((n, half), BF16))
     start, mine, rounds = lax.optimization_barrier((jnp.int32(1), mine, rounds))
@@ -407,7 +450,9 @@
     core = (lax.axis_index("rows") % 2).reshape(1).astype(jnp.int32)
     me = lax.axis_index("grp").reshape(1).astype(jnp.int32)
     close = preload(in_hbm, mine)
-    new_vectors, turned = vectors(core, pivot_columns, close, mine, other, pivot_inverse)
+    new_vectors, turned = vectors(
+        core, pivot_columns, close, in_hbm, mine, other, pivot_inverse
+    )
     half = exchange(reduce_to_owner(me, turned, orbitals, n_grp, n_rows), "rows")
     return new_vectors, final(half.reshape(-1, half.shape[-1]), slab_orbitals)
 

time: 102 us -> 100 us (0.980)
  starting transfers between devices: 11.3 us -> 8.83 us
  blocking collectives: 59.5 us -> 57.3 us
  waiting for transfers between devices: 12.4 us -> 14.4 us
  Pallas kernels: 15.6 us -> 16.7 us
    ppermute x8, starting transfers between devices: 11.2 us -> 8.74 us  [hop(): lax.ppermute(x, 'grp', [(i, (i + way) % owners) for i in range(owners)])]
    all_to_all x3, blocking collectives: 59.5 us -> 57.3 us  [exchange(): return lax.all_to_all(x, axis, split_axis=0, concat_axis=0, tiled=True)]
    ppermute x8, waiting for transfers between devices: 12.4 us -> 14.4 us  [hop(): lax.ppermute(x, 'grp', [(i, (i + way) % owners) for i in range(owners)])]
    pallas_call x1, Pallas kernels: 4.35 us -> 5.83 us  [vectors(): pl.pallas_call(vectors_kernel, out_shape=(jax.ShapeDtypeStruct((mu, nu, n...]
    pallas_call x1, Pallas kernels: 2.69 us -> 1.48 us  [preload(): pl.pallas_call(preload_kernel, out_shape=jax.ShapeDtypeStruct(previous.sh...]
  transfers between devices with their start and end apart: 9 -> 9, of which waited for: 4 -> 5; matrix products, arithmetic and copies ran while one was open for 0% -> 0% of each run, Pallas kernels for 6% -> 5%
where the time goes in v7:
time: 100 us; the launch traced here: 99.9 us
  blocking collectives  57.3 us (57%)
  Pallas kernels  16.7 us (17%)
  waiting for transfers between devices  14.4 us (14%)
  starting transfers between devices  8.83 us (9%)
    all_to_all x3, blocking collectives, exchange(): return lax.all_to_all(x, axis, split_axis=0, concat_axis=0, tiled=True)  57.3 us
    ppermute x8, waiting for transfers between devices, hop(): lax.ppermute(x, 'grp', [(i, (i + way) % owners) for i in range(owners)])  14.4 us
    ppermute x8, starting transfers between devices, hop(): lax.ppermute(x, 'grp', [(i, (i + way) % owners) for i in range(owners)])  8.74 us
    pallas_call x1, Pallas kernels, vectors(): pl.pallas_call(vectors_kernel, out_shape=(jax.ShapeDtypeStruct((mu, nu, n...  5.83 us
    pallas_call x5, Pallas kernels, parts(): pl.pallas_call(functools.partial(parts_kernel, ahead=ahead, owners=owners...  4.3 us
    pallas_call x1, Pallas kernels, final(): pl.pallas_call(final_kernel, out_shape=jax.ShapeDtypeStruct((keep, occ, w...  2.08 us
  transfers between devices with their start and end apart: 9, of which 5 were waited for; matrix products, arithmetic and copies ran while one was open for 0% of the time, Pallas kernels for 5%

profile of v7, /device:TPU:1, one launch (start us, length us, event | category | flops | bytes accessed | tf_op | source)
XLA Modules:
  0.0 99.9 jit_solution(16773940066993226336)
XLA Ops:
  0.7 1.0 pick_rows.5
  1.7 17.3 %all_to_all.30.came_ref = bf16[8,8,512]{2,1,0:T(8,128)(2,1)S(1)} all-to-all(bf16[8,8,512]{2,1,0:T(8,128)(2,1)S(1)} %broadcast_in_dim.12), channel_id=1, replica_groups=mesh['rows'=32,'grp'=8] {'grp'}, dimensions={0} | all-to-all | bytes 131072 | tf_op jit(solution)/shard_map/all_to_all | solution.py:418
  19.0 0.9 spread.5
  20.0 19.4 %all_to_all.31 = bf16[32,24,256]{2,1,0:T(8,128)(2,1)S(1)} all-to-all(bf16[32,24,256]{2,1,0:T(8,128)(2,1)S(1)} %spread.5), channel_id=1, replica_groups=mesh['rows'=32,'grp'=8] {'rows'}, dimensions={0} | all-to-all | bytes 786432 | tf_op jit(solution)/shard_map/all_to_all | solution.py:418
  39.4 1.1 %select_rows.5 = (bf16[256,256]{1,0:T(8,128)(2,1)S(1)}, s32[1]{0:T(128)}) custom-call(s32[1]{0:T(128)} %constant.87.clone.1.round_ref, s32[1,256]{1,0:T(1,128)S(1)} %bitcast.66, bf16[768,256]{1,0:T(8,128)(2,1)S(1)} %bitcast.63, bf16[256,256]{1,0:T(8,128)(2,1)S(1)} %broadcast_in_dim.13.so_far_ref), custom_call_target="tpu_custom_call" | custom-call | flops 100663296 | bytes 393216 | tf_op jit(solution)/shard_map/select_rows/pallas_call | solution.py:128
  40.4 0.7 while.12
  41.3 1.5 %preload.1.close_ref = bf16[1280,512]{1,0:T(8,128)(2,1)S(1)} custom-call(bf16[4,1280,512]{2,1,0:T(8,128)(2,1)} %get-tuple-element.221, bf16[256,256]{1,0:T(8,128)(2,1)S(1)} %get-tuple-element.111.after_ref.mine_ref), custom_call_target="tpu_custom_call" | custom-call | bytes 1310720 | tf_op jit(solution)/shard_map/preload/pallas_call | solution.py:200
  43.4 5.8 %vectors.1 = (bf16[4,1280,256]{2,1,0:T(8,128)(2,1)}, bf16[4,256,1280]{2,1,0:T(8,128)(2,1)S(1)}) custom-call(s32[1]{0:T(128)} %bitcast.8.core_ref, bf16[4,1280,256]{2,1,0:T(8,128)(2,1)S(1)} %copy-done.1, bf16[1280,512]{1,0:T(8,128)(2,1)S(1)} %preload.1.close_ref, bf16[4,1280,512]{2,1,0:T(8,128)(2,1)} %get-tuple-element.221, ...), custom_call_target="tpu_custom_call" | custom-call | flops 2013265920 | bytes 13107200 | tf_op jit(solution)/shard_map/vectors/pallas_call | solution.py:264
  49.2 0.9 parts.9
  50.2 1.5 %collective-permute-start.1 = (bf16[16,4,8,128]{3,2,1,0:T(8,128)(2,1)S(1)}, bf16[16,4,8,128]{3,2,1,0:T(8,128)(2,1)S(1)}, u32[]{:S(2)}, u32[]{:S(2)}) collective-permute-start(bf16[16,4,8,128]{3,2,1,0:T(8,128)(2,1)S(1)} %get-tuple-element.114), channel_id=1, source_target_pairs={{0,1},{1,2},{2,3},{3,4},{4,5},{5,6},{6,7},{7,0},{8,9},{9,10},{10,1... | collective-permute-start | bytes 393224 | tf_op jit(solution)/shard_map/ppermute | solution.py:365
  51.6 0.9 parts.8.own_ref
  52.5 2.2 %collective-permute-done.5.came_ref = bf16[16,4,8,128]{3,2,1,0:T(8,128)(2,1)S(1)} collective-permute-done((bf16[16,4,8,128]{3,2,1,0:T(8,128)(2,1)S(1)}, bf16[16,4,8,128]{3,2,1,0:T(8,128)(2,1)S(1)}, u32[]{:S(2)}, u32[]{:S(2)}) %collective-permute-start.5) | collective-permute-done | bytes 131104 | tf_op jit(solution)/shard_map/ppermute | solution.py:365
  54.8 1.4 %collective-permute-start.6 = (bf16[32,4,8,128]{3,2,1,0:T(8,128)(2,1)S(1)}, bf16[32,4,8,128]{3,2,1,0:T(8,128)(2,1)S(1)}, u32[]{:S(2)}, u32[]{:S(2)}) collective-permute-start(bf16[32,4,8,128]{3,2,1,0:T(8,128)(2,1)S(1)} %join.3), channel_id=1, source_target_pairs={{0,7},{1,0},{2,1},{3,2},{4,3},{5,4},{6,5},{7,6},{8,15},{9,8},{10,9... | collective-permute-start | bytes 786440 | tf_op jit(solution)/shard_map/ppermute | solution.py:365
  56.5 0.9 parts.7
  57.3 4.0 %collective-permute-done.6 = bf16[32,4,8,128]{3,2,1,0:T(8,128)(2,1)S(1)} collective-permute-done((bf16[32,4,8,128]{3,2,1,0:T(8,128)(2,1)S(1)}, bf16[32,4,8,128]{3,2,1,0:T(8,128)(2,1)S(1)}, u32[]{:S(2)}, u32[]{:S(2)}) %collective-permute-start.6) | collective-permute-done | bytes 262176 | tf_op jit(solution)/shard_map/ppermute | solution.py:365
  61.3 2.4 %collective-permute-done.2 = bf16[32,4,8,128]{3,2,1,0:T(8,128)(2,1)S(1)} collective-permute-done((bf16[32,4,8,128]{3,2,1,0:T(8,128)(2,1)S(1)}, bf16[32,4,8,128]{3,2,1,0:T(8,128)(2,1)S(1)}, u32[]{:S(2)}, u32[]{:S(2)}) %collective-permute-start.2) | collective-permute-done | bytes 262176 | tf_op jit(solution)/shard_map/ppermute | solution.py:365
  64.0 2.7 %collective-permute-start.7 = (bf16[32,4,8,128]{3,2,1,0:T(8,128)(2,1)S(1)}, bf16[32,4,8,128]{3,2,1,0:T(8,128)(2,1)S(1)}, u32[]{:S(2)}, u32[]{:S(2)}) collective-permute-start(bf16[32,4,8,128]{3,2,1,0:T(8,128)(2,1)S(1)} %get-tuple-element.133), channel_id=1, source_target_pairs={{0,7},{1,0},{2,1},{3,2},{4,3},{5,4},{6,5},{7,6},{8,15},{9,8},{10,9... | collective-permute-start | bytes 786440 | tf_op jit(solution)/shard_map/ppermute | solution.py:365
  66.7 0.9 parts.6
  67.6 2.9 %collective-permute-done.3 = bf16[32,4,8,128]{3,2,1,0:T(8,128)(2,1)S(1)} collective-permute-done((bf16[32,4,8,128]{3,2,1,0:T(8,128)(2,1)S(1)}, bf16[32,4,8,128]{3,2,1,0:T(8,128)(2,1)S(1)}, u32[]{:S(2)}, u32[]{:S(2)}) %collective-permute-start.3) | collective-permute-done | bytes 262176 | tf_op jit(solution)/shard_map/ppermute | solution.py:365
  70.7 2.7 %collective-permute-start.8 = (bf16[32,4,8,128]{3,2,1,0:T(8,128)(2,1)S(1)}, bf16[32,4,8,128]{3,2,1,0:T(8,128)(2,1)S(1)}, u32[]{:S(2)}, u32[]{:S(2)}) collective-permute-start(bf16[32,4,8,128]{3,2,1,0:T(8,128)(2,1)S(1)} %get-tuple-element.131), channel_id=1, source_target_pairs={{0,7},{1,0},{2,1},{3,2},{4,3},{5,4},{6,5},{7,6},{8,15},{9,8},{10,9... | collective-permute-start | bytes 786440 | tf_op jit(solution)/shard_map/ppermute | solution.py:365
  73.5 0.8 parts.5
  74.3 2.8 %collective-permute-done.4 = bf16[32,4,8,128]{3,2,1,0:T(8,128)(2,1)S(1)} collective-permute-done((bf16[32,4,8,128]{3,2,1,0:T(8,128)(2,1)S(1)}, bf16[32,4,8,128]{3,2,1,0:T(8,128)(2,1)S(1)}, u32[]{:S(2)}, u32[]{:S(2)}) %collective-permute-start.4) | collective-permute-done | bytes 262176 | tf_op jit(solution)/shard_map/ppermute | solution.py:365
  77.2 20.6 %all_to_all.32 = f32[32,4,8,128]{3,2,1,0:T(8,128)S(1)} all-to-all(f32[32,4,8,128]{3,2,1,0:T(8,128)S(1)} %fusion.8), channel_id=1, replica_groups=mesh['rows'=32,'grp'=8] {'rows'}, dimensions={0} | all-to-all | bytes 1048576 | tf_op jit(solution)/shard_map/all_to_all | solution.py:418
  97.9 2.1 %final.1 = bf16[8,1024,128]{2,1,0:T(8,128)(2,1)} custom-call(f32[1024,128]{1,0:T(8,128)S(1)} %bitcast.62, bf16[128,1024]{1,0:T(8,128)(2,1)S(1)} %copy-done.2), custom_call_target="tpu_custom_call" | custom-call | flops 536870912 | bytes 2621440 | tf_op jit(solution)/shard_map/final/pallas_call | solution.py:404
  (27 shorter events, 1.8 us)
Async XLA Ops:
  0.7 18.3 %copy-start.4 = (s32[256]{0:T(256)S(1)}, s32[256]{0:T(256)}, u32[]{:S(2)}) copy-start(s32[256]{0:T(256)} %param.10) | copy-start | bytes 3076
  41.1 1.6 %collective-permute-start = (bf16[256,256]{1,0:T(8,128)(2,1)S(1)}, bf16[256,256]{1,0:T(8,128)(2,1)S(1)}, u32[]{:S(2)}, u32[]{:S(2)}) collective-permute-start(bf16[256,256]{1,0:T(8,128)(2,1)S(1)} %get-tuple-element.111.after_ref.mine_ref), channel_id=1, source_target_pairs={{0,8},{8,0},{16,24},{24,16},{32,40},{40,32},{48,56},{56,48},{64,72... | collective-permute-start | bytes 393224 | tf_op jit(solution)/shard_map/ppermute | solution.py:443
  41.2 2.1 %copy-start.1 = (bf16[4,1280,256]{2,1,0:T(8,128)(2,1)S(1)}, bf16[4,1280,256]{2,1,0:T(8,128)(2,1)}, u32[]{:S(2)}) copy-start(bf16[4,1280,256]{2,1,0:T(8,128)(2,1)} %cols_ref.1) | copy-start | bytes 7864324
  41.3 2.1 %copy-start.3 = (bf16[256,256]{1,0:T(8,128)(2,1)S(1)}, bf16[256,256]{1,0:T(8,128)(2,1)}, u32[]{:S(2)}) copy-start(bf16[256,256]{1,0:T(8,128)(2,1)} %inv_ref.1) | copy-start | bytes 393220
  43.4 5.8 %copy-start = (bf16[1280,1024]{1,0:T(8,128)(2,1)S(1)}, bf16[1280,1024]{1,0:T(8,128)(2,1)}, u32[]{:S(2)}) copy-start(bf16[1280,1024]{1,0:T(8,128)(2,1)} %orb_ref.9) | copy-start | bytes 7864324
  50.1 4.7 %collective-permute-start.5 = (bf16[16,4,8,128]{3,2,1,0:T(8,128)(2,1)S(1)}, bf16[16,4,8,128]{3,2,1,0:T(8,128)(2,1)S(1)}, u32[]{:S(2)}, u32[]{:S(2)}) collective-permute-start(bf16[16,4,8,128]{3,2,1,0:T(8,128)(2,1)S(1)} %get-tuple-element.115), channel_id=1, source_target_pairs={{0,7},{1,0},{2,1},{3,2},{4,3},{5,4},{6,5},{7,6},{8,15},{9,8},{10,9... | collective-permute-start | bytes 393224 | tf_op jit(solution)/shard_map/ppermute | solution.py:365
  50.2 6.0 %collective-permute-start.1 = (bf16[16,4,8,128]{3,2,1,0:T(8,128)(2,1)S(1)}, bf16[16,4,8,128]{3,2,1,0:T(8,128)(2,1)S(1)}, u32[]{:S(2)}, u32[]{:S(2)}) collective-permute-start(bf16[16,4,8,128]{3,2,1,0:T(8,128)(2,1)S(1)} %get-tuple-element.114), channel_id=1, source_target_pairs={{0,1},{1,2},{2,3},{3,4},{4,5},{5,6},{6,7},{7,0},{8,9},{9,10},{10,1... | collective-permute-start | bytes 393224 | tf_op jit(solution)/shard_map/ppermute | solution.py:365
  54.8 6.5 %collective-permute-start.6 = (bf16[32,4,8,128]{3,2,1,0:T(8,128)(2,1)S(1)}, bf16[32,4,8,128]{3,2,1,0:T(8,128)(2,1)S(1)}, u32[]{:S(2)}, u32[]{:S(2)}) collective-permute-start(bf16[32,4,8,128]{3,2,1,0:T(8,128)(2,1)S(1)} %join.3), channel_id=1, source_target_pairs={{0,7},{1,0},{2,1},{3,2},{4,3},{5,4},{6,5},{7,6},{8,15},{9,8},{10,9... | collective-permute-start | bytes 786440 | tf_op jit(solution)/shard_map/ppermute | solution.py:365
  56.2 7.6 %collective-permute-start.2 = (bf16[32,4,8,128]{3,2,1,0:T(8,128)(2,1)S(1)}, bf16[32,4,8,128]{3,2,1,0:T(8,128)(2,1)S(1)}, u32[]{:S(2)}, u32[]{:S(2)}) collective-permute-start(bf16[32,4,8,128]{3,2,1,0:T(8,128)(2,1)S(1)} %join.2), channel_id=1, source_target_pairs={{0,1},{1,2},{2,3},{3,4},{4,5},{5,6},{6,7},{7,0},{8,9},{9,10},{10,1... | collective-permute-start | bytes 786440 | tf_op jit(solution)/shard_map/ppermute | solution.py:365
  63.9 6.5 %collective-permute-start.3 = (bf16[32,4,8,128]{3,2,1,0:T(8,128)(2,1)S(1)}, bf16[32,4,8,128]{3,2,1,0:T(8,128)(2,1)S(1)}, u32[]{:S(2)}, u32[]{:S(2)}) collective-permute-start(bf16[32,4,8,128]{3,2,1,0:T(8,128)(2,1)S(1)} %get-tuple-element.132), channel_id=1, source_target_pairs={{0,1},{1,2},{2,3},{3,4},{4,5},{5,6},{6,7},{7,0},{8,9},{9,10},{10,1... | collective-permute-start | bytes 786440 | tf_op jit(solution)/shard_map/ppermute | solution.py:365
  64.0 6.4 %collective-permute-start.7 = (bf16[32,4,8,128]{3,2,1,0:T(8,128)(2,1)S(1)}, bf16[32,4,8,128]{3,2,1,0:T(8,128)(2,1)S(1)}, u32[]{:S(2)}, u32[]{:S(2)}) collective-permute-start(bf16[32,4,8,128]{3,2,1,0:T(8,128)(2,1)S(1)} %get-tuple-element.133), channel_id=1, source_target_pairs={{0,7},{1,0},{2,1},{3,2},{4,3},{5,4},{6,5},{7,6},{8,15},{9,8},{10,9... | collective-permute-start | bytes 786440 | tf_op jit(solution)/shard_map/ppermute | solution.py:365
  70.6 6.5 %collective-permute-start.4 = (bf16[32,4,8,128]{3,2,1,0:T(8,128)(2,1)S(1)}, bf16[32,4,8,128]{3,2,1,0:T(8,128)(2,1)S(1)}, u32[]{:S(2)}, u32[]{:S(2)}) collective-permute-start(bf16[32,4,8,128]{3,2,1,0:T(8,128)(2,1)S(1)} %get-tuple-element.130), channel_id=1, source_target_pairs={{0,1},{1,2},{2,3},{3,4},{4,5},{5,6},{6,7},{7,0},{8,9},{9,10},{10,1... | collective-permute-start | bytes 786440 | tf_op jit(solution)/shard_map/ppermute | solution.py:365
  70.7 6.4 %collective-permute-start.8 = (bf16[32,4,8,128]{3,2,1,0:T(8,128)(2,1)S(1)}, bf16[32,4,8,128]{3,2,1,0:T(8,128)(2,1)S(1)}, u32[]{:S(2)}, u32[]{:S(2)}) collective-permute-start(bf16[32,4,8,128]{3,2,1,0:T(8,128)(2,1)S(1)} %get-tuple-element.131), channel_id=1, source_target_pairs={{0,7},{1,0},{2,1},{3,2},{4,3},{5,4},{6,5},{7,6},{8,15},{9,8},{10,9... | collective-permute-start | bytes 786440 | tf_op jit(solution)/shard_map/ppermute | solution.py:365
  74.3 23.5 %copy-start.2 = (bf16[128,1024]{1,0:T(8,128)(2,1)S(1)}, bf16[128,1024]{1,0:T(8,128)(2,1)}, u32[]{:S(2)}) copy-start(bf16[128,1024]{1,0:T(8,128)(2,1)} %slab_ref.1) | copy-start | bytes 786436

commit v8 on v7

--- a/solution.py
+++ b/solution.py
@@ -11,14 +11,15 @@
 F32 = jnp.float32
 BF16 = jnp.bfloat16
 DEPTH = 8
-SLOTS = 24
-PARTS = 3
+SLOTS = 64
+PARTS = 4
+PIECES = 4
 
 
 def pick_kernel(where_from_ref, piv_ref, prev_ref, out_ref, acc_ref, held, sems, rows_ref):
     mu, nu, _ = prev_ref.shape
     depth, group, _ = held.shape
-    base, turn = where_from_ref[1], where_from_ref[2]
+    base, turn = where_from_ref[0], where_from_ref[2]
     acc_ref[...] = jnp.zeros_like(acc_ref)
     pivots = piv_ref[...]
     order = lax.broadcasted_iota(jnp.int32, pivots.shape, 0) * pivots.shape[1]
@@ -62,16 +63,20 @@
         return 0
 
     lax.fori_loop(0, total, place, 0)
-    out_ref[...] = acc_ref[...].astype(BF16)
-
-
-def pick_rows(where_from, pivots, previous):
+    half = out_ref.shape[2]
+    for c in range(2):
+        piece = acc_ref[:, c * half : (c + 1) * half].astype(BF16)
+        for chip in range(out_ref.shape[0] // 2):
+            out_ref[2 * chip + c] = piece
+
+
+def pick_rows(where_from, pivots, previous, n_rows):
     n = pivots.shape[0]
     k = previous.shape[2]
     lanes = 128
     return pl.pallas_call(
         pick_kernel,
-        out_shape=jax.ShapeDtypeStruct((DEPTH, k), BF16),
+        out_shape=jax.ShapeDtypeStruct((n_rows, DEPTH, k // 2), BF16),
         in_specs=[
             pl.BlockSpec(memory_space=pltpu.SMEM),
             pl.BlockSpec(memory_space=pltpu.VMEM),
@@ -94,26 +99,26 @@
     return jnp.floor((x + 0.5) * (1.0 / by))
 
 
-def select_kernel(round_ref, piv_ref, slots_ref, so_far_ref, out_ref, rounds_ref, *, per_line, nu, owners):
+def select_kernel(round_ref, piv_ref, slots_ref, so_far_ref, out_ref, rounds_ref, *, per_line, nu, n_rows):
     total, _ = slots_ref.shape
     n = piv_ref.shape[1]
     pivot = piv_ref[...].astype(F32)
     line = whole_part(pivot, per_line)
     inside = pivot - line * per_line
     inside = inside - whole_part(inside, NBAS) * NBAS
-    device = jnp.broadcast_to(line * owners + whole_part(inside, nu), (n, n))
+    device = jnp.broadcast_to(whole_part(inside, nu) * n_rows + line, (n, n))
     mine = device.T
     before = lax.broadcasted_iota(jnp.int32, (n, n), 1) < lax.broadcasted_iota(jnp.int32, (n, n), 0)
     rank = jnp.sum(jnp.where((device == mine) & before, 1.0, 0.0), axis=1, keepdims=True)
     turn = whole_part(rank, DEPTH)
     turns = jnp.broadcast_to(turn, (n, n))
-    my_line = whole_part(mine, owners)
-    ahead = (device >= my_line * owners) & (device < mine) & (turns.T == turns)
+    plane = whole_part(mine, n_rows)
+    ahead = (device >= plane * n_rows) & (device < mine) & (turns.T == turns)
     place = jnp.sum(jnp.where(ahead, 1.0, 0.0), axis=1, keepdims=True) + rank - turn * DEPTH
     part = whole_part(place, SLOTS)
     when = turn * PARTS + part
     rounds_ref[0] = jnp.max(when).astype(jnp.int32) + 1
-    index = my_line[:, :1] * SLOTS + place - part * SLOTS
+    index = plane[:, :1] * SLOTS + place - part * SLOTS
     index = jnp.where(when == round_ref[0].astype(F32), index, -1.0).astype(jnp.int32)
     hot = index == lax.broadcasted_iota(jnp.int32, (n, total), 1)
     hot = jnp.where(hot, 1.0, 0.0).astype(BF16)
@@ -121,12 +126,12 @@
     out_ref[...] = (picked + so_far_ref[...].astype(F32)).astype(BF16)
 
 
-def select_rows(round_index, pivots, slots, so_far, per_line, nu, owners):
+def select_rows(round_index, pivots, slots, so_far, per_line, nu, n_rows):
     total, width = slots.shape
     n = pivots.shape[0]
     vmem = pl.BlockSpec(memory_space=pltpu.VMEM)
     return pl.pallas_call(
-        functools.partial(select_kernel, per_line=per_line, nu=nu, owners=owners),
+        functools.partial(select_kernel, per_line=per_line, nu=nu, n_rows=n_rows),
         out_shape=(
             jax.ShapeDtypeStruct((n, width), BF16),
             jax.ShapeDtypeStruct((1,), jnp.int32),
@@ -141,59 +146,68 @@
     )(round_index, pivots.reshape(1, n), slots, so_far)
 
 
-def spread_kernel(where_from_ref, piv_ref, came_ref, out_ref, *, mu, nu):
-    owners, depth, k = came_ref.shape
+def pack_kernel(where_from_ref, piv_ref, came_ref, out_ref, *, mu, nu):
+    n_rows, depth, half = came_ref.shape
     n = piv_ref.shape[1]
-    line, turn, part = (where_from_ref[i] for i in (0, 2, 3))
-    offset = jnp.broadcast_to(piv_ref[...] - line, (owners, n))
-    low = lax.broadcasted_iota(jnp.int32, (owners, n), 0) * nu
-    count = jnp.zeros((owners, n), F32)
+    nu_first, turn, part = (where_from_ref[i] for i in (1, 2, 3))
+    low = lax.broadcasted_iota(jnp.int32, (n_rows, n), 0) * (mu * NBAS) + nu_first
+    offset = jnp.broadcast_to(piv_ref[...], (n_rows, n)) - low
+    count = jnp.zeros((n_rows, n), F32)
     for m in range(mu):
-        inside = offset - m * NBAS - low
+        inside = offset - m * NBAS
         count += jnp.where((inside >= 0) & (inside < nu), 1.0, 0.0)
     count = jnp.sum(count, axis=1, keepdims=True) - (turn * depth).astype(F32)
     count = jnp.clip(count, 0.0, depth)
-    wide = (owners, owners * depth)
+    wide = (n_rows, n_rows * depth)
     slot = lax.broadcasted_iota(jnp.int32, wide, 1) - lax.broadcasted_iota(jnp.int32, wide, 0) * depth
     here = (slot >= 0) & (slot < depth)
+    slot = slot.astype(F32)
     start = jnp.sum(jnp.where(slot >= depth, count, 0.0), axis=0, keepdims=True)
-    used = jnp.sum(jnp.where(here & (slot.astype(F32) < count), 1.0, 0.0), axis=0, keepdims=True)
-    place = start + jnp.sum(jnp.where(here, slot.astype(F32), 0.0), axis=0, keepdims=True)
+    used = jnp.sum(jnp.where(here & (slot < count), 1.0, 0.0), axis=0, keepdims=True)
+    place = start + jnp.sum(jnp.where(here, slot, 0.0), axis=0, keepdims=True)
     place = place - (part * SLOTS).astype(F32)
     packed = lax.broadcasted_iota(jnp.int32, (SLOTS, wide[1]), 0).astype(F32)
     hot = jnp.where((packed == place) & (used > 0.0), 1.0, 0.0).astype(BF16)
-    rows = came_ref[...].astype(F32).reshape(wide[1], k).astype(BF16)
+    rows = came_ref[...].astype(F32).reshape(wide[1], half).astype(BF16)
     rows = jnp.dot(hot, rows, preferred_element_type=F32).astype(BF16)
-    half = out_ref.shape[2]
-    for c in range(2):
-        piece = rows[:, c * half : (c + 1) * half]
-
-        @pl.loop(0, out_ref.shape[0] // 2)
-        def _(chip):
-            out_ref[2 * chip + c] = piece
-
-
-def spread(where_from, pivots, came, n_rows, mu, nu):
-    k = came.shape[2]
+    for g in range(out_ref.shape[0]):
+        out_ref[g] = rows
+
+
+def pack(where_from, pivots, came, n_grp, mu, nu):
+    half = came.shape[2]
     n = pivots.shape[0]
     vmem = pl.BlockSpec(memory_space=pltpu.VMEM)
     return pl.pallas_call(
-        functools.partial(spread_kernel, mu=mu, nu=nu),
-        out_shape=jax.ShapeDtypeStruct((n_rows, SLOTS, k // 2), BF16),
+        functools.partial(pack_kernel, mu=mu, nu=nu),
+        out_shape=jax.ShapeDtypeStruct((n_grp, SLOTS, half), BF16),
         in_specs=[pl.BlockSpec(memory_space=pltpu.SMEM), vmem, vmem],
         out_specs=vmem,
         compiler_params=pltpu.CompilerParams(vmem_limit_bytes=4 << 20),
         cost_estimate=pl.CostEstimate(
-            flops=came.size, bytes_accessed=n_rows * SLOTS * k, transcendentals=0
-        ),
-        name="spread",
+            flops=came.size, bytes_accessed=2 * n_grp * SLOTS * half, transcendentals=0
+        ),
+        name="pack",
     )(where_from, pivots.reshape(1, n), came)
 
 
-def preload_kernel(prev_ref, after_ref, out_ref, sem):
-    copy = pltpu.make_async_copy(prev_ref.at[0], out_ref, sem)
-    copy.start()
-    copy.wait()
+def pieces(source, target, sems):
+    count = sems.shape[0]
+    rows = target.shape[0] // count
+    return [
+        pltpu.make_async_copy(
+            source.at[pl.ds(i * rows, rows)], target.at[pl.ds(i * rows, rows)], sems.at[i]
+        )
+        for i in range(count)
+    ]
+
+
+def preload_kernel(prev_ref, after_ref, out_ref, sems):
+    copies = pieces(prev_ref.at[0], out_ref, sems)
+    for copy in copies:
+        copy.start()
+    for copy in copies:
+        copy.wait()
 
 
 def preload(previous, after):
@@ -202,7 +216,7 @@
         out_shape=jax.ShapeDtypeStruct(previous.shape[1:], previous.dtype),
         in_specs=[pl.BlockSpec(memory_space=pltpu.HBM), pl.BlockSpec(memory_space=pl.ANY)],
         out_specs=pl.BlockSpec(memory_space=pltpu.VMEM),
-        scratch_shapes=[pltpu.SemaphoreType.DMA],
+        scratch_shapes=[pltpu.SemaphoreType.DMA((PIECES,))],
         compiler_params=pltpu.CompilerParams(vmem_limit_bytes=4 << 20),
         cost_estimate=pl.CostEstimate(
             flops=0, bytes_accessed=previous.size // 2, transcendentals=0
@@ -216,11 +230,12 @@
 ):
     mu = cols_ref.shape[0]
 
-    def load_of(m):
-        return pltpu.make_async_copy(prev_ref.at[m], came.at[m - 1], load.at[m - 1])
+    def start_load(m):
+        for copy in pieces(prev_ref.at[m], came.at[m - 1], load.at[m - 1]):
+            copy.start()
 
     def store_of(m):
-        return pltpu.make_async_copy(made.at[m], new_ref.at[m], store.at[m])
+        return pieces(made.at[m], new_ref.at[m], store.at[m])
 
     def step(m, prev):
         mine, other = mine_ref[...].astype(F32), other_ref[...].astype(F32)
@@ -236,24 +251,27 @@
         upper = jnp.where(row > column, 0.0, inv.astype(F32)).astype(BF16)
         new = jnp.dot(residual, upper, preferred_element_type=F32).astype(BF16)
         made[m] = new
-        store_of(m).start()
+        for copy in store_of(m):
+            copy.start()
         turned_ref[m] = new.T
 
-    load_of(1).start()
+    start_load(1)
     step(0, close_ref[...])
 
     @pl.loop(1, mu)
     def _(m):
-        load_of(m).wait()
+        for copy in pieces(prev_ref.at[m], came.at[m - 1], load.at[m - 1]):
+            copy.wait()
 
         @pl.when(m + 1 < mu)
         def _():
-            load_of(m + 1).start()
+            start_load(m + 1)
 
         step(m, came[m - 1])
 
     for m in range(mu):
-        store_of(m).wait()
+        for copy in store_of(m):
+            copy.wait()
 
 
 def vectors(core, pivot_columns, close, previous, mine, other, pivot_inverse):
@@ -272,8 +290,8 @@
         scratch_shapes=[
             pltpu.VMEM((mu - 1, nu, k), BF16),
             pltpu.VMEM((mu, nu, n), BF16),
-            pltpu.SemaphoreType.DMA((mu - 1,)),
-            pltpu.SemaphoreType.DMA((mu,)),
+            pltpu.SemaphoreType.DMA((mu - 1, PIECES)),
+            pltpu.SemaphoreType.DMA((mu, PIECES)),
         ],
         compiler_params=pltpu.CompilerParams(vmem_limit_bytes=24 << 20),
         cost_estimate=pl.CostEstimate(
@@ -423,19 +441,16 @@
     n = pivots.shape[0]
     half = k // 2
     per_line = mu * NBAS
-    line = lax.axis_index("rows") * per_line
-    base = line + lax.axis_index("grp") * nu
-    line, base = line.astype(jnp.int32), base.astype(jnp.int32)
+    nu_first = (lax.axis_index("grp") * nu).astype(jnp.int32)
+    base = (lax.axis_index("rows") * per_line).astype(jnp.int32) + nu_first
 
     def one_round(index, so_far):
         index = jnp.asarray(index, jnp.int32)
-        turn, part = index // PARTS, index % PARTS
-        where_from = jnp.stack([line, base, turn, part])
-        picked = pick_rows(where_from, pivots, previous)
-        came = exchange(jnp.broadcast_to(picked, (n_grp,) + picked.shape), "grp")
-        messages = spread(where_from, pivots, came, n_rows, mu, nu)
-        slots = exchange(messages, "rows").reshape(n_rows * SLOTS, half)
-        return select_rows(index.reshape(1), pivots, slots, so_far, per_line, nu, n_grp)
+        where_from = jnp.stack([base, nu_first, index // PARTS, index % PARTS])
+        came = exchange(pick_rows(where_from, pivots, previous, n_rows), "rows")
+        slots = exchange(pack(where_from, pivots, came, n_grp, mu, nu), "grp")
+        slots = slots.reshape(n_grp * SLOTS, half)
+        return select_rows(index.reshape(1), pivots, slots, so_far, per_line, nu, n_rows)
 
     mine, rounds = one_round(0, jnp.zeros((n, half), BF16))
     start, mine, rounds = lax.optimization_barrier((jnp.int32(1), mine, rounds))

time: 100 us -> 102 us (1.020)
  blocking collectives: 57.3 us -> 53.4 us
  waiting for transfers between devices: 14.4 us -> 16.6 us
  starting transfers between devices: 8.83 us -> 10.6 us
  Pallas kernels: 16.7 us -> 17.9 us
    all_to_all x3, blocking collectives: 57.3 us -> 53.4 us  [exchange(): return lax.all_to_all(x, axis, split_axis=0, concat_axis=0, tiled=True)]
    ppermute x8, waiting for transfers between devices: 14.4 us -> 16.6 us  [hop(): lax.ppermute(x, 'grp', [(i, (i + way) % owners) for i in range(owners)])]
    ppermute x1, starting transfers between devices: 0.09 us -> 1.94 us  [pivot_halves(): other = lax.ppermute(mine, 'rows', [(i, i ^ 1) for i in range(n_rows)])]
    pallas_call x2, Pallas kernels: 1.9 us -> 3.15 us  [the longest x1 2.35 us: pick_rows(): pl.pallas_call(pick_kernel, out_shape=jax.ShapeDtypeStruct((n_rows, DEPTH...]
where the time goes in v8:
time: 102 us; the launch traced here: 101 us
  blocking collectives  53.4 us (52%)
  Pallas kernels  17.9 us (18%)
  waiting for transfers between devices  16.6 us (16%)
  starting transfers between devices  10.6 us (10%)
    all_to_all x3, blocking collectives, exchange(): return lax.all_to_all(x, axis, split_axis=0, concat_axis=0, tiled=True)  53.4 us
    ppermute x8, waiting for transfers between devices, hop(): lax.ppermute(x, 'grp', [(i, (i + way) % owners) for i in range(owners)])  16.6 us
    ppermute x8, starting transfers between devices, hop(): lax.ppermute(x, 'grp', [(i, (i + way) % owners) for i in range(owners)])  8.65 us
    pallas_call x1, Pallas kernels, vectors(): pl.pallas_call(vectors_kernel, out_shape=(jax.ShapeDtypeStruct((mu, nu, n...  5.86 us
    pallas_call x5, Pallas kernels, parts(): pl.pallas_call(functools.partial(parts_kernel, ahead=ahead, owners=owners...  4.29 us
    pallas_call x1, Pallas kernels, pick_rows(): pl.pallas_call(pick_kernel, out_shape=jax.ShapeDtypeStruct((n_rows, DEPTH...  2.35 us
    pallas_call x1, Pallas kernels, final(): pl.pallas_call(final_kernel, out_shape=jax.ShapeDtypeStruct((keep, occ, w...  2.07 us
  transfers between devices with their start and end apart: 9, of which 5 were waited for; matrix products, arithmetic and copies ran while one was open for 0% of the time, Pallas kernels for 5%

profile of v8, /device:TPU:1, one launch (start us, length us, event | category | flops | bytes accessed | tf_op | source)
XLA Modules:
  0.0 101.2 jit_solution(15236393313768647551)
XLA Ops:
  0.7 2.4 %pick_rows.5 = bf16[32,8,256]{2,1,0:T(8,128)(2,1)S(1)} custom-call(s32[4]{0:T(128)S(1)} %pad_add_fusion.1.where_from_ref, s32[2,128]{1,0:T(2,128)} %bitcast.64, bf16[4,1280,512]{2,1,0:T(8,128)(2,1)} %prev_ref.5), custom_call_target="tpu_custom_call" | custom-call | flops 131072 | bytes 262144 | tf_op jit(solution)/shard_map/pick_rows/pallas_call | solution.py:77
  3.1 16.1 %all_to_all.30.came_ref = bf16[32,8,256]{2,1,0:T(8,128)(2,1)S(1)} all-to-all(bf16[32,8,256]{2,1,0:T(8,128)(2,1)S(1)} %pick_rows.5), channel_id=1, replica_groups=mesh['rows'=32,'grp'=8] {'rows'}, dimensions={0} | all-to-all | bytes 262144 | tf_op jit(solution)/shard_map/all_to_all | solution.py:436
  19.2 0.8 pack.5
  20.0 18.8 %all_to_all.31 = bf16[8,64,256]{2,1,0:T(8,128)(2,1)S(1)} all-to-all(bf16[8,64,256]{2,1,0:T(8,128)(2,1)S(1)} %pack.5), channel_id=1, replica_groups=mesh['rows'=32,'grp'=8] {'grp'}, dimensions={0} | all-to-all | bytes 524288 | tf_op jit(solution)/shard_map/all_to_all | solution.py:436
  38.8 1.0 %select_rows.5 = (bf16[256,256]{1,0:T(8,128)(2,1)S(1)}, s32[1]{0:T(128)}) custom-call(s32[1]{0:T(128)} %constant.99.clone.1.round_ref, s32[1,256]{1,0:T(1,128)S(1)} %bitcast.66, bf16[512,256]{1,0:T(8,128)(2,1)S(1)} %bitcast.63, bf16[256,256]{1,0:T(8,128)(2,1)S(1)} %broadcast_in_dim.3.so_far_ref), custom_call_target="tpu_custom_call" | custom-call | flops 67108864 | bytes 262144 | tf_op jit(solution)/shard_map/select_rows/pallas_call | solution.py:133
  40.5 1.9 %collective-permute-start = (bf16[256,256]{1,0:T(8,128)(2,1)S(1)}, bf16[256,256]{1,0:T(8,128)(2,1)S(1)}, u32[]{:S(2)}, u32[]{:S(2)}) collective-permute-start(bf16[256,256]{1,0:T(8,128)(2,1)S(1)} %get-tuple-element.111.after_ref.mine_ref), channel_id=1, source_target_pairs={{0,8},{8,0},{16,24},{24,16},{32,40},{40,32},{48,56},{56,48},{64,72... | collective-permute-start | bytes 393224 | tf_op jit(solution)/shard_map/ppermute | solution.py:458
  42.5 1.5 %preload.1.close_ref = bf16[1280,512]{1,0:T(8,128)(2,1)S(1)} custom-call(bf16[4,1280,512]{2,1,0:T(8,128)(2,1)} %get-tuple-element.227, bf16[256,256]{1,0:T(8,128)(2,1)S(1)} %get-tuple-element.111.after_ref.mine_ref), custom_call_target="tpu_custom_call" | custom-call | bytes 1310720 | tf_op jit(solution)/shard_map/preload/pallas_call | solution.py:214
  44.6 5.9 %vectors.1 = (bf16[4,1280,256]{2,1,0:T(8,128)(2,1)}, bf16[4,256,1280]{2,1,0:T(8,128)(2,1)S(1)}) custom-call(s32[1]{0:T(128)} %bitcast.8.core_ref, bf16[4,1280,256]{2,1,0:T(8,128)(2,1)S(1)} %copy-done.1, bf16[1280,512]{1,0:T(8,128)(2,1)S(1)} %preload.1.close_ref, bf16[4,1280,512]{2,1,0:T(8,128)(2,1)} %get-tuple-element.227, ...), custom_call_target="tpu_custom_call" | custom-call | flops 2013265920 | bytes 13107200 | tf_op jit(solution)/shard_map/vectors/pallas_call | solution.py:282
  50.5 0.9 parts.9
  51.4 1.5 %collective-permute-start.1 = (bf16[16,4,8,128]{3,2,1,0:T(8,128)(2,1)S(1)}, bf16[16,4,8,128]{3,2,1,0:T(8,128)(2,1)S(1)}, u32[]{:S(2)}, u32[]{:S(2)}) collective-permute-start(bf16[16,4,8,128]{3,2,1,0:T(8,128)(2,1)S(1)} %get-tuple-element.114), channel_id=1, source_target_pairs={{0,1},{1,2},{2,3},{3,4},{4,5},{5,6},{6,7},{7,0},{8,9},{9,10},{10,1... | collective-permute-start | bytes 393224 | tf_op jit(solution)/shard_map/ppermute | solution.py:383
  52.9 0.9 parts.8.own_ref
  53.8 2.8 %collective-permute-done.5.came_ref = bf16[16,4,8,128]{3,2,1,0:T(8,128)(2,1)S(1)} collective-permute-done((bf16[16,4,8,128]{3,2,1,0:T(8,128)(2,1)S(1)}, bf16[16,4,8,128]{3,2,1,0:T(8,128)(2,1)S(1)}, u32[]{:S(2)}, u32[]{:S(2)}) %collective-permute-start.5) | collective-permute-done | bytes 131104 | tf_op jit(solution)/shard_map/ppermute | solution.py:383
  56.6 1.5 %collective-permute-start.6 = (bf16[32,4,8,128]{3,2,1,0:T(8,128)(2,1)S(1)}, bf16[32,4,8,128]{3,2,1,0:T(8,128)(2,1)S(1)}, u32[]{:S(2)}, u32[]{:S(2)}) collective-permute-start(bf16[32,4,8,128]{3,2,1,0:T(8,128)(2,1)S(1)} %join.3), channel_id=1, source_target_pairs={{0,7},{1,0},{2,1},{3,2},{4,3},{5,4},{6,5},{7,6},{8,15},{9,8},{10,9... | collective-permute-start | bytes 786440 | tf_op jit(solution)/shard_map/ppermute | solution.py:383
  58.2 0.9 parts.7
  59.1 4.6 %collective-permute-done.6 = bf16[32,4,8,128]{3,2,1,0:T(8,128)(2,1)S(1)} collective-permute-done((bf16[32,4,8,128]{3,2,1,0:T(8,128)(2,1)S(1)}, bf16[32,4,8,128]{3,2,1,0:T(8,128)(2,1)S(1)}, u32[]{:S(2)}, u32[]{:S(2)}) %collective-permute-start.6) | collective-permute-done | bytes 262176 | tf_op jit(solution)/shard_map/ppermute | solution.py:383
  63.7 2.7 %collective-permute-done.2 = bf16[32,4,8,128]{3,2,1,0:T(8,128)(2,1)S(1)} collective-permute-done((bf16[32,4,8,128]{3,2,1,0:T(8,128)(2,1)S(1)}, bf16[32,4,8,128]{3,2,1,0:T(8,128)(2,1)S(1)}, u32[]{:S(2)}, u32[]{:S(2)}) %collective-permute-start.2) | collective-permute-done | bytes 262176 | tf_op jit(solution)/shard_map/ppermute | solution.py:383
  66.6 2.7 %collective-permute-start.7 = (bf16[32,4,8,128]{3,2,1,0:T(8,128)(2,1)S(1)}, bf16[32,4,8,128]{3,2,1,0:T(8,128)(2,1)S(1)}, u32[]{:S(2)}, u32[]{:S(2)}) collective-permute-start(bf16[32,4,8,128]{3,2,1,0:T(8,128)(2,1)S(1)} %get-tuple-element.133), channel_id=1, source_target_pairs={{0,7},{1,0},{2,1},{3,2},{4,3},{5,4},{6,5},{7,6},{8,15},{9,8},{10,9... | collective-permute-start | bytes 786440 | tf_op jit(solution)/shard_map/ppermute | solution.py:383
  69.3 0.9 parts.6
  70.1 3.7 %collective-permute-done.3 = bf16[32,4,8,128]{3,2,1,0:T(8,128)(2,1)S(1)} collective-permute-done((bf16[32,4,8,128]{3,2,1,0:T(8,128)(2,1)S(1)}, bf16[32,4,8,128]{3,2,1,0:T(8,128)(2,1)S(1)}, u32[]{:S(2)}, u32[]{:S(2)}) %collective-permute-start.3) | collective-permute-done | bytes 262176 | tf_op jit(solution)/shard_map/ppermute | solution.py:383
  74.1 2.7 %collective-permute-start.8 = (bf16[32,4,8,128]{3,2,1,0:T(8,128)(2,1)S(1)}, bf16[32,4,8,128]{3,2,1,0:T(8,128)(2,1)S(1)}, u32[]{:S(2)}, u32[]{:S(2)}) collective-permute-start(bf16[32,4,8,128]{3,2,1,0:T(8,128)(2,1)S(1)} %get-tuple-element.131), channel_id=1, source_target_pairs={{0,7},{1,0},{2,1},{3,2},{4,3},{5,4},{6,5},{7,6},{8,15},{9,8},{10,9... | collective-permute-start | bytes 786440 | tf_op jit(solution)/shard_map/ppermute | solution.py:383
  76.7 0.8 parts.5
  77.6 2.9 %collective-permute-done.4 = bf16[32,4,8,128]{3,2,1,0:T(8,128)(2,1)S(1)} collective-permute-done((bf16[32,4,8,128]{3,2,1,0:T(8,128)(2,1)S(1)}, bf16[32,4,8,128]{3,2,1,0:T(8,128)(2,1)S(1)}, u32[]{:S(2)}, u32[]{:S(2)}) %collective-permute-start.4) | collective-permute-done | bytes 262176 | tf_op jit(solution)/shard_map/ppermute | solution.py:383
  80.6 18.5 %all_to_all.32 = f32[32,4,8,128]{3,2,1,0:T(8,128)S(1)} all-to-all(f32[32,4,8,128]{3,2,1,0:T(8,128)S(1)} %fusion.8), channel_id=1, replica_groups=mesh['rows'=32,'grp'=8] {'rows'}, dimensions={0} | all-to-all | bytes 1048576 | tf_op jit(solution)/shard_map/all_to_all | solution.py:436
  99.1 2.1 %final.1 = bf16[8,1024,128]{2,1,0:T(8,128)(2,1)} custom-call(f32[1024,128]{1,0:T(8,128)S(1)} %bitcast.62, bf16[128,1024]{1,0:T(8,128)(2,1)S(1)} %copy-done.2), custom_call_target="tpu_custom_call" | custom-call | flops 536870912 | bytes 2621440 | tf_op jit(solution)/shard_map/final/pallas_call | solution.py:422
  (26 shorter events, 2.3 us)
Async XLA Ops:
  0.7 18.5 %copy-start.4 = (s32[256]{0:T(256)S(1)}, s32[256]{0:T(256)}, u32[]{:S(2)}) copy-start(s32[256]{0:T(256)} %param.10) | copy-start | bytes 3076
  40.5 3.4 %collective-permute-start = (bf16[256,256]{1,0:T(8,128)(2,1)S(1)}, bf16[256,256]{1,0:T(8,128)(2,1)S(1)}, u32[]{:S(2)}, u32[]{:S(2)}) collective-permute-start(bf16[256,256]{1,0:T(8,128)(2,1)S(1)} %get-tuple-element.111.after_ref.mine_ref), channel_id=1, source_target_pairs={{0,8},{8,0},{16,24},{24,16},{32,40},{40,32},{48,56},{56,48},{64,72... | collective-permute-start | bytes 393224 | tf_op jit(solution)/shard_map/ppermute | solution.py:458
  42.5 2.1 %copy-start.1 = (bf16[4,1280,256]{2,1,0:T(8,128)(2,1)S(1)}, bf16[4,1280,256]{2,1,0:T(8,128)(2,1)}, u32[]{:S(2)}) copy-start(bf16[4,1280,256]{2,1,0:T(8,128)(2,1)} %cols_ref.1) | copy-start | bytes 7864324
  42.5 2.1 %copy-start.3 = (bf16[256,256]{1,0:T(8,128)(2,1)S(1)}, bf16[256,256]{1,0:T(8,128)(2,1)}, u32[]{:S(2)}) copy-start(bf16[256,256]{1,0:T(8,128)(2,1)} %inv_ref.1) | copy-start | bytes 393220
  44.6 5.9 %copy-start = (bf16[1280,1024]{1,0:T(8,128)(2,1)S(1)}, bf16[1280,1024]{1,0:T(8,128)(2,1)}, u32[]{:S(2)}) copy-start(bf16[1280,1024]{1,0:T(8,128)(2,1)} %orb_ref.9) | copy-start | bytes 7864324
  51.4 5.2 %collective-permute-start.5 = (bf16[16,4,8,128]{3,2,1,0:T(8,128)(2,1)S(1)}, bf16[16,4,8,128]{3,2,1,0:T(8,128)(2,1)S(1)}, u32[]{:S(2)}, u32[]{:S(2)}) collective-permute-start(bf16[16,4,8,128]{3,2,1,0:T(8,128)(2,1)S(1)} %get-tuple-element.115), channel_id=1, source_target_pairs={{0,7},{1,0},{2,1},{3,2},{4,3},{5,4},{6,5},{7,6},{8,15},{9,8},{10,9... | collective-permute-start | bytes 393224 | tf_op jit(solution)/shard_map/ppermute | solution.py:383
  51.4 6.6 %collective-permute-start.1 = (bf16[16,4,8,128]{3,2,1,0:T(8,128)(2,1)S(1)}, bf16[16,4,8,128]{3,2,1,0:T(8,128)(2,1)S(1)}, u32[]{:S(2)}, u32[]{:S(2)}) collective-permute-start(bf16[16,4,8,128]{3,2,1,0:T(8,128)(2,1)S(1)} %get-tuple-element.114), channel_id=1, source_target_pairs={{0,1},{1,2},{2,3},{3,4},{4,5},{5,6},{6,7},{7,0},{8,9},{9,10},{10,1... | collective-permute-start | bytes 393224 | tf_op jit(solution)/shard_map/ppermute | solution.py:383
  56.6 7.1 %collective-permute-start.6 = (bf16[32,4,8,128]{3,2,1,0:T(8,128)(2,1)S(1)}, bf16[32,4,8,128]{3,2,1,0:T(8,128)(2,1)S(1)}, u32[]{:S(2)}, u32[]{:S(2)}) collective-permute-start(bf16[32,4,8,128]{3,2,1,0:T(8,128)(2,1)S(1)} %join.3), channel_id=1, source_target_pairs={{0,7},{1,0},{2,1},{3,2},{4,3},{5,4},{6,5},{7,6},{8,15},{9,8},{10,9... | collective-permute-start | bytes 786440 | tf_op jit(solution)/shard_map/ppermute | solution.py:383
  58.1 8.2 %collective-permute-start.2 = (bf16[32,4,8,128]{3,2,1,0:T(8,128)(2,1)S(1)}, bf16[32,4,8,128]{3,2,1,0:T(8,128)(2,1)S(1)}, u32[]{:S(2)}, u32[]{:S(2)}) collective-permute-start(bf16[32,4,8,128]{3,2,1,0:T(8,128)(2,1)S(1)} %join.2), channel_id=1, source_target_pairs={{0,1},{1,2},{2,3},{3,4},{4,5},{5,6},{6,7},{7,0},{8,9},{9,10},{10,1... | collective-permute-start | bytes 786440 | tf_op jit(solution)/shard_map/ppermute | solution.py:383
  66.5 7.3 %collective-permute-start.3 = (bf16[32,4,8,128]{3,2,1,0:T(8,128)(2,1)S(1)}, bf16[32,4,8,128]{3,2,1,0:T(8,128)(2,1)S(1)}, u32[]{:S(2)}, u32[]{:S(2)}) collective-permute-start(bf16[32,4,8,128]{3,2,1,0:T(8,128)(2,1)S(1)} %get-tuple-element.132), channel_id=1, source_target_pairs={{0,1},{1,2},{2,3},{3,4},{4,5},{5,6},{6,7},{7,0},{8,9},{9,10},{10,1... | collective-permute-start | bytes 786440 | tf_op jit(solution)/shard_map/ppermute | solution.py:383
  66.6 7.2 %collective-permute-start.7 = (bf16[32,4,8,128]{3,2,1,0:T(8,128)(2,1)S(1)}, bf16[32,4,8,128]{3,2,1,0:T(8,128)(2,1)S(1)}, u32[]{:S(2)}, u32[]{:S(2)}) collective-permute-start(bf16[32,4,8,128]{3,2,1,0:T(8,128)(2,1)S(1)} %get-tuple-element.133), channel_id=1, source_target_pairs={{0,7},{1,0},{2,1},{3,2},{4,3},{5,4},{6,5},{7,6},{8,15},{9,8},{10,9... | collective-permute-start | bytes 786440 | tf_op jit(solution)/shard_map/ppermute | solution.py:383
  74.0 6.5 %collective-permute-start.4 = (bf16[32,4,8,128]{3,2,1,0:T(8,128)(2,1)S(1)}, bf16[32,4,8,128]{3,2,1,0:T(8,128)(2,1)S(1)}, u32[]{:S(2)}, u32[]{:S(2)}) collective-permute-start(bf16[32,4,8,128]{3,2,1,0:T(8,128)(2,1)S(1)} %get-tuple-element.130), channel_id=1, source_target_pairs={{0,1},{1,2},{2,3},{3,4},{4,5},{5,6},{6,7},{7,0},{8,9},{9,10},{10,1... | collective-permute-start | bytes 786440 | tf_op jit(solution)/shard_map/ppermute | solution.py:383
  74.1 6.4 %collective-permute-start.8 = (bf16[32,4,8,128]{3,2,1,0:T(8,128)(2,1)S(1)}, bf16[32,4,8,128]{3,2,1,0:T(8,128)(2,1)S(1)}, u32[]{:S(2)}, u32[]{:S(2)}) collective-permute-start(bf16[32,4,8,128]{3,2,1,0:T(8,128)(2,1)S(1)} %get-tuple-element.131), channel_id=1, source_target_pairs={{0,7},{1,0},{2,1},{3,2},{4,3},{5,4},{6,5},{7,6},{8,15},{9,8},{10,9... | collective-permute-start | bytes 786440 | tf_op jit(solution)/shard_map/ppermute | solution.py:383
  77.6 21.5 %copy-start.2 = (bf16[128,1024]{1,0:T(8,128)(2,1)S(1)}, bf16[128,1024]{1,0:T(8,128)(2,1)}, u32[]{:S(2)}) copy-start(bf16[128,1024]{1,0:T(8,128)(2,1)} %slab_ref.1) | copy-start | bytes 786436

commit v9 on v7

--- a/solution.py
+++ b/solution.py
@@ -190,46 +190,30 @@
     )(where_from, pivots.reshape(1, n), came)
 
 
-def preload_kernel(prev_ref, after_ref, out_ref, sem):
-    copy = pltpu.make_async_copy(prev_ref.at[0], out_ref, sem)
-    copy.start()
-    copy.wait()
-
-
-def preload(previous, after):
-    return pl.pallas_call(
-        preload_kernel,
-        out_shape=jax.ShapeDtypeStruct(previous.shape[1:], previous.dtype),
-        in_specs=[pl.BlockSpec(memory_space=pltpu.HBM), pl.BlockSpec(memory_space=pl.ANY)],
-        out_specs=pl.BlockSpec(memory_space=pltpu.VMEM),
-        scratch_shapes=[pltpu.SemaphoreType.DMA],
-        compiler_params=pltpu.CompilerParams(vmem_limit_bytes=4 << 20),
-        cost_estimate=pl.CostEstimate(
-            flops=0, bytes_accessed=previous.size // 2, transcendentals=0
-        ),
-        name="preload",
-    )(previous, after)
-
-
 def vectors_kernel(
-    core_ref, cols_ref, close_ref, prev_ref, mine_ref, other_ref, inv_ref, new_ref, turned_ref, came, made, load, store
+    core_ref, cols_ref, prev_ref, mine_ref, other_ref, inv_ref, new_ref, turned_ref, came, made, load, store
 ):
-    mu = cols_ref.shape[0]
+    mu = came.shape[0]
 
     def load_of(m):
-        return pltpu.make_async_copy(prev_ref.at[m], came.at[m - 1], load.at[m - 1])
+        return pltpu.make_async_copy(prev_ref.at[m], came.at[m], load.at[m])
 
     def store_of(m):
         return pltpu.make_async_copy(made.at[m], new_ref.at[m], store.at[m])
 
-    def step(m, prev):
+    for m in range(mu):
+        load_of(m).start()
+
+    @pl.loop(0, mu)
+    def _(m):
+        load_of(m).wait()
         mine, other = mine_ref[...].astype(F32), other_ref[...].astype(F32)
         first = core_ref[0] == 0
         rows = jnp.concatenate(
             [jnp.where(first, mine, other), jnp.where(first, other, mine)], axis=1
         ).astype(BF16)
         contract = (((1,), (1,)), ((), ()))
-        correction = lax.dot_general(prev, rows, contract, preferred_element_type=F32)
+        correction = lax.dot_general(came[m], rows, contract, preferred_element_type=F32)
         residual = (cols_ref[m].astype(F32) - correction).astype(BF16)
         inv = inv_ref[...]
         row, column = (lax.broadcasted_iota(jnp.int32, inv.shape, d) for d in (0, 1))
@@ -239,40 +223,33 @@
         store_of(m).start()
         turned_ref[m] = new.T
 
-    load_of(1).start()
-    step(0, close_ref[...])
-
-    @pl.loop(1, mu)
-    def _(m):
-        load_of(m).wait()
-
-        @pl.when(m + 1 < mu)
-        def _():
-            load_of(m + 1).start()
-
-        step(m, came[m - 1])
-
     for m in range(mu):
         store_of(m).wait()
 
 
-def vectors(core, pivot_columns, close, previous, mine, other, pivot_inverse):
+def vectors(core, pivot_columns, previous, mine, other, pivot_inverse):
     mu, nu, k = previous.shape
     n = pivot_columns.shape[2]
     vmem = pl.BlockSpec(memory_space=pltpu.VMEM)
-    hbm = pl.BlockSpec(memory_space=pltpu.HBM)
     return pl.pallas_call(
         vectors_kernel,
         out_shape=(
             jax.ShapeDtypeStruct((mu, nu, n), BF16),
             jax.ShapeDtypeStruct((mu, n, nu), BF16),
         ),
-        in_specs=[pl.BlockSpec(memory_space=pltpu.SMEM), vmem, vmem, hbm, vmem, vmem, vmem],
+        in_specs=[
+            pl.BlockSpec(memory_space=pltpu.SMEM),
+            vmem,
+            pl.BlockSpec(memory_space=pltpu.HBM),
+            vmem,
+            vmem,
+            vmem,
+        ],
         out_specs=(pl.BlockSpec(memory_space=pl.ANY), vmem),
         scratch_shapes=[
-            pltpu.VMEM((mu - 1, nu, k), BF16),
+            pltpu.VMEM((mu, nu, k), BF16),
             pltpu.VMEM((mu, nu, n), BF16),
-            pltpu.SemaphoreType.DMA((mu - 1,)),
+            pltpu.SemaphoreType.DMA((mu,)),
             pltpu.SemaphoreType.DMA((mu,)),
         ],
         compiler_params=pltpu.CompilerParams(vmem_limit_bytes=24 << 20),
@@ -282,7 +259,7 @@
             transcendentals=0,
         ),
         name="vectors",
-    )(core, pivot_columns, close, previous, mine, other, pivot_inverse)
+    )(core, pivot_columns, previous, mine, other, pivot_inverse)
 
 
 def parts_kernel(me_ref, turned_ref, orb_ref, *out_refs, ahead, owners):
@@ -358,6 +335,30 @@
     )(part, came)
 
 
+def add_kernel(own_ref, came_ref, out_ref):
+    out_ref[...] = (own_ref[0] + came_ref[...].astype(F32)).astype(BF16)
+
+
+def add(part, which, came):
+    shape = came.shape
+    zeros = lambda i: (0, 0, 0, 0)
+    return pl.pallas_call(
+        add_kernel,
+        grid=(1,),
+        out_shape=jax.ShapeDtypeStruct(shape, BF16),
+        in_specs=[
+            pl.BlockSpec((1,) + shape, lambda i: (which, 0, 0, 0, 0)),
+            pl.BlockSpec(shape, zeros),
+        ],
+        out_specs=pl.BlockSpec(shape, zeros),
+        compiler_params=pltpu.CompilerParams(vmem_limit_bytes=6 << 20),
+        cost_estimate=pl.CostEstimate(
+            flops=came.size, bytes_accessed=8 * came.size, transcendentals=0
+        ),
+        name="add",
+    )(part, came)
+
+
 def reduce_to_owner(me, turned, orbitals, owners, dests):
     far = owners // 2
 
@@ -374,7 +375,7 @@
     for ahead in range(far - 2, 0, -1):
         near = own((ahead, owners - ahead))
         right, left = (
-            hop((near[q] + x.astype(F32)).astype(BF16), way)
+            hop(add(near, q, x), way)
             for q, (x, way) in enumerate(((right, 1), (left, -1)))
         )
     return own((0,))[0] + right.astype(F32) + left.astype(F32)
@@ -449,10 +450,7 @@
     mine, other = pivot_halves(n_rows, n_grp, pivots, in_hbm)
     core = (lax.axis_index("rows") % 2).reshape(1).astype(jnp.int32)
     me = lax.axis_index("grp").reshape(1).astype(jnp.int32)
-    close = preload(in_hbm, mine)
-    new_vectors, turned = vectors(
-        core, pivot_columns, close, in_hbm, mine, other, pivot_inverse
-    )
+    new_vectors, turned = vectors(core, pivot_columns, in_hbm, mine, other, pivot_inverse)
     half = exchange(reduce_to_owner(me, turned, orbitals, n_grp, n_rows), "rows")
     return new_vectors, final(half.reshape(-1, half.shape[-1]), slab_orbitals)
 

time: 100 us -> 98.9 us (0.989)
  blocking collectives: 57.3 us -> 54.2 us
  starting transfers between devices: 8.83 us -> 11.5 us
    all_to_all x3, blocking collectives: 57.3 us -> 54.2 us  [exchange(): return lax.all_to_all(x, axis, split_axis=0, concat_axis=0, tiled=True)]
    ppermute x8, starting transfers between devices: 8.74 us -> 11.4 us  [hop(): lax.ppermute(x, 'grp', [(i, (i + way) % owners) for i in range(owners)])]
    ppermute x1, waiting for transfers between devices: 0.01 us -> 1.32 us  [pivot_halves(): other = lax.ppermute(mine, 'rows', [(i, i ^ 1) for i in range(n_rows)])]
    pallas_call x1 -> x4, Pallas kernels: 1.48 us -> 0.19 us  [add(): pl.pallas_call(add_kernel, grid=(1,), out_shape=jax.ShapeDtypeStruct(shap...]
    ppermute x8, waiting for transfers between devices: 14.4 us -> 13.2 us  [hop(): lax.ppermute(x, 'grp', [(i, (i + way) % owners) for i in range(owners)])]
    pallas_call x1, Pallas kernels: 0.98 us -> 2.13 us  [pick_rows(): pl.pallas_call(pick_kernel, out_shape=jax.ShapeDtypeStruct((DEPTH, k), BF...]
  transfers between devices with their start and end apart: 9 -> 9, of which waited for: 5 -> 5; matrix products, arithmetic and copies ran while one was open for 0% -> 0% of each run, Pallas kernels for 5% -> 4%
where the time goes in v9:
time: 98.9 us; the launch traced here: 98.7 us
  blocking collectives  54.2 us (55%)
  Pallas kernels  16.6 us (17%)
  waiting for transfers between devices  14.6 us (15%)
  starting transfers between devices  11.5 us (12%)
    all_to_all x3, blocking collectives, exchange(): return lax.all_to_all(x, axis, split_axis=0, concat_axis=0, tiled=True)  54.2 us
    ppermute x8, waiting for transfers between devices, hop(): lax.ppermute(x, 'grp', [(i, (i + way) % owners) for i in range(owners)])  13.2 us
    ppermute x8, starting transfers between devices, hop(): lax.ppermute(x, 'grp', [(i, (i + way) % owners) for i in range(owners)])  11.4 us
    pallas_call x1, Pallas kernels, vectors(): pl.pallas_call(vectors_kernel, out_shape=(jax.ShapeDtypeStruct((mu, nu, n...  5.85 us
    pallas_call x5, Pallas kernels, parts(): pl.pallas_call(functools.partial(parts_kernel, ahead=ahead, owners=owners...  4.29 us
    pallas_call x1, Pallas kernels, pick_rows(): pl.pallas_call(pick_kernel, out_shape=jax.ShapeDtypeStruct((DEPTH, k), BF...  2.13 us
    pallas_call x1, Pallas kernels, final(): pl.pallas_call(final_kernel, out_shape=jax.ShapeDtypeStruct((keep, occ, w...  2.07 us
  transfers between devices with their start and end apart: 9, of which 5 were waited for; matrix products, arithmetic and copies ran while one was open for 0% of the time, Pallas kernels for 4%

profile of v9, /device:TPU:1, one launch (start us, length us, event | category | flops | bytes accessed | tf_op | source)
XLA Modules:
  0.0 98.7 jit_solution(15195560513089870156)
XLA Ops:
  0.7 2.1 %pick_rows.5 = bf16[8,512]{1,0:T(8,128)(2,1)S(1)} custom-call(s32[4]{0:T(128)S(1)} %pad_add_fusion.1.where_from_ref, s32[2,128]{1,0:T(2,128)} %bitcast.40, bf16[4,1280,512]{2,1,0:T(8,128)(2,1)} %prev_ref.3), custom_call_target="tpu_custom_call" | custom-call | flops 131072 | bytes 262144 | tf_op jit(solution)/shard_map/pick_rows/pallas_call | solution.py:72
  2.9 15.8 %all_to_all.30.came_ref = bf16[8,8,512]{2,1,0:T(8,128)(2,1)S(1)} all-to-all(bf16[8,8,512]{2,1,0:T(8,128)(2,1)S(1)} %broadcast_in_dim.12), channel_id=1, replica_groups=mesh['rows'=32,'grp'=8] {'grp'}, dimensions={0} | all-to-all | bytes 131072 | tf_op jit(solution)/shard_map/all_to_all | solution.py:419
  18.7 0.9 spread.5
  19.6 19.7 %all_to_all.31 = bf16[32,24,256]{2,1,0:T(8,128)(2,1)S(1)} all-to-all(bf16[32,24,256]{2,1,0:T(8,128)(2,1)S(1)} %spread.5), channel_id=1, replica_groups=mesh['rows'=32,'grp'=8] {'rows'}, dimensions={0} | all-to-all | bytes 786432 | tf_op jit(solution)/shard_map/all_to_all | solution.py:419
  39.4 1.1 %select_rows.5 = (bf16[256,256]{1,0:T(8,128)(2,1)S(1)}, s32[1]{0:T(128)}) custom-call(s32[1]{0:T(128)} %constant.87.clone.1.round_ref, s32[1,256]{1,0:T(1,128)S(1)} %bitcast.42, bf16[768,256]{1,0:T(8,128)(2,1)S(1)} %bitcast.39, bf16[256,256]{1,0:T(8,128)(2,1)S(1)} %broadcast_in_dim.13.so_far_ref), custom_call_target="tpu_custom_call" | custom-call | flops 100663296 | bytes 393216 | tf_op jit(solution)/shard_map/select_rows/pallas_call | solution.py:128
  40.5 0.8 while.12
  41.3 1.3 %collective-permute-done.other_ref = bf16[256,256]{1,0:T(8,128)(2,1)S(1)} collective-permute-done((bf16[256,256]{1,0:T(8,128)(2,1)S(1)}, bf16[256,256]{1,0:T(8,128)(2,1)S(1)}, u32[]{:S(2)}, u32[]{:S(2)}) %collective-permute-start) | collective-permute-done | bytes 131104 | tf_op jit(solution)/shard_map/ppermute | solution.py:444
  42.7 5.8 %vectors.1 = (bf16[4,1280,256]{2,1,0:T(8,128)(2,1)}, bf16[4,256,1280]{2,1,0:T(8,128)(2,1)S(1)}) custom-call(s32[1]{0:T(128)} %bitcast.8.core_ref, bf16[4,1280,256]{2,1,0:T(8,128)(2,1)S(1)} %copy-done.1, bf16[4,1280,512]{2,1,0:T(8,128)(2,1)} %get-tuple-element.225, bf16[256,256]{1,0:T(8,128)(2,1)S(1)} %get-tuple-element.111.mine_ref, ...), custom_call_target="tpu_custom_call" | custom-call | flops 2013265920 | bytes 13107200 | tf_op jit(solution)/shard_map/vectors/pallas_call | solution.py:234
  48.5 0.9 parts.9
  49.4 0.4 collective-permute-start.1
  49.8 2.4 %collective-permute-start.5 = (bf16[16,4,8,128]{3,2,1,0:T(8,128)(2,1)S(1)}, bf16[16,4,8,128]{3,2,1,0:T(8,128)(2,1)S(1)}, u32[]{:S(2)}, u32[]{:S(2)}) collective-permute-start(bf16[16,4,8,128]{3,2,1,0:T(8,128)(2,1)S(1)} %get-tuple-element.115), channel_id=1, source_target_pairs={{0,7},{1,0},{2,1},{3,2},{4,3},{5,4},{6,5},{7,6},{8,15},{9,8},{10,9... | collective-permute-start | bytes 393224 | tf_op jit(solution)/shard_map/ppermute | solution.py:366
  52.2 0.9 parts.8.own_ref
  53.0 2.6 %collective-permute-done.1.came_ref = bf16[16,4,8,128]{3,2,1,0:T(8,128)(2,1)S(1)} collective-permute-done((bf16[16,4,8,128]{3,2,1,0:T(8,128)(2,1)S(1)}, bf16[16,4,8,128]{3,2,1,0:T(8,128)(2,1)S(1)}, u32[]{:S(2)}, u32[]{:S(2)}) %collective-permute-start.1) | collective-permute-done | bytes 131104 | tf_op jit(solution)/shard_map/ppermute | solution.py:366
  55.8 2.7 %collective-permute-start.6 = (bf16[32,4,8,128]{3,2,1,0:T(8,128)(2,1)S(1)}, bf16[32,4,8,128]{3,2,1,0:T(8,128)(2,1)S(1)}, u32[]{:S(2)}, u32[]{:S(2)}) collective-permute-start(bf16[32,4,8,128]{3,2,1,0:T(8,128)(2,1)S(1)} %join.3), channel_id=1, source_target_pairs={{0,7},{1,0},{2,1},{3,2},{4,3},{5,4},{6,5},{7,6},{8,15},{9,8},{10,9... | collective-permute-start | bytes 786440 | tf_op jit(solution)/shard_map/ppermute | solution.py:366
  58.6 0.9 parts.7.own_ref
  59.4 4.4 %collective-permute-done.2.came_ref = bf16[32,4,8,128]{3,2,1,0:T(8,128)(2,1)S(1)} collective-permute-done((bf16[32,4,8,128]{3,2,1,0:T(8,128)(2,1)S(1)}, bf16[32,4,8,128]{3,2,1,0:T(8,128)(2,1)S(1)}, u32[]{:S(2)}, u32[]{:S(2)}) %collective-permute-start.2) | collective-permute-done | bytes 262176 | tf_op jit(solution)/shard_map/ppermute | solution.py:366
  64.0 2.7 %collective-permute-start.7 = (bf16[32,4,8,128]{3,2,1,0:T(8,128)(2,1)S(1)}, bf16[32,4,8,128]{3,2,1,0:T(8,128)(2,1)S(1)}, u32[]{:S(2)}, u32[]{:S(2)}) collective-permute-start(bf16[32,4,8,128]{3,2,1,0:T(8,128)(2,1)S(1)} %add.68), channel_id=1, source_target_pairs={{0,7},{1,0},{2,1},{3,2},{4,3},{5,4},{6,5},{7,6},{8,15},{9,8},{10,9... | collective-permute-start | bytes 786440 | tf_op jit(solution)/shard_map/ppermute | solution.py:366
  66.8 0.9 parts.6.own_ref
  67.6 3.5 %collective-permute-done.3.came_ref = bf16[32,4,8,128]{3,2,1,0:T(8,128)(2,1)S(1)} collective-permute-done((bf16[32,4,8,128]{3,2,1,0:T(8,128)(2,1)S(1)}, bf16[32,4,8,128]{3,2,1,0:T(8,128)(2,1)S(1)}, u32[]{:S(2)}, u32[]{:S(2)}) %collective-permute-start.3) | collective-permute-done | bytes 262176 | tf_op jit(solution)/shard_map/ppermute | solution.py:366
  71.5 2.7 %collective-permute-start.8 = (bf16[32,4,8,128]{3,2,1,0:T(8,128)(2,1)S(1)}, bf16[32,4,8,128]{3,2,1,0:T(8,128)(2,1)S(1)}, u32[]{:S(2)}, u32[]{:S(2)}) collective-permute-start(bf16[32,4,8,128]{3,2,1,0:T(8,128)(2,1)S(1)} %add.69), channel_id=1, source_target_pairs={{0,7},{1,0},{2,1},{3,2},{4,3},{5,4},{6,5},{7,6},{8,15},{9,8},{10,9... | collective-permute-start | bytes 786440 | tf_op jit(solution)/shard_map/ppermute | solution.py:366
  74.2 0.8 parts.5
  75.1 2.8 %collective-permute-done.4 = bf16[32,4,8,128]{3,2,1,0:T(8,128)(2,1)S(1)} collective-permute-done((bf16[32,4,8,128]{3,2,1,0:T(8,128)(2,1)S(1)}, bf16[32,4,8,128]{3,2,1,0:T(8,128)(2,1)S(1)}, u32[]{:S(2)}, u32[]{:S(2)}) %collective-permute-start.4) | collective-permute-done | bytes 262176 | tf_op jit(solution)/shard_map/ppermute | solution.py:366
  77.9 18.7 %all_to_all.32 = f32[32,4,8,128]{3,2,1,0:T(8,128)S(1)} all-to-all(f32[32,4,8,128]{3,2,1,0:T(8,128)S(1)} %fusion), channel_id=1, replica_groups=mesh['rows'=32,'grp'=8] {'rows'}, dimensions={0} | all-to-all | bytes 1048576 | tf_op jit(solution)/shard_map/all_to_all | solution.py:419
  96.6 2.1 %final.1 = bf16[8,1024,128]{2,1,0:T(8,128)(2,1)} custom-call(f32[1024,128]{1,0:T(8,128)S(1)} %bitcast.38, bf16[128,1024]{1,0:T(8,128)(2,1)S(1)} %copy-done.2), custom_call_target="tpu_custom_call" | custom-call | flops 536870912 | bytes 2621440 | tf_op jit(solution)/shard_map/final/pallas_call | solution.py:405
  (28 shorter events, 1.0 us)
Async XLA Ops:
  0.7 18.0 %copy-start.4 = (s32[256]{0:T(256)S(1)}, s32[256]{0:T(256)}, u32[]{:S(2)}) copy-start(s32[256]{0:T(256)} %param.10) | copy-start | bytes 3076
  40.4 2.2 %copy-start.1 = (bf16[4,1280,256]{2,1,0:T(8,128)(2,1)S(1)}, bf16[4,1280,256]{2,1,0:T(8,128)(2,1)}, u32[]{:S(2)}) copy-start(bf16[4,1280,256]{2,1,0:T(8,128)(2,1)} %cols_ref.1) | copy-start | bytes 7864324
  40.4 2.2 %copy-start.3 = (bf16[256,256]{1,0:T(8,128)(2,1)S(1)}, bf16[256,256]{1,0:T(8,128)(2,1)}, u32[]{:S(2)}) copy-start(bf16[256,256]{1,0:T(8,128)(2,1)} %inv_ref.1) | copy-start | bytes 393220
  41.2 1.4 %collective-permute-start = (bf16[256,256]{1,0:T(8,128)(2,1)S(1)}, bf16[256,256]{1,0:T(8,128)(2,1)S(1)}, u32[]{:S(2)}, u32[]{:S(2)}) collective-permute-start(bf16[256,256]{1,0:T(8,128)(2,1)S(1)} %get-tuple-element.111.mine_ref), channel_id=1, source_target_pairs={{0,8},{8,0},{16,24},{24,16},{32,40},{40,32},{48,56},{56,48},{64,72... | collective-permute-start | bytes 393224 | tf_op jit(solution)/shard_map/ppermute | solution.py:444
  42.7 5.9 %copy-start = (bf16[1280,1024]{1,0:T(8,128)(2,1)S(1)}, bf16[1280,1024]{1,0:T(8,128)(2,1)}, u32[]{:S(2)}) copy-start(bf16[1280,1024]{1,0:T(8,128)(2,1)} %orb_ref.9) | copy-start | bytes 7864324
  49.4 6.2 %collective-permute-start.1 = (bf16[16,4,8,128]{3,2,1,0:T(8,128)(2,1)S(1)}, bf16[16,4,8,128]{3,2,1,0:T(8,128)(2,1)S(1)}, u32[]{:S(2)}, u32[]{:S(2)}) collective-permute-start(bf16[16,4,8,128]{3,2,1,0:T(8,128)(2,1)S(1)} %get-tuple-element.114), channel_id=1, source_target_pairs={{0,1},{1,2},{2,3},{3,4},{4,5},{5,6},{6,7},{7,0},{8,9},{9,10},{10,1... | collective-permute-start | bytes 393224 | tf_op jit(solution)/shard_map/ppermute | solution.py:366
  49.8 6.0 %collective-permute-start.5 = (bf16[16,4,8,128]{3,2,1,0:T(8,128)(2,1)S(1)}, bf16[16,4,8,128]{3,2,1,0:T(8,128)(2,1)S(1)}, u32[]{:S(2)}, u32[]{:S(2)}) collective-permute-start(bf16[16,4,8,128]{3,2,1,0:T(8,128)(2,1)S(1)} %get-tuple-element.115), channel_id=1, source_target_pairs={{0,7},{1,0},{2,1},{3,2},{4,3},{5,4},{6,5},{7,6},{8,15},{9,8},{10,9... | collective-permute-start | bytes 393224 | tf_op jit(solution)/shard_map/ppermute | solution.py:366
  55.7 8.1 %collective-permute-start.2 = (bf16[32,4,8,128]{3,2,1,0:T(8,128)(2,1)S(1)}, bf16[32,4,8,128]{3,2,1,0:T(8,128)(2,1)S(1)}, u32[]{:S(2)}, u32[]{:S(2)}) collective-permute-start(bf16[32,4,8,128]{3,2,1,0:T(8,128)(2,1)S(1)} %join.2), channel_id=1, source_target_pairs={{0,1},{1,2},{2,3},{3,4},{4,5},{5,6},{6,7},{7,0},{8,9},{9,10},{10,1... | collective-permute-start | bytes 786440 | tf_op jit(solution)/shard_map/ppermute | solution.py:366
  55.8 8.1 %collective-permute-start.6 = (bf16[32,4,8,128]{3,2,1,0:T(8,128)(2,1)S(1)}, bf16[32,4,8,128]{3,2,1,0:T(8,128)(2,1)S(1)}, u32[]{:S(2)}, u32[]{:S(2)}) collective-permute-start(bf16[32,4,8,128]{3,2,1,0:T(8,128)(2,1)S(1)} %join.3), channel_id=1, source_target_pairs={{0,7},{1,0},{2,1},{3,2},{4,3},{5,4},{6,5},{7,6},{8,15},{9,8},{10,9... | collective-permute-start | bytes 786440 | tf_op jit(solution)/shard_map/ppermute | solution.py:366
  63.9 7.2 %collective-permute-start.3 = (bf16[32,4,8,128]{3,2,1,0:T(8,128)(2,1)S(1)}, bf16[32,4,8,128]{3,2,1,0:T(8,128)(2,1)S(1)}, u32[]{:S(2)}, u32[]{:S(2)}) collective-permute-start(bf16[32,4,8,128]{3,2,1,0:T(8,128)(2,1)S(1)} %add.66), channel_id=1, source_target_pairs={{0,1},{1,2},{2,3},{3,4},{4,5},{5,6},{6,7},{7,0},{8,9},{9,10},{10,1... | collective-permute-start | bytes 786440 | tf_op jit(solution)/shard_map/ppermute | solution.py:366
  64.0 7.4 %collective-permute-start.7 = (bf16[32,4,8,128]{3,2,1,0:T(8,128)(2,1)S(1)}, bf16[32,4,8,128]{3,2,1,0:T(8,128)(2,1)S(1)}, u32[]{:S(2)}, u32[]{:S(2)}) collective-permute-start(bf16[32,4,8,128]{3,2,1,0:T(8,128)(2,1)S(1)} %add.68), channel_id=1, source_target_pairs={{0,7},{1,0},{2,1},{3,2},{4,3},{5,4},{6,5},{7,6},{8,15},{9,8},{10,9... | collective-permute-start | bytes 786440 | tf_op jit(solution)/shard_map/ppermute | solution.py:366
  71.1 6.7 %collective-permute-start.4 = (bf16[32,4,8,128]{3,2,1,0:T(8,128)(2,1)S(1)}, bf16[32,4,8,128]{3,2,1,0:T(8,128)(2,1)S(1)}, u32[]{:S(2)}, u32[]{:S(2)}) collective-permute-start(bf16[32,4,8,128]{3,2,1,0:T(8,128)(2,1)S(1)} %add.67), channel_id=1, source_target_pairs={{0,1},{1,2},{2,3},{3,4},{4,5},{5,6},{6,7},{7,0},{8,9},{9,10},{10,1... | collective-permute-start | bytes 786440 | tf_op jit(solution)/shard_map/ppermute | solution.py:366
  71.5 6.4 %collective-permute-start.8 = (bf16[32,4,8,128]{3,2,1,0:T(8,128)(2,1)S(1)}, bf16[32,4,8,128]{3,2,1,0:T(8,128)(2,1)S(1)}, u32[]{:S(2)}, u32[]{:S(2)}) collective-permute-start(bf16[32,4,8,128]{3,2,1,0:T(8,128)(2,1)S(1)} %add.69), channel_id=1, source_target_pairs={{0,7},{1,0},{2,1},{3,2},{4,3},{5,4},{6,5},{7,6},{8,15},{9,8},{10,9... | collective-permute-start | bytes 786440 | tf_op jit(solution)/shard_map/ppermute | solution.py:366
  75.1 21.6 %copy-start.2 = (bf16[128,1024]{1,0:T(8,128)(2,1)S(1)}, bf16[128,1024]{1,0:T(8,128)(2,1)}, u32[]{:S(2)}) copy-start(bf16[128,1024]{1,0:T(8,128)(2,1)} %slab_ref.1) | copy-start | bytes 786436

commit v10 on v9

--- a/solution.py
+++ b/solution.py
@@ -15,7 +15,18 @@
 PARTS = 3
 
 
-def pick_kernel(where_from_ref, piv_ref, prev_ref, out_ref, acc_ref, held, sems, rows_ref):
+def pick_kernel(where_from_ref, piv_ref, prev_ref, *refs, bring):
+    if bring:
+        cols_ref, out_ref, close_ref, acc_ref, held, sems, rows_ref, close_sems = refs
+        copies = [
+            pltpu.make_async_copy(cols_ref.at[m], close_ref.at[m], close_sems.at[m])
+            for m in range(cols_ref.shape[0])
+        ]
+    else:
+        out_ref, acc_ref, held, sems, rows_ref = refs
+        copies = []
+    for copy in copies:
+        copy.start()
     mu, nu, _ = prev_ref.shape
     depth, group, _ = held.shape
     base, turn = where_from_ref[1], where_from_ref[2]
@@ -63,31 +74,39 @@
 
     lax.fori_loop(0, total, place, 0)
     out_ref[...] = acc_ref[...].astype(BF16)
-
-
-def pick_rows(where_from, pivots, previous):
+    for copy in copies:
+        copy.wait()
+
+
+def pick_rows(where_from, pivots, previous, columns=None):
     n = pivots.shape[0]
     k = previous.shape[2]
     lanes = 128
-    return pl.pallas_call(
-        pick_kernel,
-        out_shape=jax.ShapeDtypeStruct((DEPTH, k), BF16),
-        in_specs=[
-            pl.BlockSpec(memory_space=pltpu.SMEM),
-            pl.BlockSpec(memory_space=pltpu.VMEM),
-            pl.BlockSpec(memory_space=pltpu.HBM),
-        ],
-        out_specs=pl.BlockSpec(memory_space=pltpu.VMEM),
-        scratch_shapes=[
-            pltpu.VMEM((DEPTH, k), F32),
-            pltpu.VMEM((DEPTH, 16, k), BF16),
-            pltpu.SemaphoreType.DMA((DEPTH,)),
-            pltpu.SMEM((DEPTH,), jnp.int32),
-        ],
+    vmem = pl.BlockSpec(memory_space=pltpu.VMEM)
+    hbm = pl.BlockSpec(memory_space=pltpu.HBM)
+    args = [where_from, pivots.reshape(n // lanes, lanes), previous]
+    out_shape = [jax.ShapeDtypeStruct((DEPTH, k), BF16)]
+    scratch = [
+        pltpu.VMEM((DEPTH, k), F32),
+        pltpu.VMEM((DEPTH, 16, k), BF16),
+        pltpu.SemaphoreType.DMA((DEPTH,)),
+        pltpu.SMEM((DEPTH,), jnp.int32),
+    ]
+    bring = columns is not None
+    if bring:
+        args.append(columns)
+        out_shape.append(jax.ShapeDtypeStruct(columns.shape, columns.dtype))
+        scratch.append(pltpu.SemaphoreType.DMA((columns.shape[0],)))
+    return pl.pallas_call(
+        functools.partial(pick_kernel, bring=bring),
+        out_shape=out_shape,
+        in_specs=[pl.BlockSpec(memory_space=pltpu.SMEM), vmem, hbm] + [hbm] * bring,
+        out_specs=[vmem] * len(out_shape),
+        scratch_shapes=scratch,
         compiler_params=pltpu.CompilerParams(vmem_limit_bytes=4 << 20),
         cost_estimate=pl.CostEstimate(flops=n * k, bytes_accessed=2 * n * k, transcendentals=0),
         name="pick_rows",
-    )(where_from, pivots.reshape(n // lanes, lanes), previous)
+    )(*args)
 
 
 def whole_part(x, by):
@@ -191,9 +210,13 @@
 
 
 def vectors_kernel(
-    core_ref, cols_ref, prev_ref, mine_ref, other_ref, inv_ref, new_ref, turned_ref, came, made, load, store
+    core_ref, me_ref, cols_ref, prev_ref, mine_ref, other_ref, inv_ref, orb_ref,
+    new_ref, turned_ref, far_ref, came, made, load, store, far_sem, *, owners
 ):
     mu = came.shape[0]
+    width = far_ref.shape[1]
+    column = pl.multiple_of(lax.rem(me_ref[0] + owners // 2, owners) * width, width)
+    far = pltpu.make_async_copy(orb_ref.at[:, pl.ds(column, width)], far_ref, far_sem)
 
     def load_of(m):
         return pltpu.make_async_copy(prev_ref.at[m], came.at[m], load.at[m])
@@ -203,6 +226,7 @@
 
     for m in range(mu):
         load_of(m).start()
+    far.start()
 
     @pl.loop(0, mu)
     def _(m):
@@ -223,34 +247,33 @@
         store_of(m).start()
         turned_ref[m] = new.T
 
+    far.wait()
     for m in range(mu):
         store_of(m).wait()
 
 
-def vectors(core, pivot_columns, previous, mine, other, pivot_inverse):
+def vectors(core, me, pivot_columns, previous, mine, other, pivot_inverse, orbitals, owners):
     mu, nu, k = previous.shape
     n = pivot_columns.shape[2]
+    width = orbitals.shape[1] // owners
+    smem = pl.BlockSpec(memory_space=pltpu.SMEM)
     vmem = pl.BlockSpec(memory_space=pltpu.VMEM)
-    return pl.pallas_call(
-        vectors_kernel,
+    hbm = pl.BlockSpec(memory_space=pltpu.HBM)
+    return pl.pallas_call(
+        functools.partial(vectors_kernel, owners=owners),
         out_shape=(
             jax.ShapeDtypeStruct((mu, nu, n), BF16),
             jax.ShapeDtypeStruct((mu, n, nu), BF16),
-        ),
-        in_specs=[
-            pl.BlockSpec(memory_space=pltpu.SMEM),
-            vmem,
-            pl.BlockSpec(memory_space=pltpu.HBM),
-            vmem,
-            vmem,
-            vmem,
-        ],
-        out_specs=(pl.BlockSpec(memory_space=pl.ANY), vmem),
+            jax.ShapeDtypeStruct((nu, width), BF16),
+        ),
+        in_specs=[smem, smem, vmem, hbm, vmem, vmem, vmem, hbm],
+        out_specs=(pl.BlockSpec(memory_space=pl.ANY), vmem, vmem),
         scratch_shapes=[
             pltpu.VMEM((mu, nu, k), BF16),
             pltpu.VMEM((mu, nu, n), BF16),
             pltpu.SemaphoreType.DMA((mu,)),
             pltpu.SemaphoreType.DMA((mu,)),
+            pltpu.SemaphoreType.DMA,
         ],
         compiler_params=pltpu.CompilerParams(vmem_limit_bytes=24 << 20),
         cost_estimate=pl.CostEstimate(
@@ -259,15 +282,44 @@
             transcendentals=0,
         ),
         name="vectors",
-    )(core, pivot_columns, previous, mine, other, pivot_inverse)
+    )(core, me, pivot_columns, previous, mine, other, pivot_inverse, orbitals)
+
+
+def bring_kernel(orb_ref, after_ref, out_ref, sems):
+    count = sems.shape[0]
+    rows = out_ref.shape[0] // count
+    copies = [
+        pltpu.make_async_copy(
+            orb_ref.at[pl.ds(i * rows, rows)], out_ref.at[pl.ds(i * rows, rows)], sems.at[i]
+        )
+        for i in range(count)
+    ]
+    for copy in copies:
+        copy.start()
+    for copy in copies:
+        copy.wait()
+
+
+def bring(orbitals, after):
+    return pl.pallas_call(
+        bring_kernel,
+        out_shape=jax.ShapeDtypeStruct(orbitals.shape, orbitals.dtype),
+        in_specs=[pl.BlockSpec(memory_space=pltpu.HBM), pl.BlockSpec(memory_space=pl.ANY)],
+        out_specs=pl.BlockSpec(memory_space=pltpu.VMEM),
+        scratch_shapes=[pltpu.SemaphoreType.DMA((4,))],
+        compiler_params=pltpu.CompilerParams(vmem_limit_bytes=4 << 20),
+        cost_estimate=pl.CostEstimate(
+            flops=0, bytes_accessed=2 * orbitals.size, transcendentals=0
+        ),
+        name="bring",
+    )(orbitals, after)
 
 
 def parts_kernel(me_ref, turned_ref, orb_ref, *out_refs, ahead, owners):
     mu, n, nu = turned_ref.shape
-    width = orb_ref.shape[1] // owners
-    keep, last = out_refs[0].shape[-2:]
-    columns = []
-    for a in ahead:
+    keep, width = out_refs[0].shape[-2:]
+    columns = [orb_ref[...]] if len(out_refs) == 2 else []
+    for a in ahead[: 0 if columns else None]:
         start = pl.multiple_of(lax.rem(me_ref[0] + a, owners) * width, width)
         columns.append(orb_ref[:, pl.ds(start, width)])
     columns = columns[0] if len(columns) == 1 else jnp.concatenate(columns, axis=1)
@@ -276,7 +328,7 @@
         if len(out_refs) == 2:
             half = n // 2
             for h, out_ref in enumerate(out_refs):
-                piece = part[h * half : (h + 1) * half].reshape(half // keep, keep, last)
+                piece = part[h * half : (h + 1) * half].reshape(half // keep, keep, width)
                 out_ref[:, m] = piece.astype(out_ref.dtype)
         else:
             for q in range(len(ahead)):
@@ -286,7 +338,7 @@
 
 def parts(me, turned, orbitals, ahead, owners, dests, send=False):
     mu, n, nu = turned.shape
-    width = orbitals.shape[1] // owners
+    width = orbitals.shape[1] // (1 if send else owners)
     if send:
         shape = (dests // 2, mu, n // dests, width)
         out_shape = (jax.ShapeDtypeStruct(shape, BF16),) * 2
@@ -359,17 +411,19 @@
     )(part, came)
 
 
-def reduce_to_owner(me, turned, orbitals, owners, dests):
+def reduce_to_owner(me, turned, columns, orbitals, owners, dests):
     far = owners // 2
 
     def hop(x, way):
         return lax.ppermute(x, "grp", [(i, (i + way) % owners) for i in range(owners)])
 
-    def own(ahead, **more):
-        return parts(me, turned, orbitals, ahead, owners, dests, **more)
-
-    right, left = own((far,), send=True)
+    right, left = parts(me, turned, columns, (far,), owners, dests, send=True)
+    orbitals = bring(orbitals, right)
     right, left = hop(right, 1), hop(left, -1)
+
+    def own(ahead):
+        return parts(me, turned, orbitals, ahead, owners, dests)
+
     near = own((far - 1, far + 1))
     right, left = hop(join(near, 0, right, False), 1), hop(join(near, 1, left, True), -1)
     for ahead in range(far - 2, 0, -1):
@@ -419,7 +473,7 @@
     return lax.all_to_all(x, axis, split_axis=0, concat_axis=0, tiled=True)
 
 
-def pivot_halves(n_rows, n_grp, pivots, previous):
+def pivot_halves(n_rows, n_grp, pivots, previous, columns):
     mu, nu, k = previous.shape
     n = pivots.shape[0]
     half = k // 2
@@ -428,30 +482,35 @@
     base = line + lax.axis_index("grp") * nu
     line, base = line.astype(jnp.int32), base.astype(jnp.int32)
 
-    def one_round(index, so_far):
+    def one_round(index, so_far, columns=None):
         index = jnp.asarray(index, jnp.int32)
         turn, part = index // PARTS, index % PARTS
         where_from = jnp.stack([line, base, turn, part])
-        picked = pick_rows(where_from, pivots, previous)
+        picked, *close = pick_rows(where_from, pivots, previous, columns)
         came = exchange(jnp.broadcast_to(picked, (n_grp,) + picked.shape), "grp")
         messages = spread(where_from, pivots, came, n_rows, mu, nu)
         slots = exchange(messages, "rows").reshape(n_rows * SLOTS, half)
-        return select_rows(index.reshape(1), pivots, slots, so_far, per_line, nu, n_grp)
-
-    mine, rounds = one_round(0, jnp.zeros((n, half), BF16))
+        rows, rounds = select_rows(index.reshape(1), pivots, slots, so_far, per_line, nu, n_grp)
+        return rows, rounds, *close
+
+    mine, rounds, close = one_round(0, jnp.zeros((n, half), BF16), columns)
     start, mine, rounds = lax.optimization_barrier((jnp.int32(1), mine, rounds))
     mine = lax.fori_loop(start, rounds[0], lambda i, rows: one_round(i, rows)[0], mine)
     other = lax.ppermute(mine, "rows", [(i, i ^ 1) for i in range(n_rows)])
-    return mine, other
+    return mine, other, close
 
 
 def per_device(n_rows, n_grp, pivot_columns, previous, pivots, pivot_inverse, orbitals, slab_orbitals):
-    in_hbm = pltpu.with_memory_space_constraint(previous, pltpu.HBM)
-    mine, other = pivot_halves(n_rows, n_grp, pivots, in_hbm)
+    previous, pivot_columns, orbitals = (
+        pltpu.with_memory_space_constraint(x, pltpu.HBM) for x in (previous, pivot_columns, orbitals)
+    )
+    mine, other, close = pivot_halves(n_rows, n_grp, pivots, previous, pivot_columns)
     core = (lax.axis_index("rows") % 2).reshape(1).astype(jnp.int32)
     me = lax.axis_index("grp").reshape(1).astype(jnp.int32)
-    new_vectors, turned = vectors(core, pivot_columns, in_hbm, mine, other, pivot_inverse)
-    half = exchange(reduce_to_owner(me, turned, orbitals, n_grp, n_rows), "rows")
+    new_vectors, turned, far = vectors(
+        core, me, close, previous, mine, other, pivot_inverse, orbitals, n_grp
+    )
+    half = exchange(reduce_to_owner(me, turned, far, orbitals, n_grp, n_rows), "rows")
     return new_vectors, final(half.reshape(-1, half.shape[-1]), slab_orbitals)
 
 

time: 98.9 us -> 99 us (level)
  Pallas kernels: 16.6 us -> 18.6 us
  waiting for transfers between devices: 14.6 us -> 12.8 us
    pallas_call x2 -> x3, Pallas kernels: 7.98 us -> 9.96 us  [the longest x1 5.71 us: vectors(): pl.pallas_call(functools.partial(vectors_kernel, owners=owners), out_shap...]
    ppermute x8, waiting for transfers between devices: 13.2 us -> 11.5 us  [hop(): lax.ppermute(x, 'grp', [(i, (i + way) % owners) for i in range(owners)])]
  transfers between devices with their start and end apart: 9 -> 9, of which waited for: 5 -> 5; matrix products, arithmetic and copies ran while one was open for 0% -> 0% of each run, Pallas kernels for 4% -> 5%
where the time goes in v10:
time: 99 us; the launch traced here: 98.7 us
  blocking collectives  54.2 us (55%)
  Pallas kernels  18.6 us (19%)
  waiting for transfers between devices  12.8 us (13%)
  starting transfers between devices  11.5 us (12%)
    all_to_all x3, blocking collectives, exchange(): return lax.all_to_all(x, axis, split_axis=0, concat_axis=0, tiled=True)  54.2 us
    ppermute x8, waiting for transfers between devices, hop(): lax.ppermute(x, 'grp', [(i, (i + way) % owners) for i in range(owners)])  11.5 us
    ppermute x8, starting transfers between devices, hop(): lax.ppermute(x, 'grp', [(i, (i + way) % owners) for i in range(owners)])  11.4 us
    pallas_call x1, Pallas kernels, vectors(): pl.pallas_call(functools.partial(vectors_kernel, owners=owners), out_shap...  5.71 us
    pallas_call x5, Pallas kernels, parts(): pl.pallas_call(functools.partial(parts_kernel, ahead=ahead, owners=owners...  4.28 us
    pallas_call x1, Pallas kernels, pick_rows(): pl.pallas_call(functools.partial(pick_kernel, bring=bring), out_shape=out...  2.55 us
    pallas_call x1, Pallas kernels, final(): pl.pallas_call(final_kernel, out_shape=jax.ShapeDtypeStruct((keep, occ, w...  2.08 us
  transfers between devices with their start and end apart: 9, of which 5 were waited for; matrix products, arithmetic and copies ran while one was open for 0% of the time, Pallas kernels for 5%

profile of v10, /device:TPU:1, one launch (start us, length us, event | category | flops | bytes accessed | tf_op | source)
XLA Modules:
  0.0 98.7 jit_solution(1206516922978284349)
XLA Ops:
  0.7 2.5 %pick_rows.5 = (bf16[8,512]{1,0:T(8,128)(2,1)S(1)}, bf16[4,1280,256]{2,1,0:T(8,128)(2,1)S(1)}) custom-call(s32[4]{0:T(128)S(1)} %pad_add_fusion.1.where_from_ref, s32[2,128]{1,0:T(2,128)} %bitcast.40, bf16[4,1280,512]{2,1,0:T(8,128)(2,1)} %prev_ref.3, bf16[4,1280,256]{2,1,0:T(8,128)(2,1)} %refs_0_.1), custom_call_target="tpu_custom_call" | custom-call | flops 131072 | bytes 262144 | tf_op jit(solution)/shard_map/pick_rows/pallas_call | solution.py:100
  3.3 16.1 %all_to_all.30.came_ref = bf16[8,8,512]{2,1,0:T(8,128)(2,1)S(1)} all-to-all(bf16[8,8,512]{2,1,0:T(8,128)(2,1)S(1)} %broadcast_in_dim.12), channel_id=1, replica_groups=mesh['rows'=32,'grp'=8] {'grp'}, dimensions={0} | all-to-all | bytes 131072 | tf_op jit(solution)/shard_map/all_to_all | solution.py:473
  19.3 0.9 spread.5
  20.3 19.4 %all_to_all.31 = bf16[32,24,256]{2,1,0:T(8,128)(2,1)S(1)} all-to-all(bf16[32,24,256]{2,1,0:T(8,128)(2,1)S(1)} %spread.5), channel_id=1, replica_groups=mesh['rows'=32,'grp'=8] {'rows'}, dimensions={0} | all-to-all | bytes 786432 | tf_op jit(solution)/shard_map/all_to_all | solution.py:473
  39.7 1.1 %select_rows.5 = (bf16[256,256]{1,0:T(8,128)(2,1)S(1)}, s32[1]{0:T(128)}) custom-call(s32[1]{0:T(128)} %constant.90.clone.1.round_ref, s32[1,256]{1,0:T(1,128)S(1)} %bitcast.42, bf16[768,256]{1,0:T(8,128)(2,1)S(1)} %bitcast.39, bf16[256,256]{1,0:T(8,128)(2,1)S(1)} %broadcast_in_dim.13.so_far_ref), custom_call_target="tpu_custom_call" | custom-call | flops 100663296 | bytes 393216 | tf_op jit(solution)/shard_map/select_rows/pallas_call | solution.py:147
  40.8 0.7 while.12
  41.5 1.3 %collective-permute-done.other_ref = bf16[256,256]{1,0:T(8,128)(2,1)S(1)} collective-permute-done((bf16[256,256]{1,0:T(8,128)(2,1)S(1)}, bf16[256,256]{1,0:T(8,128)(2,1)S(1)}, u32[]{:S(2)}, u32[]{:S(2)}) %collective-permute-start) | collective-permute-done | bytes 131104 | tf_op jit(solution)/shard_map/ppermute | solution.py:499
  42.9 5.7 %vectors.1 = (bf16[4,1280,256]{2,1,0:T(8,128)(2,1)}, bf16[4,256,1280]{2,1,0:T(8,128)(2,1)S(1)}, bf16[1280,128]{1,0:T(8,128)(2,1)S(1)}) custom-call(s32[1]{0:T(128)} %bitcast.8.core_ref, s32[1]{0:T(128)} %bitcast.9.me_ref, bf16[4,1280,256]{2,1,0:T(8,128)(2,1)S(1)} %get-tuple-element.109.cols_ref, bf16[4,1280,512]{2,1,0:T(8,128)(2,1)} %get-tuple-element.231, ...), custom_call_target="tpu_custom_call" | custom-call | flops 2013265920 | bytes 13107200 | tf_op jit(solution)/shard_map/vectors/pallas_call | solution.py:262
  48.6 0.8 parts.5
  49.8 2.4 %collective-permute-start.5 = (bf16[16,4,8,128]{3,2,1,0:T(8,128)(2,1)S(1)}, bf16[16,4,8,128]{3,2,1,0:T(8,128)(2,1)S(1)}, u32[]{:S(2)}, u32[]{:S(2)}) collective-permute-start(bf16[16,4,8,128]{3,2,1,0:T(8,128)(2,1)S(1)} %get-tuple-element.121), channel_id=1, source_target_pairs={{0,7},{1,0},{2,1},{3,2},{4,3},{5,4},{6,5},{7,6},{8,15},{9,8},{10,9... | collective-permute-start | bytes 393224 | tf_op jit(solution)/shard_map/ppermute | solution.py:418
  52.2 1.7 %bring.1.orb_ref = bf16[1280,1024]{1,0:T(8,128)(2,1)S(1)} custom-call(bf16[1280,1024]{1,0:T(8,128)(2,1)} %orb_ref.3, bf16[16,4,8,128]{3,2,1,0:T(8,128)(2,1)S(1)} %get-tuple-element.120.after_ref), custom_call_target="tpu_custom_call" | custom-call | bytes 2621440 | tf_op jit(solution)/shard_map/bring/pallas_call | solution.py:304
  53.9 0.9 parts.9.own_ref
  54.8 0.9 collective-permute-done.1.came_ref
  55.8 2.7 %collective-permute-start.6 = (bf16[32,4,8,128]{3,2,1,0:T(8,128)(2,1)S(1)}, bf16[32,4,8,128]{3,2,1,0:T(8,128)(2,1)S(1)}, u32[]{:S(2)}, u32[]{:S(2)}) collective-permute-start(bf16[32,4,8,128]{3,2,1,0:T(8,128)(2,1)S(1)} %join.3), channel_id=1, source_target_pairs={{0,7},{1,0},{2,1},{3,2},{4,3},{5,4},{6,5},{7,6},{8,15},{9,8},{10,9... | collective-permute-start | bytes 786440 | tf_op jit(solution)/shard_map/ppermute | solution.py:418
  58.6 0.9 parts.8.own_ref
  59.4 4.4 %collective-permute-done.2.came_ref = bf16[32,4,8,128]{3,2,1,0:T(8,128)(2,1)S(1)} collective-permute-done((bf16[32,4,8,128]{3,2,1,0:T(8,128)(2,1)S(1)}, bf16[32,4,8,128]{3,2,1,0:T(8,128)(2,1)S(1)}, u32[]{:S(2)}, u32[]{:S(2)}) %collective-permute-start.2) | collective-permute-done | bytes 262176 | tf_op jit(solution)/shard_map/ppermute | solution.py:418
  64.0 2.7 %collective-permute-start.7 = (bf16[32,4,8,128]{3,2,1,0:T(8,128)(2,1)S(1)}, bf16[32,4,8,128]{3,2,1,0:T(8,128)(2,1)S(1)}, u32[]{:S(2)}, u32[]{:S(2)}) collective-permute-start(bf16[32,4,8,128]{3,2,1,0:T(8,128)(2,1)S(1)} %add.68), channel_id=1, source_target_pairs={{0,7},{1,0},{2,1},{3,2},{4,3},{5,4},{6,5},{7,6},{8,15},{9,8},{10,9... | collective-permute-start | bytes 786440 | tf_op jit(solution)/shard_map/ppermute | solution.py:418
  66.8 0.9 parts.7.own_ref
  67.6 3.4 %collective-permute-done.3.came_ref = bf16[32,4,8,128]{3,2,1,0:T(8,128)(2,1)S(1)} collective-permute-done((bf16[32,4,8,128]{3,2,1,0:T(8,128)(2,1)S(1)}, bf16[32,4,8,128]{3,2,1,0:T(8,128)(2,1)S(1)}, u32[]{:S(2)}, u32[]{:S(2)}) %collective-permute-start.3) | collective-permute-done | bytes 262176 | tf_op jit(solution)/shard_map/ppermute | solution.py:418
  71.5 2.7 %collective-permute-start.8 = (bf16[32,4,8,128]{3,2,1,0:T(8,128)(2,1)S(1)}, bf16[32,4,8,128]{3,2,1,0:T(8,128)(2,1)S(1)}, u32[]{:S(2)}, u32[]{:S(2)}) collective-permute-start(bf16[32,4,8,128]{3,2,1,0:T(8,128)(2,1)S(1)} %add.69), channel_id=1, source_target_pairs={{0,7},{1,0},{2,1},{3,2},{4,3},{5,4},{6,5},{7,6},{8,15},{9,8},{10,9... | collective-permute-start | bytes 786440 | tf_op jit(solution)/shard_map/ppermute | solution.py:418
  74.2 0.8 parts.6
  75.1 2.8 %collective-permute-done.4 = bf16[32,4,8,128]{3,2,1,0:T(8,128)(2,1)S(1)} collective-permute-done((bf16[32,4,8,128]{3,2,1,0:T(8,128)(2,1)S(1)}, bf16[32,4,8,128]{3,2,1,0:T(8,128)(2,1)S(1)}, u32[]{:S(2)}, u32[]{:S(2)}) %collective-permute-start.4) | collective-permute-done | bytes 262176 | tf_op jit(solution)/shard_map/ppermute | solution.py:418
  77.9 18.7 %all_to_all.32 = f32[32,4,8,128]{3,2,1,0:T(8,128)S(1)} all-to-all(f32[32,4,8,128]{3,2,1,0:T(8,128)S(1)} %fusion), channel_id=1, replica_groups=mesh['rows'=32,'grp'=8] {'rows'}, dimensions={0} | all-to-all | bytes 1048576 | tf_op jit(solution)/shard_map/all_to_all | solution.py:473
  96.6 2.1 %final.1 = bf16[8,1024,128]{2,1,0:T(8,128)(2,1)} custom-call(f32[1024,128]{1,0:T(8,128)S(1)} %bitcast.38, bf16[128,1024]{1,0:T(8,128)(2,1)S(1)} %copy-done), custom_call_target="tpu_custom_call" | custom-call | flops 536870912 | bytes 2621440 | tf_op jit(solution)/shard_map/final/pallas_call | solution.py:459
  (25 shorter events, 1.4 us)
Async XLA Ops:
  0.7 18.6 %copy-start.2 = (s32[256]{0:T(256)S(1)}, s32[256]{0:T(256)}, u32[]{:S(2)}) copy-start(s32[256]{0:T(256)} %param.10) | copy-start | bytes 3076
  40.7 2.1 %copy-start.1 = (bf16[256,256]{1,0:T(8,128)(2,1)S(1)}, bf16[256,256]{1,0:T(8,128)(2,1)}, u32[]{:S(2)}) copy-start(bf16[256,256]{1,0:T(8,128)(2,1)} %inv_ref.1) | copy-start | bytes 393220
  41.4 1.4 %collective-permute-start = (bf16[256,256]{1,0:T(8,128)(2,1)S(1)}, bf16[256,256]{1,0:T(8,128)(2,1)S(1)}, u32[]{:S(2)}, u32[]{:S(2)}) collective-permute-start(bf16[256,256]{1,0:T(8,128)(2,1)S(1)} %get-tuple-element.116.mine_ref), channel_id=1, source_target_pairs={{0,8},{8,0},{16,24},{24,16},{32,40},{40,32},{48,56},{56,48},{64,72... | collective-permute-start | bytes 393224 | tf_op jit(solution)/shard_map/ppermute | solution.py:499
  49.4 6.2 %collective-permute-start.1 = (bf16[16,4,8,128]{3,2,1,0:T(8,128)(2,1)S(1)}, bf16[16,4,8,128]{3,2,1,0:T(8,128)(2,1)S(1)}, u32[]{:S(2)}, u32[]{:S(2)}) collective-permute-start(bf16[16,4,8,128]{3,2,1,0:T(8,128)(2,1)S(1)} %get-tuple-element.120.after_ref), channel_id=1, source_target_pairs={{0,1},{1,2},{2,3},{3,4},{4,5},{5,6},{6,7},{7,0},{8,9},{9,10},{10,1... | collective-permute-start | bytes 393224 | tf_op jit(solution)/shard_map/ppermute | solution.py:418
  49.8 6.0 %collective-permute-start.5 = (bf16[16,4,8,128]{3,2,1,0:T(8,128)(2,1)S(1)}, bf16[16,4,8,128]{3,2,1,0:T(8,128)(2,1)S(1)}, u32[]{:S(2)}, u32[]{:S(2)}) collective-permute-start(bf16[16,4,8,128]{3,2,1,0:T(8,128)(2,1)S(1)} %get-tuple-element.121), channel_id=1, source_target_pairs={{0,7},{1,0},{2,1},{3,2},{4,3},{5,4},{6,5},{7,6},{8,15},{9,8},{10,9... | collective-permute-start | bytes 393224 | tf_op jit(solution)/shard_map/ppermute | solution.py:418
  55.7 8.1 %collective-permute-start.2 = (bf16[32,4,8,128]{3,2,1,0:T(8,128)(2,1)S(1)}, bf16[32,4,8,128]{3,2,1,0:T(8,128)(2,1)S(1)}, u32[]{:S(2)}, u32[]{:S(2)}) collective-permute-start(bf16[32,4,8,128]{3,2,1,0:T(8,128)(2,1)S(1)} %join.2), channel_id=1, source_target_pairs={{0,1},{1,2},{2,3},{3,4},{4,5},{5,6},{6,7},{7,0},{8,9},{9,10},{10,1... | collective-permute-start | bytes 786440 | tf_op jit(solution)/shard_map/ppermute | solution.py:418
  55.8 8.1 %collective-permute-start.6 = (bf16[32,4,8,128]{3,2,1,0:T(8,128)(2,1)S(1)}, bf16[32,4,8,128]{3,2,1,0:T(8,128)(2,1)S(1)}, u32[]{:S(2)}, u32[]{:S(2)}) collective-permute-start(bf16[32,4,8,128]{3,2,1,0:T(8,128)(2,1)S(1)} %join.3), channel_id=1, source_target_pairs={{0,7},{1,0},{2,1},{3,2},{4,3},{5,4},{6,5},{7,6},{8,15},{9,8},{10,9... | collective-permute-start | bytes 786440 | tf_op jit(solution)/shard_map/ppermute | solution.py:418
  63.9 7.2 %collective-permute-start.3 = (bf16[32,4,8,128]{3,2,1,0:T(8,128)(2,1)S(1)}, bf16[32,4,8,128]{3,2,1,0:T(8,128)(2,1)S(1)}, u32[]{:S(2)}, u32[]{:S(2)}) collective-permute-start(bf16[32,4,8,128]{3,2,1,0:T(8,128)(2,1)S(1)} %add.66), channel_id=1, source_target_pairs={{0,1},{1,2},{2,3},{3,4},{4,5},{5,6},{6,7},{7,0},{8,9},{9,10},{10,1... | collective-permute-start | bytes 786440 | tf_op jit(solution)/shard_map/ppermute | solution.py:418
  64.0 7.4 %collective-permute-start.7 = (bf16[32,4,8,128]{3,2,1,0:T(8,128)(2,1)S(1)}, bf16[32,4,8,128]{3,2,1,0:T(8,128)(2,1)S(1)}, u32[]{:S(2)}, u32[]{:S(2)}) collective-permute-start(bf16[32,4,8,128]{3,2,1,0:T(8,128)(2,1)S(1)} %add.68), channel_id=1, source_target_pairs={{0,7},{1,0},{2,1},{3,2},{4,3},{5,4},{6,5},{7,6},{8,15},{9,8},{10,9... | collective-permute-start | bytes 786440 | tf_op jit(solution)/shard_map/ppermute | solution.py:418
  71.1 6.7 %collective-permute-start.4 = (bf16[32,4,8,128]{3,2,1,0:T(8,128)(2,1)S(1)}, bf16[32,4,8,128]{3,2,1,0:T(8,128)(2,1)S(1)}, u32[]{:S(2)}, u32[]{:S(2)}) collective-permute-start(bf16[32,4,8,128]{3,2,1,0:T(8,128)(2,1)S(1)} %add.67), channel_id=1, source_target_pairs={{0,1},{1,2},{2,3},{3,4},{4,5},{5,6},{6,7},{7,0},{8,9},{9,10},{10,1... | collective-permute-start | bytes 786440 | tf_op jit(solution)/shard_map/ppermute | solution.py:418
  71.5 6.4 %collective-permute-start.8 = (bf16[32,4,8,128]{3,2,1,0:T(8,128)(2,1)S(1)}, bf16[32,4,8,128]{3,2,1,0:T(8,128)(2,1)S(1)}, u32[]{:S(2)}, u32[]{:S(2)}) collective-permute-start(bf16[32,4,8,128]{3,2,1,0:T(8,128)(2,1)S(1)} %add.69), channel_id=1, source_target_pairs={{0,7},{1,0},{2,1},{3,2},{4,3},{5,4},{6,5},{7,6},{8,15},{9,8},{10,9... | collective-permute-start | bytes 786440 | tf_op jit(solution)/shard_map/ppermute | solution.py:418
  75.0 21.6 %copy-start = (bf16[128,1024]{1,0:T(8,128)(2,1)S(1)}, bf16[128,1024]{1,0:T(8,128)(2,1)}, u32[]{:S(2)}) copy-start(bf16[128,1024]{1,0:T(8,128)(2,1)} %slab_ref.1) | copy-start | bytes 786436

commit v11 on v10

--- a/solution.py
+++ b/solution.py
@@ -209,35 +209,56 @@
     )(where_from, pivots.reshape(1, n), came)
 
 
+def preload_kernel(prev_ref, after_ref, out_ref, sems):
+    copies = [
+        pltpu.make_async_copy(prev_ref.at[m], out_ref.at[m], sems.at[m])
+        for m in range(out_ref.shape[0])
+    ]
+    for copy in copies:
+        copy.start()
+    for copy in copies:
+        copy.wait()
+
+
+def preload(previous, count, after):
+    shape = (count,) + previous.shape[1:]
+    return pl.pallas_call(
+        preload_kernel,
+        out_shape=jax.ShapeDtypeStruct(shape, previous.dtype),
+        in_specs=[pl.BlockSpec(memory_space=pltpu.HBM), pl.BlockSpec(memory_space=pl.ANY)],
+        out_specs=pl.BlockSpec(memory_space=pltpu.VMEM),
+        scratch_shapes=[pltpu.SemaphoreType.DMA((count,))],
+        compiler_params=pltpu.CompilerParams(vmem_limit_bytes=4 << 20),
+        cost_estimate=pl.CostEstimate(
+            flops=0, bytes_accessed=previous.size, transcendentals=0
+        ),
+        name="preload",
+    )(previous, after)
+
+
 def vectors_kernel(
-    core_ref, me_ref, cols_ref, prev_ref, mine_ref, other_ref, inv_ref, orb_ref,
+    core_ref, me_ref, cols_ref, first_ref, prev_ref, mine_ref, other_ref, inv_ref, orb_ref,
     new_ref, turned_ref, far_ref, came, made, load, store, far_sem, *, owners
 ):
-    mu = came.shape[0]
+    early, mu = first_ref.shape[0], cols_ref.shape[0]
     width = far_ref.shape[1]
     column = pl.multiple_of(lax.rem(me_ref[0] + owners // 2, owners) * width, width)
     far = pltpu.make_async_copy(orb_ref.at[:, pl.ds(column, width)], far_ref, far_sem)
 
-    def load_of(m):
-        return pltpu.make_async_copy(prev_ref.at[m], came.at[m], load.at[m])
+    def load_of(i):
+        return pltpu.make_async_copy(prev_ref.at[early + i], came.at[i], load.at[i])
 
     def store_of(m):
         return pltpu.make_async_copy(made.at[m], new_ref.at[m], store.at[m])
 
-    for m in range(mu):
-        load_of(m).start()
-    far.start()
-
-    @pl.loop(0, mu)
-    def _(m):
-        load_of(m).wait()
+    def step(m, prev):
         mine, other = mine_ref[...].astype(F32), other_ref[...].astype(F32)
         first = core_ref[0] == 0
         rows = jnp.concatenate(
             [jnp.where(first, mine, other), jnp.where(first, other, mine)], axis=1
         ).astype(BF16)
         contract = (((1,), (1,)), ((), ()))
-        correction = lax.dot_general(came[m], rows, contract, preferred_element_type=F32)
+        correction = lax.dot_general(prev, rows, contract, preferred_element_type=F32)
         residual = (cols_ref[m].astype(F32) - correction).astype(BF16)
         inv = inv_ref[...]
         row, column = (lax.broadcasted_iota(jnp.int32, inv.shape, d) for d in (0, 1))
@@ -247,12 +268,25 @@
         store_of(m).start()
         turned_ref[m] = new.T
 
+    for i in range(mu - early):
+        load_of(i).start()
+    far.start()
+
+    @pl.loop(0, early)
+    def _(m):
+        step(m, first_ref[m])
+
+    @pl.loop(0, mu - early)
+    def _(i):
+        load_of(i).wait()
+        step(early + i, came[i])
+
     far.wait()
     for m in range(mu):
         store_of(m).wait()
 
 
-def vectors(core, me, pivot_columns, previous, mine, other, pivot_inverse, orbitals, owners):
+def vectors(core, me, pivot_columns, first, previous, mine, other, pivot_inverse, orbitals, owners):
     mu, nu, k = previous.shape
     n = pivot_columns.shape[2]
     width = orbitals.shape[1] // owners
@@ -266,12 +300,12 @@
             jax.ShapeDtypeStruct((mu, n, nu), BF16),
             jax.ShapeDtypeStruct((nu, width), BF16),
         ),
-        in_specs=[smem, smem, vmem, hbm, vmem, vmem, vmem, hbm],
+        in_specs=[smem, smem, vmem, vmem, hbm, vmem, vmem, vmem, hbm],
         out_specs=(pl.BlockSpec(memory_space=pl.ANY), vmem, vmem),
         scratch_shapes=[
-            pltpu.VMEM((mu, nu, k), BF16),
+            pltpu.VMEM((mu - first.shape[0], nu, k), BF16),
             pltpu.VMEM((mu, nu, n), BF16),
-            pltpu.SemaphoreType.DMA((mu,)),
+            pltpu.SemaphoreType.DMA((mu - first.shape[0],)),
             pltpu.SemaphoreType.DMA((mu,)),
             pltpu.SemaphoreType.DMA,
         ],
@@ -282,7 +316,7 @@
             transcendentals=0,
         ),
         name="vectors",
-    )(core, me, pivot_columns, previous, mine, other, pivot_inverse, orbitals)
+    )(core, me, pivot_columns, first, previous, mine, other, pivot_inverse, orbitals)
 
 
 def bring_kernel(orb_ref, after_ref, out_ref, sems):
@@ -507,8 +541,9 @@
     mine, other, close = pivot_halves(n_rows, n_grp, pivots, previous, pivot_columns)
     core = (lax.axis_index("rows") % 2).reshape(1).astype(jnp.int32)
     me = lax.axis_index("grp").reshape(1).astype(jnp.int32)
+    first = preload(previous, previous.shape[0] // 2, mine)
     new_vectors, turned, far = vectors(
-        core, me, close, previous, mine, other, pivot_inverse, orbitals, n_grp
+        core, me, close, first, previous, mine, other, pivot_inverse, orbitals, n_grp
     )
     half = exchange(reduce_to_owner(me, turned, far, orbitals, n_grp, n_rows), "rows")
     return new_vectors, final(half.reshape(-1, half.shape[-1]), slab_orbitals)

time: 99 us -> 98.4 us (level)
  waiting for transfers between devices: 12.8 us -> 10.2 us
  blocking collectives: 54.2 us -> 55.6 us
    pallas_call x0 -> x1, Pallas kernels: none -> 1.77 us  [preload(): pl.pallas_call(preload_kernel, out_shape=jax.ShapeDtypeStruct(shape, prev...]
    all_to_all x3, blocking collectives: 54.2 us -> 55.6 us  [exchange(): return lax.all_to_all(x, axis, split_axis=0, concat_axis=0, tiled=True)]
    ppermute x1, waiting for transfers between devices: 1.32 us -> 0.01 us  [pivot_halves(): other = lax.ppermute(mine, 'rows', [(i, i ^ 1) for i in range(n_rows)])]
    pallas_call x1, Pallas kernels: 5.71 us -> 4.39 us  [vectors(): pl.pallas_call(functools.partial(vectors_kernel, owners=owners), out_shap...]
    ppermute x8, waiting for transfers between devices: 11.5 us -> 10.2 us  [hop(): lax.ppermute(x, 'grp', [(i, (i + way) % owners) for i in range(owners)])]
  transfers between devices with their start and end apart: 9 -> 9, of which waited for: 5 -> 4; matrix products, arithmetic and copies ran while one was open for 0% -> 0% of each run, Pallas kernels for 5% -> 7%
where the time goes in v11:
time: 98.4 us; the launch traced here: 98 us
  blocking collectives  55.6 us (57%)
  Pallas kernels  19 us (19%)
  starting transfers between devices  11.5 us (12%)
  waiting for transfers between devices  10.2 us (10%)
    all_to_all x3, blocking collectives, exchange(): return lax.all_to_all(x, axis, split_axis=0, concat_axis=0, tiled=True)  55.6 us
    ppermute x8, starting transfers between devices, hop(): lax.ppermute(x, 'grp', [(i, (i + way) % owners) for i in range(owners)])  11.4 us
    ppermute x8, waiting for transfers between devices, hop(): lax.ppermute(x, 'grp', [(i, (i + way) % owners) for i in range(owners)])  10.2 us
    pallas_call x1, Pallas kernels, vectors(): pl.pallas_call(functools.partial(vectors_kernel, owners=owners), out_shap...  4.39 us
    pallas_call x5, Pallas kernels, parts(): pl.pallas_call(functools.partial(parts_kernel, ahead=ahead, owners=owners...  4.27 us
    pallas_call x1, Pallas kernels, pick_rows(): pl.pallas_call(functools.partial(pick_kernel, bring=bring), out_shape=out...  2.55 us
    pallas_call x1, Pallas kernels, final(): pl.pallas_call(final_kernel, out_shape=jax.ShapeDtypeStruct((keep, occ, w...  2.07 us
  transfers between devices with their start and end apart: 9, of which 4 were waited for; matrix products, arithmetic and copies ran while one was open for 0% of the time, Pallas kernels for 7%

profile of v11, /device:TPU:1, one launch (start us, length us, event | category | flops | bytes accessed | tf_op | source)
XLA Modules:
  0.0 98.0 jit_solution(3265278463955670551)
XLA Ops:
  0.7 2.5 %pick_rows.5 = (bf16[8,512]{1,0:T(8,128)(2,1)S(1)}, bf16[4,1280,256]{2,1,0:T(8,128)(2,1)S(1)}) custom-call(s32[4]{0:T(128)S(1)} %pad_add_fusion.1.where_from_ref, s32[2,128]{1,0:T(2,128)} %bitcast.40, bf16[4,1280,512]{2,1,0:T(8,128)(2,1)} %prev_ref.5, bf16[4,1280,256]{2,1,0:T(8,128)(2,1)} %refs_0_.1), custom_call_target="tpu_custom_call" | custom-call | flops 131072 | bytes 262144 | tf_op jit(solution)/shard_map/pick_rows/pallas_call | solution.py:100
  3.3 16.1 %all_to_all.30.came_ref = bf16[8,8,512]{2,1,0:T(8,128)(2,1)S(1)} all-to-all(bf16[8,8,512]{2,1,0:T(8,128)(2,1)S(1)} %broadcast_in_dim.12), channel_id=1, replica_groups=mesh['rows'=32,'grp'=8] {'grp'}, dimensions={0} | all-to-all | bytes 131072 | tf_op jit(solution)/shard_map/all_to_all | solution.py:507
  19.3 0.9 spread.5
  20.3 19.3 %all_to_all.31 = bf16[32,24,256]{2,1,0:T(8,128)(2,1)S(1)} all-to-all(bf16[32,24,256]{2,1,0:T(8,128)(2,1)S(1)} %spread.5), channel_id=1, replica_groups=mesh['rows'=32,'grp'=8] {'rows'}, dimensions={0} | all-to-all | bytes 786432 | tf_op jit(solution)/shard_map/all_to_all | solution.py:507
  39.6 1.1 %select_rows.5 = (bf16[256,256]{1,0:T(8,128)(2,1)S(1)}, s32[1]{0:T(128)}) custom-call(s32[1]{0:T(128)} %constant.90.clone.1.round_ref, s32[1,256]{1,0:T(1,128)S(1)} %bitcast.42, bf16[768,256]{1,0:T(8,128)(2,1)S(1)} %bitcast.39, bf16[256,256]{1,0:T(8,128)(2,1)S(1)} %broadcast_in_dim.13.so_far_ref), custom_call_target="tpu_custom_call" | custom-call | flops 100663296 | bytes 393216 | tf_op jit(solution)/shard_map/select_rows/pallas_call | solution.py:147
  40.6 0.6 while.12
  41.4 1.8 %preload.1.first_ref = bf16[2,1280,512]{2,1,0:T(8,128)(2,1)S(1)} custom-call(bf16[4,1280,512]{2,1,0:T(8,128)(2,1)} %get-tuple-element.231, bf16[256,256]{1,0:T(8,128)(2,1)S(1)} %get-tuple-element.116.after_ref.mine_ref), custom_call_target="tpu_custom_call" | custom-call | bytes 2621440 | tf_op jit(solution)/shard_map/preload/pallas_call | solution.py:225
  43.2 4.4 %vectors.1 = (bf16[4,1280,256]{2,1,0:T(8,128)(2,1)}, bf16[4,256,1280]{2,1,0:T(8,128)(2,1)S(1)}, bf16[1280,128]{1,0:T(8,128)(2,1)S(1)}) custom-call(s32[1]{0:T(128)} %bitcast.8.core_ref, s32[1]{0:T(128)} %bitcast.9.me_ref, bf16[4,1280,256]{2,1,0:T(8,128)(2,1)S(1)} %get-tuple-element.109.cols_ref, bf16[2,1280,512]{2,1,0:T(8,128)(2,1)S(1)} %preload.1.first_ref, ...), custom_call_target="tpu_custom_call" | custom-call | flops 2013265920 | bytes 13107200 | tf_op jit(solution)/shard_map/vectors/pallas_call | solution.py:296
  47.6 0.8 parts.5
  48.8 2.4 %collective-permute-start.5 = (bf16[16,4,8,128]{3,2,1,0:T(8,128)(2,1)S(1)}, bf16[16,4,8,128]{3,2,1,0:T(8,128)(2,1)S(1)}, u32[]{:S(2)}, u32[]{:S(2)}) collective-permute-start(bf16[16,4,8,128]{3,2,1,0:T(8,128)(2,1)S(1)} %get-tuple-element.121), channel_id=1, source_target_pairs={{0,7},{1,0},{2,1},{3,2},{4,3},{5,4},{6,5},{7,6},{8,15},{9,8},{10,9... | collective-permute-start | bytes 393224 | tf_op jit(solution)/shard_map/ppermute | solution.py:452
  51.2 1.7 %bring.1.orb_ref = bf16[1280,1024]{1,0:T(8,128)(2,1)S(1)} custom-call(bf16[1280,1024]{1,0:T(8,128)(2,1)} %orb_ref.3, bf16[16,4,8,128]{3,2,1,0:T(8,128)(2,1)S(1)} %get-tuple-element.120.after_ref), custom_call_target="tpu_custom_call" | custom-call | bytes 2621440 | tf_op jit(solution)/shard_map/bring/pallas_call | solution.py:338
  52.9 0.9 parts.9.own_ref
  53.8 0.5 collective-permute-done.1.came_ref
  54.5 2.7 %collective-permute-start.6 = (bf16[32,4,8,128]{3,2,1,0:T(8,128)(2,1)S(1)}, bf16[32,4,8,128]{3,2,1,0:T(8,128)(2,1)S(1)}, u32[]{:S(2)}, u32[]{:S(2)}) collective-permute-start(bf16[32,4,8,128]{3,2,1,0:T(8,128)(2,1)S(1)} %join.3), channel_id=1, source_target_pairs={{0,7},{1,0},{2,1},{3,2},{4,3},{5,4},{6,5},{7,6},{8,15},{9,8},{10,9... | collective-permute-start | bytes 786440 | tf_op jit(solution)/shard_map/ppermute | solution.py:452
  57.2 0.9 parts.8.own_ref
  58.1 4.0 %collective-permute-done.2.came_ref = bf16[32,4,8,128]{3,2,1,0:T(8,128)(2,1)S(1)} collective-permute-done((bf16[32,4,8,128]{3,2,1,0:T(8,128)(2,1)S(1)}, bf16[32,4,8,128]{3,2,1,0:T(8,128)(2,1)S(1)}, u32[]{:S(2)}, u32[]{:S(2)}) %collective-permute-start.2) | collective-permute-done | bytes 262176 | tf_op jit(solution)/shard_map/ppermute | solution.py:452
  62.3 2.9 %collective-permute-start.7 = (bf16[32,4,8,128]{3,2,1,0:T(8,128)(2,1)S(1)}, bf16[32,4,8,128]{3,2,1,0:T(8,128)(2,1)S(1)}, u32[]{:S(2)}, u32[]{:S(2)}) collective-permute-start(bf16[32,4,8,128]{3,2,1,0:T(8,128)(2,1)S(1)} %add.68), channel_id=1, source_target_pairs={{0,7},{1,0},{2,1},{3,2},{4,3},{5,4},{6,5},{7,6},{8,15},{9,8},{10,9... | collective-permute-start | bytes 786440 | tf_op jit(solution)/shard_map/ppermute | solution.py:452
  65.2 0.9 parts.7.own_ref
  66.1 2.9 %collective-permute-done.3.came_ref = bf16[32,4,8,128]{3,2,1,0:T(8,128)(2,1)S(1)} collective-permute-done((bf16[32,4,8,128]{3,2,1,0:T(8,128)(2,1)S(1)}, bf16[32,4,8,128]{3,2,1,0:T(8,128)(2,1)S(1)}, u32[]{:S(2)}, u32[]{:S(2)}) %collective-permute-start.3) | collective-permute-done | bytes 262176 | tf_op jit(solution)/shard_map/ppermute | solution.py:452
  69.2 2.7 %collective-permute-start.8 = (bf16[32,4,8,128]{3,2,1,0:T(8,128)(2,1)S(1)}, bf16[32,4,8,128]{3,2,1,0:T(8,128)(2,1)S(1)}, u32[]{:S(2)}, u32[]{:S(2)}) collective-permute-start(bf16[32,4,8,128]{3,2,1,0:T(8,128)(2,1)S(1)} %add.69), channel_id=1, source_target_pairs={{0,7},{1,0},{2,1},{3,2},{4,3},{5,4},{6,5},{7,6},{8,15},{9,8},{10,9... | collective-permute-start | bytes 786440 | tf_op jit(solution)/shard_map/ppermute | solution.py:452
  71.9 0.8 parts.6
  72.8 2.8 %collective-permute-done.4 = bf16[32,4,8,128]{3,2,1,0:T(8,128)(2,1)S(1)} collective-permute-done((bf16[32,4,8,128]{3,2,1,0:T(8,128)(2,1)S(1)}, bf16[32,4,8,128]{3,2,1,0:T(8,128)(2,1)S(1)}, u32[]{:S(2)}, u32[]{:S(2)}) %collective-permute-start.4) | collective-permute-done | bytes 262176 | tf_op jit(solution)/shard_map/ppermute | solution.py:452
  75.7 20.3 %all_to_all.32 = f32[32,4,8,128]{3,2,1,0:T(8,128)S(1)} all-to-all(f32[32,4,8,128]{3,2,1,0:T(8,128)S(1)} %fusion), channel_id=1, replica_groups=mesh['rows'=32,'grp'=8] {'rows'}, dimensions={0} | all-to-all | bytes 1048576 | tf_op jit(solution)/shard_map/all_to_all | solution.py:507
  96.0 2.1 %final.1 = bf16[8,1024,128]{2,1,0:T(8,128)(2,1)} custom-call(f32[1024,128]{1,0:T(8,128)S(1)} %bitcast.38, bf16[128,1024]{1,0:T(8,128)(2,1)S(1)} %copy-done), custom_call_target="tpu_custom_call" | custom-call | flops 536870912 | bytes 2621440 | tf_op jit(solution)/shard_map/final/pallas_call | solution.py:493
  (26 shorter events, 1.2 us)
Async XLA Ops:
  0.7 18.6 %copy-start.2 = (s32[256]{0:T(256)S(1)}, s32[256]{0:T(256)}, u32[]{:S(2)}) copy-start(s32[256]{0:T(256)} %param.10) | copy-start | bytes 3076
  41.3 1.9 %collective-permute-start = (bf16[256,256]{1,0:T(8,128)(2,1)S(1)}, bf16[256,256]{1,0:T(8,128)(2,1)S(1)}, u32[]{:S(2)}, u32[]{:S(2)}) collective-permute-start(bf16[256,256]{1,0:T(8,128)(2,1)S(1)} %get-tuple-element.116.after_ref.mine_ref), channel_id=1, source_target_pairs={{0,8},{8,0},{16,24},{24,16},{32,40},{40,32},{48,56},{56,48},{64,72... | collective-permute-start | bytes 393224 | tf_op jit(solution)/shard_map/ppermute | solution.py:533
  41.4 1.8 %copy-start.1 = (bf16[256,256]{1,0:T(8,128)(2,1)S(1)}, bf16[256,256]{1,0:T(8,128)(2,1)}, u32[]{:S(2)}) copy-start(bf16[256,256]{1,0:T(8,128)(2,1)} %inv_ref.1) | copy-start | bytes 393220
  48.4 5.9 %collective-permute-start.1 = (bf16[16,4,8,128]{3,2,1,0:T(8,128)(2,1)S(1)}, bf16[16,4,8,128]{3,2,1,0:T(8,128)(2,1)S(1)}, u32[]{:S(2)}, u32[]{:S(2)}) collective-permute-start(bf16[16,4,8,128]{3,2,1,0:T(8,128)(2,1)S(1)} %get-tuple-element.120.after_ref), channel_id=1, source_target_pairs={{0,1},{1,2},{2,3},{3,4},{4,5},{5,6},{6,7},{7,0},{8,9},{9,10},{10,1... | collective-permute-start | bytes 393224 | tf_op jit(solution)/shard_map/ppermute | solution.py:452
  48.8 5.6 %collective-permute-start.5 = (bf16[16,4,8,128]{3,2,1,0:T(8,128)(2,1)S(1)}, bf16[16,4,8,128]{3,2,1,0:T(8,128)(2,1)S(1)}, u32[]{:S(2)}, u32[]{:S(2)}) collective-permute-start(bf16[16,4,8,128]{3,2,1,0:T(8,128)(2,1)S(1)} %get-tuple-element.121), channel_id=1, source_target_pairs={{0,7},{1,0},{2,1},{3,2},{4,3},{5,4},{6,5},{7,6},{8,15},{9,8},{10,9... | collective-permute-start | bytes 393224 | tf_op jit(solution)/shard_map/ppermute | solution.py:452
  54.3 7.8 %collective-permute-start.2 = (bf16[32,4,8,128]{3,2,1,0:T(8,128)(2,1)S(1)}, bf16[32,4,8,128]{3,2,1,0:T(8,128)(2,1)S(1)}, u32[]{:S(2)}, u32[]{:S(2)}) collective-permute-start(bf16[32,4,8,128]{3,2,1,0:T(8,128)(2,1)S(1)} %join.2), channel_id=1, source_target_pairs={{0,1},{1,2},{2,3},{3,4},{4,5},{5,6},{6,7},{7,0},{8,9},{9,10},{10,1... | collective-permute-start | bytes 786440 | tf_op jit(solution)/shard_map/ppermute | solution.py:452
  54.5 7.8 %collective-permute-start.6 = (bf16[32,4,8,128]{3,2,1,0:T(8,128)(2,1)S(1)}, bf16[32,4,8,128]{3,2,1,0:T(8,128)(2,1)S(1)}, u32[]{:S(2)}, u32[]{:S(2)}) collective-permute-start(bf16[32,4,8,128]{3,2,1,0:T(8,128)(2,1)S(1)} %join.3), channel_id=1, source_target_pairs={{0,7},{1,0},{2,1},{3,2},{4,3},{5,4},{6,5},{7,6},{8,15},{9,8},{10,9... | collective-permute-start | bytes 786440 | tf_op jit(solution)/shard_map/ppermute | solution.py:452
  62.2 6.8 %collective-permute-start.3 = (bf16[32,4,8,128]{3,2,1,0:T(8,128)(2,1)S(1)}, bf16[32,4,8,128]{3,2,1,0:T(8,128)(2,1)S(1)}, u32[]{:S(2)}, u32[]{:S(2)}) collective-permute-start(bf16[32,4,8,128]{3,2,1,0:T(8,128)(2,1)S(1)} %add.66), channel_id=1, source_target_pairs={{0,1},{1,2},{2,3},{3,4},{4,5},{5,6},{6,7},{7,0},{8,9},{9,10},{10,1... | collective-permute-start | bytes 786440 | tf_op jit(solution)/shard_map/ppermute | solution.py:452
  62.3 6.8 %collective-permute-start.7 = (bf16[32,4,8,128]{3,2,1,0:T(8,128)(2,1)S(1)}, bf16[32,4,8,128]{3,2,1,0:T(8,128)(2,1)S(1)}, u32[]{:S(2)}, u32[]{:S(2)}) collective-permute-start(bf16[32,4,8,128]{3,2,1,0:T(8,128)(2,1)S(1)} %add.68), channel_id=1, source_target_pairs={{0,7},{1,0},{2,1},{3,2},{4,3},{5,4},{6,5},{7,6},{8,15},{9,8},{10,9... | collective-permute-start | bytes 786440 | tf_op jit(solution)/shard_map/ppermute | solution.py:452
  69.0 6.5 %collective-permute-start.4 = (bf16[32,4,8,128]{3,2,1,0:T(8,128)(2,1)S(1)}, bf16[32,4,8,128]{3,2,1,0:T(8,128)(2,1)S(1)}, u32[]{:S(2)}, u32[]{:S(2)}) collective-permute-start(bf16[32,4,8,128]{3,2,1,0:T(8,128)(2,1)S(1)} %add.67), channel_id=1, source_target_pairs={{0,1},{1,2},{2,3},{3,4},{4,5},{5,6},{6,7},{7,0},{8,9},{9,10},{10,1... | collective-permute-start | bytes 786440 | tf_op jit(solution)/shard_map/ppermute | solution.py:452
  69.2 6.4 %collective-permute-start.8 = (bf16[32,4,8,128]{3,2,1,0:T(8,128)(2,1)S(1)}, bf16[32,4,8,128]{3,2,1,0:T(8,128)(2,1)S(1)}, u32[]{:S(2)}, u32[]{:S(2)}) collective-permute-start(bf16[32,4,8,128]{3,2,1,0:T(8,128)(2,1)S(1)} %add.69), channel_id=1, source_target_pairs={{0,7},{1,0},{2,1},{3,2},{4,3},{5,4},{6,5},{7,6},{8,15},{9,8},{10,9... | collective-permute-start | bytes 786440 | tf_op jit(solution)/shard_map/ppermute | solution.py:452
  72.8 23.2 %copy-start = (bf16[128,1024]{1,0:T(8,128)(2,1)S(1)}, bf16[128,1024]{1,0:T(8,128)(2,1)}, u32[]{:S(2)}) copy-start(bf16[128,1024]{1,0:T(8,128)(2,1)} %slab_ref.1) | copy-start | bytes 786436

commit v12 on v11

--- a/solution.py
+++ b/solution.py
@@ -238,7 +238,7 @@
 
 def vectors_kernel(
     core_ref, me_ref, cols_ref, first_ref, prev_ref, mine_ref, other_ref, inv_ref, orb_ref,
-    new_ref, turned_ref, far_ref, came, made, load, store, far_sem, *, owners
+    new_ref, turned_ref, far_ref, came, made, load, store, far_sem, rows_ref, upper_ref, *, owners
 ):
     early, mu = first_ref.shape[0], cols_ref.shape[0]
     width = far_ref.shape[1]
@@ -252,18 +252,10 @@
         return pltpu.make_async_copy(made.at[m], new_ref.at[m], store.at[m])
 
     def step(m, prev):
-        mine, other = mine_ref[...].astype(F32), other_ref[...].astype(F32)
-        first = core_ref[0] == 0
-        rows = jnp.concatenate(
-            [jnp.where(first, mine, other), jnp.where(first, other, mine)], axis=1
-        ).astype(BF16)
         contract = (((1,), (1,)), ((), ()))
-        correction = lax.dot_general(prev, rows, contract, preferred_element_type=F32)
+        correction = lax.dot_general(prev, rows_ref[...], contract, preferred_element_type=F32)
         residual = (cols_ref[m].astype(F32) - correction).astype(BF16)
-        inv = inv_ref[...]
-        row, column = (lax.broadcasted_iota(jnp.int32, inv.shape, d) for d in (0, 1))
-        upper = jnp.where(row > column, 0.0, inv.astype(F32)).astype(BF16)
-        new = jnp.dot(residual, upper, preferred_element_type=F32).astype(BF16)
+        new = jnp.dot(residual, upper_ref[...], preferred_element_type=F32).astype(BF16)
         made[m] = new
         store_of(m).start()
         turned_ref[m] = new.T
@@ -271,6 +263,13 @@
     for i in range(mu - early):
         load_of(i).start()
     far.start()
+    mine, other = mine_ref[...].astype(F32), other_ref[...].astype(F32)
+    first, half = core_ref[0] == 0, mine.shape[1]
+    rows_ref[:, :half] = jnp.where(first, mine, other).astype(BF16)
+    rows_ref[:, half:] = jnp.where(first, other, mine).astype(BF16)
+    inv = inv_ref[...]
+    row, column = (lax.broadcasted_iota(jnp.int32, inv.shape, d) for d in (0, 1))
+    upper_ref[...] = jnp.where(row > column, 0.0, inv.astype(F32)).astype(BF16)
 
     @pl.loop(0, early)
     def _(m):
@@ -308,6 +307,8 @@
             pltpu.SemaphoreType.DMA((mu - first.shape[0],)),
             pltpu.SemaphoreType.DMA((mu,)),
             pltpu.SemaphoreType.DMA,
+            pltpu.VMEM((n, k), BF16),
+            pltpu.VMEM((n, n), BF16),
         ],
         compiler_params=pltpu.CompilerParams(vmem_limit_bytes=24 << 20),
         cost_estimate=pl.CostEstimate(
@@ -469,12 +470,16 @@
     return own((0,))[0] + right.astype(F32) + left.astype(F32)
 
 
-def final_kernel(half_ref, slab_ref, out_ref):
+def final_kernel(half_ref, slab_ref, out_ref, made, store):
     rows, width = half_ref.shape
     mu = slab_ref.shape[0]
     keep = rows // mu
     slab_t = slab_ref[...].T
     slab_t = jnp.concatenate([slab_t, slab_t], axis=1)
+
+    def store_of(p):
+        return pltpu.make_async_copy(made.at[pl.ds(p, 2)], out_ref.at[pl.ds(p, 2)], store.at[p // 2])
+
     for p in range(0, keep, 2):
         pair = jnp.concatenate(
             [half_ref[pl.ds(q, mu, stride=keep), :] for q in (p, p + 1)], axis=1
@@ -482,17 +487,27 @@
         high = pair.astype(BF16)
         low = (pair - high.astype(F32)).astype(BF16)
         both = jnp.dot(slab_t, jnp.concatenate([high, low], axis=0), preferred_element_type=F32)
-        out_ref[p] = both[:, :width].astype(BF16)
-        out_ref[p + 1] = both[:, width:].astype(BF16)
+        made[p] = both[:, :width].astype(BF16)
+        made[p + 1] = both[:, width:].astype(BF16)
+        store_of(p).start()
+    for p in range(0, keep, 2):
+        store_of(p).wait()
 
 
 def final(half, slab):
     mu, occ = slab.shape
     rows, width = half.shape
     keep = rows // mu
+    vmem = pl.BlockSpec(memory_space=pltpu.VMEM)
     return pl.pallas_call(
         final_kernel,
         out_shape=jax.ShapeDtypeStruct((keep, occ, width), BF16),
+        in_specs=[vmem, vmem],
+        out_specs=pl.BlockSpec(memory_space=pl.ANY),
+        scratch_shapes=[
+            pltpu.VMEM((keep, occ, width), BF16),
+            pltpu.SemaphoreType.DMA((keep // 2,)),
+        ],
         compiler_params=pltpu.CompilerParams(vmem_limit_bytes=16 << 20),
         cost_estimate=pl.CostEstimate(
             flops=4 * rows * width * occ,

time: 98.4 us -> 98.4 us (level)
  no operation moved by 1% of the time
where the time goes in v12:
time: 98.4 us; the launch traced here: 98 us
  blocking collectives  55.6 us (57%)
  Pallas kernels  18.8 us (19%)
  starting transfers between devices  11.5 us (12%)
  waiting for transfers between devices  10.3 us (10%)
  between operations  1.05 us (1%)
    all_to_all x3, blocking collectives, exchange(): return lax.all_to_all(x, axis, split_axis=0, concat_axis=0, tiled=True)  55.6 us
    ppermute x8, starting transfers between devices, hop(): lax.ppermute(x, 'grp', [(i, (i + way) % owners) for i in range(owners)])  11.4 us
    ppermute x8, waiting for transfers between devices, hop(): lax.ppermute(x, 'grp', [(i, (i + way) % owners) for i in range(owners)])  10.3 us
    pallas_call x1, Pallas kernels, vectors(): pl.pallas_call(functools.partial(vectors_kernel, owners=owners), out_shap...  4.49 us
    pallas_call x5, Pallas kernels, parts(): pl.pallas_call(functools.partial(parts_kernel, ahead=ahead, owners=owners...  4.27 us
    pallas_call x1, Pallas kernels, pick_rows(): pl.pallas_call(functools.partial(pick_kernel, bring=bring), out_shape=out...  2.55 us
  transfers between devices with their start and end apart: 9, of which 4 were waited for; matrix products, arithmetic and copies ran while one was open for 0% of the time, Pallas kernels for 7%

profile of v12, /device:TPU:1, one launch (start us, length us, event | category | flops | bytes accessed | tf_op | source)
XLA Modules:
  0.0 98.0 jit_solution(17904558683754342590)
XLA Ops:
  0.7 2.5 %pick_rows.5 = (bf16[8,512]{1,0:T(8,128)(2,1)S(1)}, bf16[4,1280,256]{2,1,0:T(8,128)(2,1)S(1)}) custom-call(s32[4]{0:T(128)S(1)} %pad_add_fusion.1.where_from_ref, s32[2,128]{1,0:T(2,128)} %bitcast.40, bf16[4,1280,512]{2,1,0:T(8,128)(2,1)} %prev_ref.5, bf16[4,1280,256]{2,1,0:T(8,128)(2,1)} %refs_0_.1), custom_call_target="tpu_custom_call" | custom-call | flops 131072 | bytes 262144 | tf_op jit(solution)/shard_map/pick_rows/pallas_call | solution.py:100
  3.3 16.1 %all_to_all.30.came_ref = bf16[8,8,512]{2,1,0:T(8,128)(2,1)S(1)} all-to-all(bf16[8,8,512]{2,1,0:T(8,128)(2,1)S(1)} %broadcast_in_dim.12), channel_id=1, replica_groups=mesh['rows'=32,'grp'=8] {'grp'}, dimensions={0} | all-to-all | bytes 131072 | tf_op jit(solution)/shard_map/all_to_all | solution.py:522
  19.3 0.9 spread.5
  20.3 19.3 %all_to_all.31 = bf16[32,24,256]{2,1,0:T(8,128)(2,1)S(1)} all-to-all(bf16[32,24,256]{2,1,0:T(8,128)(2,1)S(1)} %spread.5), channel_id=1, replica_groups=mesh['rows'=32,'grp'=8] {'rows'}, dimensions={0} | all-to-all | bytes 786432 | tf_op jit(solution)/shard_map/all_to_all | solution.py:522
  39.6 1.1 %select_rows.5 = (bf16[256,256]{1,0:T(8,128)(2,1)S(1)}, s32[1]{0:T(128)}) custom-call(s32[1]{0:T(128)} %constant.90.clone.1.round_ref, s32[1,256]{1,0:T(1,128)S(1)} %bitcast.42, bf16[768,256]{1,0:T(8,128)(2,1)S(1)} %bitcast.39, bf16[256,256]{1,0:T(8,128)(2,1)S(1)} %broadcast_in_dim.13.so_far_ref), custom_call_target="tpu_custom_call" | custom-call | flops 100663296 | bytes 393216 | tf_op jit(solution)/shard_map/select_rows/pallas_call | solution.py:147
  40.6 0.6 while.12
  41.4 1.8 %preload.1.first_ref = bf16[2,1280,512]{2,1,0:T(8,128)(2,1)S(1)} custom-call(bf16[4,1280,512]{2,1,0:T(8,128)(2,1)} %get-tuple-element.231, bf16[256,256]{1,0:T(8,128)(2,1)S(1)} %get-tuple-element.116.after_ref.mine_ref), custom_call_target="tpu_custom_call" | custom-call | bytes 2621440 | tf_op jit(solution)/shard_map/preload/pallas_call | solution.py:225
  43.2 4.5 %vectors.1 = (bf16[4,1280,256]{2,1,0:T(8,128)(2,1)}, bf16[4,256,1280]{2,1,0:T(8,128)(2,1)S(1)}, bf16[1280,128]{1,0:T(8,128)(2,1)S(1)}) custom-call(s32[1]{0:T(128)} %bitcast.8.core_ref, s32[1]{0:T(128)} %bitcast.9.me_ref, bf16[4,1280,256]{2,1,0:T(8,128)(2,1)S(1)} %get-tuple-element.109.cols_ref, bf16[2,1280,512]{2,1,0:T(8,128)(2,1)S(1)} %preload.1.first_ref, ...), custom_call_target="tpu_custom_call" | custom-call | flops 2013265920 | bytes 13107200 | tf_op jit(solution)/shard_map/vectors/pallas_call | solution.py:295
  47.7 0.8 parts.5
  48.9 2.4 %collective-permute-start.5 = (bf16[16,4,8,128]{3,2,1,0:T(8,128)(2,1)S(1)}, bf16[16,4,8,128]{3,2,1,0:T(8,128)(2,1)S(1)}, u32[]{:S(2)}, u32[]{:S(2)}) collective-permute-start(bf16[16,4,8,128]{3,2,1,0:T(8,128)(2,1)S(1)} %get-tuple-element.121), channel_id=1, source_target_pairs={{0,7},{1,0},{2,1},{3,2},{4,3},{5,4},{6,5},{7,6},{8,15},{9,8},{10,9... | collective-permute-start | bytes 393224 | tf_op jit(solution)/shard_map/ppermute | solution.py:453
  51.3 1.7 %bring.1.orb_ref = bf16[1280,1024]{1,0:T(8,128)(2,1)S(1)} custom-call(bf16[1280,1024]{1,0:T(8,128)(2,1)} %orb_ref.3, bf16[16,4,8,128]{3,2,1,0:T(8,128)(2,1)S(1)} %get-tuple-element.120.after_ref), custom_call_target="tpu_custom_call" | custom-call | bytes 2621440 | tf_op jit(solution)/shard_map/bring/pallas_call | solution.py:339
  53.0 0.9 parts.9.own_ref
  53.9 0.5 collective-permute-done.1.came_ref
  54.6 2.7 %collective-permute-start.6 = (bf16[32,4,8,128]{3,2,1,0:T(8,128)(2,1)S(1)}, bf16[32,4,8,128]{3,2,1,0:T(8,128)(2,1)S(1)}, u32[]{:S(2)}, u32[]{:S(2)}) collective-permute-start(bf16[32,4,8,128]{3,2,1,0:T(8,128)(2,1)S(1)} %join.3), channel_id=1, source_target_pairs={{0,7},{1,0},{2,1},{3,2},{4,3},{5,4},{6,5},{7,6},{8,15},{9,8},{10,9... | collective-permute-start | bytes 786440 | tf_op jit(solution)/shard_map/ppermute | solution.py:453
  57.3 0.9 parts.8.own_ref
  58.2 4.0 %collective-permute-done.2.came_ref = bf16[32,4,8,128]{3,2,1,0:T(8,128)(2,1)S(1)} collective-permute-done((bf16[32,4,8,128]{3,2,1,0:T(8,128)(2,1)S(1)}, bf16[32,4,8,128]{3,2,1,0:T(8,128)(2,1)S(1)}, u32[]{:S(2)}, u32[]{:S(2)}) %collective-permute-start.2) | collective-permute-done | bytes 262176 | tf_op jit(solution)/shard_map/ppermute | solution.py:453
  62.4 2.9 %collective-permute-start.7 = (bf16[32,4,8,128]{3,2,1,0:T(8,128)(2,1)S(1)}, bf16[32,4,8,128]{3,2,1,0:T(8,128)(2,1)S(1)}, u32[]{:S(2)}, u32[]{:S(2)}) collective-permute-start(bf16[32,4,8,128]{3,2,1,0:T(8,128)(2,1)S(1)} %add.68), channel_id=1, source_target_pairs={{0,7},{1,0},{2,1},{3,2},{4,3},{5,4},{6,5},{7,6},{8,15},{9,8},{10,9... | collective-permute-start | bytes 786440 | tf_op jit(solution)/shard_map/ppermute | solution.py:453
  65.3 0.9 parts.7.own_ref
  66.2 2.9 %collective-permute-done.3.came_ref = bf16[32,4,8,128]{3,2,1,0:T(8,128)(2,1)S(1)} collective-permute-done((bf16[32,4,8,128]{3,2,1,0:T(8,128)(2,1)S(1)}, bf16[32,4,8,128]{3,2,1,0:T(8,128)(2,1)S(1)}, u32[]{:S(2)}, u32[]{:S(2)}) %collective-permute-start.3) | collective-permute-done | bytes 262176 | tf_op jit(solution)/shard_map/ppermute | solution.py:453
  69.3 2.7 %collective-permute-start.8 = (bf16[32,4,8,128]{3,2,1,0:T(8,128)(2,1)S(1)}, bf16[32,4,8,128]{3,2,1,0:T(8,128)(2,1)S(1)}, u32[]{:S(2)}, u32[]{:S(2)}) collective-permute-start(bf16[32,4,8,128]{3,2,1,0:T(8,128)(2,1)S(1)} %add.69), channel_id=1, source_target_pairs={{0,7},{1,0},{2,1},{3,2},{4,3},{5,4},{6,5},{7,6},{8,15},{9,8},{10,9... | collective-permute-start | bytes 786440 | tf_op jit(solution)/shard_map/ppermute | solution.py:453
  72.1 0.9 parts.6
  72.9 2.8 %collective-permute-done.4 = bf16[32,4,8,128]{3,2,1,0:T(8,128)(2,1)S(1)} collective-permute-done((bf16[32,4,8,128]{3,2,1,0:T(8,128)(2,1)S(1)}, bf16[32,4,8,128]{3,2,1,0:T(8,128)(2,1)S(1)}, u32[]{:S(2)}, u32[]{:S(2)}) %collective-permute-start.4) | collective-permute-done | bytes 262176 | tf_op jit(solution)/shard_map/ppermute | solution.py:453
  75.8 20.3 %all_to_all.32 = f32[32,4,8,128]{3,2,1,0:T(8,128)S(1)} all-to-all(f32[32,4,8,128]{3,2,1,0:T(8,128)S(1)} %fusion), channel_id=1, replica_groups=mesh['rows'=32,'grp'=8] {'rows'}, dimensions={0} | all-to-all | bytes 1048576 | tf_op jit(solution)/shard_map/all_to_all | solution.py:522
  96.0 1.8 %final.1 = bf16[8,1024,128]{2,1,0:T(8,128)(2,1)} custom-call(f32[1024,128]{1,0:T(8,128)S(1)} %bitcast.38, bf16[128,1024]{1,0:T(8,128)(2,1)S(1)} %copy-done), custom_call_target="tpu_custom_call" | custom-call | flops 536870912 | bytes 2621440 | tf_op jit(solution)/shard_map/final/pallas_call | solution.py:502
  (26 shorter events, 1.2 us)
Async XLA Ops:
  0.7 18.6 %copy-start.2 = (s32[256]{0:T(256)S(1)}, s32[256]{0:T(256)}, u32[]{:S(2)}) copy-start(s32[256]{0:T(256)} %param.10) | copy-start | bytes 3076
  41.3 1.9 %collective-permute-start = (bf16[256,256]{1,0:T(8,128)(2,1)S(1)}, bf16[256,256]{1,0:T(8,128)(2,1)S(1)}, u32[]{:S(2)}, u32[]{:S(2)}) collective-permute-start(bf16[256,256]{1,0:T(8,128)(2,1)S(1)} %get-tuple-element.116.after_ref.mine_ref), channel_id=1, source_target_pairs={{0,8},{8,0},{16,24},{24,16},{32,40},{40,32},{48,56},{56,48},{64,72... | collective-permute-start | bytes 393224 | tf_op jit(solution)/shard_map/ppermute | solution.py:548
  41.4 1.8 %copy-start.1 = (bf16[256,256]{1,0:T(8,128)(2,1)S(1)}, bf16[256,256]{1,0:T(8,128)(2,1)}, u32[]{:S(2)}) copy-start(bf16[256,256]{1,0:T(8,128)(2,1)} %inv_ref.1) | copy-start | bytes 393220
  48.5 5.9 %collective-permute-start.1 = (bf16[16,4,8,128]{3,2,1,0:T(8,128)(2,1)S(1)}, bf16[16,4,8,128]{3,2,1,0:T(8,128)(2,1)S(1)}, u32[]{:S(2)}, u32[]{:S(2)}) collective-permute-start(bf16[16,4,8,128]{3,2,1,0:T(8,128)(2,1)S(1)} %get-tuple-element.120.after_ref), channel_id=1, source_target_pairs={{0,1},{1,2},{2,3},{3,4},{4,5},{5,6},{6,7},{7,0},{8,9},{9,10},{10,1... | collective-permute-start | bytes 393224 | tf_op jit(solution)/shard_map/ppermute | solution.py:453
  48.9 5.7 %collective-permute-start.5 = (bf16[16,4,8,128]{3,2,1,0:T(8,128)(2,1)S(1)}, bf16[16,4,8,128]{3,2,1,0:T(8,128)(2,1)S(1)}, u32[]{:S(2)}, u32[]{:S(2)}) collective-permute-start(bf16[16,4,8,128]{3,2,1,0:T(8,128)(2,1)S(1)} %get-tuple-element.121), channel_id=1, source_target_pairs={{0,7},{1,0},{2,1},{3,2},{4,3},{5,4},{6,5},{7,6},{8,15},{9,8},{10,9... | collective-permute-start | bytes 393224 | tf_op jit(solution)/shard_map/ppermute | solution.py:453
  54.4 7.8 %collective-permute-start.2 = (bf16[32,4,8,128]{3,2,1,0:T(8,128)(2,1)S(1)}, bf16[32,4,8,128]{3,2,1,0:T(8,128)(2,1)S(1)}, u32[]{:S(2)}, u32[]{:S(2)}) collective-permute-start(bf16[32,4,8,128]{3,2,1,0:T(8,128)(2,1)S(1)} %join.2), channel_id=1, source_target_pairs={{0,1},{1,2},{2,3},{3,4},{4,5},{5,6},{6,7},{7,0},{8,9},{9,10},{10,1... | collective-permute-start | bytes 786440 | tf_op jit(solution)/shard_map/ppermute | solution.py:453
  54.6 7.8 %collective-permute-start.6 = (bf16[32,4,8,128]{3,2,1,0:T(8,128)(2,1)S(1)}, bf16[32,4,8,128]{3,2,1,0:T(8,128)(2,1)S(1)}, u32[]{:S(2)}, u32[]{:S(2)}) collective-permute-start(bf16[32,4,8,128]{3,2,1,0:T(8,128)(2,1)S(1)} %join.3), channel_id=1, source_target_pairs={{0,7},{1,0},{2,1},{3,2},{4,3},{5,4},{6,5},{7,6},{8,15},{9,8},{10,9... | collective-permute-start | bytes 786440 | tf_op jit(solution)/shard_map/ppermute | solution.py:453
  62.3 6.8 %collective-permute-start.3 = (bf16[32,4,8,128]{3,2,1,0:T(8,128)(2,1)S(1)}, bf16[32,4,8,128]{3,2,1,0:T(8,128)(2,1)S(1)}, u32[]{:S(2)}, u32[]{:S(2)}) collective-permute-start(bf16[32,4,8,128]{3,2,1,0:T(8,128)(2,1)S(1)} %add.66), channel_id=1, source_target_pairs={{0,1},{1,2},{2,3},{3,4},{4,5},{5,6},{6,7},{7,0},{8,9},{9,10},{10,1... | collective-permute-start | bytes 786440 | tf_op jit(solution)/shard_map/ppermute | solution.py:453
  62.4 6.8 %collective-permute-start.7 = (bf16[32,4,8,128]{3,2,1,0:T(8,128)(2,1)S(1)}, bf16[32,4,8,128]{3,2,1,0:T(8,128)(2,1)S(1)}, u32[]{:S(2)}, u32[]{:S(2)}) collective-permute-start(bf16[32,4,8,128]{3,2,1,0:T(8,128)(2,1)S(1)} %add.68), channel_id=1, source_target_pairs={{0,7},{1,0},{2,1},{3,2},{4,3},{5,4},{6,5},{7,6},{8,15},{9,8},{10,9... | collective-permute-start | bytes 786440 | tf_op jit(solution)/shard_map/ppermute | solution.py:453
  69.2 6.5 %collective-permute-start.4 = (bf16[32,4,8,128]{3,2,1,0:T(8,128)(2,1)S(1)}, bf16[32,4,8,128]{3,2,1,0:T(8,128)(2,1)S(1)}, u32[]{:S(2)}, u32[]{:S(2)}) collective-permute-start(bf16[32,4,8,128]{3,2,1,0:T(8,128)(2,1)S(1)} %add.67), channel_id=1, source_target_pairs={{0,1},{1,2},{2,3},{3,4},{4,5},{5,6},{6,7},{7,0},{8,9},{9,10},{10,1... | collective-permute-start | bytes 786440 | tf_op jit(solution)/shard_map/ppermute | solution.py:453
  69.3 6.4 %collective-permute-start.8 = (bf16[32,4,8,128]{3,2,1,0:T(8,128)(2,1)S(1)}, bf16[32,4,8,128]{3,2,1,0:T(8,128)(2,1)S(1)}, u32[]{:S(2)}, u32[]{:S(2)}) collective-permute-start(bf16[32,4,8,128]{3,2,1,0:T(8,128)(2,1)S(1)} %add.69), channel_id=1, source_target_pairs={{0,7},{1,0},{2,1},{3,2},{4,3},{5,4},{6,5},{7,6},{8,15},{9,8},{10,9... | collective-permute-start | bytes 786440 | tf_op jit(solution)/shard_map/ppermute | solution.py:453
  72.9 23.1 %copy-start = (bf16[128,1024]{1,0:T(8,128)(2,1)S(1)}, bf16[128,1024]{1,0:T(8,128)(2,1)}, u32[]{:S(2)}) copy-start(bf16[128,1024]{1,0:T(8,128)(2,1)} %slab_ref.1) | copy-start | bytes 786436

commit v13 on v12

--- a/solution.py
+++ b/solution.py
@@ -355,7 +355,7 @@
     keep, width = out_refs[0].shape[-2:]
     columns = [orb_ref[...]] if len(out_refs) == 2 else []
     for a in ahead[: 0 if columns else None]:
-        start = pl.multiple_of(lax.rem(me_ref[0] + a, owners) * width, width)
+        start = pl.multiple_of(lax.rem(me_ref[0] + me_ref[1] * a + owners, owners) * width, width)
         columns.append(orb_ref[:, pl.ds(start, width)])
     columns = columns[0] if len(columns) == 1 else jnp.concatenate(columns, axis=1)
     for m in range(mu):
@@ -450,7 +450,12 @@
     far = owners // 2
 
     def hop(x, way):
-        return lax.ppermute(x, "grp", [(i, (i + way) % owners) for i in range(owners)])
+        pairs = [
+            (r * owners + g, r * owners + (g + (way if r % 2 == 0 else -way)) % owners)
+            for r in range(dests)
+            for g in range(owners)
+        ]
+        return lax.ppermute(x, ("rows", "grp"), pairs)
 
     right, left = parts(me, turned, columns, (far,), owners, dests, send=True)
     orbitals = bring(orbitals, right)
@@ -555,7 +560,8 @@
     )
     mine, other, close = pivot_halves(n_rows, n_grp, pivots, previous, pivot_columns)
     core = (lax.axis_index("rows") % 2).reshape(1).astype(jnp.int32)
-    me = lax.axis_index("grp").reshape(1).astype(jnp.int32)
+    way = 1 - 2 * (lax.axis_index("rows") % 2)
+    me = jnp.stack([lax.axis_index("grp"), way]).astype(jnp.int32)
     first = preload(previous, previous.shape[0] // 2, mine)
     new_vectors, turned, far = vectors(
         core, me, close, first, previous, mine, other, pivot_inverse, orbitals, n_grp

time: 98.4 us -> 102 us (1.037)
  Pallas kernels: 18.8 us -> 22.1 us
  starting transfers between devices: 11.5 us -> 9.84 us
  blocking collectives: 55.6 us -> 56.8 us
    pallas_call x5, Pallas kernels: 4.27 us -> 7.02 us  [parts(): pl.pallas_call(functools.partial(parts_kernel, ahead=ahead, owners=owners...]
    ppermute x8, starting transfers between devices: 11.4 us -> 9.75 us  [hop(): return lax.ppermute(x, ('rows', 'grp'), pairs)]
    all_to_all x3, blocking collectives: 55.6 us -> 56.8 us  [exchange(): return lax.all_to_all(x, axis, split_axis=0, concat_axis=0, tiled=True)]
  transfers between devices with their start and end apart: 9 -> 9, of which waited for: 4 -> 6; matrix products, arithmetic and copies ran while one was open for 0% -> 0% of each run, Pallas kernels for 7% -> 9%
where the time goes in v13:
time: 102 us; the launch traced here: 101 us
  blocking collectives  56.8 us (56%)
  Pallas kernels  22.1 us (22%)
  waiting for transfers between devices  10.6 us (10%)
  starting transfers between devices  9.84 us (10%)
    all_to_all x3, blocking collectives, exchange(): return lax.all_to_all(x, axis, split_axis=0, concat_axis=0, tiled=True)  56.8 us
    ppermute x8, waiting for transfers between devices, hop(): return lax.ppermute(x, ('rows', 'grp'), pairs)  10.6 us
    ppermute x8, starting transfers between devices, hop(): return lax.ppermute(x, ('rows', 'grp'), pairs)  9.75 us
    pallas_call x5, Pallas kernels, parts(): pl.pallas_call(functools.partial(parts_kernel, ahead=ahead, owners=owners...  7.02 us
    pallas_call x1, Pallas kernels, vectors(): pl.pallas_call(functools.partial(vectors_kernel, owners=owners), out_shap...  5.03 us
    pallas_call x1, Pallas kernels, pick_rows(): pl.pallas_call(functools.partial(pick_kernel, bring=bring), out_shape=out...  2.55 us
  transfers between devices with their start and end apart: 9, of which 6 were waited for; matrix products, arithmetic and copies ran while one was open for 0% of the time, Pallas kernels for 9%

profile of v13, /device:TPU:1, one launch (start us, length us, event | category | flops | bytes accessed | tf_op | source)
XLA Modules:
  0.0 101.2 jit_solution(14717916900074535453)
XLA Ops:
  0.7 2.5 %pick_rows.5 = (bf16[8,512]{1,0:T(8,128)(2,1)S(1)}, bf16[4,1280,256]{2,1,0:T(8,128)(2,1)S(1)}) custom-call(s32[4]{0:T(128)S(1)} %pad_add_fusion.2.where_from_ref, s32[2,128]{1,0:T(2,128)} %bitcast.41, bf16[4,1280,512]{2,1,0:T(8,128)(2,1)} %prev_ref.5, bf16[4,1280,256]{2,1,0:T(8,128)(2,1)} %refs_0_.1), custom_call_target="tpu_custom_call" | custom-call | flops 131072 | bytes 262144 | tf_op jit(solution)/shard_map/pick_rows/pallas_call | solution.py:100
  3.3 16.1 %all_to_all.30.came_ref = bf16[8,8,512]{2,1,0:T(8,128)(2,1)S(1)} all-to-all(bf16[8,8,512]{2,1,0:T(8,128)(2,1)S(1)} %broadcast_in_dim.12), channel_id=1, replica_groups=mesh['rows'=32,'grp'=8] {'grp'}, dimensions={0} | all-to-all | bytes 131072 | tf_op jit(solution)/shard_map/all_to_all | solution.py:527
  20.3 19.3 %all_to_all.31 = bf16[32,24,256]{2,1,0:T(8,128)(2,1)S(1)} all-to-all(bf16[32,24,256]{2,1,0:T(8,128)(2,1)S(1)} %spread.5), channel_id=1, replica_groups=mesh['rows'=32,'grp'=8] {'rows'}, dimensions={0} | all-to-all | bytes 786432 | tf_op jit(solution)/shard_map/all_to_all | solution.py:527
  39.6 1.1 %select_rows.5 = (bf16[256,256]{1,0:T(8,128)(2,1)S(1)}, s32[1]{0:T(128)}) custom-call(s32[1]{0:T(128)} %constant.92.clone.1.round_ref, s32[1,256]{1,0:T(1,128)S(1)} %bitcast.43, bf16[768,256]{1,0:T(8,128)(2,1)S(1)} %bitcast.40, bf16[256,256]{1,0:T(8,128)(2,1)S(1)} %broadcast_in_dim.13.so_far_ref), custom_call_target="tpu_custom_call" | custom-call | flops 100663296 | bytes 393216 | tf_op jit(solution)/shard_map/select_rows/pallas_call | solution.py:147
  41.5 1.8 %preload.1.first_ref = bf16[2,1280,512]{2,1,0:T(8,128)(2,1)S(1)} custom-call(bf16[4,1280,512]{2,1,0:T(8,128)(2,1)} %get-tuple-element.231, bf16[256,256]{1,0:T(8,128)(2,1)S(1)} %get-tuple-element.116.after_ref.mine_ref), custom_call_target="tpu_custom_call" | custom-call | bytes 2621440 | tf_op jit(solution)/shard_map/preload/pallas_call | solution.py:225
  43.2 5.0 %vectors.1 = (bf16[4,1280,256]{2,1,0:T(8,128)(2,1)}, bf16[4,256,1280]{2,1,0:T(8,128)(2,1)S(1)}, bf16[1280,128]{1,0:T(8,128)(2,1)S(1)}) custom-call(s32[1]{0:T(128)} %bitcast.8.core_ref, s32[2]{0:T(128)S(1)} %pad_add_fusion.1.me_ref, bf16[4,1280,256]{2,1,0:T(8,128)(2,1)S(1)} %get-tuple-element.109.cols_ref, bf16[2,1280,512]{2,1,0:T(8,128)(2,1)S(1)} %preload.1.first_ref, ...), custom_call_target="tpu_custom_call" | custom-call | flops 2013265920 | bytes 13107200 | tf_op jit(solution)/shard_map/vectors/pallas_call | solution.py:295
  48.3 1.4 %parts.5 = (bf16[16,4,8,128]{3,2,1,0:T(8,128)(2,1)S(1)}, bf16[16,4,8,128]{3,2,1,0:T(8,128)(2,1)S(1)}) custom-call(s32[2]{0:T(128)S(1)} %pad_add_fusion.1.me_ref, bf16[4,256,1280]{2,1,0:T(8,128)(2,1)S(1)} %get-tuple-element.118.turned_ref, bf16[1280,128]{1,0:T(8,128)(2,1)S(1)} %get-tuple-element.119.orb_ref), custom_call_target="tpu_custom_call" | custom-call | flops 335544320 | bytes 2621440 | tf_op jit(solution)/shard_map/parts/pallas_call | solution.py:384
  49.7 1.5 %collective-permute-start.5 = (bf16[16,4,8,128]{3,2,1,0:T(8,128)(2,1)S(1)}, bf16[16,4,8,128]{3,2,1,0:T(8,128)(2,1)S(1)}, u32[]{:S(2)}, u32[]{:S(2)}) collective-permute-start(bf16[16,4,8,128]{3,2,1,0:T(8,128)(2,1)S(1)} %get-tuple-element.121), channel_id=1, source_target_pairs={{0,7},{1,0},{2,1},{3,2},{4,3},{5,4},{6,5},{7,6},{8,9},{9,10},{10,1... | collective-permute-start | bytes 393224 | tf_op jit(solution)/shard_map/ppermute | solution.py:458
  51.2 1.7 %bring.1.orb_ref = bf16[1280,1024]{1,0:T(8,128)(2,1)S(1)} custom-call(bf16[1280,1024]{1,0:T(8,128)(2,1)} %orb_ref.3, bf16[16,4,8,128]{3,2,1,0:T(8,128)(2,1)S(1)} %get-tuple-element.120.after_ref), custom_call_target="tpu_custom_call" | custom-call | bytes 2621440 | tf_op jit(solution)/shard_map/bring/pallas_call | solution.py:339
  52.9 1.4 %parts.9.own_ref = f32[2,32,4,8,128]{4,3,2,1,0:T(8,128)S(1)} custom-call(s32[2]{0:T(128)S(1)} %pad_add_fusion.1.me_ref, bf16[4,256,1280]{2,1,0:T(8,128)(2,1)S(1)} %get-tuple-element.118.turned_ref, bf16[1280,1024]{1,0:T(8,128)(2,1)S(1)} %bring.1.orb_ref), custom_call_target="tpu_custom_call" | custom-call | flops 671088640 | bytes 2621440 | tf_op jit(solution)/shard_map/parts/pallas_call | solution.py:384
  54.4 1.4 %collective-permute-start.2 = (bf16[32,4,8,128]{3,2,1,0:T(8,128)(2,1)S(1)}, bf16[32,4,8,128]{3,2,1,0:T(8,128)(2,1)S(1)}, u32[]{:S(2)}, u32[]{:S(2)}) collective-permute-start(bf16[32,4,8,128]{3,2,1,0:T(8,128)(2,1)S(1)} %join.2), channel_id=1, source_target_pairs={{0,1},{1,2},{2,3},{3,4},{4,5},{5,6},{6,7},{7,0},{8,15},{9,8},{10,9... | collective-permute-start | bytes 786440 | tf_op jit(solution)/shard_map/ppermute | solution.py:458
  56.4 1.4 %parts.8.own_ref = f32[2,32,4,8,128]{4,3,2,1,0:T(8,128)S(1)} custom-call(s32[2]{0:T(128)S(1)} %pad_add_fusion.1.me_ref, bf16[4,256,1280]{2,1,0:T(8,128)(2,1)S(1)} %get-tuple-element.118.turned_ref, bf16[1280,1024]{1,0:T(8,128)(2,1)S(1)} %bring.1.orb_ref), custom_call_target="tpu_custom_call" | custom-call | flops 671088640 | bytes 2621440 | tf_op jit(solution)/shard_map/parts/pallas_call | solution.py:384
  57.8 1.9 %collective-permute-done.2.came_ref = bf16[32,4,8,128]{3,2,1,0:T(8,128)(2,1)S(1)} collective-permute-done((bf16[32,4,8,128]{3,2,1,0:T(8,128)(2,1)S(1)}, bf16[32,4,8,128]{3,2,1,0:T(8,128)(2,1)S(1)}, u32[]{:S(2)}, u32[]{:S(2)}) %collective-permute-start.2) | collective-permute-done | bytes 262176 | tf_op jit(solution)/shard_map/ppermute | solution.py:458
  59.8 2.6 %collective-permute-start.3 = (bf16[32,4,8,128]{3,2,1,0:T(8,128)(2,1)S(1)}, bf16[32,4,8,128]{3,2,1,0:T(8,128)(2,1)S(1)}, u32[]{:S(2)}, u32[]{:S(2)}) collective-permute-start(bf16[32,4,8,128]{3,2,1,0:T(8,128)(2,1)S(1)} %add.69), channel_id=1, source_target_pairs={{0,1},{1,2},{2,3},{3,4},{4,5},{5,6},{6,7},{7,0},{8,15},{9,8},{10,9... | collective-permute-start | bytes 786440 | tf_op jit(solution)/shard_map/ppermute | solution.py:458
  62.3 1.4 %collective-permute-done.6.came_ref = bf16[32,4,8,128]{3,2,1,0:T(8,128)(2,1)S(1)} collective-permute-done((bf16[32,4,8,128]{3,2,1,0:T(8,128)(2,1)S(1)}, bf16[32,4,8,128]{3,2,1,0:T(8,128)(2,1)S(1)}, u32[]{:S(2)}, u32[]{:S(2)}) %collective-permute-start.6) | collective-permute-done | bytes 262176 | tf_op jit(solution)/shard_map/ppermute | solution.py:458
  64.2 1.4 %parts.7.own_ref = f32[2,32,4,8,128]{4,3,2,1,0:T(8,128)S(1)} custom-call(s32[2]{0:T(128)S(1)} %pad_add_fusion.1.me_ref, bf16[4,256,1280]{2,1,0:T(8,128)(2,1)S(1)} %get-tuple-element.118.turned_ref, bf16[1280,1024]{1,0:T(8,128)(2,1)S(1)} %bring.1.orb_ref), custom_call_target="tpu_custom_call" | custom-call | flops 671088640 | bytes 2621440 | tf_op jit(solution)/shard_map/parts/pallas_call | solution.py:384
  65.6 1.1 %collective-permute-done.3.came_ref = bf16[32,4,8,128]{3,2,1,0:T(8,128)(2,1)S(1)} collective-permute-done((bf16[32,4,8,128]{3,2,1,0:T(8,128)(2,1)S(1)}, bf16[32,4,8,128]{3,2,1,0:T(8,128)(2,1)S(1)}, u32[]{:S(2)}, u32[]{:S(2)}) %collective-permute-start.3) | collective-permute-done | bytes 262176 | tf_op jit(solution)/shard_map/ppermute | solution.py:458
  66.8 3.2 %collective-permute-start.4 = (bf16[32,4,8,128]{3,2,1,0:T(8,128)(2,1)S(1)}, bf16[32,4,8,128]{3,2,1,0:T(8,128)(2,1)S(1)}, u32[]{:S(2)}, u32[]{:S(2)}) collective-permute-start(bf16[32,4,8,128]{3,2,1,0:T(8,128)(2,1)S(1)} %add.70), channel_id=1, source_target_pairs={{0,1},{1,2},{2,3},{3,4},{4,5},{5,6},{6,7},{7,0},{8,15},{9,8},{10,9... | collective-permute-start | bytes 786440 | tf_op jit(solution)/shard_map/ppermute | solution.py:458
  70.0 1.1 %collective-permute-done.7.came_ref = bf16[32,4,8,128]{3,2,1,0:T(8,128)(2,1)S(1)} collective-permute-done((bf16[32,4,8,128]{3,2,1,0:T(8,128)(2,1)S(1)}, bf16[32,4,8,128]{3,2,1,0:T(8,128)(2,1)S(1)}, u32[]{:S(2)}, u32[]{:S(2)}) %collective-permute-start.7) | collective-permute-done | bytes 262176 | tf_op jit(solution)/shard_map/ppermute | solution.py:458
  71.3 1.4 %parts.6 = f32[1,32,4,8,128]{4,3,2,1,0:T(8,128)S(1)} custom-call(s32[2]{0:T(128)S(1)} %pad_add_fusion.1.me_ref, bf16[4,256,1280]{2,1,0:T(8,128)(2,1)S(1)} %get-tuple-element.118.turned_ref, bf16[1280,1024]{1,0:T(8,128)(2,1)S(1)} %bring.1.orb_ref), custom_call_target="tpu_custom_call" | custom-call | flops 335544320 | bytes 2621440 | tf_op jit(solution)/shard_map/parts/pallas_call | solution.py:384
  72.7 3.1 %collective-permute-done.4 = bf16[32,4,8,128]{3,2,1,0:T(8,128)(2,1)S(1)} collective-permute-done((bf16[32,4,8,128]{3,2,1,0:T(8,128)(2,1)S(1)}, bf16[32,4,8,128]{3,2,1,0:T(8,128)(2,1)S(1)}, u32[]{:S(2)}, u32[]{:S(2)}) %collective-permute-start.4) | collective-permute-done | bytes 262176 | tf_op jit(solution)/shard_map/ppermute | solution.py:458
  75.8 1.9 %collective-permute-done.8 = bf16[32,4,8,128]{3,2,1,0:T(8,128)(2,1)S(1)} collective-permute-done((bf16[32,4,8,128]{3,2,1,0:T(8,128)(2,1)S(1)}, bf16[32,4,8,128]{3,2,1,0:T(8,128)(2,1)S(1)}, u32[]{:S(2)}, u32[]{:S(2)}) %collective-permute-start.8) | collective-permute-done | bytes 262176 | tf_op jit(solution)/shard_map/ppermute | solution.py:458
  77.8 21.5 %all_to_all.32 = f32[32,4,8,128]{3,2,1,0:T(8,128)S(1)} all-to-all(f32[32,4,8,128]{3,2,1,0:T(8,128)S(1)} %fusion), channel_id=1, replica_groups=mesh['rows'=32,'grp'=8] {'rows'}, dimensions={0} | all-to-all | bytes 1048576 | tf_op jit(solution)/shard_map/all_to_all | solution.py:527
  99.2 1.8 %final.1 = bf16[8,1024,128]{2,1,0:T(8,128)(2,1)} custom-call(f32[1024,128]{1,0:T(8,128)S(1)} %bitcast.39, bf16[128,1024]{1,0:T(8,128)(2,1)S(1)} %copy-done), custom_call_target="tpu_custom_call" | custom-call | flops 536870912 | bytes 2621440 | tf_op jit(solution)/shard_map/final/pallas_call | solution.py:507
  (27 shorter events, 3.3 us)
Async XLA Ops:
  0.7 18.6 %copy-start.2 = (s32[256]{0:T(256)S(1)}, s32[256]{0:T(256)}, u32[]{:S(2)}) copy-start(s32[256]{0:T(256)} %param.10) | copy-start | bytes 3076
  41.3 2.0 %collective-permute-start = (bf16[256,256]{1,0:T(8,128)(2,1)S(1)}, bf16[256,256]{1,0:T(8,128)(2,1)S(1)}, u32[]{:S(2)}, u32[]{:S(2)}) collective-permute-start(bf16[256,256]{1,0:T(8,128)(2,1)S(1)} %get-tuple-element.116.after_ref.mine_ref), channel_id=1, source_target_pairs={{0,8},{8,0},{16,24},{24,16},{32,40},{40,32},{48,56},{56,48},{64,72... | collective-permute-start | bytes 393224 | tf_op jit(solution)/shard_map/ppermute | solution.py:553
  41.5 1.8 %copy-start.1 = (bf16[256,256]{1,0:T(8,128)(2,1)S(1)}, bf16[256,256]{1,0:T(8,128)(2,1)}, u32[]{:S(2)}) copy-start(bf16[256,256]{1,0:T(8,128)(2,1)} %inv_ref.1) | copy-start | bytes 393220
  49.7 4.7 %collective-permute-start.1 = (bf16[16,4,8,128]{3,2,1,0:T(8,128)(2,1)S(1)}, bf16[16,4,8,128]{3,2,1,0:T(8,128)(2,1)S(1)}, u32[]{:S(2)}, u32[]{:S(2)}) collective-permute-start(bf16[16,4,8,128]{3,2,1,0:T(8,128)(2,1)S(1)} %get-tuple-element.120.after_ref), channel_id=1, source_target_pairs={{0,1},{1,2},{2,3},{3,4},{4,5},{5,6},{6,7},{7,0},{8,15},{9,8},{10,9... | collective-permute-start | bytes 393224 | tf_op jit(solution)/shard_map/ppermute | solution.py:458
  49.7 6.0 %collective-permute-start.5 = (bf16[16,4,8,128]{3,2,1,0:T(8,128)(2,1)S(1)}, bf16[16,4,8,128]{3,2,1,0:T(8,128)(2,1)S(1)}, u32[]{:S(2)}, u32[]{:S(2)}) collective-permute-start(bf16[16,4,8,128]{3,2,1,0:T(8,128)(2,1)S(1)} %get-tuple-element.121), channel_id=1, source_target_pairs={{0,7},{1,0},{2,1},{3,2},{4,3},{5,4},{6,5},{7,6},{8,9},{9,10},{10,1... | collective-permute-start | bytes 393224 | tf_op jit(solution)/shard_map/ppermute | solution.py:458
  54.4 5.3 %collective-permute-start.2 = (bf16[32,4,8,128]{3,2,1,0:T(8,128)(2,1)S(1)}, bf16[32,4,8,128]{3,2,1,0:T(8,128)(2,1)S(1)}, u32[]{:S(2)}, u32[]{:S(2)}) collective-permute-start(bf16[32,4,8,128]{3,2,1,0:T(8,128)(2,1)S(1)} %join.2), channel_id=1, source_target_pairs={{0,1},{1,2},{2,3},{3,4},{4,5},{5,6},{6,7},{7,0},{8,15},{9,8},{10,9... | collective-permute-start | bytes 786440 | tf_op jit(solution)/shard_map/ppermute | solution.py:458
  55.8 7.9 %collective-permute-start.6 = (bf16[32,4,8,128]{3,2,1,0:T(8,128)(2,1)S(1)}, bf16[32,4,8,128]{3,2,1,0:T(8,128)(2,1)S(1)}, u32[]{:S(2)}, u32[]{:S(2)}) collective-permute-start(bf16[32,4,8,128]{3,2,1,0:T(8,128)(2,1)S(1)} %join.3), channel_id=1, source_target_pairs={{0,7},{1,0},{2,1},{3,2},{4,3},{5,4},{6,5},{7,6},{8,9},{9,10},{10,1... | collective-permute-start | bytes 786440 | tf_op jit(solution)/shard_map/ppermute | solution.py:458
  59.8 7.0 %collective-permute-start.3 = (bf16[32,4,8,128]{3,2,1,0:T(8,128)(2,1)S(1)}, bf16[32,4,8,128]{3,2,1,0:T(8,128)(2,1)S(1)}, u32[]{:S(2)}, u32[]{:S(2)}) collective-permute-start(bf16[32,4,8,128]{3,2,1,0:T(8,128)(2,1)S(1)} %add.69), channel_id=1, source_target_pairs={{0,1},{1,2},{2,3},{3,4},{4,5},{5,6},{6,7},{7,0},{8,15},{9,8},{10,9... | collective-permute-start | bytes 786440 | tf_op jit(solution)/shard_map/ppermute | solution.py:458
  63.8 7.3 %collective-permute-start.7 = (bf16[32,4,8,128]{3,2,1,0:T(8,128)(2,1)S(1)}, bf16[32,4,8,128]{3,2,1,0:T(8,128)(2,1)S(1)}, u32[]{:S(2)}, u32[]{:S(2)}) collective-permute-start(bf16[32,4,8,128]{3,2,1,0:T(8,128)(2,1)S(1)} %add.71), channel_id=1, source_target_pairs={{0,7},{1,0},{2,1},{3,2},{4,3},{5,4},{6,5},{7,6},{8,9},{9,10},{10,1... | collective-permute-start | bytes 786440 | tf_op jit(solution)/shard_map/ppermute | solution.py:458
  66.8 9.0 %collective-permute-start.4 = (bf16[32,4,8,128]{3,2,1,0:T(8,128)(2,1)S(1)}, bf16[32,4,8,128]{3,2,1,0:T(8,128)(2,1)S(1)}, u32[]{:S(2)}, u32[]{:S(2)}) collective-permute-start(bf16[32,4,8,128]{3,2,1,0:T(8,128)(2,1)S(1)} %add.70), channel_id=1, source_target_pairs={{0,1},{1,2},{2,3},{3,4},{4,5},{5,6},{6,7},{7,0},{8,15},{9,8},{10,9... | collective-permute-start | bytes 786440 | tf_op jit(solution)/shard_map/ppermute | solution.py:458
  71.2 6.5 %collective-permute-start.8 = (bf16[32,4,8,128]{3,2,1,0:T(8,128)(2,1)S(1)}, bf16[32,4,8,128]{3,2,1,0:T(8,128)(2,1)S(1)}, u32[]{:S(2)}, u32[]{:S(2)}) collective-permute-start(bf16[32,4,8,128]{3,2,1,0:T(8,128)(2,1)S(1)} %add.72), channel_id=1, source_target_pairs={{0,7},{1,0},{2,1},{3,2},{4,3},{5,4},{6,5},{7,6},{8,9},{9,10},{10,1... | collective-permute-start | bytes 786440 | tf_op jit(solution)/shard_map/ppermute | solution.py:458
  72.7 26.6 %copy-start = (bf16[128,1024]{1,0:T(8,128)(2,1)S(1)}, bf16[128,1024]{1,0:T(8,128)(2,1)}, u32[]{:S(2)}) copy-start(bf16[128,1024]{1,0:T(8,128)(2,1)} %slab_ref.1) | copy-start | bytes 786436

commit v14 on v12

--- a/solution.py
+++ b/solution.py
@@ -19,8 +19,12 @@
     if bring:
         cols_ref, out_ref, close_ref, acc_ref, held, sems, rows_ref, close_sems = refs
         copies = [
-            pltpu.make_async_copy(cols_ref.at[m], close_ref.at[m], close_sems.at[m])
+            pltpu.make_async_copy(
+                cols_ref.at[m, pl.ds(h * rows, rows)], close_ref.at[m, pl.ds(h * rows, rows)], close_sems.at[m, h]
+            )
+            for rows in (cols_ref.shape[1] // 2,)
             for m in range(cols_ref.shape[0])
+            for h in range(2)
         ]
     else:
         out_ref, acc_ref, held, sems, rows_ref = refs
@@ -96,7 +100,7 @@
     if bring:
         args.append(columns)
         out_shape.append(jax.ShapeDtypeStruct(columns.shape, columns.dtype))
-        scratch.append(pltpu.SemaphoreType.DMA((columns.shape[0],)))
+        scratch.append(pltpu.SemaphoreType.DMA((columns.shape[0], 2)))
     return pl.pallas_call(
         functools.partial(pick_kernel, bring=bring),
         out_shape=out_shape,

time: 98.4 us -> 98.4 us (level)
  no operation moved by 1% of the time
where the time goes in v14:
time: 98.4 us; the launch traced here: 98 us
  blocking collectives  55.5 us (56%)
  Pallas kernels  18.9 us (19%)
  starting transfers between devices  11.5 us (12%)
  waiting for transfers between devices  10.3 us (10%)
  between operations  1.05 us (1%)
    all_to_all x3, blocking collectives, exchange(): return lax.all_to_all(x, axis, split_axis=0, concat_axis=0, tiled=True)  55.5 us
    ppermute x8, starting transfers between devices, hop(): lax.ppermute(x, 'grp', [(i, (i + way) % owners) for i in range(owners)])  11.4 us
    ppermute x8, waiting for transfers between devices, hop(): lax.ppermute(x, 'grp', [(i, (i + way) % owners) for i in range(owners)])  10.3 us
    pallas_call x1, Pallas kernels, vectors(): pl.pallas_call(functools.partial(vectors_kernel, owners=owners), out_shap...  4.5 us
    pallas_call x5, Pallas kernels, parts(): pl.pallas_call(functools.partial(parts_kernel, ahead=ahead, owners=owners...  4.27 us
    pallas_call x1, Pallas kernels, pick_rows(): pl.pallas_call(functools.partial(pick_kernel, bring=bring), out_shape=out...  2.57 us
  transfers between devices with their start and end apart: 9, of which 4 were waited for; matrix products, arithmetic and copies ran while one was open for 0% of the time, Pallas kernels for 7%

profile of v14, /device:TPU:1, one launch (start us, length us, event | category | flops | bytes accessed | tf_op | source)
XLA Modules:
  0.0 98.0 jit_solution(1257509322604852606)
XLA Ops:
  0.7 2.6 %pick_rows.5 = (bf16[8,512]{1,0:T(8,128)(2,1)S(1)}, bf16[4,1280,256]{2,1,0:T(8,128)(2,1)S(1)}) custom-call(s32[4]{0:T(128)S(1)} %pad_add_fusion.1.where_from_ref, s32[2,128]{1,0:T(2,128)} %bitcast.40, bf16[4,1280,512]{2,1,0:T(8,128)(2,1)} %prev_ref.5, bf16[4,1280,256]{2,1,0:T(8,128)(2,1)} %refs_0_.1), custom_call_target="tpu_custom_call" | custom-call | flops 131072 | bytes 262144 | tf_op jit(solution)/shard_map/pick_rows/pallas_call | solution.py:104
  3.3 16.1 %all_to_all.30.came_ref = bf16[8,8,512]{2,1,0:T(8,128)(2,1)S(1)} all-to-all(bf16[8,8,512]{2,1,0:T(8,128)(2,1)S(1)} %broadcast_in_dim.12), channel_id=1, replica_groups=mesh['rows'=32,'grp'=8] {'grp'}, dimensions={0} | all-to-all | bytes 131072 | tf_op jit(solution)/shard_map/all_to_all | solution.py:526
  19.4 0.9 spread.5
  20.3 19.3 %all_to_all.31 = bf16[32,24,256]{2,1,0:T(8,128)(2,1)S(1)} all-to-all(bf16[32,24,256]{2,1,0:T(8,128)(2,1)S(1)} %spread.5), channel_id=1, replica_groups=mesh['rows'=32,'grp'=8] {'rows'}, dimensions={0} | all-to-all | bytes 786432 | tf_op jit(solution)/shard_map/all_to_all | solution.py:526
  39.6 1.1 %select_rows.5 = (bf16[256,256]{1,0:T(8,128)(2,1)S(1)}, s32[1]{0:T(128)}) custom-call(s32[1]{0:T(128)} %constant.90.clone.1.round_ref, s32[1,256]{1,0:T(1,128)S(1)} %bitcast.42, bf16[768,256]{1,0:T(8,128)(2,1)S(1)} %bitcast.39, bf16[256,256]{1,0:T(8,128)(2,1)S(1)} %broadcast_in_dim.13.so_far_ref), custom_call_target="tpu_custom_call" | custom-call | flops 100663296 | bytes 393216 | tf_op jit(solution)/shard_map/select_rows/pallas_call | solution.py:151
  40.6 0.6 while.12
  41.4 1.8 %preload.1.first_ref = bf16[2,1280,512]{2,1,0:T(8,128)(2,1)S(1)} custom-call(bf16[4,1280,512]{2,1,0:T(8,128)(2,1)} %get-tuple-element.231, bf16[256,256]{1,0:T(8,128)(2,1)S(1)} %get-tuple-element.116.after_ref.mine_ref), custom_call_target="tpu_custom_call" | custom-call | bytes 2621440 | tf_op jit(solution)/shard_map/preload/pallas_call | solution.py:229
  43.2 4.5 %vectors.1 = (bf16[4,1280,256]{2,1,0:T(8,128)(2,1)}, bf16[4,256,1280]{2,1,0:T(8,128)(2,1)S(1)}, bf16[1280,128]{1,0:T(8,128)(2,1)S(1)}) custom-call(s32[1]{0:T(128)} %bitcast.8.core_ref, s32[1]{0:T(128)} %bitcast.9.me_ref, bf16[4,1280,256]{2,1,0:T(8,128)(2,1)S(1)} %get-tuple-element.109.cols_ref, bf16[2,1280,512]{2,1,0:T(8,128)(2,1)S(1)} %preload.1.first_ref, ...), custom_call_target="tpu_custom_call" | custom-call | flops 2013265920 | bytes 13107200 | tf_op jit(solution)/shard_map/vectors/pallas_call | solution.py:299
  47.7 0.8 parts.5
  48.9 2.4 %collective-permute-start.5 = (bf16[16,4,8,128]{3,2,1,0:T(8,128)(2,1)S(1)}, bf16[16,4,8,128]{3,2,1,0:T(8,128)(2,1)S(1)}, u32[]{:S(2)}, u32[]{:S(2)}) collective-permute-start(bf16[16,4,8,128]{3,2,1,0:T(8,128)(2,1)S(1)} %get-tuple-element.121), channel_id=1, source_target_pairs={{0,7},{1,0},{2,1},{3,2},{4,3},{5,4},{6,5},{7,6},{8,15},{9,8},{10,9... | collective-permute-start | bytes 393224 | tf_op jit(solution)/shard_map/ppermute | solution.py:457
  51.3 1.7 %bring.1.orb_ref = bf16[1280,1024]{1,0:T(8,128)(2,1)S(1)} custom-call(bf16[1280,1024]{1,0:T(8,128)(2,1)} %orb_ref.3, bf16[16,4,8,128]{3,2,1,0:T(8,128)(2,1)S(1)} %get-tuple-element.120.after_ref), custom_call_target="tpu_custom_call" | custom-call | bytes 2621440 | tf_op jit(solution)/shard_map/bring/pallas_call | solution.py:343
  53.0 0.9 parts.9.own_ref
  53.9 0.5 collective-permute-done.1.came_ref
  54.6 2.7 %collective-permute-start.6 = (bf16[32,4,8,128]{3,2,1,0:T(8,128)(2,1)S(1)}, bf16[32,4,8,128]{3,2,1,0:T(8,128)(2,1)S(1)}, u32[]{:S(2)}, u32[]{:S(2)}) collective-permute-start(bf16[32,4,8,128]{3,2,1,0:T(8,128)(2,1)S(1)} %join.3), channel_id=1, source_target_pairs={{0,7},{1,0},{2,1},{3,2},{4,3},{5,4},{6,5},{7,6},{8,15},{9,8},{10,9... | collective-permute-start | bytes 786440 | tf_op jit(solution)/shard_map/ppermute | solution.py:457
  57.3 0.9 parts.8.own_ref
  58.2 4.0 %collective-permute-done.2.came_ref = bf16[32,4,8,128]{3,2,1,0:T(8,128)(2,1)S(1)} collective-permute-done((bf16[32,4,8,128]{3,2,1,0:T(8,128)(2,1)S(1)}, bf16[32,4,8,128]{3,2,1,0:T(8,128)(2,1)S(1)}, u32[]{:S(2)}, u32[]{:S(2)}) %collective-permute-start.2) | collective-permute-done | bytes 262176 | tf_op jit(solution)/shard_map/ppermute | solution.py:457
  62.4 2.9 %collective-permute-start.7 = (bf16[32,4,8,128]{3,2,1,0:T(8,128)(2,1)S(1)}, bf16[32,4,8,128]{3,2,1,0:T(8,128)(2,1)S(1)}, u32[]{:S(2)}, u32[]{:S(2)}) collective-permute-start(bf16[32,4,8,128]{3,2,1,0:T(8,128)(2,1)S(1)} %add.68), channel_id=1, source_target_pairs={{0,7},{1,0},{2,1},{3,2},{4,3},{5,4},{6,5},{7,6},{8,15},{9,8},{10,9... | collective-permute-start | bytes 786440 | tf_op jit(solution)/shard_map/ppermute | solution.py:457
  65.4 0.9 parts.7.own_ref
  66.2 2.9 %collective-permute-done.3.came_ref = bf16[32,4,8,128]{3,2,1,0:T(8,128)(2,1)S(1)} collective-permute-done((bf16[32,4,8,128]{3,2,1,0:T(8,128)(2,1)S(1)}, bf16[32,4,8,128]{3,2,1,0:T(8,128)(2,1)S(1)}, u32[]{:S(2)}, u32[]{:S(2)}) %collective-permute-start.3) | collective-permute-done | bytes 262176 | tf_op jit(solution)/shard_map/ppermute | solution.py:457
  69.3 2.7 %collective-permute-start.8 = (bf16[32,4,8,128]{3,2,1,0:T(8,128)(2,1)S(1)}, bf16[32,4,8,128]{3,2,1,0:T(8,128)(2,1)S(1)}, u32[]{:S(2)}, u32[]{:S(2)}) collective-permute-start(bf16[32,4,8,128]{3,2,1,0:T(8,128)(2,1)S(1)} %add.69), channel_id=1, source_target_pairs={{0,7},{1,0},{2,1},{3,2},{4,3},{5,4},{6,5},{7,6},{8,15},{9,8},{10,9... | collective-permute-start | bytes 786440 | tf_op jit(solution)/shard_map/ppermute | solution.py:457
  72.1 0.9 parts.6
  72.9 2.8 %collective-permute-done.4 = bf16[32,4,8,128]{3,2,1,0:T(8,128)(2,1)S(1)} collective-permute-done((bf16[32,4,8,128]{3,2,1,0:T(8,128)(2,1)S(1)}, bf16[32,4,8,128]{3,2,1,0:T(8,128)(2,1)S(1)}, u32[]{:S(2)}, u32[]{:S(2)}) %collective-permute-start.4) | collective-permute-done | bytes 262176 | tf_op jit(solution)/shard_map/ppermute | solution.py:457
  75.8 20.2 %all_to_all.32 = f32[32,4,8,128]{3,2,1,0:T(8,128)S(1)} all-to-all(f32[32,4,8,128]{3,2,1,0:T(8,128)S(1)} %fusion), channel_id=1, replica_groups=mesh['rows'=32,'grp'=8] {'rows'}, dimensions={0} | all-to-all | bytes 1048576 | tf_op jit(solution)/shard_map/all_to_all | solution.py:526
  96.0 1.8 %final.1 = bf16[8,1024,128]{2,1,0:T(8,128)(2,1)} custom-call(f32[1024,128]{1,0:T(8,128)S(1)} %bitcast.38, bf16[128,1024]{1,0:T(8,128)(2,1)S(1)} %copy-done), custom_call_target="tpu_custom_call" | custom-call | flops 536870912 | bytes 2621440 | tf_op jit(solution)/shard_map/final/pallas_call | solution.py:506
  (26 shorter events, 1.2 us)
Async XLA Ops:
  0.7 18.6 %copy-start.2 = (s32[256]{0:T(256)S(1)}, s32[256]{0:T(256)}, u32[]{:S(2)}) copy-start(s32[256]{0:T(256)} %param.10) | copy-start | bytes 3076
  41.3 1.9 %collective-permute-start = (bf16[256,256]{1,0:T(8,128)(2,1)S(1)}, bf16[256,256]{1,0:T(8,128)(2,1)S(1)}, u32[]{:S(2)}, u32[]{:S(2)}) collective-permute-start(bf16[256,256]{1,0:T(8,128)(2,1)S(1)} %get-tuple-element.116.after_ref.mine_ref), channel_id=1, source_target_pairs={{0,8},{8,0},{16,24},{24,16},{32,40},{40,32},{48,56},{56,48},{64,72... | collective-permute-start | bytes 393224 | tf_op jit(solution)/shard_map/ppermute | solution.py:552
  41.4 1.8 %copy-start.1 = (bf16[256,256]{1,0:T(8,128)(2,1)S(1)}, bf16[256,256]{1,0:T(8,128)(2,1)}, u32[]{:S(2)}) copy-start(bf16[256,256]{1,0:T(8,128)(2,1)} %inv_ref.1) | copy-start | bytes 393220
  48.5 5.9 %collective-permute-start.1 = (bf16[16,4,8,128]{3,2,1,0:T(8,128)(2,1)S(1)}, bf16[16,4,8,128]{3,2,1,0:T(8,128)(2,1)S(1)}, u32[]{:S(2)}, u32[]{:S(2)}) collective-permute-start(bf16[16,4,8,128]{3,2,1,0:T(8,128)(2,1)S(1)} %get-tuple-element.120.after_ref), channel_id=1, source_target_pairs={{0,1},{1,2},{2,3},{3,4},{4,5},{5,6},{6,7},{7,0},{8,9},{9,10},{10,1... | collective-permute-start | bytes 393224 | tf_op jit(solution)/shard_map/ppermute | solution.py:457
  48.9 5.7 %collective-permute-start.5 = (bf16[16,4,8,128]{3,2,1,0:T(8,128)(2,1)S(1)}, bf16[16,4,8,128]{3,2,1,0:T(8,128)(2,1)S(1)}, u32[]{:S(2)}, u32[]{:S(2)}) collective-permute-start(bf16[16,4,8,128]{3,2,1,0:T(8,128)(2,1)S(1)} %get-tuple-element.121), channel_id=1, source_target_pairs={{0,7},{1,0},{2,1},{3,2},{4,3},{5,4},{6,5},{7,6},{8,15},{9,8},{10,9... | collective-permute-start | bytes 393224 | tf_op jit(solution)/shard_map/ppermute | solution.py:457
  54.5 7.8 %collective-permute-start.2 = (bf16[32,4,8,128]{3,2,1,0:T(8,128)(2,1)S(1)}, bf16[32,4,8,128]{3,2,1,0:T(8,128)(2,1)S(1)}, u32[]{:S(2)}, u32[]{:S(2)}) collective-permute-start(bf16[32,4,8,128]{3,2,1,0:T(8,128)(2,1)S(1)} %join.2), channel_id=1, source_target_pairs={{0,1},{1,2},{2,3},{3,4},{4,5},{5,6},{6,7},{7,0},{8,9},{9,10},{10,1... | collective-permute-start | bytes 786440 | tf_op jit(solution)/shard_map/ppermute | solution.py:457
  54.6 7.8 %collective-permute-start.6 = (bf16[32,4,8,128]{3,2,1,0:T(8,128)(2,1)S(1)}, bf16[32,4,8,128]{3,2,1,0:T(8,128)(2,1)S(1)}, u32[]{:S(2)}, u32[]{:S(2)}) collective-permute-start(bf16[32,4,8,128]{3,2,1,0:T(8,128)(2,1)S(1)} %join.3), channel_id=1, source_target_pairs={{0,7},{1,0},{2,1},{3,2},{4,3},{5,4},{6,5},{7,6},{8,15},{9,8},{10,9... | collective-permute-start | bytes 786440 | tf_op jit(solution)/shard_map/ppermute | solution.py:457
  62.3 6.8 %collective-permute-start.3 = (bf16[32,4,8,128]{3,2,1,0:T(8,128)(2,1)S(1)}, bf16[32,4,8,128]{3,2,1,0:T(8,128)(2,1)S(1)}, u32[]{:S(2)}, u32[]{:S(2)}) collective-permute-start(bf16[32,4,8,128]{3,2,1,0:T(8,128)(2,1)S(1)} %add.66), channel_id=1, source_target_pairs={{0,1},{1,2},{2,3},{3,4},{4,5},{5,6},{6,7},{7,0},{8,9},{9,10},{10,1... | collective-permute-start | bytes 786440 | tf_op jit(solution)/shard_map/ppermute | solution.py:457
  62.4 6.8 %collective-permute-start.7 = (bf16[32,4,8,128]{3,2,1,0:T(8,128)(2,1)S(1)}, bf16[32,4,8,128]{3,2,1,0:T(8,128)(2,1)S(1)}, u32[]{:S(2)}, u32[]{:S(2)}) collective-permute-start(bf16[32,4,8,128]{3,2,1,0:T(8,128)(2,1)S(1)} %add.68), channel_id=1, source_target_pairs={{0,7},{1,0},{2,1},{3,2},{4,3},{5,4},{6,5},{7,6},{8,15},{9,8},{10,9... | collective-permute-start | bytes 786440 | tf_op jit(solution)/shard_map/ppermute | solution.py:457
  69.2 6.5 %collective-permute-start.4 = (bf16[32,4,8,128]{3,2,1,0:T(8,128)(2,1)S(1)}, bf16[32,4,8,128]{3,2,1,0:T(8,128)(2,1)S(1)}, u32[]{:S(2)}, u32[]{:S(2)}) collective-permute-start(bf16[32,4,8,128]{3,2,1,0:T(8,128)(2,1)S(1)} %add.67), channel_id=1, source_target_pairs={{0,1},{1,2},{2,3},{3,4},{4,5},{5,6},{6,7},{7,0},{8,9},{9,10},{10,1... | collective-permute-start | bytes 786440 | tf_op jit(solution)/shard_map/ppermute | solution.py:457
  69.3 6.4 %collective-permute-start.8 = (bf16[32,4,8,128]{3,2,1,0:T(8,128)(2,1)S(1)}, bf16[32,4,8,128]{3,2,1,0:T(8,128)(2,1)S(1)}, u32[]{:S(2)}, u32[]{:S(2)}) collective-permute-start(bf16[32,4,8,128]{3,2,1,0:T(8,128)(2,1)S(1)} %add.69), channel_id=1, source_target_pairs={{0,7},{1,0},{2,1},{3,2},{4,3},{5,4},{6,5},{7,6},{8,15},{9,8},{10,9... | collective-permute-start | bytes 786440 | tf_op jit(solution)/shard_map/ppermute | solution.py:457
  72.9 23.1 %copy-start = (bf16[128,1024]{1,0:T(8,128)(2,1)S(1)}, bf16[128,1024]{1,0:T(8,128)(2,1)}, u32[]{:S(2)}) copy-start(bf16[128,1024]{1,0:T(8,128)(2,1)} %slab_ref.1) | copy-start | bytes 786436
